TPU v7x, 32 devices: a whole 2x2x4 slice. The times are simulated.
32 devices in a mesh: rows: 16 (over z, y, core), heads: 2 (over x).
Axes of the slice: x: 2, y: 2, z: 4, core: 2. Of those that a mesh axis runs over, the one named last changes fastest.
Arguments:
- features: bfloat16 [8192, 1664], P(('rows', 'heads')), may hold values from -6 to 6
- segment_ids: int32 [8192], P(('rows', 'heads')), may hold values from 0 to 1, as said below
- padding_mask: int32 [8192], P(('rows', 'heads')), may hold values from 0 to 1, as said below
- w_proj: bfloat16 [1664, 1024], replicated, may hold values from -0.15625 to 0.15625
- proj_bias: float32 [1024], replicated, may hold values from -3 to 3
- gain_attn: float32 [1024], replicated, may hold values from 0.1 to 1.9
- w_qkv: bfloat16 [1024, 3, 1024], P(None, None, 'heads'), may hold values from -0.09375 to 0.09375
- w_out: bfloat16 [1024, 1024], P('heads'), may hold values from -3 to 3
- gain_ffn: float32 [1024], replicated, may hold values from 0.1 to 1.9
- w_gate_up: bfloat16 [1024, 2, 2816], P(None, None, 'heads'), may hold values from -0.1875 to 0.1875
- w_down: bfloat16 [2816, 1024], P('heads'), may hold values from -0.109375 to 0.109375
- cotangent: bfloat16 [8192, 1024], P(('rows', 'heads')), may hold values from -6 to 6
Outputs:
- layer_out: bfloat16 [8192, 1024], P(('rows', 'heads'))
- grad_features: float32 [8192, 1664], P(('rows', 'heads'))
- grad_proj: float32 [1664, 1024], replicated
- grad_bias: float32 [1024], replicated
- grad_gain_attn: float32 [1024], replicated
- grad_qkv: float32 [1024, 3, 1024], P(None, None, 'heads')
- grad_out: float32 [1024, 1024], P('heads')
- grad_gain_ffn: float32 [1024], replicated
- grad_gate_up: float32 [1024, 2, 2816], P(None, None, 'heads')
- grad_down: float32 [2816, 1024], P('heads')
Inputs may be any that keep to these rules, and one draw needn't show every extreme that they name: `segment_ids`: within each aligned block of 512 tokens (one packed row) the ids start at 0 and never fall; each pair holds 256 patches followed by its text, and the padding at a row's end has one id of its own. `padding_mask`: in each packed row the ones form a leading run that ends where the row's last whole pair ends; the rest is 0.
All inputs are finite; a program needn't handle non-finite values.
Results may differ from a plain program's by a relative error of at most 0.024.
Values may be sent and summed in bfloat16 or wider, within the bound.
No kernel may reach another device: no remote copies, remote signals or barrier semaphores. Data moves between devices by JAX's collectives and lax.ppermute only.
A program may use at most 128 MiB of HBM per device.

v0:
```python
import jax
import jax.numpy as jnp
from jax import lax
from jax.experimental import pallas as pl
from jax.experimental.pallas import tpu as pltpu
from jax.sharding import PartitionSpec as P

HEAD_DIM = 64


EPSILON = 1e-06
MASKED = -1000000000.0


def gelu_tanh(values):
    return jax.nn.gelu(values, approximate=True)


def contract(left, right, left_dim, right_dim):
    return lax.dot_general(
        left, right, (((left_dim,), (right_dim,)), ((), ())), preferred_element_type=jnp.float32
    )


def swap_rows(value, masks):
    count = lax.axis_size("rows")
    return lax.ppermute(value, "rows", [(r, r ^ masks[r % 2]) for r in range(count)])


def core_swap(value):
    return swap_rows(value, (1, 1))


def peer_swap(value):
    return lax.ppermute(value, "heads", [(0, 1), (1, 0)])


def gather_group(value):
    if lax.axis_size("heads") == 2:
        return jnp.concatenate([value, peer_swap(value)], axis=0)
    return lax.all_gather(value, "heads", axis=0, tiled=True)


def scatter_group(value):
    if lax.axis_size("heads") == 2:
        mine = value.shape[0] // 2
        return value[:mine].astype(jnp.float32) + peer_swap(value[mine:]).astype(jnp.float32)
    return lax.psum_scatter(value, "heads", scatter_dimension=0, tiled=True).astype(jnp.float32)


def to_owners(product, left):
    if lax.axis_size("heads") == 2:
        mine = left.shape[0] // 2
        given = peer_swap(product(left[mine:]).astype(jnp.bfloat16))
        return (given, product(left[:mine]))
    given = lax.psum_scatter(
        product(left).astype(jnp.bfloat16), "heads", scatter_dimension=0, tiled=True
    )
    return (given, jnp.zeros((), jnp.float32))


def columns_to_group(value):
    size = lax.axis_size("heads")
    if size == 2:
        width = value.shape[1] // 2
        place = lax.axis_index("heads")
        mine = lax.dynamic_slice_in_dim(value, place * width, width, 1)
        theirs = lax.dynamic_slice_in_dim(value, (1 - place) * width, width, 1)
        return jnp.concatenate([mine, peer_swap(theirs)], axis=0)
    return lax.all_to_all(value, "heads", 1, 0, tiled=True)


def columns_to_pair(value, axis=1):
    width = value.shape[axis] // 2
    core = lax.axis_index("rows") % 2
    mine = lax.dynamic_slice_in_dim(value, core * width, width, axis)
    theirs = lax.dynamic_slice_in_dim(value, (1 - core) * width, width, axis)
    return jnp.concatenate([mine, core_swap(theirs)], axis=0)


def mixed_columns_to_pair(value, pieces):
    width = value.shape[1] // (2 * pieces)
    core = lax.axis_index("rows") % 2
    mine, theirs = (
        jnp.concatenate(
            [
                lax.dynamic_slice_in_dim(value, (2 * k + which) * width, width, 1)
                for k in range(pieces)
            ],
            axis=1,
        )
        for which in (core, 1 - core)
    )
    return jnp.concatenate([mine, core_swap(theirs)], axis=0)


def with_pair(value):
    return jnp.concatenate([value, core_swap(value)], axis=0)


def plane_steps(same=False):
    bits = (lax.axis_size("rows") // 2).bit_length() - 1
    low = bits // 2

    def line(first, count):
        return [
            ((1 << first, (first,) if count == 1 else (first, first + 1)))
        ] if count == 1 else [
            (1 << first, (first, first + 1)),
            (3 << first, (first + 1,)),
        ]

    near = line(1, low)
    far = line(1 + low, bits - low)

    def weave(one, two):
        one, two, order = list(one), list(two), []
        while one or two:
            if one:
                order.append(one.pop(0))
            if two:
                order.append(two.pop(0))
        return order

    first = weave(near, far)
    return list(zip(first, first if same else weave(far, near)))


def side(step, index=None):
    index = lax.axis_index("rows") if index is None else index

    def parity(places):
        total = jnp.zeros((), jnp.int32)
        for place in places:
            total = total ^ ((index >> place) & 1)
        return total

    return jnp.where(index % 2 == 0, parity(step[0][1]), parity(step[1][1]))


def block_place(steps, index):
    place = jnp.zeros((), jnp.int32)
    for step in steps:
        place = place * 2 + side(step, index)
    return place


class Summing:
    def __init__(self, steps, value, send=None):
        self.steps, self.done = steps, 0
        self.sides = [side(step) for step in steps]
        self.size = value.shape[0] if send is None else 2 * value.shape[0]
        self.terms, self.send = [(value, jnp.zeros((), jnp.int32))], send
        self.pieces, self.others = [], []

    def last(self):
        return self.pieces[-1] if self.pieces else self.terms[-1][0]

    def update(self, value):
        if self.pieces:
            self.pieces = self.pieces[:-1] + [value]
        else:
            self.terms = self.terms[:-1] + [(value, self.terms[-1][1])]

    def masks(self, number):
        step = self.steps[number]
        return (step[0][0], step[1][0])

    def part(self, offset, size):
        total = sum(
            lax.dynamic_slice_in_dim(term, base + offset, size, 0).astype(jnp.float32)
            for term, base in self.terms
        )
        return total.astype(jnp.bfloat16)

    def step(self):
        count = len(self.steps)
        if self.done < count:
            place, half = self.sides[self.done], self.size // 2
            if self.send is None:
                send = self.part((1 - place) * half, half)
                self.terms = [(term, base + place * half) for term, base in self.terms]
            else:
                send, self.send = self.send, None
            got = swap_rows(send, self.masks(self.done))
            self.terms = self.terms + [(got, jnp.zeros((), jnp.int32))]
            self.size = half
        else:
            number = 2 * count - 1 - self.done
            if self.done == count:
                self.pieces, self.terms = [self.part(0, self.size)], []
            elif number > 0:
                self.pieces = [jnp.concatenate(self.pieces, axis=0)]
            if number > 0:
                self.pieces = self.pieces + [swap_rows(self.pieces[0], self.masks(number))]
                if number == 1:
                    self.others = [swap_rows(self.pieces[0], self.masks(0))]
            else:
                self.pieces = self.pieces + [
                    self.others[0],
                    swap_rows(self.pieces[1], self.masks(0)),
                ]
                self.others = []
        self.done += 1

    def peers(self):
        own = self.part(0, self.size)
        if lax.axis_size("heads") == 2:
            total = own.astype(jnp.float32) + peer_swap(own).astype(jnp.float32)
        else:
            total = lax.psum(own.astype(jnp.float32), "heads")
        self.terms = [(total.astype(jnp.bfloat16), jnp.zeros((), jnp.int32))]

    def cores(self):
        self.others = [core_swap(piece) for piece in self.pieces]


class Gathering(Summing):
    def __init__(self, steps, own):
        super().__init__(steps, own)
        self.done, self.size = len(steps), 1


def tie_sums(*sums_and_others):
    sums = [item for item in sums_and_others if isinstance(item, Summing)]
    others = [item for item in sums_and_others if not isinstance(item, Summing)]
    values, others = lax.optimization_barrier(([item.last() for item in sums], others))
    for item, value in zip(sums, values):
        item.update(value)
    return others


def ordered(pieces, place):
    value = jnp.concatenate(pieces, axis=0)
    return jnp.concatenate(
        [
            lax.dynamic_slice_in_dim(value, place ^ block, 1, 0)
            for block in range(value.shape[0])
        ],
        axis=0,
    ).reshape(-1, value.shape[2])


def two_cores(sums, places, axis, reshape=None):
    mine, theirs = ordered(sums.pieces, places[0]), ordered(sums.others, places[1])
    if reshape is not None:
        mine, theirs = (value.reshape(reshape) for value in (mine, theirs))
    return jnp.where(
        lax.axis_index("rows") % 2 == 0,
        jnp.concatenate([mine, theirs], axis=axis),
        jnp.concatenate([theirs, mine], axis=axis),
    )


def place_blocks(kernel, index, pieces, out_specs, out_shape, name):
    height, rows, width = pieces[0].shape

    def body(index, *refs):
        sources, results = refs[:8], refs[8:]
        quarter = pl.program_id(0)
        for number, source in enumerate(sources):
            own = index[number // 4]
            slot = index[2] if number < 4 else 1 - index[2]
            for core in range(2):

                @pl.when(((quarter ^ (own // height)) == number % 4) & (slot == core))
                def _(source=source, core=core, own=own):
                    kernel(index, source, own % height, core, *results)

    whole = pl.BlockSpec((height, rows, width), lambda b, i: (0, 0, 0))
    return pl.pallas_call(
        body,
        grid_spec=pltpu.PrefetchScalarGridSpec(
            num_scalar_prefetch=1, grid=(4,), in_specs=[whole] * 8, out_specs=out_specs
        ),
        out_shape=out_shape,
        cost_estimate=pl.CostEstimate(
            flops=0, bytes_accessed=48 * height * rows * width, transcendentals=0
        ),
        compiler_params=pltpu.CompilerParams(vmem_limit_bytes=26 << 20),
        name=name,
    )(index, *pieces)


def place_ffn(index, sums, split):
    height, rows, width = sums.pieces[0].shape
    columns = height * (rows - split)

    def kernel(index, source, low, core, gate_up, down):
        parts = [source[k ^ low] for k in range(height)]
        for k, part in enumerate(parts):
            gate_up[k * split : (k + 1) * split, core, :] = part[:split].astype(jnp.float32)
        value = jnp.concatenate([part[split:] for part in parts], axis=0)
        down[:, core * columns : (core + 1) * columns] = value.astype(jnp.float32).T

    return place_blocks(
        kernel,
        index,
        sums.pieces + sums.others,
        [
            pl.BlockSpec((height * split, 2, width), lambda b, i: (b, 0, 0)),
            pl.BlockSpec((width, 2 * columns), lambda b, i: (0, b)),
        ],
        [
            jax.ShapeDtypeStruct((4 * height * split, 2, width), jnp.float32),
            jax.ShapeDtypeStruct((width, 8 * columns), jnp.float32),
        ],
        "place_ffn",
    )


def place_attn(index, sums, attn_cols):
    height, rows, width = sums.pieces[0].shape
    part = attn_cols // 2

    def kernel(index, source, low, core, result, out):
        value = jnp.concatenate([source[k ^ low] for k in range(height)], axis=0)
        value = value.astype(jnp.float32)
        place = slice(core * part, (core + 1) * part)

        @pl.when(pl.program_id(0) < 3)
        def _():
            result[0, :, place] = value.T

        @pl.when(pl.program_id(0) == 3)
        def _():
            out[place, :] = value

    return place_blocks(
        kernel,
        index,
        sums.pieces + sums.others,
        [
            pl.BlockSpec((1, width, attn_cols), lambda b, i: (jnp.minimum(b, 2), 0, 0)),
            pl.BlockSpec((attn_cols, width), lambda b, i: (0, 0)),
        ],
        [
            jax.ShapeDtypeStruct((3, width, attn_cols), jnp.float32),
            jax.ShapeDtypeStruct((attn_cols, width), jnp.float32),
        ],
        "place_attn",
    )


def place_proj(index, sums, total, extra):
    height, rows, width = sums.pieces[0].shape
    last = total - (4 * height - 1) * rows

    def kernel(index, source, low, core, result, others):
        columns = slice(core * width, (core + 1) * width)
        for k in range(height):
            value = source[k ^ low].astype(jnp.float32)
            result[k * rows : (k + 1) * rows, columns] = value

            @pl.when((pl.program_id(0) == 3) & (k == height - 1))
            def _(value=value):
                others[:, columns] = value[last : last + extra]

    return place_blocks(
        kernel,
        index,
        sums.pieces + sums.others,
        [
            pl.BlockSpec((height * rows, 2 * width), lambda b, i: (b, 0)),
            pl.BlockSpec((extra, 2 * width), lambda b, i: (0, 0)),
        ],
        [
            jax.ShapeDtypeStruct((total, 2 * width), jnp.float32),
            jax.ShapeDtypeStruct((extra, 2 * width), jnp.float32),
        ],
        "place_proj",
    )


def rms_forward(values, gain):
    scale = lax.rsqrt(jnp.mean(values * values, axis=-1, keepdims=True) + EPSILON)
    return (values * scale * gain, scale)


def rms_backward(values, scale, gain, grad_normed):
    unit = values * scale
    grad_unit = grad_normed * gain
    grad_values = scale * (grad_unit - unit * jnp.mean(grad_unit * unit, axis=-1, keepdims=True))
    return (grad_values, jnp.sum(grad_normed * unit, axis=0))


def block_scores(
    queries, key_rows, segments, padding, query_start, row_start, query_count, seq_len
):
    query_block = lax.dynamic_slice_in_dim(queries, query_start, query_count, 0)
    scores = jnp.einsum("qhd,khd->hqk", query_block, key_rows, preferred_element_type=jnp.float32)
    query_segment = lax.dynamic_slice_in_dim(segments, query_start, query_count, 0)
    query_place = query_start + jnp.arange(query_count)
    key_place = row_start + jnp.arange(seq_len)
    allowed = (query_segment[:, None] == segments[None, :]) & (
        (padding[None, :] == 1) | (query_place[:, None] == key_place[None, :])
    )
    return (jnp.where(allowed[None], scores, MASKED), query_block, key_rows)


def attention_forward(queries, key_rows, value_rows, segments, padding, seq_len, query_count):
    group_tokens = queries.shape[0]
    per_seq = seq_len // query_count

    def one_block(number):
        query_start = number * query_count
        row_start = number // per_seq * seq_len
        scores, _, _ = block_scores(
            queries, key_rows, segments, padding, query_start, row_start, query_count, seq_len
        )
        top = jnp.max(scores, axis=-1, keepdims=True)
        expo = jnp.exp(scores - top)
        weight_sum = jnp.sum(expo, axis=-1, keepdims=True)
        probs = (expo / weight_sum).astype(jnp.bfloat16)
        mixed = jnp.einsum("hqk,khd->qhd", probs, value_rows, preferred_element_type=jnp.float32)
        return (mixed.astype(jnp.bfloat16), (top + jnp.log(weight_sum))[:, :, 0])

    mixed, log_sums = lax.map(one_block, jnp.arange(group_tokens // query_count))
    return (mixed.reshape(group_tokens, -1), log_sums)


def attention_backward(
    queries, key_rows, value_rows, segments, padding, log_sums, grad_mixed, seq_len, query_count
):
    group_tokens, heads_here, head_size = queries.shape
    per_seq = seq_len // query_count

    def one_block(carry, item):
        grad_keys, grad_values = carry
        number, log_sum = item
        query_start = number * query_count
        row_start = number // per_seq * seq_len
        scores, query_block, key_block = block_scores(
            queries, key_rows, segments, padding, query_start, row_start, query_count, seq_len
        )
        grad_block = lax.dynamic_slice_in_dim(grad_mixed, query_start, query_count, 0)
        probs = jnp.exp(scores - log_sum[:, :, None])
        grad_probs = jnp.einsum(
            "qhd,khd->hqk", grad_block, value_rows, preferred_element_type=jnp.float32
        )
        grad_scores = probs * (grad_probs - jnp.sum(grad_probs * probs, axis=-1, keepdims=True))
        grad_scores = grad_scores.astype(jnp.bfloat16)
        grad_query = jnp.einsum(
            "hqk,khd->qhd", grad_scores, key_block, preferred_element_type=jnp.float32
        )
        key_part = jnp.einsum(
            "hqk,qhd->khd", grad_scores, query_block, preferred_element_type=jnp.float32
        )
        value_part = jnp.einsum(
            "hqk,qhd->khd",
            probs.astype(jnp.bfloat16),
            grad_block,
            preferred_element_type=jnp.float32,
        )
        grad_keys = grad_keys + key_part
        grad_values = grad_values + value_part
        return ((grad_keys, grad_values), grad_query)

    zero_grads = jnp.zeros((group_tokens, heads_here, head_size), jnp.float32)
    (grad_keys, grad_values), grad_queries = lax.scan(
        one_block, (zero_grads, zero_grads), (jnp.arange(group_tokens // query_count), log_sums)
    )
    return (grad_queries.reshape(group_tokens, heads_here, head_size), grad_keys, grad_values)


def local(
    features,
    segment_ids,
    padding_mask,
    w_proj,
    proj_bias,
    gain_attn,
    w_qkv,
    w_out,
    gain_ffn,
    w_gate_up,
    w_down,
    cotangent,
):
    local_tokens = features.shape[0]
    model_width = w_proj.shape[1]
    attn_cols = w_qkv.shape[2]
    heads_here = attn_cols // HEAD_DIM
    group_tokens = local_tokens * lax.axis_size("heads")
    query_count = min(512, group_tokens)
    ff_here = w_gate_up.shape[2]
    core = lax.axis_index("rows") % 2
    steps = plane_steps()
    count = len(steps)
    blocks = 1 << count
    rows_index = lax.axis_index("rows")
    places = [block_place(steps, rows_index ^ other) for other in range(2)]
    index = jnp.stack(places + [core, lax.axis_index("heads")]).astype(jnp.int32)
    fast = lax.axis_size("heads") == 2 and blocks == 8 and attn_cols % 256 == 0
    w_heads = jnp.transpose(w_qkv, (1, 0, 2))
    gate_flat = w_gate_up.reshape(model_width, 2 * ff_here)
    lifted = jnp.dot(features, w_proj, preferred_element_type=jnp.float32) + proj_bias
    normed, scale_attn = rms_forward(lifted, gain_attn)
    gathered = gather_group(normed.astype(jnp.bfloat16))
    segments = gather_group(segment_ids)
    padding = gather_group(padding_mask)
    gathered, cot_here = tie_sums(gathered, cotangent)
    grad_gathered = gather_group(cot_here)
    queries, key_rows, value_rows = (
        jnp.dot(gathered, w_heads[i], preferred_element_type=jnp.float32)
        .astype(jnp.bfloat16)
        .reshape(group_tokens, heads_here, HEAD_DIM)
        for i in range(3)
    )
    mixed, log_sums = attention_forward(
        queries, key_rows, value_rows, segments, padding, group_tokens, query_count
    )
    mixed, grad_gathered = tie_sums(mixed, grad_gathered)
    middle = lifted + scatter_group(
        jnp.dot(mixed, w_out, preferred_element_type=jnp.float32).astype(jnp.bfloat16)
    )
    normed_ffn, scale_ffn = rms_forward(middle, gain_ffn)
    gathered_ffn = gather_group(normed_ffn.astype(jnp.bfloat16))
    pair_normed = with_pair(gathered)
    pair_mixed = columns_to_pair(mixed)
    pair_cot = mixed_columns_to_pair(grad_gathered, blocks // 2)
    pair_features = with_pair(features)
    gathered_ffn, gate_flat, pair_normed, pair_mixed, pair_cot, pair_features = tie_sums(
        gathered_ffn, gate_flat, pair_normed, pair_mixed, pair_cot, pair_features
    )
    gate_up = jnp.dot(gathered_ffn, gate_flat, preferred_element_type=jnp.float32)
    activ, gelu_pull = jax.vjp(gelu_tanh, gate_up[:, :ff_here])
    up_part = gate_up[:, ff_here:]
    hidden = (activ * up_part).astype(jnp.bfloat16)
    pair_hidden = with_pair(hidden)
    grad_hidden = contract(grad_gathered, w_down, 1, 1)
    grad_gate = gelu_pull(grad_hidden * up_part)[0].astype(jnp.bfloat16)
    grad_up = (grad_hidden * activ).astype(jnp.bfloat16)
    pair_ffn = with_pair(gathered_ffn)
    pre_own = jnp.where(core == 0, grad_gate, grad_up)
    pre_other = jnp.where(core == 0, grad_up, grad_gate)
    pair_hidden, pre_own, pre_other, pair_ffn = tie_sums(pair_hidden, pre_own, pre_other, pair_ffn)
    pre_other = core_swap(pre_other)
    down_part = contract(pair_cot, pair_hidden, 0, 0)
    down = Summing(steps, down_part.astype(jnp.bfloat16).reshape(blocks, -1, ff_here))
    down.step()
    pair_pre = jnp.concatenate([pre_own, pre_other], axis=0)
    width = model_width // 2
    place = side(steps[0])
    grad_pre = jnp.concatenate([grad_gate, grad_up], axis=1)
    grad_pre, pair_pre = tie_sums(grad_pre, pair_pre)
    given, own = to_owners(lambda part: contract(part, gate_flat, 1, 1), grad_pre)
    gate_send, gate_keep = (
        contract(lax.dynamic_slice_in_dim(pair_ffn, which * width, width, 1), pair_pre, 0, 0)
        .astype(jnp.bfloat16)
        .reshape(blocks // 2, -1, ff_here)
        for which in (1 - place, place)
    )
    gate = Summing(steps, gate_keep, gate_send)
    gate.step()
    given, own, gate_send = tie_sums(down, given, own, gate_send)
    down.step()
    grad_normed_ffn = own + given.astype(jnp.float32)
    grad_ffn_norm, grad_gain_ffn = rms_backward(middle, scale_ffn, gain_ffn, grad_normed_ffn)
    grad_middle = cotangent.astype(jnp.float32) + grad_ffn_norm
    grad_mid_b = grad_middle.astype(jnp.bfloat16)
    grad_attn_in = gather_group(grad_mid_b)
    (grad_attn_in,) = tie_sums(gate, down, grad_attn_in)
    gate.step()
    down.step()
    grad_mixed = contract(grad_attn_in, w_out, 1, 1).astype(jnp.bfloat16)
    pair_mid = with_pair(grad_attn_in)
    grad_mixed, pair_mid = tie_sums(grad_mixed, pair_mid)
    grad_queries, grad_keys, grad_values = attention_backward(
        queries,
        key_rows,
        value_rows,
        segments,
        padding,
        log_sums,
        grad_mixed.reshape(group_tokens, heads_here, HEAD_DIM),
        group_tokens,
        query_count,
    )
    grad_flat = jnp.concatenate(
        [
            part.astype(jnp.bfloat16).reshape(group_tokens, attn_cols)
            for part in (grad_queries, grad_keys, grad_values)
        ],
        axis=1,
    )
    w_flat = jnp.concatenate([w_heads[i] for i in range(3)], axis=1)
    grad_flat, pair_mid = tie_sums(grad_flat, pair_mid)
    given, own = to_owners(lambda part: contract(part, w_flat, 1, 1), grad_flat)
    grad_flat, own, pair_mid = tie_sums(gate, down, grad_flat, own, pair_mid)
    gate.step()
    while down.done < count:
        down.step()
    pair_heads = jnp.concatenate(
        [columns_to_pair(grad_flat[:, i * attn_cols : (i + 1) * attn_cols]) for i in range(3)],
        axis=1,
    )
    attn_part = jnp.concatenate(
        [
            contract(pair_heads, pair_normed, 0, 0).astype(jnp.bfloat16),
            contract(pair_mixed, pair_mid, 0, 0).astype(jnp.bfloat16),
        ],
        axis=0,
    )
    attn = Summing(steps, attn_part.reshape(blocks, -1, attn_part.shape[1]))
    attn.step()
    given, own, attn_part = tie_sums(given, own, attn_part)
    grad_normed = own + given.astype(jnp.float32)
    grad_attn_norm, grad_gain_attn = rms_backward(lifted, scale_attn, gain_attn, grad_normed)
    grad_lifted = grad_middle + grad_attn_norm
    grad_lift_b = grad_lifted.astype(jnp.bfloat16)
    sums = jnp.stack([jnp.sum(grad_lifted, axis=0), grad_gain_attn, grad_gain_ffn])
    sums = jnp.pad(sums, ((0, 16 - sums.shape[0]), (0, 0)))
    half = model_width // 2
    mine, theirs = (
        lax.dynamic_slice_in_dim(sums, which * half, half, 1) for which in (core, 1 - core)
    )
    sums = (mine + core_swap(theirs)).astype(jnp.bfloat16)
    sums = jnp.pad(sums, ((0, 16 * blocks - sums.shape[0]), (0, 0)))
    proj_part = contract(pair_features, columns_to_pair(grad_lift_b), 0, 0).astype(jnp.bfloat16)
    proj_part = jnp.concatenate([proj_part, sums], axis=0)
    proj = Summing(steps, proj_part.reshape(blocks, -1, proj_part.shape[1]))
    proj.step()
    while gate.done < count:
        gate.step()
    ffn_rows = model_width // blocks
    ffn = Gathering(steps, jnp.concatenate([gate.part(0, 1), down.part(0, 1)], axis=1))
    ffn.step()
    hidden, grad_lift_b = tie_sums(proj, ffn, attn, hidden, grad_lift_b)
    proj.step()
    attn.step()
    while ffn.done < 2 * count - 1:
        ffn.step()
    tie_sums(proj)
    while proj.done < count:
        proj.step()
    layer_out = scatter_group(
        jnp.dot(hidden, w_down, preferred_element_type=jnp.float32).astype(jnp.bfloat16)
    )
    grad_features = contract(grad_lift_b, w_proj, 1, 1)
    tie_sums(proj, attn, ffn)
    proj.peers()
    while attn.done < count:
        attn.step()
    ffn.step()
    layer_out, grad_features = tie_sums(attn, ffn, proj, layer_out, grad_features)
    layer_out = middle + layer_out
    proj.step()
    attn.step()
    ffn.cores()
    if fast:
        grad_gate_up, grad_down = place_ffn(index, ffn, ffn_rows)
        tie_sums(proj, attn, grad_gate_up, grad_down)
    while proj.done < 2 * count:
        proj.step()
    while attn.done < 2 * count:
        attn.step()
    proj.cores()
    attn.cores()
    if fast:
        grad_proj, sums = place_proj(index, proj, w_proj.shape[0], 16)
        grad_qkv, grad_out = place_attn(index, attn, attn_cols)
        grad_qkv = jnp.transpose(grad_qkv, (1, 0, 2))
    else:
        half = attn_cols // 2
        mine, theirs = ordered(ffn.pieces, places[0]), ordered(ffn.others, places[1])
        pair = jnp.stack([jnp.where(core == 0, mine, theirs), jnp.where(core == 0, theirs, mine)])
        pair = pair.reshape(2, blocks, -1, ff_here).astype(jnp.float32)
        grad_gate_up = jnp.moveaxis(pair[:, :, :ffn_rows], 0, 2).reshape(model_width, 2, ff_here)
        grad_down = pair[:, :, ffn_rows:].reshape(2, blocks // 2, -1, ff_here)
        grad_down = jnp.moveaxis(grad_down, 0, 1).reshape(model_width, ff_here).T
        pair = two_cores(proj, places, 1).astype(jnp.float32)
        grad_proj, sums = pair[: w_proj.shape[0]], pair[w_proj.shape[0] :]
        pair = two_cores(attn, places, 0).reshape(2, 4, half, model_width)
        pair = jnp.moveaxis(pair, 0, 1).reshape(4, attn_cols, model_width).astype(jnp.float32)
        grad_qkv, grad_out = jnp.transpose(pair[:3], (2, 0, 1)), pair[3]
    return (
        layer_out.astype(jnp.bfloat16),
        grad_features,
        grad_proj,
        sums[0],
        sums[1],
        grad_qkv,
        grad_out,
        sums[2],
        grad_gate_up,
        grad_down,
    )


def solution(mesh):
    in_specs = (
        P(("rows", "heads"), None),
        P(("rows", "heads")),
        P(("rows", "heads")),
        P(),
        P(),
        P(),
        P(None, None, "heads"),
        P("heads", None),
        P(),
        P(None, None, "heads"),
        P("heads", None),
        P(("rows", "heads"), None),
    )
    out_specs = (
        P(("rows", "heads"), None),
        P(("rows", "heads"), None),
        P(),
        P(),
        P(),
        P(None, None, "heads"),
        P("heads", None),
        P(),
        P(None, None, "heads"),
        P("heads", None),
    )
    return jax.shard_map(local, mesh=mesh, in_specs=in_specs, out_specs=out_specs, check_vma=False)
```

profile of v0, /device:TPU:0, one launch (start us, length us, event | category | flops | bytes accessed | tf_op | source)
XLA Modules:
  0.0 356.0 jit_solution(16999271183972254249)
XLA Ops:
  0.7 1.9 copy-done
  2.6 2.4 multiply_reduce_fusion.6
  6.9 2.9 collective-permute-start
  9.9 2.0 collective-permute-start.2
  11.9 10.2 %collective-permute-done.2 = s32[256]{0:T(256)S(1)} collective-permute-done((s32[256]{0:T(256)S(1)}, s32[256]{0:T(256)S(1)}, u32[]{:S(2)}, u32[]{:S(2)}) %collective-permute-start.2) | collective-permute-done | bytes 1056 | tf_op jit(solution)/shard_map/ppermute | solution.py:35
  24.0 2.4 convolution_convert_fusion.13
  28.0 1.8 collective-permute-start.3
  32.7 1.9 copy-done.1
  34.6 2.5 fusion.32
  37.1 4.1 %collective-permute-done.3 = bf16[256,1024]{1,0:T(8,128)(2,1)S(1)} collective-permute-done((bf16[256,1024]{1,0:T(8,128)(2,1)S(1)}, bf16[256,1024]{1,0:T(8,128)(2,1)S(1)}, u32[]{:S(2)}, u32[]{:S(2)}) %collective-permute-start.3) | collective-permute-done | bytes 524320 | tf_op jit(solution)/shard_map/ppermute | solution.py:35
  46.1 6.2 %copy.37 = bf16[128,8,2,1408]{3,1,2,0:T(8,128)(2,1)} copy(bf16[128,8,2,1408]{3,2,1,0:T(2,128)(2,1)} %bitcast.91) | data formatting | bytes 11534336
  55.2 2.0 collective-permute-done.4
  60.9 2.9 pad_maximum_fusion.8
  67.3 4.4 %collective-permute-done.5 = bf16[256,1024]{1,0:T(8,128)(2,1)S(1)} collective-permute-done((bf16[256,1024]{1,0:T(8,128)(2,1)S(1)}, bf16[256,1024]{1,0:T(8,128)(2,1)S(1)}, u32[]{:S(2)}, u32[]{:S(2)}) %collective-permute-start.5) | collective-permute-done | bytes 524320 | tf_op jit(solution)/shard_map/ppermute | solution.py:35
  71.8 3.2 fusion.62
  77.5 5.4 %broadcast_select_fusion = (bf16[512,1408]{1,0:T(8,128)(2,1)}, bf16[512,1408]{1,0:T(8,128)(2,1)S(1)}, bf16[512,1408]{1,0:T(8,128)(2,1)S(1)}) fusion(pred[]{:T(512)S(6)} %eq.144, f32[512,2816]{1,0:T(8,128)S(1)} %fusion.62, bf16[512,1024]{1,0:T(8,128)(2,1)S(1)} %copy-done.18, bf16[1408,1024]{1,0:T(8,128)(2,1)S(1)} %copy-done.57), kind=kOutput, calls=%fused_computation.61 | convolution fusion | flops 1494417408 | bytes 14024705 | tf_op jit(solution)/shard_map/dot_general | solution.py:20
  85.9 1.8 pad_maximum_fusion.1
  88.2 2.1 pad_maximum_fusion.2
  90.4 4.0 %convolution_convert_fusion.1 = bf16[512,1408]{1,0:T(8,128)(2,1)S(1)} fusion(bf16[1024,512]{1,0:T(8,128)(2,1)S(1)} %copy-done.40, bf16[1024,1408]{1,0:T(8,128)(2,1)} %pad_maximum_fusion.1), kind=kOutput, calls=%fused_computation.19 | convolution fusion | flops 1477115904 | bytes 5373952 | tf_op jit(solution)/shard_map/dot_general | solution.py:20
  97.7 1.7 fusion.36
  100.3 3.0 convolution_convert_fusion.2
  104.2 1.7 fusion.28
  105.9 7.1 %collective-permute-done.15 = bf16[256,1024]{1,0:T(8,128)(2,1)S(1)} collective-permute-done((bf16[256,1024]{1,0:T(8,128)(2,1)S(1)}, bf16[256,1024]{1,0:T(8,128)(2,1)S(1)}, u32[]{:S(2)}, u32[]{:S(2)}) %collective-permute-start.15) | collective-permute-done | bytes 524320 | tf_op jit(solution)/shard_map/ppermute | solution.py:35
  116.0 1.8 slice_bitcast_fusion.1
  120.4 7.8 %collective-permute-done.17 = bf16[256,1024]{1,0:T(8,128)(2,1)} collective-permute-done((bf16[256,1024]{1,0:T(8,128)(2,1)}, bf16[256,1024]{1,0:T(8,128)(2,1)}, u32[]{:S(2)}, u32[]{:S(2)}) %collective-permute-start.17) | collective-permute-done | bytes 524320 | tf_op jit(solution)/shard_map/ppermute | solution.py:35
  129.6 3.3 convolution_convert_fusion.3
  132.9 2.2 add_convert_fusion.13
  135.1 2.9 collective-permute-start.19
  138.0 2.2 add_convert_fusion
  143.6 2.1 copy.29
  145.6 6.8 %multiply_reduce_fusion = (f32[8,512]{1,0:T(8,128)S(1)}, f32[8,512,512]{1,2,0:T(8,128)S(1)}) fusion(f32[8,512,512]{1,2,0:T(8,128)} %copy-done.1, f32[8,512]{1,0:T(8,128)S(1)} %log_add_fusion, pred[512,512]{0,1:T(8,128)(4,1)} %copy-done.9, bf16[512,8,64]{0,2,1:T(8,128)(2,1)} %bitcast.107, bf16[512,8,64]{0,2,1:T(8,128)(2,1)} %bitcast.119), kind=kOutput, calls=%fused_computation.1 | convolution fusion | flops 276819968 | bytes 18120704 | tf_op jit(solution)/shard_map/while/body/eval_jaxpr/qhd,khd->hqk/dot_general | solution.py:438
  152.5 2.6 multiply_convert_fusion
  157.5 2.1 fusion.33
  163.6 2.1 add_convert_fusion.5
  169.4 1.9 add_convert_fusion.12
  172.1 1.8 convolution_convert_fusion.4
  175.4 7.4 %collective-permute-done.24 = bf16[256,1024]{1,0:T(8,128)(2,1)S(1)} collective-permute-done((bf16[256,1024]{1,0:T(8,128)(2,1)S(1)}, bf16[256,1024]{1,0:T(8,128)(2,1)S(1)}, u32[]{:S(2)}, u32[]{:S(2)}) %collective-permute-start.24) | collective-permute-done | bytes 524320 | tf_op jit(solution)/shard_map/ppermute | solution.py:35
  190.8 2.6 convolution_convert_fusion
  196.0 3.0 collective-permute-start.29
  199.0 14.1 %collective-permute-done.29 = bf16[1,192,1408]{2,1,0:T(8,128)(2,1)S(1)} collective-permute-done((bf16[1,192,1408]{2,1,0:T(8,128)(2,1)S(1)}, bf16[1,192,1408]{2,1,0:T(8,128)(2,1)S(1)}, u32[]{:S(2)}, u32[]{:S(2)}) %collective-permute-start.29) | collective-permute-done | bytes 540704 | tf_op jit(solution)/shard_map/ppermute | solution.py:27
  215.2 2.1 collective-permute-start.34
  217.5 1.8 collective-permute-start.41
  219.3 13.8 %collective-permute-start.42 = (bf16[2,192,1408]{2,1,0:T(8,128)(2,1)}, bf16[2,192,1408]{2,1,0:T(8,128)(2,1)}, u32[]{:S(2)}, u32[]{:S(2)}) collective-permute-start(bf16[2,192,1408]{2,1,0:T(8,128)(2,1)} %pad_maximum_fusion.12.refs_0_), channel_id=1, source_target_pairs={{0,2},{2,0},{4,6},{6,4},{8,10},{10,8},{12,14},{14,12},{16,18},{18,... | collective-permute-start | bytes 3244040 | tf_op jit(solution)/shard_map/ppermute | solution.py:27
  233.2 1.7 collective-permute-start.33
  235.0 11.9 %collective-permute-done.31 = bf16[2,224,512]{2,1,0:T(8,128)(2,1)S(1)} collective-permute-done((bf16[2,224,512]{2,1,0:T(8,128)(2,1)S(1)}, bf16[2,224,512]{2,1,0:T(8,128)(2,1)S(1)}, u32[]{:S(2)}, u32[]{:S(2)}) %collective-permute-start.31) | collective-permute-done | bytes 458784 | tf_op jit(solution)/shard_map/ppermute | solution.py:27
  247.0 5.0 %collective-permute-start.32 = (bf16[1,224,512]{2,1,0:T(8,128)(2,1)S(1)}, bf16[1,224,512]{2,1,0:T(8,128)(2,1)S(1)}, u32[]{:S(2)}, u32[]{:S(2)}) collective-permute-start(bf16[1,224,512]{2,1,0:T(8,128)(2,1)S(1)} %add_convert_fusion.11), channel_id=1, source_target_pairs={{0,24},{2,26},{4,28},{6,30},{8,16},{10,18},{12,20},{14,22},{16,8},... | collective-permute-start | bytes 688136 | tf_op jit(solution)/shard_map/ppermute | solution.py:27
  252.0 2.1 convolution_convert_fusion.5
  254.1 4.2 %collective-permute-done.33 = bf16[2,128,1024]{2,1,0:T(8,128)(2,1)S(1)} collective-permute-done((bf16[2,128,1024]{2,1,0:T(8,128)(2,1)S(1)}, bf16[2,128,1024]{2,1,0:T(8,128)(2,1)S(1)}, u32[]{:S(2)}, u32[]{:S(2)}) %collective-permute-start.33) | collective-permute-done | bytes 524320 | tf_op jit(solution)/shard_map/ppermute | solution.py:27
  258.7 5.9 %collective-permute-done.32 = bf16[1,224,512]{2,1,0:T(8,128)(2,1)S(1)} collective-permute-done((bf16[1,224,512]{2,1,0:T(8,128)(2,1)S(1)}, bf16[1,224,512]{2,1,0:T(8,128)(2,1)S(1)}, u32[]{:S(2)}, u32[]{:S(2)}) %collective-permute-start.32) | collective-permute-done | bytes 229408 | tf_op jit(solution)/shard_map/ppermute | solution.py:27
  264.6 1.8 collective-permute-start.36
  266.4 2.3 fusion.63
  269.6 2.5 collective-permute-done.38
  272.0 5.9 %collective-permute-start.35 = (bf16[1,128,1024]{2,1,0:T(8,128)(2,1)S(1)}, bf16[1,128,1024]{2,1,0:T(8,128)(2,1)S(1)}, u32[]{:S(2)}, u32[]{:S(2)}) collective-permute-start(bf16[1,128,1024]{2,1,0:T(8,128)(2,1)S(1)} %add_convert_fusion.8), channel_id=1, source_target_pairs={{0,24},{2,26},{4,28},{6,30},{8,16},{10,18},{12,20},{14,22},{16,8},... | collective-permute-start | bytes 786440 | tf_op jit(solution)/shard_map/ppermute | solution.py:27
  280.3 3.4 collective-permute-done.35
  284.7 2.4 collective-permute-start.40
  289.6 12.1 %place_ffn.1 = (f32[1024,2,1408]{2,1,0:T(2,128)}, f32[1408,1024]{1,0:T(8,128)}) custom-call(s32[4]{0:T(128)S(1)} %pad_add_fusion.index, bf16[2,192,1408]{2,1,0:T(8,128)(2,1)} %pad_maximum_fusion.12.refs_0_, bf16[2,192,1408]{2,1,0:T(8,128)(2,1)} %collective-permute-done.34.refs_1_, bf16[2,192,1408]{2,1,0:T(8,128)(2,1)} %collective-permute-done.41.refs_2_, ...), custom_call_target="tpu_custom_call" | custom-call | bytes 25952256 | tf_op jit(solution)/shard_map/place_ffn/pallas_call | solution.py:271
  301.7 9.8 %collective-permute-start.46 = (bf16[2,224,512]{2,1,0:T(8,128)(2,1)S(1)}, bf16[2,224,512]{2,1,0:T(8,128)(2,1)S(1)}, u32[]{:S(2)}, u32[]{:S(2)}) collective-permute-start(bf16[2,224,512]{2,1,0:T(8,128)(2,1)S(1)} %constant_dynamic-update-slice_fusion.1.refs_0_), channel_id=1, source_target_pairs={{0,8},{2,6},{4,12},{6,2},{8,0},{10,14},{12,4},{14,10},{16,24},{18,... | collective-permute-start | bytes 1376264 | tf_op jit(solution)/shard_map/ppermute | solution.py:27
  313.9 6.9 %collective-permute-done.46.refs_1_ = bf16[2,224,512]{2,1,0:T(8,128)(2,1)S(1)} collective-permute-done((bf16[2,224,512]{2,1,0:T(8,128)(2,1)S(1)}, bf16[2,224,512]{2,1,0:T(8,128)(2,1)S(1)}, u32[]{:S(2)}, u32[]{:S(2)}) %collective-permute-start.46) | collective-permute-done | bytes 458784 | tf_op jit(solution)/shard_map/ppermute | solution.py:27
  320.8 2.0 collective-permute-start.54
  322.8 9.2 %collective-permute-done.53.refs_1_ = bf16[2,128,1024]{2,1,0:T(8,128)(2,1)S(1)} collective-permute-done((bf16[2,128,1024]{2,1,0:T(8,128)(2,1)S(1)}, bf16[2,128,1024]{2,1,0:T(8,128)(2,1)S(1)}, u32[]{:S(2)}, u32[]{:S(2)}) %collective-permute-start.53) | collective-permute-done | bytes 524320 | tf_op jit(solution)/shard_map/ppermute | solution.py:27
  334.9 4.2 %collective-permute-start.56 = (bf16[2,128,1024]{2,1,0:T(8,128)(2,1)S(1)}, bf16[2,128,1024]{2,1,0:T(8,128)(2,1)S(1)}, u32[]{:S(2)}, u32[]{:S(2)}) collective-permute-start(bf16[2,128,1024]{2,1,0:T(8,128)(2,1)S(1)} %pad_maximum_fusion.21.refs_0_), channel_id=1, source_target_pairs={{0,2},{2,0},{4,6},{6,4},{8,10},{10,8},{12,14},{14,12},{16,18},{18,... | collective-permute-start | bytes 1572872 | tf_op jit(solution)/shard_map/ppermute | solution.py:27
  341.2 3.2 collective-permute-start.59
  345.4 4.0 %place_proj.1 = (f32[1664,1024]{1,0:T(8,128)}, f32[16,1024]{1,0:T(8,128)S(1)}) custom-call(s32[4]{0:T(128)S(1)} %pad_add_fusion.index, bf16[2,224,512]{2,1,0:T(8,128)(2,1)S(1)} %constant_dynamic-update-slice_fusion.1.refs_0_, bf16[2,224,512]{2,1,0:T(8,128)(2,1)S(1)} %collective-permute-done.46.refs_1_, ...), custom_call_target="tpu_custom_call" | custom-call | bytes 11010048 | tf_op jit(solution)/shard_map/place_proj/pallas_call | solution.py:271
  350.0 5.6 %place_attn.1 = (f32[3,1024,512]{2,1,0:T(8,128)}, f32[512,1024]{1,0:T(8,128)}) custom-call(s32[4]{0:T(128)S(1)} %pad_add_fusion.index, bf16[2,128,1024]{2,1,0:T(8,128)(2,1)S(1)} %pad_maximum_fusion.21.refs_0_, bf16[2,128,1024]{2,1,0:T(8,128)(2,1)S(1)} %collective-permute-done.53.refs_1_, bf16[2,128,1024]{2,1,0:T(8,128)(2,1)S(1)} %collective-permute-done.54.refs_2_, ...), custom_call_target="tpu_custom_call" | custom-call | bytes 12582912 | tf_op jit(solution)/shard_map/place_attn/pallas_call | solution.py:271
  (301 shorter events, 85.7 us)
Async XLA Ops:
  6.9 15.5 %collective-permute-start = (bf16[256,1024]{1,0:T(8,128)(2,1)}, bf16[256,1024]{1,0:T(8,128)(2,1)}, u32[]{:S(2)}, u32[]{:S(2)}) collective-permute-start(bf16[256,1024]{1,0:T(8,128)(2,1)} %multiply_convert_fusion.4), channel_id=1, source_target_pairs={{0,1},{1,0},{2,3},{3,2},{4,5},{5,4},{6,7},{7,6},{8,9},{9,8},{10,11... | collective-permute-start | bytes 1572872 | tf_op jit(solution)/shard_map/ppermute | solution.py:35
  9.9 12.3 %collective-permute-start.1 = (s32[256]{0:T(256)S(1)}, s32[256]{0:T(256)S(1)}, u32[]{:S(2)}, u32[]{:S(2)}) collective-permute-start(s32[256]{0:T(256)S(1)} %copy-done.56), channel_id=1, source_target_pairs={{0,1},{1,0},{2,3},{3,2},{4,5},{5,4},{6,7},{7,6},{8,9},{9,8},{10,11... | collective-permute-start | bytes 3080 | tf_op jit(solution)/shard_map/ppermute | solution.py:35
  9.9 12.2 %collective-permute-start.2 = (s32[256]{0:T(256)S(1)}, s32[256]{0:T(256)S(1)}, u32[]{:S(2)}, u32[]{:S(2)}) collective-permute-start(s32[256]{0:T(256)S(1)} %copy-done.55), channel_id=1, source_target_pairs={{0,1},{1,0},{2,3},{3,2},{4,5},{5,4},{6,7},{7,6},{8,9},{9,8},{10,11... | collective-permute-start | bytes 3080 | tf_op jit(solution)/shard_map/ppermute | solution.py:35
  28.0 13.2 %collective-permute-start.3 = (bf16[256,1024]{1,0:T(8,128)(2,1)S(1)}, bf16[256,1024]{1,0:T(8,128)(2,1)S(1)}, u32[]{:S(2)}, u32[]{:S(2)}) collective-permute-start(bf16[256,1024]{1,0:T(8,128)(2,1)S(1)} %copy-done.33), channel_id=1, source_target_pairs={{0,1},{1,0},{2,3},{3,2},{4,5},{5,4},{6,7},{7,6},{8,9},{9,8},{10,11... | collective-permute-start | bytes 1572872 | tf_op jit(solution)/shard_map/ppermute | solution.py:35
  44.7 12.5 %collective-permute-start.4 = (bf16[256,1024]{1,0:T(8,128)(2,1)}, bf16[256,1024]{1,0:T(8,128)(2,1)}, u32[]{:S(2)}, u32[]{:S(2)}) collective-permute-start(bf16[256,1024]{1,0:T(8,128)(2,1)} %slice.83), channel_id=1, source_target_pairs={{0,1},{1,0},{2,3},{3,2},{4,5},{5,4},{6,7},{7,6},{8,9},{9,8},{10,11... | collective-permute-start | bytes 1572872 | tf_op jit(solution)/shard_map/ppermute | solution.py:35
  46.1 14.8 %collective-permute-start.9 = (bf16[256,1664]{1,0:T(8,128)(2,1)}, bf16[256,1664]{1,0:T(8,128)(2,1)}, u32[]{:S(2)}, u32[]{:S(2)}) collective-permute-start(bf16[256,1664]{1,0:T(8,128)(2,1)} %param.12), channel_id=1, source_target_pairs={{0,2},{2,0},{4,6},{6,4},{8,10},{10,8},{12,14},{14,12},{16,18},{18,... | collective-permute-start | bytes 2555912 | tf_op jit(solution)/shard_map/ppermute | solution.py:27
  52.3 13.4 %collective-permute-start.6 = (bf16[512,1024]{1,0:T(8,128)(2,1)}, bf16[512,1024]{1,0:T(8,128)(2,1)S(1)}, u32[]{:S(2)}, u32[]{:S(2)}) collective-permute-start(bf16[512,1024]{1,0:T(8,128)(2,1)} %copy-done.19), channel_id=1, source_target_pairs={{0,2},{2,0},{4,6},{6,4},{8,10},{10,8},{12,14},{14,12},{16,18},{18,... | collective-permute-start | bytes 3145736 | tf_op jit(solution)/shard_map/ppermute | solution.py:27
  54.5 10.1 %collective-permute-start.8 = (bf16[512,512]{1,0:T(8,128)(2,1)S(1)}, bf16[512,512]{1,0:T(8,128)(2,1)S(1)}, u32[]{:S(2)}, u32[]{:S(2)}) collective-permute-start(bf16[512,512]{1,0:T(8,128)(2,1)S(1)} %pad_maximum_fusion.20), channel_id=1, source_target_pairs={{0,2},{2,0},{4,6},{6,4},{8,10},{10,8},{12,14},{14,12},{16,18},{18,... | collective-permute-start | bytes 1572872 | tf_op jit(solution)/shard_map/ppermute | solution.py:27
  54.7 9.1 %collective-permute-start.7 = (bf16[512,256]{0,1:T(8,128)(2,1)S(1)}, bf16[512,256]{0,1:T(8,128)(2,1)S(1)}, u32[]{:S(2)}, u32[]{:S(2)}) collective-permute-start(bf16[512,256]{0,1:T(8,128)(2,1)S(1)} %get-tuple-element.211), channel_id=1, source_target_pairs={{0,2},{2,0},{4,6},{6,4},{8,10},{10,8},{12,14},{14,12},{16,18},{18,... | collective-permute-start | bytes 786440 | tf_op jit(solution)/shard_map/ppermute | solution.py:27
  59.7 11.9 %collective-permute-start.5 = (bf16[256,1024]{1,0:T(8,128)(2,1)S(1)}, bf16[256,1024]{1,0:T(8,128)(2,1)S(1)}, u32[]{:S(2)}, u32[]{:S(2)}) collective-permute-start(bf16[256,1024]{1,0:T(8,128)(2,1)S(1)} %multiply_convert_fusion.3), channel_id=1, source_target_pairs={{0,1},{1,0},{2,3},{3,2},{4,5},{5,4},{6,7},{7,6},{8,9},{9,8},{10,11... | collective-permute-start | bytes 1572872 | tf_op jit(solution)/shard_map/ppermute | solution.py:35
  71.7 12.6 %collective-permute-start.11 = (bf16[512,1024]{1,0:T(8,128)(2,1)S(1)}, bf16[512,1024]{1,0:T(8,128)(2,1)S(1)}, u32[]{:S(2)}, u32[]{:S(2)}) collective-permute-start(bf16[512,1024]{1,0:T(8,128)(2,1)S(1)} %pad_maximum_fusion.15), channel_id=1, source_target_pairs={{0,2},{2,0},{4,6},{6,4},{8,10},{10,8},{12,14},{14,12},{16,18},{18,... | collective-permute-start | bytes 3145736 | tf_op jit(solution)/shard_map/ppermute | solution.py:27
  76.1 9.8 %collective-permute-start.10 = (bf16[512,1408]{1,0:T(8,128)(2,1)S(1)}, bf16[512,1408]{1,0:T(8,128)(2,1)S(1)}, u32[]{:S(2)}, u32[]{:S(2)}) collective-permute-start(bf16[512,1408]{1,0:T(8,128)(2,1)S(1)} %multiply_convert_fusion.2), channel_id=1, source_target_pairs={{0,2},{2,0},{4,6},{6,4},{8,10},{10,8},{12,14},{14,12},{16,18},{18,... | collective-permute-start | bytes 4325384 | tf_op jit(solution)/shard_map/ppermute | solution.py:27
  87.7 8.3 %collective-permute-start.12 = (bf16[512,1408]{1,0:T(8,128)(2,1)}, bf16[512,1408]{1,0:T(8,128)(2,1)}, u32[]{:S(2)}, u32[]{:S(2)}) collective-permute-start(bf16[512,1408]{1,0:T(8,128)(2,1)} %get-tuple-element.129), channel_id=1, source_target_pairs={{0,2},{2,0},{4,6},{6,4},{8,10},{10,8},{12,14},{14,12},{16,18},{18,... | collective-permute-start | bytes 4325384 | tf_op jit(solution)/shard_map/ppermute | solution.py:27
  94.4 11.5 %collective-permute-start.14 = (bf16[4,64,1408]{2,1,0:T(8,128)(2,1)S(1)}, bf16[4,64,1408]{2,1,0:T(8,128)(2,1)S(1)}, u32[]{:S(2)}, u32[]{:S(2)}) collective-permute-start(bf16[4,64,1408]{2,1,0:T(8,128)(2,1)S(1)} %constant_dynamic-slice_fusion.11), channel_id=1, source_target_pairs={{0,4},{2,10},{4,0},{6,14},{8,12},{10,2},{12,8},{14,6},{16,20},{18,... | collective-permute-start | bytes 2162696 | tf_op jit(solution)/shard_map/ppermute | solution.py:27
  99.4 13.7 %collective-permute-start.15 = (bf16[256,1024]{1,0:T(8,128)(2,1)S(1)}, bf16[256,1024]{1,0:T(8,128)(2,1)S(1)}, u32[]{:S(2)}, u32[]{:S(2)}) collective-permute-start(bf16[256,1024]{1,0:T(8,128)(2,1)S(1)} %fusion.36), channel_id=1, source_target_pairs={{0,1},{1,0},{2,3},{3,2},{4,5},{5,4},{6,7},{7,6},{8,9},{9,8},{10,11... | collective-permute-start | bytes 1572872 | tf_op jit(solution)/shard_map/ppermute | solution.py:35
  103.3 26.2 %collective-permute-start.13 = (bf16[4,128,1408]{2,1,0:T(8,128)(2,1)}, bf16[4,128,1408]{2,1,0:T(8,128)(2,1)}, u32[]{:S(2)}, u32[]{:S(2)}) collective-permute-start(bf16[4,128,1408]{2,1,0:T(8,128)(2,1)} %bitcast.10), channel_id=1, source_target_pairs={{0,4},{2,10},{4,0},{6,14},{8,12},{10,2},{12,8},{14,6},{16,20},{18,... | collective-permute-start | bytes 4325384 | tf_op jit(solution)/shard_map/ppermute | solution.py:27
  115.0 13.2 %collective-permute-start.17 = (bf16[256,1024]{1,0:T(8,128)(2,1)}, bf16[256,1024]{1,0:T(8,128)(2,1)}, u32[]{:S(2)}, u32[]{:S(2)}) collective-permute-start(bf16[256,1024]{1,0:T(8,128)(2,1)} %get-tuple-element.181), channel_id=1, source_target_pairs={{0,1},{1,0},{2,3},{3,2},{4,5},{5,4},{6,7},{7,6},{8,9},{9,8},{10,11... | collective-permute-start | bytes 1572872 | tf_op jit(solution)/shard_map/ppermute | solution.py:35
  119.1 10.4 %collective-permute-start.16 = (bf16[2,64,1408]{2,1,0:T(8,128)(2,1)S(1)}, bf16[2,64,1408]{2,1,0:T(8,128)(2,1)S(1)}, u32[]{:S(2)}, u32[]{:S(2)}) collective-permute-start(bf16[2,64,1408]{2,1,0:T(8,128)(2,1)S(1)} %add_convert_fusion.6), channel_id=1, source_target_pairs={{0,8},{2,6},{4,12},{6,2},{8,0},{10,14},{12,4},{14,10},{16,24},{18,... | collective-permute-start | bytes 1081352 | tf_op jit(solution)/shard_map/ppermute | solution.py:27
  129.5 12.5 %collective-permute-start.20 = (bf16[512,1024]{1,0:T(8,128)(2,1)S(1)}, bf16[512,1024]{1,0:T(8,128)(2,1)S(1)}, u32[]{:S(2)}, u32[]{:S(2)}) collective-permute-start(bf16[512,1024]{1,0:T(8,128)(2,1)S(1)} %pad_maximum_fusion.17), channel_id=1, source_target_pairs={{0,2},{2,0},{4,6},{6,4},{8,10},{10,8},{12,14},{14,12},{16,18},{18,... | collective-permute-start | bytes 3145736 | tf_op jit(solution)/shard_map/ppermute | solution.py:27
  135.1 28.4 %collective-permute-start.19 = (bf16[1,64,1408]{2,1,0:T(8,128)(2,1)}, bf16[1,64,1408]{2,1,0:T(8,128)(2,1)}, u32[]{:S(2)}, u32[]{:S(2)}) collective-permute-start(bf16[1,64,1408]{2,1,0:T(8,128)(2,1)} %add_convert_fusion.13), channel_id=1, source_target_pairs={{0,24},{2,26},{4,28},{6,30},{8,16},{10,18},{12,20},{14,22},{16,8},... | collective-permute-start | bytes 540680 | tf_op jit(solution)/shard_map/ppermute | solution.py:27
  140.2 23.3 %collective-permute-start.18 = (bf16[2,128,1408]{2,1,0:T(8,128)(2,1)}, bf16[2,128,1408]{2,1,0:T(8,128)(2,1)}, u32[]{:S(2)}, u32[]{:S(2)}) collective-permute-start(bf16[2,128,1408]{2,1,0:T(8,128)(2,1)} %add_convert_fusion), channel_id=1, source_target_pairs={{0,8},{2,6},{4,12},{6,2},{8,0},{10,14},{12,4},{14,10},{16,24},{18,... | collective-permute-start | bytes 2162696 | tf_op jit(solution)/shard_map/ppermute | solution.py:27
  165.7 28.8 %collective-permute-start.28 = (bf16[1,128,1408]{2,1,0:T(8,128)(2,1)}, bf16[1,128,1408]{2,1,0:T(8,128)(2,1)}, u32[]{:S(2)}, u32[]{:S(2)}) collective-permute-start(bf16[1,128,1408]{2,1,0:T(8,128)(2,1)} %add_convert_fusion.5), channel_id=1, source_target_pairs={{0,24},{2,26},{4,28},{6,30},{8,16},{10,18},{12,20},{14,22},{16,8},... | collective-permute-start | bytes 1081352 | tf_op jit(solution)/shard_map/ppermute | solution.py:27
  166.8 5.3 %collective-permute-start.21 = (bf16[512,256]{0,1:T(8,128)(2,1)S(1)}, bf16[512,256]{0,1:T(8,128)(2,1)S(1)}, u32[]{:S(2)}, u32[]{:S(2)}) collective-permute-start(bf16[512,256]{0,1:T(8,128)(2,1)S(1)} %get-tuple-element.205), channel_id=1, source_target_pairs={{0,2},{2,0},{4,6},{6,4},{8,10},{10,8},{12,14},{14,12},{16,18},{18,... | collective-permute-start | bytes 786440 | tf_op jit(solution)/shard_map/ppermute | solution.py:27
  168.2 3.8 %collective-permute-start.22 = (bf16[512,256]{0,1:T(8,128)(2,1)S(1)}, bf16[512,256]{0,1:T(8,128)(2,1)S(1)}, u32[]{:S(2)}, u32[]{:S(2)}) collective-permute-start(bf16[512,256]{0,1:T(8,128)(2,1)S(1)} %get-tuple-element.207), channel_id=1, source_target_pairs={{0,2},{2,0},{4,6},{6,4},{8,10},{10,8},{12,14},{14,12},{16,18},{18,... | collective-permute-start | bytes 786440 | tf_op jit(solution)/shard_map/ppermute | solution.py:27
  168.3 3.7 %collective-permute-start.23 = (bf16[512,256]{0,1:T(8,128)(2,1)S(1)}, bf16[512,256]{0,1:T(8,128)(2,1)S(1)}, u32[]{:S(2)}, u32[]{:S(2)}) collective-permute-start(bf16[512,256]{0,1:T(8,128)(2,1)S(1)} %get-tuple-element.209), channel_id=1, source_target_pairs={{0,2},{2,0},{4,6},{6,4},{8,10},{10,8},{12,14},{14,12},{16,18},{18,... | collective-permute-start | bytes 786440 | tf_op jit(solution)/shard_map/ppermute | solution.py:27
  168.9 13.9 %collective-permute-start.24 = (bf16[256,1024]{1,0:T(8,128)(2,1)S(1)}, bf16[256,1024]{1,0:T(8,128)(2,1)S(1)}, u32[]{:S(2)}, u32[]{:S(2)}) collective-permute-start(bf16[256,1024]{1,0:T(8,128)(2,1)S(1)} %convolution_convert_fusion.10), channel_id=1, source_target_pairs={{0,1},{1,0},{2,3},{3,2},{4,5},{5,4},{6,7},{7,6},{8,9},{9,8},{10,11... | collective-permute-start | bytes 1572872 | tf_op jit(solution)/shard_map/ppermute | solution.py:35
  186.2 4.6 %collective-permute-start.25 = (bf16[256,512]{1,0:T(8,128)(2,1)}, bf16[256,512]{1,0:T(8,128)(2,1)}, u32[]{:S(2)}, u32[]{:S(2)}) collective-permute-start(bf16[256,512]{1,0:T(8,128)(2,1)} %get-tuple-element.203), channel_id=1, source_target_pairs={{0,2},{2,0},{4,6},{6,4},{8,10},{10,8},{12,14},{14,12},{16,18},{18,... | collective-permute-start | bytes 786440 | tf_op jit(solution)/shard_map/ppermute | solution.py:27
  187.6 3.2 collective-permute-start.26
  189.4 23.7 %collective-permute-start.30 = (bf16[4,128,1024]{2,1,0:T(8,128)(2,1)S(1)}, bf16[4,128,1024]{2,1,0:T(8,128)(2,1)S(1)}, u32[]{:S(2)}, u32[]{:S(2)}) collective-permute-start(bf16[4,128,1024]{2,1,0:T(8,128)(2,1)S(1)} %constant_dynamic-slice_fusion), channel_id=1, source_target_pairs={{0,4},{2,10},{4,0},{6,14},{8,12},{10,2},{12,8},{14,6},{16,20},{18,... | collective-permute-start | bytes 3145736 | tf_op jit(solution)/shard_map/ppermute | solution.py:27
  193.6 20.5 %collective-permute-start.27 = (bf16[4,224,512]{2,1,0:T(8,128)(2,1)S(1)}, bf16[4,224,512]{2,1,0:T(8,128)(2,1)S(1)}, u32[]{:S(2)}, u32[]{:S(2)}) collective-permute-start(bf16[4,224,512]{2,1,0:T(8,128)(2,1)S(1)} %constant_dynamic-slice_fusion.1), channel_id=1, source_target_pairs={{0,4},{2,10},{4,0},{6,14},{8,12},{10,2},{12,8},{14,6},{16,20},{18,... | collective-permute-start | bytes 2752520 | tf_op jit(solution)/shard_map/ppermute | solution.py:27
  196.0 56.0 %copy-start.12 = (bf16[512,1408]{1,0:T(8,128)(2,1)S(1)}, bf16[512,1408]{1,0:T(8,128)(2,1)}, u32[]{:S(2)}) copy-start(bf16[512,1408]{1,0:T(8,128)(2,1)} %copy-done.11) | copy-start | bytes 4325380
  196.0 56.0 %copy-start.58 = (bf16[1408,1024]{1,0:T(8,128)(2,1)S(1)}, bf16[1408,1024]{1,0:T(8,128)(2,1)}, u32[]{:S(2)}) copy-start(bf16[1408,1024]{1,0:T(8,128)(2,1)} %param.22) | copy-start | bytes 8650756
  196.0 17.1 %collective-permute-start.29 = (bf16[1,192,1408]{2,1,0:T(8,128)(2,1)S(1)}, bf16[1,192,1408]{2,1,0:T(8,128)(2,1)S(1)}, u32[]{:S(2)}, u32[]{:S(2)}) collective-permute-start(bf16[1,192,1408]{2,1,0:T(8,128)(2,1)S(1)} %pad_maximum_fusion.18), channel_id=1, source_target_pairs={{0,24},{2,26},{4,28},{6,30},{8,16},{10,18},{12,20},{14,22},{16,8},... | collective-permute-start | bytes 1622024 | tf_op jit(solution)/shard_map/ppermute | solution.py:27
  215.2 49.4 %collective-permute-start.34 = (bf16[2,192,1408]{2,1,0:T(8,128)(2,1)}, bf16[2,192,1408]{2,1,0:T(8,128)(2,1)}, u32[]{:S(2)}, u32[]{:S(2)}) collective-permute-start(bf16[2,192,1408]{2,1,0:T(8,128)(2,1)} %pad_maximum_fusion.12.refs_0_), channel_id=1, source_target_pairs={{0,8},{2,6},{4,12},{6,2},{8,0},{10,14},{12,4},{14,10},{16,24},{18,... | collective-permute-start | bytes 3244040 | tf_op jit(solution)/shard_map/ppermute | solution.py:27
  217.4 29.5 %collective-permute-start.31 = (bf16[2,224,512]{2,1,0:T(8,128)(2,1)S(1)}, bf16[2,224,512]{2,1,0:T(8,128)(2,1)S(1)}, u32[]{:S(2)}, u32[]{:S(2)}) collective-permute-start(bf16[2,224,512]{2,1,0:T(8,128)(2,1)S(1)} %add_convert_fusion.3), channel_id=1, source_target_pairs={{0,8},{2,6},{4,12},{6,2},{8,0},{10,14},{12,4},{14,10},{16,24},{18,... | collective-permute-start | bytes 1376264 | tf_op jit(solution)/shard_map/ppermute | solution.py:27
  217.5 61.6 %collective-permute-start.41 = (bf16[2,192,1408]{2,1,0:T(8,128)(2,1)}, bf16[2,192,1408]{2,1,0:T(8,128)(2,1)}, u32[]{:S(2)}, u32[]{:S(2)}) collective-permute-start(bf16[2,192,1408]{2,1,0:T(8,128)(2,1)} %pad_maximum_fusion.12.refs_0_), channel_id=1, source_target_pairs={{0,4},{2,10},{4,0},{6,14},{8,12},{10,2},{12,8},{14,6},{16,20},{18,... | collective-permute-start | bytes 3244040 | tf_op jit(solution)/shard_map/ppermute | solution.py:27
  219.3 67.8 %collective-permute-start.42 = (bf16[2,192,1408]{2,1,0:T(8,128)(2,1)}, bf16[2,192,1408]{2,1,0:T(8,128)(2,1)}, u32[]{:S(2)}, u32[]{:S(2)}) collective-permute-start(bf16[2,192,1408]{2,1,0:T(8,128)(2,1)} %pad_maximum_fusion.12.refs_0_), channel_id=1, source_target_pairs={{0,2},{2,0},{4,6},{6,4},{8,10},{10,8},{12,14},{14,12},{16,18},{18,... | collective-permute-start | bytes 3244040 | tf_op jit(solution)/shard_map/ppermute | solution.py:27
  233.2 25.1 %collective-permute-start.33 = (bf16[2,128,1024]{2,1,0:T(8,128)(2,1)S(1)}, bf16[2,128,1024]{2,1,0:T(8,128)(2,1)S(1)}, u32[]{:S(2)}, u32[]{:S(2)}) collective-permute-start(bf16[2,128,1024]{2,1,0:T(8,128)(2,1)S(1)} %add_convert_fusion.2), channel_id=1, source_target_pairs={{0,8},{2,6},{4,12},{6,2},{8,0},{10,14},{12,4},{14,10},{16,24},{18,... | collective-permute-start | bytes 1572872 | tf_op jit(solution)/shard_map/ppermute | solution.py:27
  247.0 17.6 %collective-permute-start.32 = (bf16[1,224,512]{2,1,0:T(8,128)(2,1)S(1)}, bf16[1,224,512]{2,1,0:T(8,128)(2,1)S(1)}, u32[]{:S(2)}, u32[]{:S(2)}) collective-permute-start(bf16[1,224,512]{2,1,0:T(8,128)(2,1)S(1)} %add_convert_fusion.11), channel_id=1, source_target_pairs={{0,24},{2,26},{4,28},{6,30},{8,16},{10,18},{12,20},{14,22},{16,8},... | collective-permute-start | bytes 688136 | tf_op jit(solution)/shard_map/ppermute | solution.py:27
  258.3 13.7 %collective-permute-start.38 = (bf16[256,1024]{1,0:T(8,128)(2,1)S(1)}, bf16[256,1024]{1,0:T(8,128)(2,1)S(1)}, u32[]{:S(2)}, u32[]{:S(2)}) collective-permute-start(bf16[256,1024]{1,0:T(8,128)(2,1)S(1)} %slice.87), channel_id=1, source_target_pairs={{0,1},{1,0},{2,3},{3,2},{4,5},{5,4},{6,7},{7,6},{8,9},{9,8},{10,11... | collective-permute-start | bytes 1572872 | tf_op jit(solution)/shard_map/ppermute | solution.py:35
  264.6 19.2 %collective-permute-start.36 = (bf16[2,192,1408]{2,1,0:T(8,128)(2,1)}, bf16[2,192,1408]{2,1,0:T(8,128)(2,1)}, u32[]{:S(2)}, u32[]{:S(2)}) collective-permute-start(bf16[2,192,1408]{2,1,0:T(8,128)(2,1)} %collective-permute-done.34.refs_1_), channel_id=1, source_target_pairs={{0,4},{2,10},{4,0},{6,14},{8,12},{10,2},{12,8},{14,6},{16,20},{18,... | collective-permute-start | bytes 3244040 | tf_op jit(solution)/shard_map/ppermute | solution.py:27
  268.9 10.2 %collective-permute-start.37 = (bf16[1,224,512]{2,1,0:T(8,128)(2,1)S(1)}, bf16[1,224,512]{2,1,0:T(8,128)(2,1)S(1)}, u32[]{:S(2)}, u32[]{:S(2)}) collective-permute-start(bf16[1,224,512]{2,1,0:T(8,128)(2,1)S(1)} %add_convert_fusion.10), channel_id=1, source_target_pairs={{0,1},{1,0},{2,3},{3,2},{4,5},{5,4},{6,7},{7,6},{8,9},{9,8},{10,11... | collective-permute-start | bytes 688136 | tf_op jit(solution)/shard_map/ppermute | solution.py:35
  272.0 11.7 %collective-permute-start.35 = (bf16[1,128,1024]{2,1,0:T(8,128)(2,1)S(1)}, bf16[1,128,1024]{2,1,0:T(8,128)(2,1)S(1)}, u32[]{:S(2)}, u32[]{:S(2)}) collective-permute-start(bf16[1,128,1024]{2,1,0:T(8,128)(2,1)S(1)} %add_convert_fusion.8), channel_id=1, source_target_pairs={{0,24},{2,26},{4,28},{6,30},{8,16},{10,18},{12,20},{14,22},{16,8},... | collective-permute-start | bytes 786440 | tf_op jit(solution)/shard_map/ppermute | solution.py:27
  279.1 10.5 %collective-permute-start.43 = (bf16[2,192,1408]{2,1,0:T(8,128)(2,1)}, bf16[2,192,1408]{2,1,0:T(8,128)(2,1)}, u32[]{:S(2)}, u32[]{:S(2)}) collective-permute-start(bf16[2,192,1408]{2,1,0:T(8,128)(2,1)} %collective-permute-done.34.refs_1_), channel_id=1, source_target_pairs={{0,2},{2,0},{4,6},{6,4},{8,10},{10,8},{12,14},{14,12},{16,18},{18,... | collective-permute-start | bytes 3244040 | tf_op jit(solution)/shard_map/ppermute | solution.py:27
  279.1 10.5 %collective-permute-start.44 = (bf16[2,192,1408]{2,1,0:T(8,128)(2,1)}, bf16[2,192,1408]{2,1,0:T(8,128)(2,1)}, u32[]{:S(2)}, u32[]{:S(2)}) collective-permute-start(bf16[2,192,1408]{2,1,0:T(8,128)(2,1)} %collective-permute-done.41.refs_2_), channel_id=1, source_target_pairs={{0,2},{2,0},{4,6},{6,4},{8,10},{10,8},{12,14},{14,12},{16,18},{18,... | collective-permute-start | bytes 3244040 | tf_op jit(solution)/shard_map/ppermute | solution.py:27
  283.8 5.8 %collective-permute-start.45 = (bf16[2,192,1408]{2,1,0:T(8,128)(2,1)}, bf16[2,192,1408]{2,1,0:T(8,128)(2,1)}, u32[]{:S(2)}, u32[]{:S(2)}) collective-permute-start(bf16[2,192,1408]{2,1,0:T(8,128)(2,1)} %collective-permute-done.36.refs_3_), channel_id=1, source_target_pairs={{0,2},{2,0},{4,6},{6,4},{8,10},{10,8},{12,14},{14,12},{16,18},{18,... | collective-permute-start | bytes 3244040 | tf_op jit(solution)/shard_map/ppermute | solution.py:27
  284.7 17.0 %collective-permute-start.40 = (bf16[1,128,1024]{2,1,0:T(8,128)(2,1)}, bf16[1,128,1024]{2,1,0:T(8,128)(2,1)}, u32[]{:S(2)}, u32[]{:S(2)}) collective-permute-start(bf16[1,128,1024]{2,1,0:T(8,128)(2,1)} %add_convert_fusion.7), channel_id=1, source_target_pairs={{0,24},{2,26},{4,28},{6,30},{8,16},{10,18},{12,20},{14,22},{16,8},... | collective-permute-start | bytes 786440 | tf_op jit(solution)/shard_map/ppermute | solution.py:27
  287.1 14.6 %collective-permute-start.39 = (bf16[1,224,512]{2,1,0:T(8,128)(2,1)}, bf16[1,224,512]{2,1,0:T(8,128)(2,1)S(1)}, u32[]{:S(2)}, u32[]{:S(2)}) collective-permute-start(bf16[1,224,512]{2,1,0:T(8,128)(2,1)} %add_convert_fusion.9), channel_id=1, source_target_pairs={{0,24},{2,26},{4,28},{6,30},{8,16},{10,18},{12,20},{14,22},{16,8},... | collective-permute-start | bytes 688136 | tf_op jit(solution)/shard_map/ppermute | solution.py:27
  289.5 54.9 %copy-start.4 = (f32[256,1024]{1,0:T(8,128)S(1)}, f32[256,1024]{1,0:T(8,128)}, u32[]{:S(2)}) copy-start(f32[256,1024]{1,0:T(8,128)} %copy-done.2) | copy-start | bytes 3145732
  289.5 54.9 %copy-start.17 = (f32[256,1024]{1,0:T(8,128)S(1)}, f32[256,1024]{1,0:T(8,128)}, u32[]{:S(2)}) copy-start(f32[256,1024]{1,0:T(8,128)} %convert_add_fusion) | copy-start | bytes 3145732
  301.7 19.1 %collective-permute-start.46 = (bf16[2,224,512]{2,1,0:T(8,128)(2,1)S(1)}, bf16[2,224,512]{2,1,0:T(8,128)(2,1)S(1)}, u32[]{:S(2)}, u32[]{:S(2)}) collective-permute-start(bf16[2,224,512]{2,1,0:T(8,128)(2,1)S(1)} %constant_dynamic-update-slice_fusion.1.refs_0_), channel_id=1, source_target_pairs={{0,8},{2,6},{4,12},{6,2},{8,0},{10,14},{12,4},{14,10},{16,24},{18,... | collective-permute-start | bytes 1376264 | tf_op jit(solution)/shard_map/ppermute | solution.py:27
  312.6 19.5 %collective-permute-start.53 = (bf16[2,128,1024]{2,1,0:T(8,128)(2,1)S(1)}, bf16[2,128,1024]{2,1,0:T(8,128)(2,1)S(1)}, u32[]{:S(2)}, u32[]{:S(2)}) collective-permute-start(bf16[2,128,1024]{2,1,0:T(8,128)(2,1)S(1)} %pad_maximum_fusion.21.refs_0_), channel_id=1, source_target_pairs={{0,8},{2,6},{4,12},{6,2},{8,0},{10,14},{12,4},{14,10},{16,24},{18,... | collective-permute-start | bytes 1572872 | tf_op jit(solution)/shard_map/ppermute | solution.py:27
  312.6 19.4 %collective-permute-start.47 = (bf16[2,224,512]{2,1,0:T(8,128)(2,1)S(1)}, bf16[2,224,512]{2,1,0:T(8,128)(2,1)S(1)}, u32[]{:S(2)}, u32[]{:S(2)}) collective-permute-start(bf16[2,224,512]{2,1,0:T(8,128)(2,1)S(1)} %constant_dynamic-update-slice_fusion.1.refs_0_), channel_id=1, source_target_pairs={{0,4},{2,10},{4,0},{6,14},{8,12},{10,2},{12,8},{14,6},{16,20},{18,... | collective-permute-start | bytes 1376264 | tf_op jit(solution)/shard_map/ppermute | solution.py:27
  312.7 19.3 %collective-permute-start.49 = (bf16[2,224,512]{2,1,0:T(8,128)(2,1)S(1)}, bf16[2,224,512]{2,1,0:T(8,128)(2,1)S(1)}, u32[]{:S(2)}, u32[]{:S(2)}) collective-permute-start(bf16[2,224,512]{2,1,0:T(8,128)(2,1)S(1)} %constant_dynamic-update-slice_fusion.1.refs_0_), channel_id=1, source_target_pairs={{0,2},{2,0},{4,6},{6,4},{8,10},{10,8},{12,14},{14,12},{16,18},{18,... | collective-permute-start | bytes 1376264 | tf_op jit(solution)/shard_map/ppermute | solution.py:27
  320.8 11.8 %collective-permute-start.48 = (bf16[2,224,512]{2,1,0:T(8,128)(2,1)S(1)}, bf16[2,224,512]{2,1,0:T(8,128)(2,1)S(1)}, u32[]{:S(2)}, u32[]{:S(2)}) collective-permute-start(bf16[2,224,512]{2,1,0:T(8,128)(2,1)S(1)} %collective-permute-done.46.refs_1_), channel_id=1, source_target_pairs={{0,4},{2,10},{4,0},{6,14},{8,12},{10,2},{12,8},{14,6},{16,20},{18,... | collective-permute-start | bytes 1376264 | tf_op jit(solution)/shard_map/ppermute | solution.py:27
  320.8 14.1 %collective-permute-start.54 = (bf16[2,128,1024]{2,1,0:T(8,128)(2,1)S(1)}, bf16[2,128,1024]{2,1,0:T(8,128)(2,1)S(1)}, u32[]{:S(2)}, u32[]{:S(2)}) collective-permute-start(bf16[2,128,1024]{2,1,0:T(8,128)(2,1)S(1)} %pad_maximum_fusion.21.refs_0_), channel_id=1, source_target_pairs={{0,4},{2,10},{4,0},{6,14},{8,12},{10,2},{12,8},{14,6},{16,20},{18,... | collective-permute-start | bytes 1572872 | tf_op jit(solution)/shard_map/ppermute | solution.py:27
  332.0 9.2 %collective-permute-start.55 = (bf16[2,128,1024]{2,1,0:T(8,128)(2,1)S(1)}, bf16[2,128,1024]{2,1,0:T(8,128)(2,1)S(1)}, u32[]{:S(2)}, u32[]{:S(2)}) collective-permute-start(bf16[2,128,1024]{2,1,0:T(8,128)(2,1)S(1)} %collective-permute-done.53.refs_1_), channel_id=1, source_target_pairs={{0,4},{2,10},{4,0},{6,14},{8,12},{10,2},{12,8},{14,6},{16,20},{18,... | collective-permute-start | bytes 1572872 | tf_op jit(solution)/shard_map/ppermute | solution.py:27
  332.0 7.1 %collective-permute-start.50 = (bf16[2,224,512]{2,1,0:T(8,128)(2,1)S(1)}, bf16[2,224,512]{2,1,0:T(8,128)(2,1)S(1)}, u32[]{:S(2)}, u32[]{:S(2)}) collective-permute-start(bf16[2,224,512]{2,1,0:T(8,128)(2,1)S(1)} %collective-permute-done.46.refs_1_), channel_id=1, source_target_pairs={{0,2},{2,0},{4,6},{6,4},{8,10},{10,8},{12,14},{14,12},{16,18},{18,... | collective-permute-start | bytes 1376264 | tf_op jit(solution)/shard_map/ppermute | solution.py:27
  332.1 7.1 %collective-permute-start.51 = (bf16[2,224,512]{2,1,0:T(8,128)(2,1)S(1)}, bf16[2,224,512]{2,1,0:T(8,128)(2,1)S(1)}, u32[]{:S(2)}, u32[]{:S(2)}) collective-permute-start(bf16[2,224,512]{2,1,0:T(8,128)(2,1)S(1)} %collective-permute-done.47.refs_2_), channel_id=1, source_target_pairs={{0,2},{2,0},{4,6},{6,4},{8,10},{10,8},{12,14},{14,12},{16,18},{18,... | collective-permute-start | bytes 1376264 | tf_op jit(solution)/shard_map/ppermute | solution.py:27
  332.6 12.8 %collective-permute-start.52 = (bf16[2,224,512]{2,1,0:T(8,128)(2,1)S(1)}, bf16[2,224,512]{2,1,0:T(8,128)(2,1)S(1)}, u32[]{:S(2)}, u32[]{:S(2)}) collective-permute-start(bf16[2,224,512]{2,1,0:T(8,128)(2,1)S(1)} %collective-permute-done.48.refs_3_), channel_id=1, source_target_pairs={{0,2},{2,0},{4,6},{6,4},{8,10},{10,8},{12,14},{14,12},{16,18},{18,... | collective-permute-start | bytes 1376264 | tf_op jit(solution)/shard_map/ppermute | solution.py:27
  334.9 15.1 %collective-permute-start.56 = (bf16[2,128,1024]{2,1,0:T(8,128)(2,1)S(1)}, bf16[2,128,1024]{2,1,0:T(8,128)(2,1)S(1)}, u32[]{:S(2)}, u32[]{:S(2)}) collective-permute-start(bf16[2,128,1024]{2,1,0:T(8,128)(2,1)S(1)} %pad_maximum_fusion.21.refs_0_), channel_id=1, source_target_pairs={{0,2},{2,0},{4,6},{6,4},{8,10},{10,8},{12,14},{14,12},{16,18},{18,... | collective-permute-start | bytes 1572872 | tf_op jit(solution)/shard_map/ppermute | solution.py:27
  339.1 10.9 %collective-permute-start.57 = (bf16[2,128,1024]{2,1,0:T(8,128)(2,1)S(1)}, bf16[2,128,1024]{2,1,0:T(8,128)(2,1)S(1)}, u32[]{:S(2)}, u32[]{:S(2)}) collective-permute-start(bf16[2,128,1024]{2,1,0:T(8,128)(2,1)S(1)} %collective-permute-done.53.refs_1_), channel_id=1, source_target_pairs={{0,2},{2,0},{4,6},{6,4},{8,10},{10,8},{12,14},{14,12},{16,18},{18,... | collective-permute-start | bytes 1572872 | tf_op jit(solution)/shard_map/ppermute | solution.py:27
  339.1 10.8 %collective-permute-start.58 = (bf16[2,128,1024]{2,1,0:T(8,128)(2,1)S(1)}, bf16[2,128,1024]{2,1,0:T(8,128)(2,1)S(1)}, u32[]{:S(2)}, u32[]{:S(2)}) collective-permute-start(bf16[2,128,1024]{2,1,0:T(8,128)(2,1)S(1)} %collective-permute-done.54.refs_2_), channel_id=1, source_target_pairs={{0,2},{2,0},{4,6},{6,4},{8,10},{10,8},{12,14},{14,12},{16,18},{18,... | collective-permute-start | bytes 1572872 | tf_op jit(solution)/shard_map/ppermute | solution.py:27
  341.2 8.8 %collective-permute-start.59 = (bf16[2,128,1024]{2,1,0:T(8,128)(2,1)S(1)}, bf16[2,128,1024]{2,1,0:T(8,128)(2,1)S(1)}, u32[]{:S(2)}, u32[]{:S(2)}) collective-permute-start(bf16[2,128,1024]{2,1,0:T(8,128)(2,1)S(1)} %collective-permute-done.55.refs_3_), channel_id=1, source_target_pairs={{0,2},{2,0},{4,6},{6,4},{8,10},{10,8},{12,14},{14,12},{16,18},{18,... | collective-permute-start | bytes 1572872 | tf_op jit(solution)/shard_map/ppermute | solution.py:27
  (63 other events, 367.1 us)
where the time goes:
time: 362 us; the launch traced here: 356 us
  waiting for transfers between devices  105 us (29%)
  starting transfers between devices  88.9 us (25%)
  matrix products  57.1 us (16%)
  other arithmetic  52.6 us (15%)
  local copies, waits for them, and re-layouts  28 us (8%)
  Pallas kernels  21.6 us (6%)
    ppermute x49, starting transfers between devices, swap_rows(): lax.ppermute(value, 'rows', [(r, r ^ masks[r % 2]) for r in range(count)])  77 us
    ppermute x49, waiting for transfers between devices, swap_rows(): lax.ppermute(value, 'rows', [(r, r ^ masks[r % 2]) for r in range(count)])  59.7 us
    ppermute x11, waiting for transfers between devices, peer_swap(): return lax.ppermute(value, 'heads', [(0, 1), (1, 0)])  45.6 us
    dot_general x13, matrix products, contract(): lax.dot_general(left, right, (((left_dim,), (right_dim,)), ((), ())), pre...  30 us
    pallas_call x3, Pallas kernels, place_blocks(): pl.pallas_call(body, grid_spec=pltpu.PrefetchScalarGridSpec(num_scalar_pr...  21.6 us
    unnamed x137, local copies, waits for them, and re-layouts  18.5 us
    convert_element_type x12, other arithmetic, part(): return total.astype(jnp.bfloat16)  12.7 us
    ppermute x11, starting transfers between devices, peer_swap(): return lax.ppermute(value, 'heads', [(0, 1), (1, 0)])  12 us
  transfers between devices with their start and end apart: 60, of which 18 were waited for; matrix products, arithmetic and copies ran while one was open for 31% of the time, Pallas kernels for 5%

commit v1 on v0

--- a/solution.py
+++ b/solution.py
@@ -151,7 +151,7 @@
         self.sides = [side(step) for step in steps]
         self.size = value.shape[0] if send is None else 2 * value.shape[0]
         self.terms, self.send = [(value, jnp.zeros((), jnp.int32))], send
-        self.pieces, self.others = [], []
+        self.pieces, self.others, self.sent = [], [], None
 
     def last(self):
         return self.pieces[-1] if self.pieces else self.terms[-1][0]
@@ -183,24 +183,17 @@
             else:
                 send, self.send = self.send, None
             got = swap_rows(send, self.masks(self.done))
+            self.sent = send
             self.terms = self.terms + [(got, jnp.zeros((), jnp.int32))]
             self.size = half
         else:
             number = 2 * count - 1 - self.done
             if self.done == count:
                 self.pieces, self.terms = [self.part(0, self.size)], []
-            elif number > 0:
+            else:
                 self.pieces = [jnp.concatenate(self.pieces, axis=0)]
-            if number > 0:
-                self.pieces = self.pieces + [swap_rows(self.pieces[0], self.masks(number))]
-                if number == 1:
-                    self.others = [swap_rows(self.pieces[0], self.masks(0))]
-            else:
-                self.pieces = self.pieces + [
-                    self.others[0],
-                    swap_rows(self.pieces[1], self.masks(0)),
-                ]
-                self.others = []
+            self.sent = self.pieces[0]
+            self.pieces = self.pieces + [swap_rows(self.sent, self.masks(number))]
         self.done += 1
 
     def peers(self):
@@ -209,16 +202,10 @@
             total = own.astype(jnp.float32) + peer_swap(own).astype(jnp.float32)
         else:
             total = lax.psum(own.astype(jnp.float32), "heads")
-        self.terms = [(total.astype(jnp.bfloat16), jnp.zeros((), jnp.int32))]
+        self.terms, self.sent = [(total.astype(jnp.bfloat16), jnp.zeros((), jnp.int32))], own
 
     def cores(self):
         self.others = [core_swap(piece) for piece in self.pieces]
-
-
-class Gathering(Summing):
-    def __init__(self, steps, own):
-        super().__init__(steps, own)
-        self.done, self.size = len(steps), 1
 
 
 def tie_sums(*sums_and_others):
@@ -228,6 +215,16 @@
     for item, value in zip(sums, values):
         item.update(value)
     return others
+
+
+def advance(item, *earlier):
+    item.update(lax.optimization_barrier((item.last(), earlier))[0])
+    item.step()
+    return item.sent
+
+
+def behind(sums, *values):
+    return lax.optimization_barrier(([item.sent for item in sums], values))[1]
 
 
 def ordered(pieces, place):
@@ -252,70 +249,82 @@
     )
 
 
-def place_blocks(kernel, index, pieces, out_specs, out_shape, name):
-    height, rows, width = pieces[0].shape
+def place_blocks(kernel, index, sums, out_specs, out_shape, name):
+    pieces = sums.pieces + sums.others
+    blocks, rows, width = pieces[0].shape
+    here = blocks // 2
 
     def body(index, *refs):
-        sources, results = refs[:8], refs[8:]
-        quarter = pl.program_id(0)
+        sources, results = refs[:4], refs[4:]
         for number, source in enumerate(sources):
-            own = index[number // 4]
-            slot = index[2] if number < 4 else 1 - index[2]
+            own = index[number // 2]
+            slot = index[2] if number < 2 else 1 - index[2]
+            quarter = pl.program_id(0) ^ (own // here)
+            inside = quarter // 2 == number % 2
+            first = quarter % 2 * here
             for core in range(2):
 
-                @pl.when(((quarter ^ (own // height)) == number % 4) & (slot == core))
-                def _(source=source, core=core, own=own):
-                    kernel(index, source, own % height, core, *results)
-
-    whole = pl.BlockSpec((height, rows, width), lambda b, i: (0, 0, 0))
+                @pl.when(inside & (slot == core))
+                def _(source=source, core=core, own=own, first=first):
+                    parts = [source[first + (k ^ (own % here))] for k in range(here)]
+                    kernel(parts, core, *results)
+
+    whole = pl.BlockSpec((blocks, rows, width), lambda b, i: (0, 0, 0))
     return pl.pallas_call(
         body,
         grid_spec=pltpu.PrefetchScalarGridSpec(
-            num_scalar_prefetch=1, grid=(4,), in_specs=[whole] * 8, out_specs=out_specs
+            num_scalar_prefetch=1, grid=(4,), in_specs=[whole] * 4, out_specs=out_specs
         ),
         out_shape=out_shape,
         cost_estimate=pl.CostEstimate(
-            flops=0, bytes_accessed=48 * height * rows * width, transcendentals=0
+            flops=0, bytes_accessed=24 * blocks * rows * width, transcendentals=0
         ),
         compiler_params=pltpu.CompilerParams(vmem_limit_bytes=26 << 20),
         name=name,
     )(index, *pieces)
 
 
-def place_ffn(index, sums, split):
-    height, rows, width = sums.pieces[0].shape
-    columns = height * (rows - split)
-
-    def kernel(index, source, low, core, gate_up, down):
-        parts = [source[k ^ low] for k in range(height)]
+def place_gate_up(index, sums):
+    blocks, rows, width = sums.pieces[0].shape
+
+    def kernel(parts, core, result):
         for k, part in enumerate(parts):
-            gate_up[k * split : (k + 1) * split, core, :] = part[:split].astype(jnp.float32)
-        value = jnp.concatenate([part[split:] for part in parts], axis=0)
-        down[:, core * columns : (core + 1) * columns] = value.astype(jnp.float32).T
+            result[k * rows : (k + 1) * rows, core, :] = part.astype(jnp.float32)
 
     return place_blocks(
         kernel,
         index,
-        sums.pieces + sums.others,
-        [
-            pl.BlockSpec((height * split, 2, width), lambda b, i: (b, 0, 0)),
-            pl.BlockSpec((width, 2 * columns), lambda b, i: (0, b)),
-        ],
-        [
-            jax.ShapeDtypeStruct((4 * height * split, 2, width), jnp.float32),
-            jax.ShapeDtypeStruct((width, 8 * columns), jnp.float32),
-        ],
-        "place_ffn",
+        sums,
+        pl.BlockSpec((blocks // 2 * rows, 2, width), lambda b, i: (b, 0, 0)),
+        jax.ShapeDtypeStruct((2 * blocks * rows, 2, width), jnp.float32),
+        "place_gate_up",
+    )
+
+
+def place_down(index, sums):
+    blocks, rows, width = sums.pieces[0].shape
+    columns = blocks // 2 * rows
+
+    def kernel(parts, core, result):
+        value = jnp.concatenate(parts, axis=0).astype(jnp.float32)
+        result[:, core * columns : (core + 1) * columns] = value.T
+
+    return place_blocks(
+        kernel,
+        index,
+        sums,
+        pl.BlockSpec((width, 2 * columns), lambda b, i: (0, b)),
+        jax.ShapeDtypeStruct((width, 8 * columns), jnp.float32),
+        "place_down",
     )
 
 
 def place_attn(index, sums, attn_cols):
-    height, rows, width = sums.pieces[0].shape
+    blocks, rows, width = sums.pieces[0].shape
     part = attn_cols // 2
 
-    def kernel(index, source, low, core, result, out):
-        value = jnp.concatenate([source[k ^ low] for k in range(height)], axis=0)
-        value = value.astype(jnp.float32)
+    def kernel(parts, core, result, out):
+        value = jnp.concatenate(parts, axis=0).astype(jnp.float32)
         place = slice(core * part, (core + 1) * part)
 
         @pl.when(pl.program_id(0) < 3)
@@ -329,7 +338,7 @@
     return place_blocks(
         kernel,
         index,
-        sums.pieces + sums.others,
+        sums,
         [
             pl.BlockSpec((1, width, attn_cols), lambda b, i: (jnp.minimum(b, 2), 0, 0)),
             pl.BlockSpec((attn_cols, width), lambda b, i: (0, 0)),
@@ -343,25 +352,25 @@
 
 
 def place_proj(index, sums, total, extra):
-    height, rows, width = sums.pieces[0].shape
-    last = total - (4 * height - 1) * rows
-
-    def kernel(index, source, low, core, result, others):
+    blocks, rows, width = sums.pieces[0].shape
+    last = total - (2 * blocks - 1) * rows
+
+    def kernel(parts, core, result, others):
         columns = slice(core * width, (core + 1) * width)
-        for k in range(height):
-            value = source[k ^ low].astype(jnp.float32)
+        for k, part in enumerate(parts):
+            value = part.astype(jnp.float32)
             result[k * rows : (k + 1) * rows, columns] = value
 
-            @pl.when((pl.program_id(0) == 3) & (k == height - 1))
-            def _(value=value):
-                others[:, columns] = value[last : last + extra]
+        @pl.when(pl.program_id(0) == 3)
+        def _():
+            others[:, columns] = value[last : last + extra]
 
     return place_blocks(
         kernel,
         index,
-        sums.pieces + sums.others,
+        sums,
         [
-            pl.BlockSpec((height * rows, 2 * width), lambda b, i: (b, 0)),
+            pl.BlockSpec((blocks // 2 * rows, 2 * width), lambda b, i: (b, 0)),
             pl.BlockSpec((extra, 2 * width), lambda b, i: (0, 0)),
         ],
         [
@@ -420,26 +429,23 @@
 
 
 def attention_backward(
-    queries, key_rows, value_rows, segments, padding, log_sums, grad_mixed, seq_len, query_count
+    queries, key_rows, value_rows, segments, padding, log_sums, grad_mixed, query_count, between
 ):
-    group_tokens, heads_here, head_size = queries.shape
-    per_seq = seq_len // query_count
-
-    def one_block(carry, item):
+    tokens, heads_here, head_size = queries.shape
+
+    def one_block(carry, item, between=lambda value: value):
         grad_keys, grad_values = carry
-        number, log_sum = item
-        query_start = number * query_count
-        row_start = number // per_seq * seq_len
+        start, log_sum = item
         scores, query_block, key_block = block_scores(
-            queries, key_rows, segments, padding, query_start, row_start, query_count, seq_len
-        )
-        grad_block = lax.dynamic_slice_in_dim(grad_mixed, query_start, query_count, 0)
+            queries, key_rows, segments, padding, start, 0, query_count, tokens
+        )
+        grad_block = lax.dynamic_slice_in_dim(grad_mixed, start, query_count, 0)
         probs = jnp.exp(scores - log_sum[:, :, None])
         grad_probs = jnp.einsum(
             "qhd,khd->hqk", grad_block, value_rows, preferred_element_type=jnp.float32
         )
-        grad_scores = probs * (grad_probs - jnp.sum(grad_probs * probs, axis=-1, keepdims=True))
-        grad_scores = grad_scores.astype(jnp.bfloat16)
+        mean = between(jnp.sum(grad_probs * probs, axis=-1, keepdims=True))
+        grad_scores = (probs * (grad_probs - mean)).astype(jnp.bfloat16)
         grad_query = jnp.einsum(
             "hqk,khd->qhd", grad_scores, key_block, preferred_element_type=jnp.float32
         )
@@ -452,15 +458,19 @@
             grad_block,
             preferred_element_type=jnp.float32,
         )
-        grad_keys = grad_keys + key_part
-        grad_values = grad_values + value_part
-        return ((grad_keys, grad_values), grad_query)
-
-    zero_grads = jnp.zeros((group_tokens, heads_here, head_size), jnp.float32)
-    (grad_keys, grad_values), grad_queries = lax.scan(
-        one_block, (zero_grads, zero_grads), (jnp.arange(group_tokens // query_count), log_sums)
-    )
-    return (grad_queries.reshape(group_tokens, heads_here, head_size), grad_keys, grad_values)
+        return ((grad_keys + key_part, grad_values + value_part), grad_query)
+
+    zero_grads = jnp.zeros((tokens, heads_here, head_size), jnp.float32)
+    starts = query_count * jnp.arange(tokens // query_count)
+    if tokens == query_count:
+        (grad_keys, grad_values), grad_queries = one_block(
+            (zero_grads, zero_grads), (0, log_sums[0]), between
+        )
+    else:
+        (grad_keys, grad_values), grad_queries = lax.scan(
+            one_block, (zero_grads, zero_grads), (starts, log_sums)
+        )
+    return (grad_queries.reshape(tokens, heads_here, head_size), grad_keys, grad_values)
 
 
 def local(
@@ -491,7 +501,7 @@
     rows_index = lax.axis_index("rows")
     places = [block_place(steps, rows_index ^ other) for other in range(2)]
     index = jnp.stack(places + [core, lax.axis_index("heads")]).astype(jnp.int32)
-    fast = lax.axis_size("heads") == 2 and blocks == 8 and attn_cols % 256 == 0
+    fast = blocks == 8 and attn_cols % 256 == 0 and ff_here % 128 == 0
     w_heads = jnp.transpose(w_qkv, (1, 0, 2))
     gate_flat = w_gate_up.reshape(model_width, 2 * ff_here)
     lifted = jnp.dot(features, w_proj, preferred_element_type=jnp.float32) + proj_bias
@@ -527,24 +537,20 @@
     activ, gelu_pull = jax.vjp(gelu_tanh, gate_up[:, :ff_here])
     up_part = gate_up[:, ff_here:]
     hidden = (activ * up_part).astype(jnp.bfloat16)
-    pair_hidden = with_pair(hidden)
     grad_hidden = contract(grad_gathered, w_down, 1, 1)
     grad_gate = gelu_pull(grad_hidden * up_part)[0].astype(jnp.bfloat16)
     grad_up = (grad_hidden * activ).astype(jnp.bfloat16)
+    grad_pre = jnp.concatenate([grad_gate, grad_up], axis=1)
+    given, own = to_owners(lambda part: contract(part, gate_flat, 1, 1), grad_pre)
+    pre_other = core_swap(jnp.where(core == 0, grad_up, grad_gate))
+    pair_hidden = with_pair(hidden)
     pair_ffn = with_pair(gathered_ffn)
-    pre_own = jnp.where(core == 0, grad_gate, grad_up)
-    pre_other = jnp.where(core == 0, grad_up, grad_gate)
-    pair_hidden, pre_own, pre_other, pair_ffn = tie_sums(pair_hidden, pre_own, pre_other, pair_ffn)
-    pre_other = core_swap(pre_other)
+    pair_pre = jnp.concatenate([jnp.where(core == 0, grad_gate, grad_up), pre_other], axis=0)
     down_part = contract(pair_cot, pair_hidden, 0, 0)
     down = Summing(steps, down_part.astype(jnp.bfloat16).reshape(blocks, -1, ff_here))
     down.step()
-    pair_pre = jnp.concatenate([pre_own, pre_other], axis=0)
     width = model_width // 2
     place = side(steps[0])
-    grad_pre = jnp.concatenate([grad_gate, grad_up], axis=1)
-    grad_pre, pair_pre = tie_sums(grad_pre, pair_pre)
-    given, own = to_owners(lambda part: contract(part, gate_flat, 1, 1), grad_pre)
     gate_send, gate_keep = (
         contract(lax.dynamic_slice_in_dim(pair_ffn, which * width, width, 1), pair_pre, 0, 0)
         .astype(jnp.bfloat16)
@@ -553,7 +559,7 @@
     )
     gate = Summing(steps, gate_keep, gate_send)
     gate.step()
-    given, own, gate_send = tie_sums(down, given, own, gate_send)
+    given, own, gate_send, gate_keep = tie_sums(down, given, own, gate_send, gate_keep)
     down.step()
     grad_normed_ffn = own + given.astype(jnp.float32)
     grad_ffn_norm, grad_gain_ffn = rms_backward(middle, scale_ffn, gain_ffn, grad_normed_ffn)
@@ -563,9 +569,18 @@
     (grad_attn_in,) = tie_sums(gate, down, grad_attn_in)
     gate.step()
     down.step()
+    (grad_attn_in,) = behind((gate, down), grad_attn_in)
     grad_mixed = contract(grad_attn_in, w_out, 1, 1).astype(jnp.bfloat16)
-    pair_mid = with_pair(grad_attn_in)
-    grad_mixed, pair_mid = tie_sums(grad_mixed, pair_mid)
+    pair_mid = []
+
+    def between(value):
+        (value,) = tie_sums(gate, down, value)
+        gate.step()
+        down.step()
+        value, group_mid = behind((gate, down), value, grad_attn_in)
+        pair_mid.append(with_pair(group_mid))
+        return value
+
     grad_queries, grad_keys, grad_values = attention_backward(
         queries,
         key_rows,
@@ -574,27 +589,30 @@
         padding,
         log_sums,
         grad_mixed.reshape(group_tokens, heads_here, HEAD_DIM),
-        group_tokens,
         query_count,
-    )
-    grad_flat = jnp.concatenate(
-        [
-            part.astype(jnp.bfloat16).reshape(group_tokens, attn_cols)
-            for part in (grad_queries, grad_keys, grad_values)
-        ],
-        axis=1,
-    )
-    w_flat = jnp.concatenate([w_heads[i] for i in range(3)], axis=1)
-    grad_flat, pair_mid = tie_sums(grad_flat, pair_mid)
-    given, own = to_owners(lambda part: contract(part, w_flat, 1, 1), grad_flat)
-    grad_flat, own, pair_mid = tie_sums(gate, down, grad_flat, own, pair_mid)
-    gate.step()
-    while down.done < count:
-        down.step()
-    pair_heads = jnp.concatenate(
-        [columns_to_pair(grad_flat[:, i * attn_cols : (i + 1) * attn_cols]) for i in range(3)],
-        axis=1,
-    )
+        between,
+    )
+    pair_mid = pair_mid[0] if pair_mid else with_pair(grad_attn_in)
+    grad_heads = [
+        part.astype(jnp.bfloat16).reshape(group_tokens, attn_cols)
+        for part in (grad_queries, grad_keys, grad_values)
+    ]
+    grad_heads = tie_sums(*grad_heads)
+    grad_all = jnp.stack(grad_heads, axis=1)
+
+    def to_normed(part):
+        return sum(contract(part[:, i], w_heads[i], 1, 1) for i in range(3))
+
+    given, own = to_owners(to_normed, grad_all)
+    width = attn_cols // 2
+    mine, theirs = (
+        jnp.concatenate(
+            [lax.dynamic_slice_in_dim(part, which * width, width, 1) for part in grad_heads],
+            axis=1,
+        )
+        for which in (core, 1 - core)
+    )
+    pair_heads = jnp.concatenate([mine, core_swap(theirs)], axis=0)
     attn_part = jnp.concatenate(
         [
             contract(pair_heads, pair_normed, 0, 0).astype(jnp.bfloat16),
@@ -604,7 +622,8 @@
     )
     attn = Summing(steps, attn_part.reshape(blocks, -1, attn_part.shape[1]))
     attn.step()
-    given, own, attn_part = tie_sums(given, own, attn_part)
+    given, own = tie_sums(gate, given, own)
+    gate.step()
     grad_normed = own + given.astype(jnp.float32)
     grad_attn_norm, grad_gain_attn = rms_backward(lifted, scale_attn, gain_attn, grad_normed)
     grad_lifted = grad_middle + grad_attn_norm
@@ -621,54 +640,63 @@
     proj_part = jnp.concatenate([proj_part, sums], axis=0)
     proj = Summing(steps, proj_part.reshape(blocks, -1, proj_part.shape[1]))
     proj.step()
-    while gate.done < count:
+    sent = advance(down, proj.sent)
+    sent = advance(attn, sent)
+    sent = advance(gate, sent)
+    hidden, grad_lift_b = lax.optimization_barrier((sent, hidden, grad_lift_b))[1:]
+    layer_out = jnp.dot(hidden, w_down, preferred_element_type=jnp.float32).astype(jnp.bfloat16)
+    layer_out = scatter_group(layer_out)
+    grad_features = contract(grad_lift_b, w_proj, 1, 1)
+    sent = advance(proj, grad_features)
+    while down.done < 2 * count:
+        sent = advance(down, sent)
+    while attn.done < count:
+        sent = advance(attn, sent)
+    sent = advance(gate, sent)
+    while proj.done < count:
+        sent = advance(proj, sent)
+    sent = advance(attn, sent)
+    layer_out, sent = lax.optimization_barrier((layer_out, sent))
+    layer_out = middle + layer_out
+    down.update(lax.optimization_barrier((down.last(), sent, layer_out))[0])
+    while down.done < 2 * count:
+        down.step()
+    down.cores()
+    if fast:
+        grad_down = place_down(index, down)
+        sent = grad_down
+    proj.update(lax.optimization_barrier((proj.last(), sent))[0])
+    proj.peers()
+    sent = advance(attn, proj.sent)
+    sent = advance(proj, sent)
+    gate.update(lax.optimization_barrier((gate.last(), sent))[0])
+    while gate.done < 2 * count:
         gate.step()
-    ffn_rows = model_width // blocks
-    ffn = Gathering(steps, jnp.concatenate([gate.part(0, 1), down.part(0, 1)], axis=1))
-    ffn.step()
-    hidden, grad_lift_b = tie_sums(proj, ffn, attn, hidden, grad_lift_b)
-    proj.step()
-    attn.step()
-    while ffn.done < 2 * count - 1:
-        ffn.step()
-    tie_sums(proj)
-    while proj.done < count:
-        proj.step()
-    layer_out = scatter_group(
-        jnp.dot(hidden, w_down, preferred_element_type=jnp.float32).astype(jnp.bfloat16)
-    )
-    grad_features = contract(grad_lift_b, w_proj, 1, 1)
-    tie_sums(proj, attn, ffn)
-    proj.peers()
-    while attn.done < count:
-        attn.step()
-    ffn.step()
-    layer_out, grad_features = tie_sums(attn, ffn, proj, layer_out, grad_features)
-    layer_out = middle + layer_out
-    proj.step()
-    attn.step()
-    ffn.cores()
+    gate.cores()
     if fast:
-        grad_gate_up, grad_down = place_ffn(index, ffn, ffn_rows)
-        tie_sums(proj, attn, grad_gate_up, grad_down)
+        grad_gate_up = place_gate_up(index, gate)
+        sent = grad_gate_up
+    sent = advance(proj, sent)
+    while attn.done < 2 * count:
+        sent = advance(attn, sent)
     while proj.done < 2 * count:
-        proj.step()
-    while attn.done < 2 * count:
-        attn.step()
-    proj.cores()
+        sent = advance(proj, sent)
+    attn.update(lax.optimization_barrier((attn.last(), sent))[0])
     attn.cores()
     if fast:
-        grad_proj, sums = place_proj(index, proj, w_proj.shape[0], 16)
         grad_qkv, grad_out = place_attn(index, attn, attn_cols)
         grad_qkv = jnp.transpose(grad_qkv, (1, 0, 2))
+        sent = grad_qkv
+    proj.update(lax.optimization_barrier((proj.last(), sent))[0])
+    proj.cores()
+    if fast:
+        grad_proj, sums = place_proj(index, proj, w_proj.shape[0], 16)
     else:
         half = attn_cols // 2
-        mine, theirs = ordered(ffn.pieces, places[0]), ordered(ffn.others, places[1])
-        pair = jnp.stack([jnp.where(core == 0, mine, theirs), jnp.where(core == 0, theirs, mine)])
-        pair = pair.reshape(2, blocks, -1, ff_here).astype(jnp.float32)
-        grad_gate_up = jnp.moveaxis(pair[:, :, :ffn_rows], 0, 2).reshape(model_width, 2, ff_here)
-        grad_down = pair[:, :, ffn_rows:].reshape(2, blocks // 2, -1, ff_here)
-        grad_down = jnp.moveaxis(grad_down, 0, 1).reshape(model_width, ff_here).T
+        pair = two_cores(gate, places, 1, (model_width, 1, ff_here))
+        grad_gate_up = pair.astype(jnp.float32)
+        pair = two_cores(down, places, 0).reshape(2, blocks // 2, -1, ff_here)
+        grad_down = jnp.moveaxis(pair, 0, 1).reshape(model_width, ff_here).T.astype(jnp.float32)
         pair = two_cores(proj, places, 1).astype(jnp.float32)
         grad_proj, sums = pair[: w_proj.shape[0]], pair[w_proj.shape[0] :]
         pair = two_cores(attn, places, 0).reshape(2, 4, half, model_width)

time: 362 us -> 329 us (0.909)
  starting transfers between devices: 88.9 us -> 70.4 us
  local copies, waits for them, and re-layouts: 28 us -> 18.6 us
  other arithmetic: 52.6 us -> 43.4 us
  waiting for transfers between devices: 105 us -> 112 us
    ppermute x49 -> x43, starting transfers between devices: 77 us -> 57.8 us  [swap_rows(): lax.ppermute(value, 'rows', [(r, r ^ masks[r % 2]) for r in range(count)])]
    unnamed x137 -> x118, local copies, waits for them, and re-layouts: 18.5 us -> 11.5 us
    ppermute x11, waiting for transfers between devices: 45.6 us -> 51.3 us  [peer_swap(): return lax.ppermute(value, 'heads', [(0, 1), (1, 0)])]
    concatenate x5 -> x2, other arithmetic: 9.14 us -> 4.36 us  [with_pair(): return jnp.concatenate([value, core_swap(value)], axis=0)]
    pallas_call x3 -> x4, Pallas kernels: 21.6 us -> 23 us  [place_blocks(): pl.pallas_call(body, grid_spec=pltpu.PrefetchScalarGridSpec(num_scalar_pr...]
    dot_general x13 -> x17, matrix products: 30 us -> 29.3 us  [contract(): lax.dot_general(left, right, (((left_dim,), (right_dim,)), ((), ())), pre...]
    ppermute x49 -> x43, waiting for transfers between devices: 59.7 us -> 60.3 us  [swap_rows(): lax.ppermute(value, 'rows', [(r, r ^ masks[r % 2]) for r in range(count)])]
  transfers between devices with their start and end apart: 60 -> 54, of which waited for: 18 -> 22; matrix products, arithmetic and copies ran while one was open for 31% -> 31% of each run, Pallas kernels for 5% -> 6%
where the time goes in v1:
time: 329 us; the launch traced here: 323 us
  waiting for transfers between devices  112 us (34%)
  starting transfers between devices  70.4 us (21%)
  matrix products  54.3 us (17%)
  other arithmetic  43.4 us (13%)
  Pallas kernels  23 us (7%)
  local copies, waits for them, and re-layouts  18.6 us (6%)
    ppermute x43, waiting for transfers between devices, swap_rows(): lax.ppermute(value, 'rows', [(r, r ^ masks[r % 2]) for r in range(count)])  60.3 us
    ppermute x43, starting transfers between devices, swap_rows(): lax.ppermute(value, 'rows', [(r, r ^ masks[r % 2]) for r in range(count)])  57.8 us
    ppermute x11, waiting for transfers between devices, peer_swap(): return lax.ppermute(value, 'heads', [(0, 1), (1, 0)])  51.3 us
    dot_general x17, matrix products, contract(): lax.dot_general(left, right, (((left_dim,), (right_dim,)), ((), ())), pre...  29.3 us
    pallas_call x4, Pallas kernels, place_blocks(): pl.pallas_call(body, grid_spec=pltpu.PrefetchScalarGridSpec(num_scalar_pr...  23 us
    ppermute x11, starting transfers between devices, peer_swap(): return lax.ppermute(value, 'heads', [(0, 1), (1, 0)])  12.7 us
    convert_element_type x12, other arithmetic, part(): return total.astype(jnp.bfloat16)  11.8 us
    unnamed x118, local copies, waits for them, and re-layouts  11.5 us
  transfers between devices with their start and end apart: 54, of which 22 were waited for; matrix products, arithmetic and copies ran while one was open for 31% of the time, Pallas kernels for 6%

profile of v1, /device:TPU:0, one launch (start us, length us, event | category | flops | bytes accessed | tf_op | source)
XLA Modules:
  0.0 323.4 jit_solution(6474843054639502094)
XLA Ops:
  0.7 3.0 collective-permute-start.1
  3.8 2.4 multiply_reduce_fusion.6
  8.1 1.9 collective-permute-start
  10.4 11.7 %collective-permute-done = bf16[256,1024]{1,0:T(8,128)(2,1)} collective-permute-done((bf16[256,1024]{1,0:T(8,128)(2,1)}, bf16[256,1024]{1,0:T(8,128)(2,1)}, u32[]{:S(2)}, u32[]{:S(2)}) %collective-permute-start) | collective-permute-done | bytes 524320 | tf_op jit(solution)/shard_map/ppermute | solution.py:35
  23.4 2.4 convolution_convert_fusion.10
  27.4 1.8 collective-permute-start.3
  32.1 1.9 copy-done.1
  34.0 2.4 fusion.39
  36.5 3.8 %collective-permute-done.3 = bf16[256,1024]{1,0:T(8,128)(2,1)S(1)} collective-permute-done((bf16[256,1024]{1,0:T(8,128)(2,1)S(1)}, bf16[256,1024]{1,0:T(8,128)(2,1)S(1)}, u32[]{:S(2)}, u32[]{:S(2)}) %collective-permute-start.3) | collective-permute-done | bytes 524320 | tf_op jit(solution)/shard_map/ppermute | solution.py:35
  45.4 6.2 %copy.30 = bf16[128,8,2,1408]{3,1,2,0:T(8,128)(2,1)} copy(bf16[128,8,2,1408]{3,2,1,0:T(2,128)(2,1)} %bitcast.104) | data formatting | bytes 11534336
  59.0 2.9 pad_maximum_fusion.5
  64.4 6.5 %collective-permute-done.5 = bf16[256,1024]{1,0:T(8,128)(2,1)S(1)} collective-permute-done((bf16[256,1024]{1,0:T(8,128)(2,1)S(1)}, bf16[256,1024]{1,0:T(8,128)(2,1)S(1)}, u32[]{:S(2)}, u32[]{:S(2)}) %collective-permute-start.5) | collective-permute-done | bytes 524320 | tf_op jit(solution)/shard_map/ppermute | solution.py:35
  71.0 3.2 fusion.78
  76.4 4.5 %broadcast_select_fusion.1 = (bf16[512,1408]{1,0:T(8,128)(2,1)S(1)}, bf16[512,1408]{1,0:T(8,128)(2,1)S(1)}, bf16[512,1408]{1,0:T(8,128)(2,1)S(1)}) fusion(pred[]{:T(512)S(6)} %eq.133, f32[512,2816]{1,0:T(8,128)S(1)} %fusion.78, bf16[512,1024]{1,0:T(8,128)(2,1)S(1)} %copy-done.12, bf16[1408,1024]{1,0:T(8,128)(2,1)S(1)} %copy-done.49), kind=kOutput, calls=%fused_computation.63 | convolution fusion | flops 1494417408 | bytes 14024705 | tf_op jit(solution)/shard_map/dot_general | solution.py:20
  81.7 1.7 fusion.36
  83.4 1.7 fusion.34
  85.1 1.8 convolution_convert_fusion.1
  87.0 1.6 collective-permute-start.14
  89.3 2.9 convolution_convert_fusion.2
  92.8 3.0 convolution_convert_fusion.3
  95.7 7.0 %collective-permute-done.15 = bf16[256,1024]{1,0:T(8,128)(2,1)S(1)} collective-permute-done((bf16[256,1024]{1,0:T(8,128)(2,1)S(1)}, bf16[256,1024]{1,0:T(8,128)(2,1)S(1)}, u32[]{:S(2)}, u32[]{:S(2)}) %collective-permute-start.15) | collective-permute-done | bytes 524320 | tf_op jit(solution)/shard_map/ppermute | solution.py:35
  103.3 1.6 fusion.75
  107.2 11.3 %collective-permute-done.17 = bf16[256,1024]{1,0:T(8,128)(2,1)} collective-permute-done((bf16[256,1024]{1,0:T(8,128)(2,1)}, bf16[256,1024]{1,0:T(8,128)(2,1)}, u32[]{:S(2)}, u32[]{:S(2)}) %collective-permute-start.17) | collective-permute-done | bytes 524320 | tf_op jit(solution)/shard_map/ppermute | solution.py:35
  118.6 2.2 pad_maximum_fusion.13
  124.5 2.0 collective-permute-start.18
  126.5 2.1 convolution_convert_fusion.9
  128.6 4.9 %multiply_reduce_fusion = (f32[8,512]{1,0:T(8,128)S(1)}, f32[8,512,512]{1,2,0:T(8,128)S(1)}) fusion(f32[8,512,512]{1,2,0:T(8,128)} %copy-done.1, f32[8,512]{1,0:T(8,128)S(1)} %log_add_fusion, pred[512,512]{0,1:T(8,128)(4,1)S(1)} %copy-done.11, bf16[512,8,64]{0,2,1:T(8,128)(2,1)S(1)} %bitcast.132, bf16[512,8,64]{0,2,1:T(8,128)(2,1)S(1)} %bitcast.131), kind=kOutput, calls=%fused_computation.1 | convolution fusion | flops 276819968 | bytes 18120704 | tf_op jit(solution)/shard_map/qhd,khd->hqk/dot_general | solution.py:444
  133.6 2.1 fusion.40
  137.0 1.9 add_convert_fusion.11
  141.4 2.8 multiply_convert_fusion
  146.5 2.5 collective-permute-start.20
  155.4 2.3 collective-permute-done.20
  157.7 10.2 %collective-permute-done.21 = bf16[256,1024]{1,0:T(8,128)(2,1)S(1)} collective-permute-done((bf16[256,1024]{1,0:T(8,128)(2,1)S(1)}, bf16[256,1024]{1,0:T(8,128)(2,1)S(1)}, u32[]{:S(2)}, u32[]{:S(2)}) %collective-permute-start.21) | collective-permute-done | bytes 524320 | tf_op jit(solution)/shard_map/ppermute | solution.py:35
  171.4 1.6 add_convert_fusion.3
  175.7 3.0 convolution_convert_fusion.4
  178.8 2.3 fusion.44
  181.3 2.5 collective-permute-start.25
  186.3 1.8 pad_maximum_fusion.21
  188.2 12.3 %collective-permute-done.25 = bf16[4,128,1024]{2,1,0:T(8,128)(2,1)S(1)} collective-permute-done((bf16[4,128,1024]{2,1,0:T(8,128)(2,1)S(1)}, bf16[4,128,1024]{2,1,0:T(8,128)(2,1)S(1)}, u32[]{:S(2)}, u32[]{:S(2)}) %collective-permute-start.25) | collective-permute-done | bytes 1048608 | tf_op jit(solution)/shard_map/ppermute | solution.py:27
  200.8 2.1 collective-permute-start.35
  202.9 1.8 convolution_convert_fusion.5
  205.4 2.3 fusion.79
  207.8 8.1 %collective-permute-done.32 = bf16[4,224,512]{2,1,0:T(8,128)(2,1)S(1)} collective-permute-done((bf16[4,224,512]{2,1,0:T(8,128)(2,1)S(1)}, bf16[4,224,512]{2,1,0:T(8,128)(2,1)S(1)}, u32[]{:S(2)}, u32[]{:S(2)}) %collective-permute-start.32) | collective-permute-done | bytes 917536 | tf_op jit(solution)/shard_map/ppermute | solution.py:27
  216.1 2.1 pad_maximum_fusion.17.refs_0_
  218.2 3.9 %collective-permute-start.38 = (bf16[4,64,1408]{2,1,0:T(8,128)(2,1)}, bf16[4,64,1408]{2,1,0:T(8,128)(2,1)}, u32[]{:S(2)}, u32[]{:S(2)}) collective-permute-start(bf16[4,64,1408]{2,1,0:T(8,128)(2,1)} %pad_maximum_fusion.17.refs_0_), channel_id=1, source_target_pairs={{0,2},{2,0},{4,6},{6,4},{8,10},{10,8},{12,14},{14,12},{16,18},{18,... | collective-permute-start | bytes 2162696 | tf_op jit(solution)/shard_map/ppermute | solution.py:27
  222.6 1.9 collective-permute-start.33
  226.2 2.8 collective-permute-start.43
  229.0 4.1 %collective-permute-done.34 = bf16[2,224,512]{2,1,0:T(8,128)(2,1)S(1)} collective-permute-done((bf16[2,224,512]{2,1,0:T(8,128)(2,1)S(1)}, bf16[2,224,512]{2,1,0:T(8,128)(2,1)S(1)}, u32[]{:S(2)}, u32[]{:S(2)}) %collective-permute-start.34) | collective-permute-done | bytes 458784 | tf_op jit(solution)/shard_map/ppermute | solution.py:27
  234.1 3.8 %collective-permute-done.33 = bf16[1,128,1024]{2,1,0:T(8,128)(2,1)S(1)} collective-permute-done((bf16[1,128,1024]{2,1,0:T(8,128)(2,1)S(1)}, bf16[1,128,1024]{2,1,0:T(8,128)(2,1)S(1)}, u32[]{:S(2)}, u32[]{:S(2)}) %collective-permute-start.33) | collective-permute-done | bytes 262176 | tf_op jit(solution)/shard_map/ppermute | solution.py:27
  239.7 4.2 %collective-permute-start.39 = (bf16[4,64,1408]{2,1,0:T(8,128)(2,1)}, bf16[4,64,1408]{2,1,0:T(8,128)(2,1)}, u32[]{:S(2)}, u32[]{:S(2)}) collective-permute-start(bf16[4,64,1408]{2,1,0:T(8,128)(2,1)} %collective-permute-done.37.refs_1_), channel_id=1, source_target_pairs={{0,2},{2,0},{4,6},{6,4},{8,10},{10,8},{12,14},{14,12},{16,18},{18,... | collective-permute-start | bytes 2162696 | tf_op jit(solution)/shard_map/ppermute | solution.py:27
  245.4 2.5 collective-permute-start.41
  247.9 5.8 %place_down.1 = f32[1408,1024]{1,0:T(8,128)} custom-call(s32[4]{0:T(128)S(1)} %pad_add_fusion.index, bf16[4,64,1408]{2,1,0:T(8,128)(2,1)} %pad_maximum_fusion.17.refs_0_, bf16[4,64,1408]{2,1,0:T(8,128)(2,1)} %collective-permute-done.37.refs_1_, bf16[4,64,1408]{2,1,0:T(8,128)(2,1)} %collective-permute-done.38.refs_2_, ...), custom_call_target="tpu_custom_call" | custom-call | bytes 8650752 | tf_op jit(solution)/shard_map/place_down/pallas_call | solution.py:273
  256.5 10.4 %collective-permute-start.44 = (bf16[4,128,1408]{2,1,0:T(8,128)(2,1)}, bf16[4,128,1408]{2,1,0:T(8,128)(2,1)S(1)}, u32[]{:S(2)}, u32[]{:S(2)}) collective-permute-start(bf16[4,128,1408]{2,1,0:T(8,128)(2,1)} %pad_maximum_fusion.8.refs_0_), channel_id=1, source_target_pairs={{0,2},{2,0},{4,6},{6,4},{8,10},{10,8},{12,14},{14,12},{16,18},{18,... | collective-permute-start | bytes 4325384 | tf_op jit(solution)/shard_map/ppermute | solution.py:27
  267.0 4.6 %collective-permute-start.45 = (bf16[4,128,1408]{2,1,0:T(8,128)(2,1)}, bf16[4,128,1408]{2,1,0:T(8,128)(2,1)S(1)}, u32[]{:S(2)}, u32[]{:S(2)}) collective-permute-start(bf16[4,128,1408]{2,1,0:T(8,128)(2,1)} %collective-permute-done.43.refs_1_), channel_id=1, source_target_pairs={{0,2},{2,0},{4,6},{6,4},{8,10},{10,8},{12,14},{14,12},{16,18},{18,... | collective-permute-start | bytes 4325384 | tf_op jit(solution)/shard_map/ppermute | solution.py:27
  273.1 1.5 collective-permute-done.45.refs_3_
  274.7 7.8 %place_gate_up.1 = f32[1024,2,1408]{2,1,0:T(2,128)} custom-call(s32[4]{0:T(128)S(1)} %pad_add_fusion.index, bf16[4,128,1408]{2,1,0:T(8,128)(2,1)} %pad_maximum_fusion.8.refs_0_, bf16[4,128,1408]{2,1,0:T(8,128)(2,1)} %collective-permute-done.43.refs_1_, bf16[4,128,1408]{2,1,0:T(8,128)(2,1)S(1)} %collective-permute-done.44.refs_2_, ...), custom_call_target="tpu_custom_call" | custom-call | bytes 17301504 | tf_op jit(solution)/shard_map/place_gate_up/pallas_call | solution.py:273
  282.5 2.8 collective-permute-done.42
  285.8 2.7 collective-permute-start.49
  288.6 13.5 %collective-permute-done.46 = bf16[2,224,512]{2,1,0:T(8,128)(2,1)S(1)} collective-permute-done((bf16[2,224,512]{2,1,0:T(8,128)(2,1)S(1)}, bf16[2,224,512]{2,1,0:T(8,128)(2,1)S(1)}, u32[]{:S(2)}, u32[]{:S(2)}) %collective-permute-start.46) | collective-permute-done | bytes 458784 | tf_op jit(solution)/shard_map/ppermute | solution.py:27
  302.8 1.8 collective-permute-start.48
  305.5 5.5 %place_attn.1 = (f32[3,1024,512]{2,1,0:T(8,128)}, f32[512,1024]{1,0:T(8,128)}) custom-call(s32[4]{0:T(128)S(1)} %pad_add_fusion.index, bf16[4,128,1024]{2,1,0:T(8,128)(2,1)S(1)} %pad_maximum_fusion.14.refs_0_, bf16[4,128,1024]{2,1,0:T(8,128)(2,1)S(1)} %collective-permute-done.49.refs_1_, bf16[4,128,1024]{2,1,0:T(8,128)(2,1)S(1)} %collective-permute-done.50.refs_2_, ...), custom_call_target="tpu_custom_call" | custom-call | bytes 12582912 | tf_op jit(solution)/shard_map/place_attn/pallas_call | solution.py:273
  311.0 5.3 %collective-permute-done.48.refs_1_ = bf16[4,224,512]{2,1,0:T(8,128)(2,1)S(1)} collective-permute-done((bf16[4,224,512]{2,1,0:T(8,128)(2,1)S(1)}, bf16[4,224,512]{2,1,0:T(8,128)(2,1)S(1)}, u32[]{:S(2)}, u32[]{:S(2)}) %collective-permute-start.48) | collective-permute-done | bytes 917536 | tf_op jit(solution)/shard_map/ppermute | solution.py:27
  316.2 2.5 collective-permute-done.53.refs_3_
  318.7 3.9 %place_proj.1 = (f32[1664,1024]{1,0:T(8,128)}, f32[16,1024]{1,0:T(8,128)S(1)}) custom-call(s32[4]{0:T(128)S(1)} %pad_add_fusion.index, bf16[4,224,512]{2,1,0:T(8,128)(2,1)S(1)} %constant_dynamic-update-slice_fusion.5.refs_0_, bf16[4,224,512]{2,1,0:T(8,128)(2,1)S(1)} %collective-permute-done.48.refs_1_, ...), custom_call_target="tpu_custom_call" | custom-call | bytes 11010048 | tf_op jit(solution)/shard_map/place_proj/pallas_call | solution.py:273
  (270 shorter events, 70.0 us)
Async XLA Ops:
  0.7 9.4 %collective-permute-start.1 = (s32[256]{0:T(256)}, s32[256]{0:T(256)S(1)}, u32[]{:S(2)}, u32[]{:S(2)}) collective-permute-start(s32[256]{0:T(256)} %param.13), channel_id=1, source_target_pairs={{0,1},{1,0},{2,3},{3,2},{4,5},{5,4},{6,7},{7,6},{8,9},{9,8},{10,11... | collective-permute-start | bytes 3080 | tf_op jit(solution)/shard_map/ppermute | solution.py:35
  3.7 6.4 %collective-permute-start.2 = (s32[256]{0:T(256)}, s32[256]{0:T(256)S(1)}, u32[]{:S(2)}, u32[]{:S(2)}) collective-permute-start(s32[256]{0:T(256)} %param.14), channel_id=1, source_target_pairs={{0,1},{1,0},{2,3},{3,2},{4,5},{5,4},{6,7},{7,6},{8,9},{9,8},{10,11... | collective-permute-start | bytes 3080 | tf_op jit(solution)/shard_map/ppermute | solution.py:35
  8.1 14.0 %collective-permute-start = (bf16[256,1024]{1,0:T(8,128)(2,1)}, bf16[256,1024]{1,0:T(8,128)(2,1)}, u32[]{:S(2)}, u32[]{:S(2)}) collective-permute-start(bf16[256,1024]{1,0:T(8,128)(2,1)} %multiply_convert_fusion.4), channel_id=1, source_target_pairs={{0,1},{1,0},{2,3},{3,2},{4,5},{5,4},{6,7},{7,6},{8,9},{9,8},{10,11... | collective-permute-start | bytes 1572872 | tf_op jit(solution)/shard_map/ppermute | solution.py:35
  10.1 15.7 %copy-start.7 = (bf16[1024,3,512]{2,0,1:T(8,128)(2,1)S(1)}, bf16[1024,3,512]{2,0,1:T(8,128)(2,1)}, u32[]{:S(2)}) copy-start(bf16[1024,3,512]{2,0,1:T(8,128)(2,1)} %param.18) | copy-start | bytes 9437188
  10.4 21.7 %copy-start.10 = (pred[512,512]{0,1:T(8,128)(4,1)}, pred[512,512]{0,1:T(8,128)(4,1)S(1)}, u32[]{:S(2)}) copy-start(pred[512,512]{0,1:T(8,128)(4,1)S(1)} %fusion.50) | copy-start | bytes 786436
  27.4 12.9 %collective-permute-start.3 = (bf16[256,1024]{1,0:T(8,128)(2,1)S(1)}, bf16[256,1024]{1,0:T(8,128)(2,1)S(1)}, u32[]{:S(2)}, u32[]{:S(2)}) collective-permute-start(bf16[256,1024]{1,0:T(8,128)(2,1)S(1)} %copy-done.22), channel_id=1, source_target_pairs={{0,1},{1,0},{2,3},{3,2},{4,5},{5,4},{6,7},{7,6},{8,9},{9,8},{10,11... | collective-permute-start | bytes 1572872 | tf_op jit(solution)/shard_map/ppermute | solution.py:35
  43.9 12.2 %collective-permute-start.4 = (bf16[256,1024]{1,0:T(8,128)(2,1)}, bf16[256,1024]{1,0:T(8,128)(2,1)}, u32[]{:S(2)}, u32[]{:S(2)}) collective-permute-start(bf16[256,1024]{1,0:T(8,128)(2,1)} %slice.110), channel_id=1, source_target_pairs={{0,1},{1,0},{2,3},{3,2},{4,5},{5,4},{6,7},{7,6},{8,9},{9,8},{10,11... | collective-permute-start | bytes 1572872 | tf_op jit(solution)/shard_map/ppermute | solution.py:35
  45.4 13.6 %collective-permute-start.9 = (bf16[256,1664]{1,0:T(8,128)(2,1)}, bf16[256,1664]{1,0:T(8,128)(2,1)}, u32[]{:S(2)}, u32[]{:S(2)}) collective-permute-start(bf16[256,1664]{1,0:T(8,128)(2,1)} %param.12), channel_id=1, source_target_pairs={{0,2},{2,0},{4,6},{6,4},{8,10},{10,8},{12,14},{14,12},{16,18},{18,... | collective-permute-start | bytes 2555912 | tf_op jit(solution)/shard_map/ppermute | solution.py:27
  51.5 11.3 %collective-permute-start.6 = (bf16[512,1024]{1,0:T(8,128)(2,1)}, bf16[512,1024]{1,0:T(8,128)(2,1)S(1)}, u32[]{:S(2)}, u32[]{:S(2)}) collective-permute-start(bf16[512,1024]{1,0:T(8,128)(2,1)} %copy-done.14), channel_id=1, source_target_pairs={{0,2},{2,0},{4,6},{6,4},{8,10},{10,8},{12,14},{14,12},{16,18},{18,... | collective-permute-start | bytes 3145736 | tf_op jit(solution)/shard_map/ppermute | solution.py:27
  53.2 8.6 %collective-permute-start.7 = (bf16[512,256]{0,1:T(8,128)(2,1)S(1)}, bf16[512,256]{0,1:T(8,128)(2,1)S(1)}, u32[]{:S(2)}, u32[]{:S(2)}) collective-permute-start(bf16[512,256]{0,1:T(8,128)(2,1)S(1)} %get-tuple-element.172), channel_id=1, source_target_pairs={{0,2},{2,0},{4,6},{6,4},{8,10},{10,8},{12,14},{14,12},{16,18},{18,... | collective-permute-start | bytes 786440 | tf_op jit(solution)/shard_map/ppermute | solution.py:27
  54.8 8.0 %collective-permute-start.8 = (bf16[512,512]{1,0:T(8,128)(2,1)S(1)}, bf16[512,512]{1,0:T(8,128)(2,1)S(1)}, u32[]{:S(2)}, u32[]{:S(2)}) collective-permute-start(bf16[512,512]{1,0:T(8,128)(2,1)S(1)} %pad_maximum_fusion.19), channel_id=1, source_target_pairs={{0,2},{2,0},{4,6},{6,4},{8,10},{10,8},{12,14},{14,12},{16,18},{18,... | collective-permute-start | bytes 1572872 | tf_op jit(solution)/shard_map/ppermute | solution.py:27
  57.4 45.8 %copy-start.2 = (f32[256,1024]{1,0:T(8,128)}, f32[256,1024]{1,0:T(8,128)S(1)}, u32[]{:S(2)}) copy-start(f32[256,1024]{1,0:T(8,128)S(1)} %get-tuple-element.154) | copy-start | bytes 3145732
  57.6 13.2 %collective-permute-start.5 = (bf16[256,1024]{1,0:T(8,128)(2,1)S(1)}, bf16[256,1024]{1,0:T(8,128)(2,1)S(1)}, u32[]{:S(2)}, u32[]{:S(2)}) collective-permute-start(bf16[256,1024]{1,0:T(8,128)(2,1)S(1)} %multiply_convert_fusion.3), channel_id=1, source_target_pairs={{0,1},{1,0},{2,3},{3,2},{4,5},{5,4},{6,7},{7,6},{8,9},{9,8},{10,11... | collective-permute-start | bytes 1572872 | tf_op jit(solution)/shard_map/ppermute | solution.py:35
  70.9 18.3 %collective-permute-start.10 = (bf16[512,1024]{1,0:T(8,128)(2,1)S(1)}, bf16[512,1024]{1,0:T(8,128)(2,1)S(1)}, u32[]{:S(2)}, u32[]{:S(2)}) collective-permute-start(bf16[512,1024]{1,0:T(8,128)(2,1)S(1)} %pad_maximum_fusion.11), channel_id=1, source_target_pairs={{0,2},{2,0},{4,6},{6,4},{8,10},{10,8},{12,14},{14,12},{16,18},{18,... | collective-permute-start | bytes 3145736 | tf_op jit(solution)/shard_map/ppermute | solution.py:27
  80.9 4.2 %collective-permute-start.13 = (bf16[512,1408]{1,0:T(8,128)(2,1)S(1)}, bf16[512,1408]{1,0:T(8,128)(2,1)S(1)}, u32[]{:S(2)}, u32[]{:S(2)}) collective-permute-start(bf16[512,1408]{1,0:T(8,128)(2,1)S(1)} %multiply_convert_fusion.1), channel_id=1, source_target_pairs={{0,2},{2,0},{4,6},{6,4},{8,10},{10,8},{12,14},{14,12},{16,18},{18,... | collective-permute-start | bytes 4325384 | tf_op jit(solution)/shard_map/ppermute | solution.py:27
  81.6 7.7 %collective-permute-start.11 = (bf16[512,1408]{1,0:T(8,128)(2,1)S(1)}, bf16[512,1408]{1,0:T(8,128)(2,1)S(1)}, u32[]{:S(2)}, u32[]{:S(2)}) collective-permute-start(bf16[512,1408]{1,0:T(8,128)(2,1)S(1)} %broadcast_select_fusion), channel_id=1, source_target_pairs={{0,2},{2,0},{4,6},{6,4},{8,10},{10,8},{12,14},{14,12},{16,18},{18,... | collective-permute-start | bytes 4325384 | tf_op jit(solution)/shard_map/ppermute | solution.py:27
  87.0 15.8 %collective-permute-start.14 = (bf16[4,64,1408]{2,1,0:T(8,128)(2,1)S(1)}, bf16[4,64,1408]{2,1,0:T(8,128)(2,1)S(1)}, u32[]{:S(2)}, u32[]{:S(2)}) collective-permute-start(bf16[4,64,1408]{2,1,0:T(8,128)(2,1)S(1)} %constant_dynamic-slice_fusion.11), channel_id=1, source_target_pairs={{0,4},{2,10},{4,0},{6,14},{8,12},{10,2},{12,8},{14,6},{16,20},{18,... | collective-permute-start | bytes 2162696 | tf_op jit(solution)/shard_map/ppermute | solution.py:27
  88.6 14.1 %collective-permute-start.15 = (bf16[256,1024]{1,0:T(8,128)(2,1)S(1)}, bf16[256,1024]{1,0:T(8,128)(2,1)S(1)}, u32[]{:S(2)}, u32[]{:S(2)}) collective-permute-start(bf16[256,1024]{1,0:T(8,128)(2,1)S(1)} %fusion.36), channel_id=1, source_target_pairs={{0,1},{1,0},{2,3},{3,2},{4,5},{5,4},{6,7},{7,6},{8,9},{9,8},{10,11... | collective-permute-start | bytes 1572872 | tf_op jit(solution)/shard_map/ppermute | solution.py:35
  92.3 28.5 %collective-permute-start.12 = (bf16[4,128,1408]{2,1,0:T(8,128)(2,1)}, bf16[4,128,1408]{2,1,0:T(8,128)(2,1)}, u32[]{:S(2)}, u32[]{:S(2)}) collective-permute-start(bf16[4,128,1408]{2,1,0:T(8,128)(2,1)} %bitcast.10), channel_id=1, source_target_pairs={{0,4},{2,10},{4,0},{6,14},{8,12},{10,2},{12,8},{14,6},{16,20},{18,... | collective-permute-start | bytes 4325384 | tf_op jit(solution)/shard_map/ppermute | solution.py:27
  104.9 13.7 %collective-permute-start.17 = (bf16[256,1024]{1,0:T(8,128)(2,1)}, bf16[256,1024]{1,0:T(8,128)(2,1)}, u32[]{:S(2)}, u32[]{:S(2)}) collective-permute-start(bf16[256,1024]{1,0:T(8,128)(2,1)} %get-tuple-element.148), channel_id=1, source_target_pairs={{0,1},{1,0},{2,3},{3,2},{4,5},{5,4},{6,7},{7,6},{8,9},{9,8},{10,11... | collective-permute-start | bytes 1572872 | tf_op jit(solution)/shard_map/ppermute | solution.py:35
  105.4 17.7 %copy-start.28 = (bf16[512,1408]{1,0:T(8,128)(2,1)S(1)}, bf16[512,1408]{1,0:T(8,128)(2,1)}, u32[]{:S(2)}) copy-start(bf16[512,1408]{1,0:T(8,128)(2,1)} %convolution_convert_fusion.3) | copy-start | bytes 4325380
  105.4 21.0 %copy-start.52 = (bf16[512,1024]{1,0:T(8,128)(2,1)S(1)}, bf16[512,1024]{1,0:T(8,128)(2,1)}, u32[]{:S(2)}) copy-start(bf16[512,1024]{1,0:T(8,128)(2,1)} %param.19) | copy-start | bytes 3145732
  106.7 14.1 %collective-permute-start.16 = (bf16[2,64,1408]{2,1,0:T(8,128)(2,1)S(1)}, bf16[2,64,1408]{2,1,0:T(8,128)(2,1)S(1)}, u32[]{:S(2)}, u32[]{:S(2)}) collective-permute-start(bf16[2,64,1408]{2,1,0:T(8,128)(2,1)S(1)} %add_convert_fusion.5), channel_id=1, source_target_pairs={{0,8},{2,6},{4,12},{6,2},{8,0},{10,14},{12,4},{14,10},{16,24},{18,... | collective-permute-start | bytes 1081352 | tf_op jit(solution)/shard_map/ppermute | solution.py:27
  121.8 13.8 %collective-permute-start.19 = (bf16[1,64,1408]{2,1,0:T(8,128)(2,1)S(1)}, bf16[1,64,1408]{2,1,0:T(8,128)(2,1)S(1)}, u32[]{:S(2)}, u32[]{:S(2)}) collective-permute-start(bf16[1,64,1408]{2,1,0:T(8,128)(2,1)S(1)} %add_convert_fusion.12), channel_id=1, source_target_pairs={{0,24},{2,26},{4,28},{6,30},{8,16},{10,18},{12,20},{14,22},{16,8},... | collective-permute-start | bytes 540680 | tf_op jit(solution)/shard_map/ppermute | solution.py:27
  124.5 12.5 %collective-permute-start.18 = (bf16[2,128,1408]{2,1,0:T(8,128)(2,1)S(1)}, bf16[2,128,1408]{2,1,0:T(8,128)(2,1)S(1)}, u32[]{:S(2)}, u32[]{:S(2)}) collective-permute-start(bf16[2,128,1408]{2,1,0:T(8,128)(2,1)S(1)} %add_convert_fusion), channel_id=1, source_target_pairs={{0,8},{2,6},{4,12},{6,2},{8,0},{10,14},{12,4},{14,10},{16,24},{18,... | collective-permute-start | bytes 2162696 | tf_op jit(solution)/shard_map/ppermute | solution.py:27
  138.9 47.4 %collective-permute-start.26 = (bf16[1,64,1408]{2,1,0:T(8,128)(2,1)}, bf16[1,64,1408]{2,1,0:T(8,128)(2,1)}, u32[]{:S(2)}, u32[]{:S(2)}) collective-permute-start(bf16[1,64,1408]{2,1,0:T(8,128)(2,1)} %add_convert_fusion.11), channel_id=1, source_target_pairs={{0,24},{2,26},{4,28},{6,30},{8,16},{10,18},{12,20},{14,22},{16,8},... | collective-permute-start | bytes 540680 | tf_op jit(solution)/shard_map/ppermute | solution.py:27
  146.5 11.2 %collective-permute-start.20 = (bf16[1,128,1408]{2,1,0:T(8,128)(2,1)S(1)}, bf16[1,128,1408]{2,1,0:T(8,128)(2,1)}, u32[]{:S(2)}, u32[]{:S(2)}) collective-permute-start(bf16[1,128,1408]{2,1,0:T(8,128)(2,1)S(1)} %add_convert_fusion.4), channel_id=1, source_target_pairs={{0,24},{2,26},{4,28},{6,30},{8,16},{10,18},{12,20},{14,22},{16,8},... | collective-permute-start | bytes 1081352 | tf_op jit(solution)/shard_map/ppermute | solution.py:27
  152.5 23.1 %collective-permute-start.23 = (bf16[512,768]{0,1:T(8,128)(2,1)}, bf16[512,768]{0,1:T(8,128)(2,1)}, u32[]{:S(2)}, u32[]{:S(2)}) collective-permute-start(bf16[512,768]{0,1:T(8,128)(2,1)} %pad_maximum_fusion.15), channel_id=1, source_target_pairs={{0,2},{2,0},{4,6},{6,4},{8,10},{10,8},{12,14},{14,12},{16,18},{18,... | collective-permute-start | bytes 2359304 | tf_op jit(solution)/shard_map/ppermute | solution.py:27
  153.5 14.4 %collective-permute-start.21 = (bf16[256,1024]{1,0:T(8,128)(2,1)S(1)}, bf16[256,1024]{1,0:T(8,128)(2,1)S(1)}, u32[]{:S(2)}, u32[]{:S(2)}) collective-permute-start(bf16[256,1024]{1,0:T(8,128)(2,1)S(1)} %fusion.43), channel_id=1, source_target_pairs={{0,1},{1,0},{2,3},{3,2},{4,5},{5,4},{6,7},{7,6},{8,9},{9,8},{10,11... | collective-permute-start | bytes 1572872 | tf_op jit(solution)/shard_map/ppermute | solution.py:35
  154.6 24.1 %collective-permute-start.24 = (bf16[512,1024]{1,0:T(8,128)(2,1)}, bf16[512,1024]{1,0:T(8,128)(2,1)}, u32[]{:S(2)}, u32[]{:S(2)}) collective-permute-start(bf16[512,1024]{1,0:T(8,128)(2,1)} %pad_maximum_fusion.13), channel_id=1, source_target_pairs={{0,2},{2,0},{4,6},{6,4},{8,10},{10,8},{12,14},{14,12},{16,18},{18,... | collective-permute-start | bytes 3145736 | tf_op jit(solution)/shard_map/ppermute | solution.py:27
  171.3 12.5 %collective-permute-start.28 = (f32[16,512]{1,0:T(8,128)S(1)}, f32[16,512]{1,0:T(8,128)S(1)}, u32[]{:S(2)}, u32[]{:S(2)}) collective-permute-start(f32[16,512]{1,0:T(8,128)S(1)} %constant_dynamic-slice_fusion.1), channel_id=1, source_target_pairs={{0,2},{2,0},{4,6},{6,4},{8,10},{10,8},{12,14},{14,12},{16,18},{18,... | collective-permute-start | bytes 98312 | tf_op jit(solution)/shard_map/ppermute | solution.py:27
  173.0 27.7 %collective-permute-start.22 = (bf16[1,128,1408]{2,1,0:T(8,128)(2,1)S(1)}, bf16[1,128,1408]{2,1,0:T(8,128)(2,1)S(1)}, u32[]{:S(2)}, u32[]{:S(2)}) collective-permute-start(bf16[1,128,1408]{2,1,0:T(8,128)(2,1)S(1)} %add_convert_fusion.3), channel_id=1, source_target_pairs={{0,24},{2,26},{4,28},{6,30},{8,16},{10,18},{12,20},{14,22},{16,8},... | collective-permute-start | bytes 1081352 | tf_op jit(solution)/shard_map/ppermute | solution.py:27
  175.6 8.2 %collective-permute-start.27 = (bf16[256,512]{1,0:T(8,128)(2,1)S(1)}, bf16[256,512]{1,0:T(8,128)(2,1)S(1)}, u32[]{:S(2)}, u32[]{:S(2)}) collective-permute-start(bf16[256,512]{1,0:T(8,128)(2,1)S(1)} %get-tuple-element.164), channel_id=1, source_target_pairs={{0,2},{2,0},{4,6},{6,4},{8,10},{10,8},{12,14},{14,12},{16,18},{18,... | collective-permute-start | bytes 786440 | tf_op jit(solution)/shard_map/ppermute | solution.py:27
  181.3 19.1 %collective-permute-start.25 = (bf16[4,128,1024]{2,1,0:T(8,128)(2,1)S(1)}, bf16[4,128,1024]{2,1,0:T(8,128)(2,1)S(1)}, u32[]{:S(2)}, u32[]{:S(2)}) collective-permute-start(bf16[4,128,1024]{2,1,0:T(8,128)(2,1)S(1)} %constant_dynamic-slice_fusion.4), channel_id=1, source_target_pairs={{0,4},{2,10},{4,0},{6,14},{8,12},{10,2},{12,8},{14,6},{16,20},{18,... | collective-permute-start | bytes 3145736 | tf_op jit(solution)/shard_map/ppermute | solution.py:27
  185.1 48.1 %copy-start.9 = (bf16[1792,512]{1,0:T(8,128)(2,1)}, bf16[1792,512]{1,0:T(8,128)(2,1)S(1)}, u32[]{:S(2)}) copy-start(bf16[1792,512]{1,0:T(8,128)(2,1)S(1)} %fusion.23) | copy-start | bytes 5505028
  185.1 17.8 %copy-start.27 = (bf16[512,1408]{1,0:T(8,128)(2,1)S(1)}, bf16[512,1408]{1,0:T(8,128)(2,1)}, u32[]{:S(2)}) copy-start(bf16[512,1408]{1,0:T(8,128)(2,1)} %copy-done.26) | copy-start | bytes 4325380
  185.1 17.8 %copy-start.50 = (bf16[1408,1024]{1,0:T(8,128)(2,1)S(1)}, bf16[1408,1024]{1,0:T(8,128)(2,1)}, u32[]{:S(2)}) copy-start(bf16[1408,1024]{1,0:T(8,128)(2,1)} %param.22) | copy-start | bytes 8650756
  185.2 30.7 %collective-permute-start.32 = (bf16[4,224,512]{2,1,0:T(8,128)(2,1)S(1)}, bf16[4,224,512]{2,1,0:T(8,128)(2,1)S(1)}, u32[]{:S(2)}, u32[]{:S(2)}) collective-permute-start(bf16[4,224,512]{2,1,0:T(8,128)(2,1)S(1)} %constant_dynamic-slice_fusion), channel_id=1, source_target_pairs={{0,4},{2,10},{4,0},{6,14},{8,12},{10,2},{12,8},{14,6},{16,20},{18,... | collective-permute-start | bytes 2752520 | tf_op jit(solution)/shard_map/ppermute | solution.py:27
  188.1 28.0 %collective-permute-start.31 = (bf16[2,64,1408]{2,1,0:T(8,128)(2,1)S(1)}, bf16[2,64,1408]{2,1,0:T(8,128)(2,1)S(1)}, u32[]{:S(2)}, u32[]{:S(2)}) collective-permute-start(bf16[2,64,1408]{2,1,0:T(8,128)(2,1)S(1)} %pad_maximum_fusion.21), channel_id=1, source_target_pairs={{0,8},{2,6},{4,12},{6,2},{8,0},{10,14},{12,4},{14,10},{16,24},{18,... | collective-permute-start | bytes 1081352 | tf_op jit(solution)/shard_map/ppermute | solution.py:27
  200.7 21.4 %collective-permute-start.30 = (bf16[2,128,1024]{2,1,0:T(8,128)(2,1)S(1)}, bf16[2,128,1024]{2,1,0:T(8,128)(2,1)S(1)}, u32[]{:S(2)}, u32[]{:S(2)}) collective-permute-start(bf16[2,128,1024]{2,1,0:T(8,128)(2,1)S(1)} %add_convert_fusion.1), channel_id=1, source_target_pairs={{0,8},{2,6},{4,12},{6,2},{8,0},{10,14},{12,4},{14,10},{16,24},{18,... | collective-permute-start | bytes 1572872 | tf_op jit(solution)/shard_map/ppermute | solution.py:27
  200.8 24.1 %collective-permute-start.35 = (bf16[2,128,1408]{2,1,0:T(8,128)(2,1)S(1)}, bf16[2,128,1408]{2,1,0:T(8,128)(2,1)S(1)}, u32[]{:S(2)}, u32[]{:S(2)}) collective-permute-start(bf16[2,128,1408]{2,1,0:T(8,128)(2,1)S(1)} %pad_maximum_fusion.16), channel_id=1, source_target_pairs={{0,8},{2,6},{4,12},{6,2},{8,0},{10,14},{12,4},{14,10},{16,24},{18,... | collective-permute-start | bytes 2162696 | tf_op jit(solution)/shard_map/ppermute | solution.py:27
  204.8 17.8 %collective-permute-start.29 = (bf16[256,1024]{1,0:T(8,128)(2,1)S(1)}, bf16[256,1024]{1,0:T(8,128)(2,1)S(1)}, u32[]{:S(2)}, u32[]{:S(2)}) collective-permute-start(bf16[256,1024]{1,0:T(8,128)(2,1)S(1)} %slice.116), channel_id=1, source_target_pairs={{0,1},{1,0},{2,3},{3,2},{4,5},{5,4},{6,7},{7,6},{8,9},{9,8},{10,11... | collective-permute-start | bytes 1572872 | tf_op jit(solution)/shard_map/ppermute | solution.py:35
  215.9 17.3 %copy-start.32 = (bf16[4,224,512]{2,1,0:T(8,128)(2,1)}, bf16[4,224,512]{2,1,0:T(8,128)(2,1)S(1)}, u32[]{:S(2)}) copy-start(bf16[4,224,512]{2,1,0:T(8,128)(2,1)S(1)} %collective-permute-done.32) | copy-start | bytes 2752516
  216.0 17.1 %collective-permute-start.34 = (bf16[2,224,512]{2,1,0:T(8,128)(2,1)S(1)}, bf16[2,224,512]{2,1,0:T(8,128)(2,1)S(1)}, u32[]{:S(2)}, u32[]{:S(2)}) collective-permute-start(bf16[2,224,512]{2,1,0:T(8,128)(2,1)S(1)} %add_convert_fusion.2), channel_id=1, source_target_pairs={{0,8},{2,6},{4,12},{6,2},{8,0},{10,14},{12,4},{14,10},{16,24},{18,... | collective-permute-start | bytes 1376264 | tf_op jit(solution)/shard_map/ppermute | solution.py:27
  218.2 29.7 %collective-permute-start.38 = (bf16[4,64,1408]{2,1,0:T(8,128)(2,1)}, bf16[4,64,1408]{2,1,0:T(8,128)(2,1)}, u32[]{:S(2)}, u32[]{:S(2)}) collective-permute-start(bf16[4,64,1408]{2,1,0:T(8,128)(2,1)} %pad_maximum_fusion.17.refs_0_), channel_id=1, source_target_pairs={{0,2},{2,0},{4,6},{6,4},{8,10},{10,8},{12,14},{14,12},{16,18},{18,... | collective-permute-start | bytes 2162696 | tf_op jit(solution)/shard_map/ppermute | solution.py:27
  222.1 17.6 %collective-permute-start.37 = (bf16[4,64,1408]{2,1,0:T(8,128)(2,1)}, bf16[4,64,1408]{2,1,0:T(8,128)(2,1)}, u32[]{:S(2)}, u32[]{:S(2)}) collective-permute-start(bf16[4,64,1408]{2,1,0:T(8,128)(2,1)} %pad_maximum_fusion.17.refs_0_), channel_id=1, source_target_pairs={{0,4},{2,10},{4,0},{6,14},{8,12},{10,2},{12,8},{14,6},{16,20},{18,... | collective-permute-start | bytes 2162696 | tf_op jit(solution)/shard_map/ppermute | solution.py:27
  222.6 15.3 %collective-permute-start.33 = (bf16[1,128,1024]{2,1,0:T(8,128)(2,1)S(1)}, bf16[1,128,1024]{2,1,0:T(8,128)(2,1)S(1)}, u32[]{:S(2)}, u32[]{:S(2)}) collective-permute-start(bf16[1,128,1024]{2,1,0:T(8,128)(2,1)S(1)} %add_convert_fusion.7), channel_id=1, source_target_pairs={{0,24},{2,26},{4,28},{6,30},{8,16},{10,18},{12,20},{14,22},{16,8},... | collective-permute-start | bytes 786440 | tf_op jit(solution)/shard_map/ppermute | solution.py:27
  226.2 40.8 %collective-permute-start.43 = (bf16[4,128,1408]{2,1,0:T(8,128)(2,1)}, bf16[4,128,1408]{2,1,0:T(8,128)(2,1)}, u32[]{:S(2)}, u32[]{:S(2)}) collective-permute-start(bf16[4,128,1408]{2,1,0:T(8,128)(2,1)} %pad_maximum_fusion.8.refs_0_), channel_id=1, source_target_pairs={{0,4},{2,10},{4,0},{6,14},{8,12},{10,2},{12,8},{14,6},{16,20},{18,... | collective-permute-start | bytes 4325384 | tf_op jit(solution)/shard_map/ppermute | solution.py:27
  239.7 8.1 %collective-permute-start.39 = (bf16[4,64,1408]{2,1,0:T(8,128)(2,1)}, bf16[4,64,1408]{2,1,0:T(8,128)(2,1)}, u32[]{:S(2)}, u32[]{:S(2)}) collective-permute-start(bf16[4,64,1408]{2,1,0:T(8,128)(2,1)} %collective-permute-done.37.refs_1_), channel_id=1, source_target_pairs={{0,2},{2,0},{4,6},{6,4},{8,10},{10,8},{12,14},{14,12},{16,18},{18,... | collective-permute-start | bytes 2162696 | tf_op jit(solution)/shard_map/ppermute | solution.py:27
  243.9 10.7 %collective-permute-start.36 = (bf16[1,224,512]{2,1,0:T(8,128)(2,1)}, bf16[1,224,512]{2,1,0:T(8,128)(2,1)}, u32[]{:S(2)}, u32[]{:S(2)}) collective-permute-start(bf16[1,224,512]{2,1,0:T(8,128)(2,1)} %add_convert_fusion.10), channel_id=1, source_target_pairs={{0,24},{2,26},{4,28},{6,30},{8,16},{10,18},{12,20},{14,22},{16,8},... | collective-permute-start | bytes 688136 | tf_op jit(solution)/shard_map/ppermute | solution.py:27
  245.4 21.5 %copy-start.16 = (bf16[1,128,1024]{2,1,0:T(8,128)(2,1)S(1)}, bf16[1,128,1024]{2,1,0:T(8,128)(2,1)}, u32[]{:S(2)}) copy-start(bf16[1,128,1024]{2,1,0:T(8,128)(2,1)} %add_convert_fusion.6) | copy-start | bytes 786436
  245.4 21.5 %collective-permute-start.41 = (bf16[1,128,1024]{2,1,0:T(8,128)(2,1)}, bf16[1,128,1024]{2,1,0:T(8,128)(2,1)S(1)}, u32[]{:S(2)}, u32[]{:S(2)}) collective-permute-start(bf16[1,128,1024]{2,1,0:T(8,128)(2,1)} %add_convert_fusion.6), channel_id=1, source_target_pairs={{0,24},{2,26},{4,28},{6,30},{8,16},{10,18},{12,20},{14,22},{16,8},... | collective-permute-start | bytes 786440 | tf_op jit(solution)/shard_map/ppermute | solution.py:27
  255.9 11.1 %collective-permute-start.40 = (bf16[1,224,512]{2,1,0:T(8,128)(2,1)S(1)}, bf16[1,224,512]{2,1,0:T(8,128)(2,1)S(1)}, u32[]{:S(2)}, u32[]{:S(2)}) collective-permute-start(bf16[1,224,512]{2,1,0:T(8,128)(2,1)S(1)} %add_convert_fusion.9), channel_id=1, source_target_pairs={{0,1},{1,0},{2,3},{3,2},{4,5},{5,4},{6,7},{7,6},{8,9},{9,8},{10,11... | collective-permute-start | bytes 688136 | tf_op jit(solution)/shard_map/ppermute | solution.py:35
  256.5 16.7 %collective-permute-start.44 = (bf16[4,128,1408]{2,1,0:T(8,128)(2,1)}, bf16[4,128,1408]{2,1,0:T(8,128)(2,1)S(1)}, u32[]{:S(2)}, u32[]{:S(2)}) collective-permute-start(bf16[4,128,1408]{2,1,0:T(8,128)(2,1)} %pad_maximum_fusion.8.refs_0_), channel_id=1, source_target_pairs={{0,2},{2,0},{4,6},{6,4},{8,10},{10,8},{12,14},{14,12},{16,18},{18,... | collective-permute-start | bytes 4325384 | tf_op jit(solution)/shard_map/ppermute | solution.py:27
  267.0 7.7 %collective-permute-start.45 = (bf16[4,128,1408]{2,1,0:T(8,128)(2,1)}, bf16[4,128,1408]{2,1,0:T(8,128)(2,1)S(1)}, u32[]{:S(2)}, u32[]{:S(2)}) collective-permute-start(bf16[4,128,1408]{2,1,0:T(8,128)(2,1)} %collective-permute-done.43.refs_1_), channel_id=1, source_target_pairs={{0,2},{2,0},{4,6},{6,4},{8,10},{10,8},{12,14},{14,12},{16,18},{18,... | collective-permute-start | bytes 4325384 | tf_op jit(solution)/shard_map/ppermute | solution.py:27
  271.6 14.1 %collective-permute-start.47 = (bf16[2,128,1024]{2,1,0:T(8,128)(2,1)S(1)}, bf16[2,128,1024]{2,1,0:T(8,128)(2,1)S(1)}, u32[]{:S(2)}, u32[]{:S(2)}) collective-permute-start(bf16[2,128,1024]{2,1,0:T(8,128)(2,1)S(1)} %pad_maximum_fusion.20), channel_id=1, source_target_pairs={{0,8},{2,6},{4,12},{6,2},{8,0},{10,14},{12,4},{14,10},{16,24},{18,... | collective-permute-start | bytes 1572872 | tf_op jit(solution)/shard_map/ppermute | solution.py:27
  271.6 13.6 %collective-permute-start.42 = (bf16[1,224,512]{2,1,0:T(8,128)(2,1)S(1)}, bf16[1,224,512]{2,1,0:T(8,128)(2,1)S(1)}, u32[]{:S(2)}, u32[]{:S(2)}) collective-permute-start(bf16[1,224,512]{2,1,0:T(8,128)(2,1)S(1)} %add_convert_fusion.8), channel_id=1, source_target_pairs={{0,24},{2,26},{4,28},{6,30},{8,16},{10,18},{12,20},{14,22},{16,8},... | collective-permute-start | bytes 688136 | tf_op jit(solution)/shard_map/ppermute | solution.py:27
  285.8 17.0 %collective-permute-start.49 = (bf16[4,128,1024]{2,1,0:T(8,128)(2,1)S(1)}, bf16[4,128,1024]{2,1,0:T(8,128)(2,1)S(1)}, u32[]{:S(2)}, u32[]{:S(2)}) collective-permute-start(bf16[4,128,1024]{2,1,0:T(8,128)(2,1)S(1)} %pad_maximum_fusion.14.refs_0_), channel_id=1, source_target_pairs={{0,4},{2,10},{4,0},{6,14},{8,12},{10,2},{12,8},{14,6},{16,20},{18,... | collective-permute-start | bytes 3145736 | tf_op jit(solution)/shard_map/ppermute | solution.py:27
  288.6 13.5 %collective-permute-start.46 = (bf16[2,224,512]{2,1,0:T(8,128)(2,1)S(1)}, bf16[2,224,512]{2,1,0:T(8,128)(2,1)S(1)}, u32[]{:S(2)}, u32[]{:S(2)}) collective-permute-start(bf16[2,224,512]{2,1,0:T(8,128)(2,1)S(1)} %get-tuple-element.173), channel_id=1, source_target_pairs={{0,8},{2,6},{4,12},{6,2},{8,0},{10,14},{12,4},{14,10},{16,24},{18,... | collective-permute-start | bytes 1376264 | tf_op jit(solution)/shard_map/ppermute | solution.py:27
  288.6 16.2 %collective-permute-start.50 = (bf16[4,128,1024]{2,1,0:T(8,128)(2,1)S(1)}, bf16[4,128,1024]{2,1,0:T(8,128)(2,1)S(1)}, u32[]{:S(2)}, u32[]{:S(2)}) collective-permute-start(bf16[4,128,1024]{2,1,0:T(8,128)(2,1)S(1)} %pad_maximum_fusion.14.refs_0_), channel_id=1, source_target_pairs={{0,2},{2,0},{4,6},{6,4},{8,10},{10,8},{12,14},{14,12},{16,18},{18,... | collective-permute-start | bytes 3145736 | tf_op jit(solution)/shard_map/ppermute | solution.py:27
  302.8 2.7 collective-permute-start.51
  302.8 13.4 %collective-permute-start.48 = (bf16[4,224,512]{2,1,0:T(8,128)(2,1)S(1)}, bf16[4,224,512]{2,1,0:T(8,128)(2,1)S(1)}, u32[]{:S(2)}, u32[]{:S(2)}) collective-permute-start(bf16[4,224,512]{2,1,0:T(8,128)(2,1)S(1)} %constant_dynamic-update-slice_fusion.5.refs_0_), channel_id=1, source_target_pairs={{0,4},{2,10},{4,0},{6,14},{8,12},{10,2},{12,8},{14,6},{16,20},{18,... | collective-permute-start | bytes 2752520 | tf_op jit(solution)/shard_map/ppermute | solution.py:27
  304.7 11.6 %collective-permute-start.52 = (bf16[4,224,512]{2,1,0:T(8,128)(2,1)S(1)}, bf16[4,224,512]{2,1,0:T(8,128)(2,1)S(1)}, u32[]{:S(2)}, u32[]{:S(2)}) collective-permute-start(bf16[4,224,512]{2,1,0:T(8,128)(2,1)S(1)} %constant_dynamic-update-slice_fusion.5.refs_0_), channel_id=1, source_target_pairs={{0,2},{2,0},{4,6},{6,4},{8,10},{10,8},{12,14},{14,12},{16,18},{18,... | collective-permute-start | bytes 2752520 | tf_op jit(solution)/shard_map/ppermute | solution.py:27
  316.2 2.5 collective-permute-start.53
  (47 other events, 271.2 us)

commit v2 on v1

--- a/solution.py
+++ b/solution.py
@@ -173,39 +173,65 @@
         )
         return total.astype(jnp.bfloat16)
 
-    def step(self):
+    def prepare(self):
         count = len(self.steps)
         if self.done < count:
             place, half = self.sides[self.done], self.size // 2
             if self.send is None:
-                send = self.part((1 - place) * half, half)
+                self.sent = self.part((1 - place) * half, half)
                 self.terms = [(term, base + place * half) for term, base in self.terms]
             else:
-                send, self.send = self.send, None
-            got = swap_rows(send, self.masks(self.done))
-            self.sent = send
-            self.terms = self.terms + [(got, jnp.zeros((), jnp.int32))]
+                self.sent, self.send = self.send, None
             self.size = half
         else:
-            number = 2 * count - 1 - self.done
             if self.done == count:
                 self.pieces, self.terms = [self.part(0, self.size)], []
             else:
                 self.pieces = [jnp.concatenate(self.pieces, axis=0)]
             self.sent = self.pieces[0]
-            self.pieces = self.pieces + [swap_rows(self.sent, self.masks(number))]
+
+    def issue(self):
+        count = len(self.steps)
+        if self.done < count:
+            got = swap_rows(self.sent, self.masks(self.done))
+            self.terms = self.terms + [(got, jnp.zeros((), jnp.int32))]
+        else:
+            self.pieces = [self.sent, swap_rows(self.sent, self.masks(2 * count - 1 - self.done))]
         self.done += 1
 
-    def peers(self):
-        own = self.part(0, self.size)
-        if lax.axis_size("heads") == 2:
-            total = own.astype(jnp.float32) + peer_swap(own).astype(jnp.float32)
-        else:
-            total = lax.psum(own.astype(jnp.float32), "heads")
-        self.terms, self.sent = [(total.astype(jnp.bfloat16), jnp.zeros((), jnp.int32))], own
+    def step(self, *values):
+        self.prepare()
+        if values:
+            self.sent, values = lax.optimization_barrier((self.sent, values))
+        self.issue()
+        return values if len(values) != 1 else values[0]
 
     def cores(self):
         self.others = [core_swap(piece) for piece in self.pieces]
+
+
+def over_peers(steps, value):
+    size = lax.axis_size("heads")
+    width = value.shape[2] // size
+    if size != 2:
+        value = lax.psum_scatter(value, "heads", scatter_dimension=2, tiled=True)
+        return Summing(steps, value)
+    mine, theirs = (
+        lax.dynamic_slice_in_dim(value, which * width, width, 2)
+        for which in (lax.axis_index("heads"), 1 - lax.axis_index("heads"))
+    )
+    half = value.shape[0] // 2
+    place = side(steps[0])
+
+    def cut(part, which):
+        return lax.dynamic_slice_in_dim(part, which * half, half, 0)
+
+    got_send = peer_swap(cut(theirs, 1 - place))
+    send = cut(mine, 1 - place).astype(jnp.float32) + got_send.astype(jnp.float32)
+    got_keep = peer_swap(cut(theirs, place))
+    total = Summing(steps, cut(mine, place), send.astype(jnp.bfloat16))
+    total.terms.append((got_keep, jnp.zeros((), jnp.int32)))
+    return total
 
 
 def tie_sums(*sums_and_others):
@@ -351,34 +377,55 @@
     )
 
 
-def place_proj(index, sums, total, extra):
-    blocks, rows, width = sums.pieces[0].shape
+def place_proj(index, pieces, total, extra):
+    blocks, rows, width = pieces[0].shape
+    here = blocks // 2
     last = total - (2 * blocks - 1) * rows
 
-    def kernel(parts, core, result, others):
-        columns = slice(core * width, (core + 1) * width)
-        for k, part in enumerate(parts):
-            value = part.astype(jnp.float32)
-            result[k * rows : (k + 1) * rows, columns] = value
-
-        @pl.when(pl.program_id(0) == 3)
-        def _():
-            others[:, columns] = value[last : last + extra]
-
-    return place_blocks(
-        kernel,
-        index,
-        sums,
-        [
-            pl.BlockSpec((blocks // 2 * rows, 2 * width), lambda b, i: (b, 0)),
-            pl.BlockSpec((extra, 2 * width), lambda b, i: (0, 0)),
+    def body(index, *refs):
+        sources, result, others = refs[:8], refs[8], refs[9]
+        for number, source in enumerate(sources):
+            mine, peer, half = number // 4, number // 2 % 2, number % 2
+            own = index[mine]
+            slot = index[2] if mine == 0 else 1 - index[2]
+            group = index[3] if peer == 0 else 1 - index[3]
+            quarter = pl.program_id(0) ^ (own // here)
+            first = quarter % 2 * here
+            for column in range(4):
+
+                @pl.when((quarter // 2 == half) & (slot * 2 + group == column))
+                def _(source=source, column=column, own=own, first=first):
+                    columns = slice(column * width, (column + 1) * width)
+                    for k in range(here):
+                        value = source[first + (k ^ (own % here))].astype(jnp.float32)
+                        result[k * rows : (k + 1) * rows, columns] = value
+
+                    @pl.when(pl.program_id(0) == 3)
+                    def _():
+                        others[:, columns] = value[last : last + extra]
+
+    whole = pl.BlockSpec((blocks, rows, width), lambda b, i: (0, 0, 0))
+    return pl.pallas_call(
+        body,
+        grid_spec=pltpu.PrefetchScalarGridSpec(
+            num_scalar_prefetch=1,
+            grid=(4,),
+            in_specs=[whole] * 8,
+            out_specs=[
+                pl.BlockSpec((here * rows, 4 * width), lambda b, i: (b, 0)),
+                pl.BlockSpec((extra, 4 * width), lambda b, i: (0, 0)),
+            ],
+        ),
+        out_shape=[
+            jax.ShapeDtypeStruct((total, 4 * width), jnp.float32),
+            jax.ShapeDtypeStruct((extra, 4 * width), jnp.float32),
         ],
-        [
-            jax.ShapeDtypeStruct((total, 2 * width), jnp.float32),
-            jax.ShapeDtypeStruct((extra, 2 * width), jnp.float32),
-        ],
-        "place_proj",
-    )
+        cost_estimate=pl.CostEstimate(
+            flops=0, bytes_accessed=48 * blocks * rows * width, transcendentals=0
+        ),
+        compiler_params=pltpu.CompilerParams(vmem_limit_bytes=26 << 20),
+        name="place_proj",
+    )(index, *pieces)
 
 
 def rms_forward(values, gain):
@@ -501,7 +548,7 @@
     rows_index = lax.axis_index("rows")
     places = [block_place(steps, rows_index ^ other) for other in range(2)]
     index = jnp.stack(places + [core, lax.axis_index("heads")]).astype(jnp.int32)
-    fast = blocks == 8 and attn_cols % 256 == 0 and ff_here % 128 == 0
+    fast = lax.axis_size("heads") == 2 and blocks == 8 and attn_cols % 256 == 0 and ff_here % 128 == 0
     w_heads = jnp.transpose(w_qkv, (1, 0, 2))
     gate_flat = w_gate_up.reshape(model_width, 2 * ff_here)
     lifted = jnp.dot(features, w_proj, preferred_element_type=jnp.float32) + proj_bias
@@ -621,9 +668,9 @@
         axis=0,
     )
     attn = Summing(steps, attn_part.reshape(blocks, -1, attn_part.shape[1]))
-    attn.step()
-    given, own = tie_sums(gate, given, own)
-    gate.step()
+    own = attn.step(own)
+    (own,) = tie_sums(gate, own)
+    own = gate.step(own)
     grad_normed = own + given.astype(jnp.float32)
     grad_attn_norm, grad_gain_attn = rms_backward(lifted, scale_attn, gain_attn, grad_normed)
     grad_lifted = grad_middle + grad_attn_norm
@@ -638,7 +685,7 @@
     sums = jnp.pad(sums, ((0, 16 * blocks - sums.shape[0]), (0, 0)))
     proj_part = contract(pair_features, columns_to_pair(grad_lift_b), 0, 0).astype(jnp.bfloat16)
     proj_part = jnp.concatenate([proj_part, sums], axis=0)
-    proj = Summing(steps, proj_part.reshape(blocks, -1, proj_part.shape[1]))
+    proj = over_peers(steps, proj_part.reshape(blocks, -1, proj_part.shape[1]))
     proj.step()
     sent = advance(down, proj.sent)
     sent = advance(attn, sent)
@@ -665,10 +712,8 @@
     if fast:
         grad_down = place_down(index, down)
         sent = grad_down
-    proj.update(lax.optimization_barrier((proj.last(), sent))[0])
-    proj.peers()
-    sent = advance(attn, proj.sent)
     sent = advance(proj, sent)
+    sent = advance(attn, sent)
     gate.update(lax.optimization_barrier((gate.last(), sent))[0])
     while gate.done < 2 * count:
         gate.step()
@@ -677,27 +722,37 @@
         grad_gate_up = place_gate_up(index, gate)
         sent = grad_gate_up
     sent = advance(proj, sent)
+    while proj.done < 2 * count - 1:
+        sent = advance(proj, sent)
+    near = [peer_swap(proj.pieces[0])] if fast else []
     while attn.done < 2 * count:
         sent = advance(attn, sent)
-    while proj.done < 2 * count:
-        sent = advance(proj, sent)
+    last, near = lax.optimization_barrier((proj.last(), near))
+    proj.update(last)
+    near += [peer_swap(proj.pieces[1])] if fast else []
+    sent = advance(proj, sent)
+    low, high = proj.pieces
     attn.update(lax.optimization_barrier((attn.last(), sent))[0])
     attn.cores()
+    attn.others, near = lax.optimization_barrier((attn.others, near))
     if fast:
+        pieces = [low, high, jnp.concatenate(near, axis=0), peer_swap(high)]
         grad_qkv, grad_out = place_attn(index, attn, attn_cols)
+        grad_qkv, pieces[3] = lax.optimization_barrier((grad_qkv, pieces[3]))
+        pieces += [core_swap(piece) for piece in pieces]
         grad_qkv = jnp.transpose(grad_qkv, (1, 0, 2))
-        sent = grad_qkv
-    proj.update(lax.optimization_barrier((proj.last(), sent))[0])
-    proj.cores()
-    if fast:
-        grad_proj, sums = place_proj(index, proj, w_proj.shape[0], 16)
+        grad_proj, sums = place_proj(index, pieces, w_proj.shape[0], 16)
     else:
+        proj.cores()
         half = attn_cols // 2
         pair = two_cores(gate, places, 1, (model_width, 1, ff_here))
         grad_gate_up = pair.astype(jnp.float32)
         pair = two_cores(down, places, 0).reshape(2, blocks // 2, -1, ff_here)
         grad_down = jnp.moveaxis(pair, 0, 1).reshape(model_width, ff_here).T.astype(jnp.float32)
-        pair = two_cores(proj, places, 1).astype(jnp.float32)
+        pair = two_cores(proj, places, 1)
+        pair = pair.reshape(pair.shape[0], 2, 1, -1)
+        pair = lax.all_gather(pair, "heads", axis=2, tiled=True).astype(jnp.float32)
+        pair = pair.reshape(pair.shape[0], -1)
         grad_proj, sums = pair[: w_proj.shape[0]], pair[w_proj.shape[0] :]
         pair = two_cores(attn, places, 0).reshape(2, 4, half, model_width)
         pair = jnp.moveaxis(pair, 0, 1).reshape(4, attn_cols, model_width).astype(jnp.float32)

time: 329 us -> 321 us (0.976)
  waiting for transfers between devices: 112 us -> 93.1 us
  local copies, waits for them, and re-layouts: 18.6 us -> 25.2 us
    ppermute x43 -> x45, waiting for transfers between devices: 60.3 us -> 30.3 us  [swap_rows(): lax.ppermute(value, 'rows', [(r, r ^ masks[r % 2]) for r in range(count)])]
    ppermute x11 -> x15, waiting for transfers between devices: 51.3 us -> 62.8 us  [peer_swap(): return lax.ppermute(value, 'heads', [(0, 1), (1, 0)])]
    unnamed x118, local copies, waits for them, and re-layouts: 11.5 us -> 16.8 us
    convert_element_type x12, other arithmetic: 11.8 us -> 16.9 us  [part(): return total.astype(jnp.bfloat16)]
    ppermute x11 -> x15, starting transfers between devices: 12.7 us -> 17.6 us  [peer_swap(): return lax.ppermute(value, 'heads', [(0, 1), (1, 0)])]
    ppermute x43 -> x45, starting transfers between devices: 57.8 us -> 53.1 us  [swap_rows(): lax.ppermute(value, 'rows', [(r, r ^ masks[r % 2]) for r in range(count)])]
    pallas_call x0 -> x1, Pallas kernels: none -> 4.28 us  [place_proj(): pl.pallas_call(body, grid_spec=pltpu.PrefetchScalarGridSpec(num_scalar_pr...]
    pallas_call x4 -> x3, Pallas kernels: 23 us -> 19.1 us  [place_blocks(): pl.pallas_call(body, grid_spec=pltpu.PrefetchScalarGridSpec(num_scalar_pr...]
  transfers between devices with their start and end apart: 54 -> 60, of which waited for: 22 -> 19; matrix products, arithmetic and copies ran while one was open for 31% -> 31% of each run, Pallas kernels for 6% -> 6%
where the time goes in v2:
time: 321 us; the launch traced here: 315 us
  waiting for transfers between devices  93.1 us (29%)
  starting transfers between devices  70.8 us (22%)
  matrix products  53.9 us (17%)
  other arithmetic  46.3 us (14%)
  local copies, waits for them, and re-layouts  25.2 us (8%)
  Pallas kernels  23.4 us (7%)
    ppermute x15, waiting for transfers between devices, peer_swap(): return lax.ppermute(value, 'heads', [(0, 1), (1, 0)])  62.8 us
    ppermute x45, starting transfers between devices, swap_rows(): lax.ppermute(value, 'rows', [(r, r ^ masks[r % 2]) for r in range(count)])  53.1 us
    ppermute x45, waiting for transfers between devices, swap_rows(): lax.ppermute(value, 'rows', [(r, r ^ masks[r % 2]) for r in range(count)])  30.3 us
    dot_general x17, matrix products, contract(): lax.dot_general(left, right, (((left_dim,), (right_dim,)), ((), ())), pre...  26.8 us
    pallas_call x3, Pallas kernels, place_blocks(): pl.pallas_call(body, grid_spec=pltpu.PrefetchScalarGridSpec(num_scalar_pr...  19.1 us
    ppermute x15, starting transfers between devices, peer_swap(): return lax.ppermute(value, 'heads', [(0, 1), (1, 0)])  17.6 us
    convert_element_type x12, other arithmetic, part(): return total.astype(jnp.bfloat16)  16.9 us
    unnamed x118, local copies, waits for them, and re-layouts  16.8 us
  transfers between devices with their start and end apart: 60, of which 19 were waited for; matrix products, arithmetic and copies ran while one was open for 31% of the time, Pallas kernels for 6%

profile of v2, /device:TPU:0, one launch (start us, length us, event | category | flops | bytes accessed | tf_op | source)
XLA Modules:
  0.0 314.6 jit_solution(1064941109314899667)
XLA Ops:
  0.7 3.0 collective-permute-start.1
  3.8 2.4 multiply_reduce_fusion.6
  8.1 1.9 collective-permute-start
  10.4 11.7 %collective-permute-done = bf16[256,1024]{1,0:T(8,128)(2,1)} collective-permute-done((bf16[256,1024]{1,0:T(8,128)(2,1)}, bf16[256,1024]{1,0:T(8,128)(2,1)}, u32[]{:S(2)}, u32[]{:S(2)}) %collective-permute-start) | collective-permute-done | bytes 524320 | tf_op jit(solution)/shard_map/ppermute | solution.py:35
  23.4 2.4 convolution_convert_fusion.10
  27.4 1.8 collective-permute-start.3
  32.1 1.9 copy-done.1
  34.0 2.4 fusion.39
  36.4 3.8 %collective-permute-done.3 = bf16[256,1024]{1,0:T(8,128)(2,1)S(1)} collective-permute-done((bf16[256,1024]{1,0:T(8,128)(2,1)S(1)}, bf16[256,1024]{1,0:T(8,128)(2,1)S(1)}, u32[]{:S(2)}, u32[]{:S(2)}) %collective-permute-start.3) | collective-permute-done | bytes 524320 | tf_op jit(solution)/shard_map/ppermute | solution.py:35
  45.4 6.2 %copy.30 = bf16[128,8,2,1408]{3,1,2,0:T(8,128)(2,1)} copy(bf16[128,8,2,1408]{3,2,1,0:T(2,128)(2,1)} %bitcast.105) | data formatting | bytes 11534336
  59.0 2.9 pad_maximum_fusion.5
  64.4 6.5 %collective-permute-done.5 = bf16[256,1024]{1,0:T(8,128)(2,1)S(1)} collective-permute-done((bf16[256,1024]{1,0:T(8,128)(2,1)S(1)}, bf16[256,1024]{1,0:T(8,128)(2,1)S(1)}, u32[]{:S(2)}, u32[]{:S(2)}) %collective-permute-start.5) | collective-permute-done | bytes 524320 | tf_op jit(solution)/shard_map/ppermute | solution.py:35
  71.0 3.2 %fusion.78 = f32[512,2816]{1,0:T(8,128)S(1)} fusion(bf16[512,1024]{1,0:T(8,128)(2,1)S(1)} %pad_maximum_fusion.10, bf16[1024,2816]{1,0:T(8,128)(2,1)S(1)} %bitcast.108), kind=kOutput, calls=%fused_computation.198 | convolution fusion | flops 2952790016 | bytes 12582912 | tf_op jit(solution)/shard_map/dot_general | solution.py:583
  76.4 4.5 %broadcast_select_fusion.1 = (bf16[512,1408]{1,0:T(8,128)(2,1)S(1)}, bf16[512,1408]{1,0:T(8,128)(2,1)S(1)}, bf16[512,1408]{1,0:T(8,128)(2,1)S(1)}) fusion(pred[]{:T(512)S(6)} %eq.133, f32[512,2816]{1,0:T(8,128)S(1)} %fusion.78, bf16[512,1024]{1,0:T(8,128)(2,1)S(1)} %copy-done.14, bf16[1408,1024]{1,0:T(8,128)(2,1)S(1)} %copy-done.49), kind=kOutput, calls=%fused_computation.62 | convolution fusion | flops 1494417408 | bytes 14024705 | tf_op jit(solution)/shard_map/dot_general | solution.py:20
  81.7 1.7 fusion.36
  83.4 1.7 fusion.34
  85.1 1.8 convolution_convert_fusion.1
  87.0 1.6 collective-permute-start.14
  89.3 3.0 convolution_convert_fusion.2
  92.8 3.0 convolution_convert_fusion.3
  95.8 7.0 %collective-permute-done.15 = bf16[256,1024]{1,0:T(8,128)(2,1)S(1)} collective-permute-done((bf16[256,1024]{1,0:T(8,128)(2,1)S(1)}, bf16[256,1024]{1,0:T(8,128)(2,1)S(1)}, u32[]{:S(2)}, u32[]{:S(2)}) %collective-permute-start.15) | collective-permute-done | bytes 524320 | tf_op jit(solution)/shard_map/ppermute | solution.py:35
  103.3 1.6 fusion.75
  107.3 11.3 %collective-permute-done.17 = bf16[256,1024]{1,0:T(8,128)(2,1)} collective-permute-done((bf16[256,1024]{1,0:T(8,128)(2,1)}, bf16[256,1024]{1,0:T(8,128)(2,1)}, u32[]{:S(2)}, u32[]{:S(2)}) %collective-permute-start.17) | collective-permute-done | bytes 524320 | tf_op jit(solution)/shard_map/ppermute | solution.py:35
  120.9 1.6 collective-permute-start.19
  123.8 1.7 collective-permute-start.18
  126.3 5.2 %multiply_reduce_fusion = (f32[8,512]{1,0:T(8,128)S(1)}, f32[8,512,512]{1,2,0:T(8,128)S(1)}) fusion(f32[8,512,512]{1,2,0:T(8,128)} %copy-done.1, f32[8,512]{1,0:T(8,128)S(1)} %log_add_fusion, pred[512,512]{0,1:T(8,128)(4,1)S(1)} %copy-done.13, bf16[512,8,64]{0,2,1:T(8,128)(2,1)S(1)} %bitcast.133, bf16[512,8,64]{0,2,1:T(8,128)(2,1)S(1)} %bitcast.132), kind=kOutput, calls=%fused_computation.1 | convolution fusion | flops 276819968 | bytes 18120704 | tf_op jit(solution)/shard_map/qhd,khd->hqk/dot_general | solution.py:491
  131.6 2.1 fusion.40
  133.7 2.3 collective-permute-done.18
  137.2 1.7 add_convert_fusion.9
  138.9 2.8 multiply_convert_fusion
  143.9 2.2 collective-permute-start.20
  150.6 1.8 convolution_convert_fusion.4
  154.4 2.6 add_convert_fusion.3
  157.0 5.2 %collective-permute-done.26 = bf16[256,1024]{1,0:T(8,128)(2,1)S(1)} collective-permute-done((bf16[256,1024]{1,0:T(8,128)(2,1)S(1)}, bf16[256,1024]{1,0:T(8,128)(2,1)S(1)}, u32[]{:S(2)}, u32[]{:S(2)}) %collective-permute-start.26) | collective-permute-done | bytes 524320 | tf_op jit(solution)/shard_map/ppermute | solution.py:35
  167.6 1.7 collective-permute-start.24
  169.3 2.6 convolution_convert_fusion
  175.2 2.6 collective-permute-start.25
  179.0 1.8 constant_dynamic-update-slice_fusion.7
  182.3 6.1 %collective-permute-done.29 = bf16[4,224,256]{2,1,0:T(8,128)(2,1)} collective-permute-done((bf16[4,224,256]{2,1,0:T(8,128)(2,1)}, bf16[4,224,256]{2,1,0:T(8,128)(2,1)}, u32[]{:S(2)}, u32[]{:S(2)}) %collective-permute-start.29) | collective-permute-done | bytes 458784 | tf_op jit(solution)/shard_map/ppermute | solution.py:35
  191.6 5.0 %collective-permute-start.32 = (bf16[2,64,1408]{2,1,0:T(8,128)(2,1)S(1)}, bf16[2,64,1408]{2,1,0:T(8,128)(2,1)S(1)}, u32[]{:S(2)}, u32[]{:S(2)}) collective-permute-start(bf16[2,64,1408]{2,1,0:T(8,128)(2,1)S(1)} %pad_maximum_fusion.20), channel_id=1, source_target_pairs={{0,8},{2,6},{4,12},{6,2},{8,0},{10,14},{12,4},{14,10},{16,24},{18,... | collective-permute-start | bytes 1081352 | tf_op jit(solution)/shard_map/ppermute | solution.py:27
  198.8 3.5 %collective-permute-start.37 = (bf16[2,128,1408]{2,1,0:T(8,128)(2,1)S(1)}, bf16[2,128,1408]{2,1,0:T(8,128)(2,1)S(1)}, u32[]{:S(2)}, u32[]{:S(2)}) collective-permute-start(bf16[2,128,1408]{2,1,0:T(8,128)(2,1)S(1)} %get-tuple-element.194), channel_id=1, source_target_pairs={{0,8},{2,6},{4,12},{6,2},{8,0},{10,14},{12,4},{14,10},{16,24},{18,... | collective-permute-start | bytes 2162696 | tf_op jit(solution)/shard_map/ppermute | solution.py:27
  202.3 3.6 %convolution_convert_fusion.5 = bf16[512,1024]{1,0:T(8,128)(2,1)S(1)} fusion(bf16[512,1408]{1,0:T(8,128)(2,1)S(1)} %copy-done.30, bf16[1408,1024]{1,0:T(8,128)(2,1)} %param.22), kind=kOutput, calls=%fused_computation.53 | convolution fusion | flops 1476919296 | bytes 5373952 | tf_op jit(solution)/shard_map/dot_general | solution.py:694
  205.9 2.3 fusion.79
  208.3 1.8 collective-permute-start.30
  212.6 1.7 collective-permute-start.39
  216.0 3.7 %collective-permute-start.35 = (bf16[1,128,1024]{2,1,0:T(8,128)(2,1)S(1)}, bf16[1,128,1024]{2,1,0:T(8,128)(2,1)S(1)}, u32[]{:S(2)}, u32[]{:S(2)}) collective-permute-start(bf16[1,128,1024]{2,1,0:T(8,128)(2,1)S(1)} %add_convert_fusion.7), channel_id=1, source_target_pairs={{0,24},{2,26},{4,28},{6,30},{8,16},{10,18},{12,20},{14,22},{16,8},... | collective-permute-start | bytes 786440 | tf_op jit(solution)/shard_map/ppermute | solution.py:27
  222.9 4.1 %collective-permute-done.35 = bf16[1,128,1024]{2,1,0:T(8,128)(2,1)S(1)} collective-permute-done((bf16[1,128,1024]{2,1,0:T(8,128)(2,1)S(1)}, bf16[1,128,1024]{2,1,0:T(8,128)(2,1)S(1)}, u32[]{:S(2)}, u32[]{:S(2)}) %collective-permute-start.35) | collective-permute-done | bytes 262176 | tf_op jit(solution)/shard_map/ppermute | solution.py:27
  227.1 1.8 add_convert_fusion.6
  229.8 4.7 %collective-permute-start.41 = (bf16[4,64,1408]{2,1,0:T(8,128)(2,1)}, bf16[4,64,1408]{2,1,0:T(8,128)(2,1)}, u32[]{:S(2)}, u32[]{:S(2)}) collective-permute-start(bf16[4,64,1408]{2,1,0:T(8,128)(2,1)} %collective-permute-done.39.refs_1_), channel_id=1, source_target_pairs={{0,2},{2,0},{4,6},{6,4},{8,10},{10,8},{12,14},{14,12},{16,18},{18,... | collective-permute-start | bytes 2162696 | tf_op jit(solution)/shard_map/ppermute | solution.py:27
  234.5 3.3 %collective-permute-start.38 = (bf16[1,224,256]{2,1,0:T(8,128)(2,1)S(1)}, bf16[1,224,256]{2,1,0:T(8,128)(2,1)}, u32[]{:S(2)}, u32[]{:S(2)}) collective-permute-start(bf16[1,224,256]{2,1,0:T(8,128)(2,1)S(1)} %add_convert_fusion.12), channel_id=1, source_target_pairs={{0,24},{2,26},{4,28},{6,30},{8,16},{10,18},{12,20},{14,22},{16,8},... | collective-permute-start | bytes 344072 | tf_op jit(solution)/shard_map/ppermute | solution.py:27
  238.5 5.8 %place_down.1 = f32[1408,1024]{1,0:T(8,128)} custom-call(s32[4]{0:T(128)S(1)} %pad_add_fusion.index, bf16[4,64,1408]{2,1,0:T(8,128)(2,1)} %pad_maximum_fusion.15.refs_0_, bf16[4,64,1408]{2,1,0:T(8,128)(2,1)} %collective-permute-done.39.refs_1_, bf16[4,64,1408]{2,1,0:T(8,128)(2,1)} %collective-permute-done.40.refs_2_, ...), custom_call_target="tpu_custom_call" | custom-call | bytes 8650752 | tf_op jit(solution)/shard_map/place_down/pallas_call | solution.py:299
  245.6 3.6 %collective-permute-done.44 = bf16[1,128,1024]{2,1,0:T(8,128)(2,1)} collective-permute-done((bf16[1,128,1024]{2,1,0:T(8,128)(2,1)}, bf16[1,128,1024]{2,1,0:T(8,128)(2,1)}, u32[]{:S(2)}, u32[]{:S(2)}) %collective-permute-start.44) | collective-permute-done | bytes 262176 | tf_op jit(solution)/shard_map/ppermute | solution.py:27
  250.2 6.2 %collective-permute-start.46 = (bf16[4,128,1408]{2,1,0:T(8,128)(2,1)}, bf16[4,128,1408]{2,1,0:T(8,128)(2,1)S(1)}, u32[]{:S(2)}, u32[]{:S(2)}) collective-permute-start(bf16[4,128,1408]{2,1,0:T(8,128)(2,1)} %collective-permute-done.43.refs_1_), channel_id=1, source_target_pairs={{0,2},{2,0},{4,6},{6,4},{8,10},{10,8},{12,14},{14,12},{16,18},{18,... | collective-permute-start | bytes 4325384 | tf_op jit(solution)/shard_map/ppermute | solution.py:27
  256.3 3.3 %collective-permute-start.42 = (bf16[1,224,256]{2,1,0:T(8,128)(2,1)S(1)}, bf16[1,224,256]{2,1,0:T(8,128)(2,1)S(1)}, u32[]{:S(2)}, u32[]{:S(2)}) collective-permute-start(bf16[1,224,256]{2,1,0:T(8,128)(2,1)S(1)} %add_convert_fusion.11), channel_id=1, source_target_pairs={{0,24},{2,26},{4,28},{6,30},{8,16},{10,18},{12,20},{14,22},{16,8},... | collective-permute-start | bytes 344072 | tf_op jit(solution)/shard_map/ppermute | solution.py:27
  259.7 7.8 %place_gate_up.1 = f32[1024,2,1408]{2,1,0:T(2,128)} custom-call(s32[4]{0:T(128)S(1)} %pad_add_fusion.index, bf16[4,128,1408]{2,1,0:T(8,128)(2,1)} %constant_dynamic-update-slice_fusion.5.refs_0_, bf16[4,128,1408]{2,1,0:T(8,128)(2,1)} %collective-permute-done.43.refs_1_, bf16[4,128,1408]{2,1,0:T(8,128)(2,1)S(1)} %collective-permute-done.45.refs_2_, ...), custom_call_target="tpu_custom_call" | custom-call | bytes 17301504 | tf_op jit(solution)/shard_map/place_gate_up/pallas_call | solution.py:299
  267.5 1.8 collective-permute-done.42
  272.8 4.8 %collective-permute-done.48 = bf16[2,224,256]{2,1,0:T(8,128)(2,1)S(1)} collective-permute-done((bf16[2,224,256]{2,1,0:T(8,128)(2,1)S(1)}, bf16[2,224,256]{2,1,0:T(8,128)(2,1)S(1)}, u32[]{:S(2)}, u32[]{:S(2)}) %collective-permute-start.48) | collective-permute-done | bytes 229408 | tf_op jit(solution)/shard_map/ppermute | solution.py:35
  277.5 3.8 %collective-permute-done.47 = bf16[2,224,256]{2,1,0:T(8,128)(2,1)S(1)} collective-permute-done((bf16[2,224,256]{2,1,0:T(8,128)(2,1)S(1)}, bf16[2,224,256]{2,1,0:T(8,128)(2,1)S(1)}, u32[]{:S(2)}, u32[]{:S(2)}) %collective-permute-start.47) | collective-permute-done | bytes 229408 | tf_op jit(solution)/shard_map/ppermute | solution.py:27
  281.3 5.7 %collective-permute-done.52.refs_1_ = bf16[4,128,1024]{2,1,0:T(8,128)(2,1)S(1)} collective-permute-done((bf16[4,128,1024]{2,1,0:T(8,128)(2,1)S(1)}, bf16[4,128,1024]{2,1,0:T(8,128)(2,1)S(1)}, u32[]{:S(2)}, u32[]{:S(2)}) %collective-permute-start.52) | collective-permute-done | bytes 1048608 | tf_op jit(solution)/shard_map/ppermute | solution.py:27
  289.1 6.5 %collective-permute-done.50.refs_1_ = bf16[4,224,256]{2,1,0:T(8,128)(2,1)S(1)} collective-permute-done((bf16[4,224,256]{2,1,0:T(8,128)(2,1)S(1)}, bf16[4,224,256]{2,1,0:T(8,128)(2,1)S(1)}, u32[]{:S(2)}, u32[]{:S(2)}) %collective-permute-start.50) | collective-permute-done | bytes 458784 | tf_op jit(solution)/shard_map/ppermute | solution.py:27
  296.6 5.5 %place_attn.1 = (f32[3,1024,512]{2,1,0:T(8,128)}, f32[512,1024]{1,0:T(8,128)}) custom-call(s32[4]{0:T(128)S(1)} %pad_add_fusion.index, bf16[4,128,1024]{2,1,0:T(8,128)(2,1)S(1)} %pad_maximum_fusion.13.refs_0_, bf16[4,128,1024]{2,1,0:T(8,128)(2,1)S(1)} %collective-permute-done.52.refs_1_, bf16[4,128,1024]{2,1,0:T(8,128)(2,1)S(1)} %collective-permute-done.51.refs_2_, ...), custom_call_target="tpu_custom_call" | custom-call | bytes 12582912 | tf_op jit(solution)/shard_map/place_attn/pallas_call | solution.py:299
  302.0 5.6 %collective-permute-done.55.refs_3_ = bf16[4,224,256]{2,1,0:T(8,128)(2,1)S(1)} collective-permute-done((bf16[4,224,256]{2,1,0:T(8,128)(2,1)S(1)}, bf16[4,224,256]{2,1,0:T(8,128)(2,1)S(1)}, u32[]{:S(2)}, u32[]{:S(2)}) %collective-permute-start.55) | collective-permute-done | bytes 458784 | tf_op jit(solution)/shard_map/ppermute | solution.py:35
  307.7 1.8 collective-permute-done.59.refs_7_
  309.5 4.3 %place_proj.1 = (f32[1664,1024]{1,0:T(8,128)}, f32[16,1024]{1,0:T(8,128)S(1)}) custom-call(s32[4]{0:T(128)S(1)} %pad_add_fusion.index, bf16[4,224,256]{2,1,0:T(8,128)(2,1)S(1)} %pad_maximum_fusion.19.refs_0_, bf16[4,224,256]{2,1,0:T(8,128)(2,1)S(1)} %collective-permute-done.50.refs_1_, bf16[4,224,256]{2,1,0:T(8,128)(2,1)S(1)} %constant_dynamic-update-slice_fusion.8.refs_2_, ...), custom_call_target="tpu_custom_call" | custom-call | bytes 11010048 | tf_op jit(solution)/shard_map/place_proj/pallas_call | solution.py:408
  (282 shorter events, 79.2 us)
Async XLA Ops:
  0.7 9.4 %collective-permute-start.1 = (s32[256]{0:T(256)}, s32[256]{0:T(256)S(1)}, u32[]{:S(2)}, u32[]{:S(2)}) collective-permute-start(s32[256]{0:T(256)} %param.13), channel_id=1, source_target_pairs={{0,1},{1,0},{2,3},{3,2},{4,5},{5,4},{6,7},{7,6},{8,9},{9,8},{10,11... | collective-permute-start | bytes 3080 | tf_op jit(solution)/shard_map/ppermute | solution.py:35
  3.7 6.3 %collective-permute-start.2 = (s32[256]{0:T(256)}, s32[256]{0:T(256)S(1)}, u32[]{:S(2)}, u32[]{:S(2)}) collective-permute-start(s32[256]{0:T(256)} %param.14), channel_id=1, source_target_pairs={{0,1},{1,0},{2,3},{3,2},{4,5},{5,4},{6,7},{7,6},{8,9},{9,8},{10,11... | collective-permute-start | bytes 3080 | tf_op jit(solution)/shard_map/ppermute | solution.py:35
  8.1 14.0 %collective-permute-start = (bf16[256,1024]{1,0:T(8,128)(2,1)}, bf16[256,1024]{1,0:T(8,128)(2,1)}, u32[]{:S(2)}, u32[]{:S(2)}) collective-permute-start(bf16[256,1024]{1,0:T(8,128)(2,1)} %multiply_convert_fusion.4), channel_id=1, source_target_pairs={{0,1},{1,0},{2,3},{3,2},{4,5},{5,4},{6,7},{7,6},{8,9},{9,8},{10,11... | collective-permute-start | bytes 1572872 | tf_op jit(solution)/shard_map/ppermute | solution.py:35
  10.4 21.7 %copy-start.12 = (pred[512,512]{0,1:T(8,128)(4,1)}, pred[512,512]{0,1:T(8,128)(4,1)S(1)}, u32[]{:S(2)}) copy-start(pred[512,512]{0,1:T(8,128)(4,1)S(1)} %fusion.50) | copy-start | bytes 786436
  27.4 12.9 %collective-permute-start.3 = (bf16[256,1024]{1,0:T(8,128)(2,1)S(1)}, bf16[256,1024]{1,0:T(8,128)(2,1)S(1)}, u32[]{:S(2)}, u32[]{:S(2)}) collective-permute-start(bf16[256,1024]{1,0:T(8,128)(2,1)S(1)} %copy-done.24), channel_id=1, source_target_pairs={{0,1},{1,0},{2,3},{3,2},{4,5},{5,4},{6,7},{7,6},{8,9},{9,8},{10,11... | collective-permute-start | bytes 1572872 | tf_op jit(solution)/shard_map/ppermute | solution.py:35
  43.8 12.2 %collective-permute-start.4 = (bf16[256,1024]{1,0:T(8,128)(2,1)}, bf16[256,1024]{1,0:T(8,128)(2,1)}, u32[]{:S(2)}, u32[]{:S(2)}) collective-permute-start(bf16[256,1024]{1,0:T(8,128)(2,1)} %slice.110), channel_id=1, source_target_pairs={{0,1},{1,0},{2,3},{3,2},{4,5},{5,4},{6,7},{7,6},{8,9},{9,8},{10,11... | collective-permute-start | bytes 1572872 | tf_op jit(solution)/shard_map/ppermute | solution.py:35
  45.4 13.6 %collective-permute-start.9 = (bf16[256,1664]{1,0:T(8,128)(2,1)}, bf16[256,1664]{1,0:T(8,128)(2,1)}, u32[]{:S(2)}, u32[]{:S(2)}) collective-permute-start(bf16[256,1664]{1,0:T(8,128)(2,1)} %param.12), channel_id=1, source_target_pairs={{0,2},{2,0},{4,6},{6,4},{8,10},{10,8},{12,14},{14,12},{16,18},{18,... | collective-permute-start | bytes 2555912 | tf_op jit(solution)/shard_map/ppermute | solution.py:27
  51.5 11.3 %collective-permute-start.6 = (bf16[512,1024]{1,0:T(8,128)(2,1)}, bf16[512,1024]{1,0:T(8,128)(2,1)S(1)}, u32[]{:S(2)}, u32[]{:S(2)}) collective-permute-start(bf16[512,1024]{1,0:T(8,128)(2,1)} %copy-done.16), channel_id=1, source_target_pairs={{0,2},{2,0},{4,6},{6,4},{8,10},{10,8},{12,14},{14,12},{16,18},{18,... | collective-permute-start | bytes 3145736 | tf_op jit(solution)/shard_map/ppermute | solution.py:27
  53.2 8.6 %collective-permute-start.7 = (bf16[512,256]{0,1:T(8,128)(2,1)S(1)}, bf16[512,256]{0,1:T(8,128)(2,1)S(1)}, u32[]{:S(2)}, u32[]{:S(2)}) collective-permute-start(bf16[512,256]{0,1:T(8,128)(2,1)S(1)} %get-tuple-element.192), channel_id=1, source_target_pairs={{0,2},{2,0},{4,6},{6,4},{8,10},{10,8},{12,14},{14,12},{16,18},{18,... | collective-permute-start | bytes 786440 | tf_op jit(solution)/shard_map/ppermute | solution.py:27
  54.8 7.9 %collective-permute-start.8 = (bf16[512,512]{1,0:T(8,128)(2,1)S(1)}, bf16[512,512]{1,0:T(8,128)(2,1)S(1)}, u32[]{:S(2)}, u32[]{:S(2)}) collective-permute-start(bf16[512,512]{1,0:T(8,128)(2,1)S(1)} %pad_maximum_fusion.17), channel_id=1, source_target_pairs={{0,2},{2,0},{4,6},{6,4},{8,10},{10,8},{12,14},{14,12},{16,18},{18,... | collective-permute-start | bytes 1572872 | tf_op jit(solution)/shard_map/ppermute | solution.py:27
  57.4 45.9 %copy-start.2 = (f32[256,1024]{1,0:T(8,128)}, f32[256,1024]{1,0:T(8,128)S(1)}, u32[]{:S(2)}) copy-start(f32[256,1024]{1,0:T(8,128)S(1)} %get-tuple-element.172) | copy-start | bytes 3145732
  57.6 13.2 %collective-permute-start.5 = (bf16[256,1024]{1,0:T(8,128)(2,1)S(1)}, bf16[256,1024]{1,0:T(8,128)(2,1)S(1)}, u32[]{:S(2)}, u32[]{:S(2)}) collective-permute-start(bf16[256,1024]{1,0:T(8,128)(2,1)S(1)} %multiply_convert_fusion.3), channel_id=1, source_target_pairs={{0,1},{1,0},{2,3},{3,2},{4,5},{5,4},{6,7},{7,6},{8,9},{9,8},{10,11... | collective-permute-start | bytes 1572872 | tf_op jit(solution)/shard_map/ppermute | solution.py:35
  70.9 18.3 %collective-permute-start.10 = (bf16[512,1024]{1,0:T(8,128)(2,1)S(1)}, bf16[512,1024]{1,0:T(8,128)(2,1)S(1)}, u32[]{:S(2)}, u32[]{:S(2)}) collective-permute-start(bf16[512,1024]{1,0:T(8,128)(2,1)S(1)} %pad_maximum_fusion.10), channel_id=1, source_target_pairs={{0,2},{2,0},{4,6},{6,4},{8,10},{10,8},{12,14},{14,12},{16,18},{18,... | collective-permute-start | bytes 3145736 | tf_op jit(solution)/shard_map/ppermute | solution.py:27
  80.9 4.2 %collective-permute-start.13 = (bf16[512,1408]{1,0:T(8,128)(2,1)S(1)}, bf16[512,1408]{1,0:T(8,128)(2,1)S(1)}, u32[]{:S(2)}, u32[]{:S(2)}) collective-permute-start(bf16[512,1408]{1,0:T(8,128)(2,1)S(1)} %multiply_convert_fusion.1), channel_id=1, source_target_pairs={{0,2},{2,0},{4,6},{6,4},{8,10},{10,8},{12,14},{14,12},{16,18},{18,... | collective-permute-start | bytes 4325384 | tf_op jit(solution)/shard_map/ppermute | solution.py:27
  81.6 7.7 %collective-permute-start.11 = (bf16[512,1408]{1,0:T(8,128)(2,1)S(1)}, bf16[512,1408]{1,0:T(8,128)(2,1)S(1)}, u32[]{:S(2)}, u32[]{:S(2)}) collective-permute-start(bf16[512,1408]{1,0:T(8,128)(2,1)S(1)} %broadcast_select_fusion), channel_id=1, source_target_pairs={{0,2},{2,0},{4,6},{6,4},{8,10},{10,8},{12,14},{14,12},{16,18},{18,... | collective-permute-start | bytes 4325384 | tf_op jit(solution)/shard_map/ppermute | solution.py:27
  87.0 15.8 %collective-permute-start.14 = (bf16[4,64,1408]{2,1,0:T(8,128)(2,1)S(1)}, bf16[4,64,1408]{2,1,0:T(8,128)(2,1)S(1)}, u32[]{:S(2)}, u32[]{:S(2)}) collective-permute-start(bf16[4,64,1408]{2,1,0:T(8,128)(2,1)S(1)} %constant_dynamic-slice_fusion.12), channel_id=1, source_target_pairs={{0,4},{2,10},{4,0},{6,14},{8,12},{10,2},{12,8},{14,6},{16,20},{18,... | collective-permute-start | bytes 2162696 | tf_op jit(solution)/shard_map/ppermute | solution.py:27
  88.7 14.1 %collective-permute-start.15 = (bf16[256,1024]{1,0:T(8,128)(2,1)S(1)}, bf16[256,1024]{1,0:T(8,128)(2,1)S(1)}, u32[]{:S(2)}, u32[]{:S(2)}) collective-permute-start(bf16[256,1024]{1,0:T(8,128)(2,1)S(1)} %fusion.36), channel_id=1, source_target_pairs={{0,1},{1,0},{2,3},{3,2},{4,5},{5,4},{6,7},{7,6},{8,9},{9,8},{10,11... | collective-permute-start | bytes 1572872 | tf_op jit(solution)/shard_map/ppermute | solution.py:35
  92.3 27.5 %collective-permute-start.12 = (bf16[4,128,1408]{2,1,0:T(8,128)(2,1)}, bf16[4,128,1408]{2,1,0:T(8,128)(2,1)}, u32[]{:S(2)}, u32[]{:S(2)}) collective-permute-start(bf16[4,128,1408]{2,1,0:T(8,128)(2,1)} %bitcast.10), channel_id=1, source_target_pairs={{0,4},{2,10},{4,0},{6,14},{8,12},{10,2},{12,8},{14,6},{16,20},{18,... | collective-permute-start | bytes 4325384 | tf_op jit(solution)/shard_map/ppermute | solution.py:27
  104.9 13.7 %collective-permute-start.17 = (bf16[256,1024]{1,0:T(8,128)(2,1)}, bf16[256,1024]{1,0:T(8,128)(2,1)}, u32[]{:S(2)}, u32[]{:S(2)}) collective-permute-start(bf16[256,1024]{1,0:T(8,128)(2,1)} %get-tuple-element.166), channel_id=1, source_target_pairs={{0,1},{1,0},{2,3},{3,2},{4,5},{5,4},{6,7},{7,6},{8,9},{9,8},{10,11... | collective-permute-start | bytes 1572872 | tf_op jit(solution)/shard_map/ppermute | solution.py:35
  106.8 13.1 %collective-permute-start.16 = (bf16[2,64,1408]{2,1,0:T(8,128)(2,1)S(1)}, bf16[2,64,1408]{2,1,0:T(8,128)(2,1)S(1)}, u32[]{:S(2)}, u32[]{:S(2)}) collective-permute-start(bf16[2,64,1408]{2,1,0:T(8,128)(2,1)S(1)} %add_convert_fusion.5), channel_id=1, source_target_pairs={{0,8},{2,6},{4,12},{6,2},{8,0},{10,14},{12,4},{14,10},{16,24},{18,... | collective-permute-start | bytes 1081352 | tf_op jit(solution)/shard_map/ppermute | solution.py:27
  120.9 12.8 %collective-permute-start.19 = (bf16[1,64,1408]{2,1,0:T(8,128)(2,1)S(1)}, bf16[1,64,1408]{2,1,0:T(8,128)(2,1)S(1)}, u32[]{:S(2)}, u32[]{:S(2)}) collective-permute-start(bf16[1,64,1408]{2,1,0:T(8,128)(2,1)S(1)} %add_convert_fusion.10), channel_id=1, source_target_pairs={{0,24},{2,26},{4,28},{6,30},{8,16},{10,18},{12,20},{14,22},{16,8},... | collective-permute-start | bytes 540680 | tf_op jit(solution)/shard_map/ppermute | solution.py:27
  123.8 12.2 %collective-permute-start.18 = (bf16[2,128,1408]{2,1,0:T(8,128)(2,1)S(1)}, bf16[2,128,1408]{2,1,0:T(8,128)(2,1)S(1)}, u32[]{:S(2)}, u32[]{:S(2)}) collective-permute-start(bf16[2,128,1408]{2,1,0:T(8,128)(2,1)S(1)} %add_convert_fusion), channel_id=1, source_target_pairs={{0,8},{2,6},{4,12},{6,2},{8,0},{10,14},{12,4},{14,10},{16,24},{18,... | collective-permute-start | bytes 2162696 | tf_op jit(solution)/shard_map/ppermute | solution.py:27
  143.9 10.5 %collective-permute-start.20 = (bf16[1,128,1408]{2,1,0:T(8,128)(2,1)S(1)}, bf16[1,128,1408]{2,1,0:T(8,128)(2,1)S(1)}, u32[]{:S(2)}, u32[]{:S(2)}) collective-permute-start(bf16[1,128,1408]{2,1,0:T(8,128)(2,1)S(1)} %add_convert_fusion.4), channel_id=1, source_target_pairs={{0,24},{2,26},{4,28},{6,30},{8,16},{10,18},{12,20},{14,22},{16,8},... | collective-permute-start | bytes 1081352 | tf_op jit(solution)/shard_map/ppermute | solution.py:27
  146.8 3.2 %collective-permute-start.21 = (bf16[512,768]{0,1:T(8,128)(2,1)S(1)}, bf16[512,768]{0,1:T(8,128)(2,1)S(1)}, u32[]{:S(2)}, u32[]{:S(2)}) collective-permute-start(bf16[512,768]{0,1:T(8,128)(2,1)S(1)} %pad_maximum_fusion.14), channel_id=1, source_target_pairs={{0,2},{2,0},{4,6},{6,4},{8,10},{10,8},{12,14},{14,12},{16,18},{18,... | collective-permute-start | bytes 2359304 | tf_op jit(solution)/shard_map/ppermute | solution.py:27
  147.8 14.4 %collective-permute-start.26 = (bf16[256,1024]{1,0:T(8,128)(2,1)S(1)}, bf16[256,1024]{1,0:T(8,128)(2,1)S(1)}, u32[]{:S(2)}, u32[]{:S(2)}) collective-permute-start(bf16[256,1024]{1,0:T(8,128)(2,1)S(1)} %fusion.43), channel_id=1, source_target_pairs={{0,1},{1,0},{2,3},{3,2},{4,5},{5,4},{6,7},{7,6},{8,9},{9,8},{10,11... | collective-permute-start | bytes 1572872 | tf_op jit(solution)/shard_map/ppermute | solution.py:35
  147.9 4.5 %collective-permute-start.22 = (bf16[512,1024]{1,0:T(8,128)(2,1)S(1)}, bf16[512,1024]{1,0:T(8,128)(2,1)S(1)}, u32[]{:S(2)}, u32[]{:S(2)}) collective-permute-start(bf16[512,1024]{1,0:T(8,128)(2,1)S(1)} %pad_maximum_fusion.12), channel_id=1, source_target_pairs={{0,2},{2,0},{4,6},{6,4},{8,10},{10,8},{12,14},{14,12},{16,18},{18,... | collective-permute-start | bytes 3145736 | tf_op jit(solution)/shard_map/ppermute | solution.py:27
  165.7 3.7 %collective-permute-start.27 = (bf16[256,512]{1,0:T(8,128)(2,1)}, bf16[256,512]{1,0:T(8,128)(2,1)}, u32[]{:S(2)}, u32[]{:S(2)}) collective-permute-start(bf16[256,512]{1,0:T(8,128)(2,1)} %get-tuple-element.184), channel_id=1, source_target_pairs={{0,2},{2,0},{4,6},{6,4},{8,10},{10,8},{12,14},{14,12},{16,18},{18,... | collective-permute-start | bytes 786440 | tf_op jit(solution)/shard_map/ppermute | solution.py:27
  167.0 2.3 collective-permute-start.28
  167.6 29.0 %collective-permute-start.24 = (bf16[4,128,1024]{2,1,0:T(8,128)(2,1)}, bf16[4,128,1024]{2,1,0:T(8,128)(2,1)}, u32[]{:S(2)}, u32[]{:S(2)}) collective-permute-start(bf16[4,128,1024]{2,1,0:T(8,128)(2,1)} %constant_dynamic-slice_fusion.5), channel_id=1, source_target_pairs={{0,4},{2,10},{4,0},{6,14},{8,12},{10,2},{12,8},{14,6},{16,20},{18,... | collective-permute-start | bytes 3145736 | tf_op jit(solution)/shard_map/ppermute | solution.py:27
  174.6 13.8 %collective-permute-start.29 = (bf16[4,224,256]{2,1,0:T(8,128)(2,1)}, bf16[4,224,256]{2,1,0:T(8,128)(2,1)}, u32[]{:S(2)}, u32[]{:S(2)}) collective-permute-start(bf16[4,224,256]{2,1,0:T(8,128)(2,1)} %get-tuple-element.174), channel_id=1, source_target_pairs={{0,1},{1,0},{2,3},{3,2},{4,5},{5,4},{6,7},{7,6},{8,9},{9,8},{10,11... | collective-permute-start | bytes 1376264 | tf_op jit(solution)/shard_map/ppermute | solution.py:35
  175.2 21.5 %copy-start.10 = (bf16[1024,1024]{1,0:T(8,128)(2,1)S(1)}, bf16[1024,1024]{1,0:T(8,128)(2,1)}, u32[]{:S(2)}) copy-start(bf16[1024,1024]{1,0:T(8,128)(2,1)} %copy-done.9) | copy-start | bytes 6291460
  175.2 27.1 %copy-start.30 = (bf16[512,1408]{1,0:T(8,128)(2,1)S(1)}, bf16[512,1408]{1,0:T(8,128)(2,1)}, u32[]{:S(2)}) copy-start(bf16[512,1408]{1,0:T(8,128)(2,1)} %copy-done.29) | copy-start | bytes 4325380
  175.2 15.5 %collective-permute-start.25 = (bf16[1,64,1408]{2,1,0:T(8,128)(2,1)}, bf16[1,64,1408]{2,1,0:T(8,128)(2,1)S(1)}, u32[]{:S(2)}, u32[]{:S(2)}) collective-permute-start(bf16[1,64,1408]{2,1,0:T(8,128)(2,1)} %add_convert_fusion.9), channel_id=1, source_target_pairs={{0,24},{2,26},{4,28},{6,30},{8,16},{10,18},{12,20},{14,22},{16,8},... | collective-permute-start | bytes 540680 | tf_op jit(solution)/shard_map/ppermute | solution.py:27
  177.8 20.2 %collective-permute-start.23 = (bf16[1,128,1408]{2,1,0:T(8,128)(2,1)}, bf16[1,128,1408]{2,1,0:T(8,128)(2,1)S(1)}, u32[]{:S(2)}, u32[]{:S(2)}) collective-permute-start(bf16[1,128,1408]{2,1,0:T(8,128)(2,1)} %add_convert_fusion.3), channel_id=1, source_target_pairs={{0,24},{2,26},{4,28},{6,30},{8,16},{10,18},{12,20},{14,22},{16,8},... | collective-permute-start | bytes 1081352 | tf_op jit(solution)/shard_map/ppermute | solution.py:27
  180.8 29.4 %collective-permute-start.33 = (bf16[4,224,256]{2,1,0:T(8,128)(2,1)}, bf16[4,224,256]{2,1,0:T(8,128)(2,1)S(1)}, u32[]{:S(2)}, u32[]{:S(2)}) collective-permute-start(bf16[4,224,256]{2,1,0:T(8,128)(2,1)} %get-tuple-element.173), channel_id=1, source_target_pairs={{0,1},{1,0},{2,3},{3,2},{4,5},{5,4},{6,7},{7,6},{8,9},{9,8},{10,11... | collective-permute-start | bytes 1376264 | tf_op jit(solution)/shard_map/ppermute | solution.py:35
  189.8 18.5 %collective-permute-start.34 = (bf16[4,224,256]{2,1,0:T(8,128)(2,1)S(1)}, bf16[4,224,256]{2,1,0:T(8,128)(2,1)S(1)}, u32[]{:S(2)}, u32[]{:S(2)}) collective-permute-start(bf16[4,224,256]{2,1,0:T(8,128)(2,1)S(1)} %add_convert_fusion.2), channel_id=1, source_target_pairs={{0,4},{2,10},{4,0},{6,14},{8,12},{10,2},{12,8},{14,6},{16,20},{18,... | collective-permute-start | bytes 1376264 | tf_op jit(solution)/shard_map/ppermute | solution.py:27
  191.6 20.0 %collective-permute-start.32 = (bf16[2,64,1408]{2,1,0:T(8,128)(2,1)S(1)}, bf16[2,64,1408]{2,1,0:T(8,128)(2,1)S(1)}, u32[]{:S(2)}, u32[]{:S(2)}) collective-permute-start(bf16[2,64,1408]{2,1,0:T(8,128)(2,1)S(1)} %pad_maximum_fusion.20), channel_id=1, source_target_pairs={{0,8},{2,6},{4,12},{6,2},{8,0},{10,14},{12,4},{14,10},{16,24},{18,... | collective-permute-start | bytes 1081352 | tf_op jit(solution)/shard_map/ppermute | solution.py:27
  197.9 14.7 %collective-permute-start.31 = (bf16[2,128,1024]{2,1,0:T(8,128)(2,1)S(1)}, bf16[2,128,1024]{2,1,0:T(8,128)(2,1)S(1)}, u32[]{:S(2)}, u32[]{:S(2)}) collective-permute-start(bf16[2,128,1024]{2,1,0:T(8,128)(2,1)S(1)} %add_convert_fusion.1), channel_id=1, source_target_pairs={{0,8},{2,6},{4,12},{6,2},{8,0},{10,14},{12,4},{14,10},{16,24},{18,... | collective-permute-start | bytes 1572872 | tf_op jit(solution)/shard_map/ppermute | solution.py:27
  198.8 17.2 %collective-permute-start.37 = (bf16[2,128,1408]{2,1,0:T(8,128)(2,1)S(1)}, bf16[2,128,1408]{2,1,0:T(8,128)(2,1)S(1)}, u32[]{:S(2)}, u32[]{:S(2)}) collective-permute-start(bf16[2,128,1408]{2,1,0:T(8,128)(2,1)S(1)} %get-tuple-element.194), channel_id=1, source_target_pairs={{0,8},{2,6},{4,12},{6,2},{8,0},{10,14},{12,4},{14,10},{16,24},{18,... | collective-permute-start | bytes 2162696 | tf_op jit(solution)/shard_map/ppermute | solution.py:27
  208.3 12.2 %collective-permute-start.30 = (bf16[256,1024]{1,0:T(8,128)(2,1)S(1)}, bf16[256,1024]{1,0:T(8,128)(2,1)S(1)}, u32[]{:S(2)}, u32[]{:S(2)}) collective-permute-start(bf16[256,1024]{1,0:T(8,128)(2,1)S(1)} %slice.116), channel_id=1, source_target_pairs={{0,1},{1,0},{2,3},{3,2},{4,5},{5,4},{6,7},{7,6},{8,9},{9,8},{10,11... | collective-permute-start | bytes 1572872 | tf_op jit(solution)/shard_map/ppermute | solution.py:35
  211.5 10.2 %collective-permute-start.36 = (bf16[2,224,256]{2,1,0:T(8,128)(2,1)S(1)}, bf16[2,224,256]{2,1,0:T(8,128)(2,1)S(1)}, u32[]{:S(2)}, u32[]{:S(2)}) collective-permute-start(bf16[2,224,256]{2,1,0:T(8,128)(2,1)S(1)} %add_convert_fusion.8), channel_id=1, source_target_pairs={{0,8},{2,6},{4,12},{6,2},{8,0},{10,14},{12,4},{14,10},{16,24},{18,... | collective-permute-start | bytes 688136 | tf_op jit(solution)/shard_map/ppermute | solution.py:27
  212.6 25.8 %collective-permute-start.40 = (bf16[4,64,1408]{2,1,0:T(8,128)(2,1)}, bf16[4,64,1408]{2,1,0:T(8,128)(2,1)}, u32[]{:S(2)}, u32[]{:S(2)}) collective-permute-start(bf16[4,64,1408]{2,1,0:T(8,128)(2,1)} %pad_maximum_fusion.15.refs_0_), channel_id=1, source_target_pairs={{0,2},{2,0},{4,6},{6,4},{8,10},{10,8},{12,14},{14,12},{16,18},{18,... | collective-permute-start | bytes 2162696 | tf_op jit(solution)/shard_map/ppermute | solution.py:27
  212.6 17.2 %collective-permute-start.39 = (bf16[4,64,1408]{2,1,0:T(8,128)(2,1)}, bf16[4,64,1408]{2,1,0:T(8,128)(2,1)}, u32[]{:S(2)}, u32[]{:S(2)}) collective-permute-start(bf16[4,64,1408]{2,1,0:T(8,128)(2,1)} %pad_maximum_fusion.15.refs_0_), channel_id=1, source_target_pairs={{0,4},{2,10},{4,0},{6,14},{8,12},{10,2},{12,8},{14,6},{16,20},{18,... | collective-permute-start | bytes 2162696 | tf_op jit(solution)/shard_map/ppermute | solution.py:27
  216.0 11.0 %collective-permute-start.35 = (bf16[1,128,1024]{2,1,0:T(8,128)(2,1)S(1)}, bf16[1,128,1024]{2,1,0:T(8,128)(2,1)S(1)}, u32[]{:S(2)}, u32[]{:S(2)}) collective-permute-start(bf16[1,128,1024]{2,1,0:T(8,128)(2,1)S(1)} %add_convert_fusion.7), channel_id=1, source_target_pairs={{0,24},{2,26},{4,28},{6,30},{8,16},{10,18},{12,20},{14,22},{16,8},... | collective-permute-start | bytes 786440 | tf_op jit(solution)/shard_map/ppermute | solution.py:27
  220.6 29.6 %collective-permute-start.43 = (bf16[4,128,1408]{2,1,0:T(8,128)(2,1)}, bf16[4,128,1408]{2,1,0:T(8,128)(2,1)}, u32[]{:S(2)}, u32[]{:S(2)}) collective-permute-start(bf16[4,128,1408]{2,1,0:T(8,128)(2,1)} %constant_dynamic-update-slice_fusion.5.refs_0_), channel_id=1, source_target_pairs={{0,4},{2,10},{4,0},{6,14},{8,12},{10,2},{12,8},{14,6},{16,20},{18,... | collective-permute-start | bytes 4325384 | tf_op jit(solution)/shard_map/ppermute | solution.py:27
  229.8 8.7 %collective-permute-start.41 = (bf16[4,64,1408]{2,1,0:T(8,128)(2,1)}, bf16[4,64,1408]{2,1,0:T(8,128)(2,1)}, u32[]{:S(2)}, u32[]{:S(2)}) collective-permute-start(bf16[4,64,1408]{2,1,0:T(8,128)(2,1)} %collective-permute-done.39.refs_1_), channel_id=1, source_target_pairs={{0,2},{2,0},{4,6},{6,4},{8,10},{10,8},{12,14},{14,12},{16,18},{18,... | collective-permute-start | bytes 2162696 | tf_op jit(solution)/shard_map/ppermute | solution.py:27
  234.5 9.8 %collective-permute-start.38 = (bf16[1,224,256]{2,1,0:T(8,128)(2,1)S(1)}, bf16[1,224,256]{2,1,0:T(8,128)(2,1)}, u32[]{:S(2)}, u32[]{:S(2)}) collective-permute-start(bf16[1,224,256]{2,1,0:T(8,128)(2,1)S(1)} %add_convert_fusion.12), channel_id=1, source_target_pairs={{0,24},{2,26},{4,28},{6,30},{8,16},{10,18},{12,20},{14,22},{16,8},... | collective-permute-start | bytes 344072 | tf_op jit(solution)/shard_map/ppermute | solution.py:27
  237.8 11.4 %collective-permute-start.44 = (bf16[1,128,1024]{2,1,0:T(8,128)(2,1)}, bf16[1,128,1024]{2,1,0:T(8,128)(2,1)}, u32[]{:S(2)}, u32[]{:S(2)}) collective-permute-start(bf16[1,128,1024]{2,1,0:T(8,128)(2,1)} %add_convert_fusion.6), channel_id=1, source_target_pairs={{0,24},{2,26},{4,28},{6,30},{8,16},{10,18},{12,20},{14,22},{16,8},... | collective-permute-start | bytes 786440 | tf_op jit(solution)/shard_map/ppermute | solution.py:27
  238.4 21.3 %collective-permute-start.45 = (bf16[4,128,1408]{2,1,0:T(8,128)(2,1)}, bf16[4,128,1408]{2,1,0:T(8,128)(2,1)S(1)}, u32[]{:S(2)}, u32[]{:S(2)}) collective-permute-start(bf16[4,128,1408]{2,1,0:T(8,128)(2,1)} %constant_dynamic-update-slice_fusion.5.refs_0_), channel_id=1, source_target_pairs={{0,2},{2,0},{4,6},{6,4},{8,10},{10,8},{12,14},{14,12},{16,18},{18,... | collective-permute-start | bytes 4325384 | tf_op jit(solution)/shard_map/ppermute | solution.py:27
  250.2 9.5 %collective-permute-start.46 = (bf16[4,128,1408]{2,1,0:T(8,128)(2,1)}, bf16[4,128,1408]{2,1,0:T(8,128)(2,1)S(1)}, u32[]{:S(2)}, u32[]{:S(2)}) collective-permute-start(bf16[4,128,1408]{2,1,0:T(8,128)(2,1)} %collective-permute-done.43.refs_1_), channel_id=1, source_target_pairs={{0,2},{2,0},{4,6},{6,4},{8,10},{10,8},{12,14},{14,12},{16,18},{18,... | collective-permute-start | bytes 4325384 | tf_op jit(solution)/shard_map/ppermute | solution.py:27
  256.3 13.0 %collective-permute-start.49 = (bf16[2,128,1024]{2,1,0:T(8,128)(2,1)S(1)}, bf16[2,128,1024]{2,1,0:T(8,128)(2,1)S(1)}, u32[]{:S(2)}, u32[]{:S(2)}) collective-permute-start(bf16[2,128,1024]{2,1,0:T(8,128)(2,1)S(1)} %pad_maximum_fusion.18), channel_id=1, source_target_pairs={{0,8},{2,6},{4,12},{6,2},{8,0},{10,14},{12,4},{14,10},{16,24},{18,... | collective-permute-start | bytes 1572872 | tf_op jit(solution)/shard_map/ppermute | solution.py:27
  256.3 12.9 %collective-permute-start.42 = (bf16[1,224,256]{2,1,0:T(8,128)(2,1)S(1)}, bf16[1,224,256]{2,1,0:T(8,128)(2,1)S(1)}, u32[]{:S(2)}, u32[]{:S(2)}) collective-permute-start(bf16[1,224,256]{2,1,0:T(8,128)(2,1)S(1)} %add_convert_fusion.11), channel_id=1, source_target_pairs={{0,24},{2,26},{4,28},{6,30},{8,16},{10,18},{12,20},{14,22},{16,8},... | collective-permute-start | bytes 344072 | tf_op jit(solution)/shard_map/ppermute | solution.py:27
  270.4 16.7 %collective-permute-start.52 = (bf16[4,128,1024]{2,1,0:T(8,128)(2,1)S(1)}, bf16[4,128,1024]{2,1,0:T(8,128)(2,1)S(1)}, u32[]{:S(2)}, u32[]{:S(2)}) collective-permute-start(bf16[4,128,1024]{2,1,0:T(8,128)(2,1)S(1)} %pad_maximum_fusion.13.refs_0_), channel_id=1, source_target_pairs={{0,4},{2,10},{4,0},{6,14},{8,12},{10,2},{12,8},{14,6},{16,20},{18,... | collective-permute-start | bytes 3145736 | tf_op jit(solution)/shard_map/ppermute | solution.py:27
  271.5 6.0 %collective-permute-start.48 = (bf16[2,224,256]{2,1,0:T(8,128)(2,1)S(1)}, bf16[2,224,256]{2,1,0:T(8,128)(2,1)S(1)}, u32[]{:S(2)}, u32[]{:S(2)}) collective-permute-start(bf16[2,224,256]{2,1,0:T(8,128)(2,1)S(1)} %pad_maximum_fusion.21), channel_id=1, source_target_pairs={{0,1},{1,0},{2,3},{3,2},{4,5},{5,4},{6,7},{7,6},{8,9},{9,8},{10,11... | collective-permute-start | bytes 688136 | tf_op jit(solution)/shard_map/ppermute | solution.py:35
  272.8 8.5 %collective-permute-start.47 = (bf16[2,224,256]{2,1,0:T(8,128)(2,1)S(1)}, bf16[2,224,256]{2,1,0:T(8,128)(2,1)S(1)}, u32[]{:S(2)}, u32[]{:S(2)}) collective-permute-start(bf16[2,224,256]{2,1,0:T(8,128)(2,1)S(1)} %pad_maximum_fusion.21), channel_id=1, source_target_pairs={{0,8},{2,6},{4,12},{6,2},{8,0},{10,14},{12,4},{14,10},{16,24},{18,... | collective-permute-start | bytes 688136 | tf_op jit(solution)/shard_map/ppermute | solution.py:27
  272.8 23.7 %collective-permute-start.51 = (bf16[4,128,1024]{2,1,0:T(8,128)(2,1)S(1)}, bf16[4,128,1024]{2,1,0:T(8,128)(2,1)S(1)}, u32[]{:S(2)}, u32[]{:S(2)}) collective-permute-start(bf16[4,128,1024]{2,1,0:T(8,128)(2,1)S(1)} %pad_maximum_fusion.13.refs_0_), channel_id=1, source_target_pairs={{0,2},{2,0},{4,6},{6,4},{8,10},{10,8},{12,14},{14,12},{16,18},{18,... | collective-permute-start | bytes 3145736 | tf_op jit(solution)/shard_map/ppermute | solution.py:27
  287.1 9.4 %collective-permute-start.53 = (bf16[4,128,1024]{2,1,0:T(8,128)(2,1)S(1)}, bf16[4,128,1024]{2,1,0:T(8,128)(2,1)S(1)}, u32[]{:S(2)}, u32[]{:S(2)}) collective-permute-start(bf16[4,128,1024]{2,1,0:T(8,128)(2,1)S(1)} %collective-permute-done.52.refs_1_), channel_id=1, source_target_pairs={{0,2},{2,0},{4,6},{6,4},{8,10},{10,8},{12,14},{14,12},{16,18},{18,... | collective-permute-start | bytes 3145736 | tf_op jit(solution)/shard_map/ppermute | solution.py:27
  287.1 8.5 %collective-permute-start.50 = (bf16[4,224,256]{2,1,0:T(8,128)(2,1)S(1)}, bf16[4,224,256]{2,1,0:T(8,128)(2,1)S(1)}, u32[]{:S(2)}, u32[]{:S(2)}) collective-permute-start(bf16[4,224,256]{2,1,0:T(8,128)(2,1)S(1)} %pad_maximum_fusion.19.refs_0_), channel_id=1, source_target_pairs={{0,4},{2,10},{4,0},{6,14},{8,12},{10,2},{12,8},{14,6},{16,20},{18,... | collective-permute-start | bytes 1376264 | tf_op jit(solution)/shard_map/ppermute | solution.py:27
  287.8 8.1 %collective-permute-start.54 = (bf16[2,224,256]{2,1,0:T(8,128)(2,1)S(1)}, bf16[2,224,256]{2,1,0:T(8,128)(2,1)S(1)}, u32[]{:S(2)}, u32[]{:S(2)}) collective-permute-start(bf16[2,224,256]{2,1,0:T(8,128)(2,1)S(1)} %collective-permute-done.47), channel_id=1, source_target_pairs={{0,1},{1,0},{2,3},{3,2},{4,5},{5,4},{6,7},{7,6},{8,9},{9,8},{10,11... | collective-permute-start | bytes 688136 | tf_op jit(solution)/shard_map/ppermute | solution.py:35
  295.6 12.1 %collective-permute-start.55 = (bf16[4,224,256]{2,1,0:T(8,128)(2,1)S(1)}, bf16[4,224,256]{2,1,0:T(8,128)(2,1)S(1)}, u32[]{:S(2)}, u32[]{:S(2)}) collective-permute-start(bf16[4,224,256]{2,1,0:T(8,128)(2,1)S(1)} %collective-permute-done.50.refs_1_), channel_id=1, source_target_pairs={{0,1},{1,0},{2,3},{3,2},{4,5},{5,4},{6,7},{7,6},{8,9},{9,8},{10,11... | collective-permute-start | bytes 1376264 | tf_op jit(solution)/shard_map/ppermute | solution.py:35
  295.9 11.7 %collective-permute-start.56 = (bf16[4,224,256]{2,1,0:T(8,128)(2,1)S(1)}, bf16[4,224,256]{2,1,0:T(8,128)(2,1)S(1)}, u32[]{:S(2)}, u32[]{:S(2)}) collective-permute-start(bf16[4,224,256]{2,1,0:T(8,128)(2,1)S(1)} %pad_maximum_fusion.19.refs_0_), channel_id=1, source_target_pairs={{0,2},{2,0},{4,6},{6,4},{8,10},{10,8},{12,14},{14,12},{16,18},{18,... | collective-permute-start | bytes 1376264 | tf_op jit(solution)/shard_map/ppermute | solution.py:27
  295.9 11.7 %collective-permute-start.57 = (bf16[4,224,256]{2,1,0:T(8,128)(2,1)S(1)}, bf16[4,224,256]{2,1,0:T(8,128)(2,1)S(1)}, u32[]{:S(2)}, u32[]{:S(2)}) collective-permute-start(bf16[4,224,256]{2,1,0:T(8,128)(2,1)S(1)} %collective-permute-done.50.refs_1_), channel_id=1, source_target_pairs={{0,2},{2,0},{4,6},{6,4},{8,10},{10,8},{12,14},{14,12},{16,18},{18,... | collective-permute-start | bytes 1376264 | tf_op jit(solution)/shard_map/ppermute | solution.py:27
  296.5 11.2 %collective-permute-start.58 = (bf16[4,224,256]{2,1,0:T(8,128)(2,1)S(1)}, bf16[4,224,256]{2,1,0:T(8,128)(2,1)S(1)}, u32[]{:S(2)}, u32[]{:S(2)}) collective-permute-start(bf16[4,224,256]{2,1,0:T(8,128)(2,1)S(1)} %constant_dynamic-update-slice_fusion.8.refs_2_), channel_id=1, source_target_pairs={{0,2},{2,0},{4,6},{6,4},{8,10},{10,8},{12,14},{14,12},{16,18},{18,... | collective-permute-start | bytes 1376264 | tf_op jit(solution)/shard_map/ppermute | solution.py:27
  307.6 1.8 collective-permute-start.59
  (52 other events, 336.9 us)

commit v3 on v2

--- a/solution.py
+++ b/solution.py
@@ -247,10 +247,6 @@
     item.update(lax.optimization_barrier((item.last(), earlier))[0])
     item.step()
     return item.sent
-
-
-def behind(sums, *values):
-    return lax.optimization_barrier(([item.sent for item in sums], values))[1]
 
 
 def ordered(pieces, place):
@@ -576,7 +572,14 @@
     pair_normed = with_pair(gathered)
     pair_mixed = columns_to_pair(mixed)
     pair_cot = mixed_columns_to_pair(grad_gathered, blocks // 2)
-    pair_features = with_pair(features)
+    features_more = jnp.concatenate(
+        [
+            jnp.pad(features, ((0, 0), (0, 16 * blocks))),
+            jnp.eye(16, w_proj.shape[0] + 16 * blocks, w_proj.shape[0], dtype=features.dtype),
+        ],
+        axis=0,
+    )
+    pair_features = with_pair(features_more)
     gathered_ffn, gate_flat, pair_normed, pair_mixed, pair_cot, pair_features = tie_sums(
         gathered_ffn, gate_flat, pair_normed, pair_mixed, pair_cot, pair_features
     )
@@ -616,7 +619,6 @@
     (grad_attn_in,) = tie_sums(gate, down, grad_attn_in)
     gate.step()
     down.step()
-    (grad_attn_in,) = behind((gate, down), grad_attn_in)
     grad_mixed = contract(grad_attn_in, w_out, 1, 1).astype(jnp.bfloat16)
     pair_mid = []
 
@@ -624,8 +626,7 @@
         (value,) = tie_sums(gate, down, value)
         gate.step()
         down.step()
-        value, group_mid = behind((gate, down), value, grad_attn_in)
-        pair_mid.append(with_pair(group_mid))
+        pair_mid.append(with_pair(grad_attn_in))
         return value
 
     grad_queries, grad_keys, grad_values = attention_backward(
@@ -676,15 +677,9 @@
     grad_lifted = grad_middle + grad_attn_norm
     grad_lift_b = grad_lifted.astype(jnp.bfloat16)
     sums = jnp.stack([jnp.sum(grad_lifted, axis=0), grad_gain_attn, grad_gain_ffn])
-    sums = jnp.pad(sums, ((0, 16 - sums.shape[0]), (0, 0)))
-    half = model_width // 2
-    mine, theirs = (
-        lax.dynamic_slice_in_dim(sums, which * half, half, 1) for which in (core, 1 - core)
-    )
-    sums = (mine + core_swap(theirs)).astype(jnp.bfloat16)
-    sums = jnp.pad(sums, ((0, 16 * blocks - sums.shape[0]), (0, 0)))
-    proj_part = contract(pair_features, columns_to_pair(grad_lift_b), 0, 0).astype(jnp.bfloat16)
-    proj_part = jnp.concatenate([proj_part, sums], axis=0)
+    sums = jnp.pad(sums, ((0, 16 - sums.shape[0]), (0, 0))).astype(jnp.bfloat16)
+    lift_more = jnp.concatenate([grad_lift_b, sums], axis=0)
+    proj_part = contract(pair_features, columns_to_pair(lift_more), 0, 0).astype(jnp.bfloat16)
     proj = over_peers(steps, proj_part.reshape(blocks, -1, proj_part.shape[1]))
     proj.step()
     sent = advance(down, proj.sent)

time: 321 us -> 318 us (level)
  other arithmetic: 46.3 us -> 38.4 us
  starting transfers between devices: 70.8 us -> 75.6 us
  waiting for transfers between devices: 93.1 us -> 96.5 us
    ppermute x45 -> x44, waiting for transfers between devices: 30.3 us -> 35.8 us  [swap_rows(): lax.ppermute(value, 'rows', [(r, r ^ masks[r % 2]) for r in range(count)])]
    convert_element_type x12, other arithmetic: 16.9 us -> 11.7 us  [part(): return total.astype(jnp.bfloat16)]
    ppermute x45 -> x44, starting transfers between devices: 53.1 us -> 58.1 us  [swap_rows(): lax.ppermute(value, 'rows', [(r, r ^ masks[r % 2]) for r in range(count)])]
    dot_general x1, matrix products: 2.09 us -> 5.48 us  [one_block(): jnp.einsum('hqk,qhd->khd', probs.astype(jnp.bfloat16), grad_block, prefer...]
    unnamed x118 -> x130, local copies, waits for them, and re-layouts: 16.8 us -> 15.7 us
  transfers between devices with their start and end apart: 60 -> 59, of which waited for: 19 -> 20; matrix products, arithmetic and copies ran while one was open for 31% -> 31% of each run, Pallas kernels for 6% -> 6%
where the time goes in v3:
time: 318 us; the launch traced here: 312 us
  waiting for transfers between devices  96.5 us (30%)
  starting transfers between devices  75.6 us (24%)
  matrix products  52.4 us (16%)
  other arithmetic  38.4 us (12%)
  local copies, waits for them, and re-layouts  23.7 us (7%)
  Pallas kernels  23.4 us (7%)
    ppermute x15, waiting for transfers between devices, peer_swap(): return lax.ppermute(value, 'heads', [(0, 1), (1, 0)])  60.7 us
    ppermute x44, starting transfers between devices, swap_rows(): lax.ppermute(value, 'rows', [(r, r ^ masks[r % 2]) for r in range(count)])  58.1 us
    ppermute x44, waiting for transfers between devices, swap_rows(): lax.ppermute(value, 'rows', [(r, r ^ masks[r % 2]) for r in range(count)])  35.8 us
    dot_general x17, matrix products, contract(): lax.dot_general(left, right, (((left_dim,), (right_dim,)), ((), ())), pre...  27.7 us
    pallas_call x3, Pallas kernels, place_blocks(): pl.pallas_call(body, grid_spec=pltpu.PrefetchScalarGridSpec(num_scalar_pr...  19.1 us
    ppermute x15, starting transfers between devices, peer_swap(): return lax.ppermute(value, 'heads', [(0, 1), (1, 0)])  17.4 us
    unnamed x130, local copies, waits for them, and re-layouts  15.7 us
    convert_element_type x12, other arithmetic, part(): return total.astype(jnp.bfloat16)  11.7 us
  transfers between devices with their start and end apart: 59, of which 20 were waited for; matrix products, arithmetic and copies ran while one was open for 31% of the time, Pallas kernels for 6%

profile of v3, /device:TPU:0, one launch (start us, length us, event | category | flops | bytes accessed | tf_op | source)
XLA Modules:
  0.0 312.1 jit_solution(15593179379850522028)
XLA Ops:
  0.7 3.0 collective-permute-start.1
  3.8 2.4 multiply_reduce_fusion.6
  8.1 1.9 collective-permute-start
  11.9 10.2 %collective-permute-done = bf16[256,1024]{1,0:T(8,128)(2,1)} collective-permute-done((bf16[256,1024]{1,0:T(8,128)(2,1)}, bf16[256,1024]{1,0:T(8,128)(2,1)}, u32[]{:S(2)}, u32[]{:S(2)}) %collective-permute-start) | collective-permute-done | bytes 524320 | tf_op jit(solution)/shard_map/ppermute | solution.py:35
  25.8 1.8 collective-permute-start.3
  30.5 1.9 copy-done.1
  32.4 2.4 fusion.37
  34.9 3.8 %collective-permute-done.3 = bf16[256,1024]{1,0:T(8,128)(2,1)S(1)} collective-permute-done((bf16[256,1024]{1,0:T(8,128)(2,1)S(1)}, bf16[256,1024]{1,0:T(8,128)(2,1)S(1)}, u32[]{:S(2)}, u32[]{:S(2)}) %collective-permute-start.3) | collective-permute-done | bytes 524320 | tf_op jit(solution)/shard_map/ppermute | solution.py:35
  42.3 1.5 collective-permute-start.4
  44.8 6.2 %copy.30 = bf16[128,8,2,1408]{3,1,2,0:T(8,128)(2,1)} copy(bf16[128,8,2,1408]{3,2,1,0:T(2,128)(2,1)} %bitcast.97) | data formatting | bytes 11534336
  57.4 2.7 pad_maximum_fusion.3
  62.7 7.7 %collective-permute-done.5 = bf16[256,1024]{1,0:T(8,128)(2,1)S(1)} collective-permute-done((bf16[256,1024]{1,0:T(8,128)(2,1)S(1)}, bf16[256,1024]{1,0:T(8,128)(2,1)S(1)}, u32[]{:S(2)}, u32[]{:S(2)}) %collective-permute-start.5) | collective-permute-done | bytes 524320 | tf_op jit(solution)/shard_map/ppermute | solution.py:35
  70.5 3.2 %fusion.84 = f32[512,2816]{1,0:T(8,128)S(1)} fusion(bf16[512,1024]{1,0:T(8,128)(2,1)S(1)} %pad_maximum_fusion.10, bf16[1024,2816]{1,0:T(8,128)(2,1)S(1)} %bitcast.100), kind=kOutput, calls=%fused_computation.204 | convolution fusion | flops 2952790016 | bytes 12582912 | tf_op jit(solution)/shard_map/dot_general | solution.py:586
  75.9 4.5 %broadcast_select_fusion.1 = (bf16[512,1408]{1,0:T(8,128)(2,1)S(1)}, bf16[512,1408]{1,0:T(8,128)(2,1)S(1)}, bf16[512,1408]{1,0:T(8,128)(2,1)S(1)}) fusion(pred[]{:T(512)S(6)} %eq.139, f32[512,2816]{1,0:T(8,128)S(1)} %fusion.84, bf16[512,1024]{1,0:T(8,128)(2,1)S(1)} %copy-done.15, bf16[1408,1024]{1,0:T(8,128)(2,1)S(1)} %copy-done.54), kind=kOutput, calls=%fused_computation.59 | convolution fusion | flops 1494417408 | bytes 14024705 | tf_op jit(solution)/shard_map/dot_general | solution.py:20
  81.2 1.7 fusion.34
  82.9 1.7 fusion.32
  84.6 1.8 convolution_convert_fusion.1
  86.5 1.6 collective-permute-start.14
  88.8 3.0 convolution_convert_fusion.2
  92.3 3.0 convolution_convert_fusion.3
  95.3 7.0 %collective-permute-done.15 = bf16[256,1024]{1,0:T(8,128)(2,1)S(1)} collective-permute-done((bf16[256,1024]{1,0:T(8,128)(2,1)S(1)}, bf16[256,1024]{1,0:T(8,128)(2,1)S(1)}, u32[]{:S(2)}, u32[]{:S(2)}) %collective-permute-start.15) | collective-permute-done | bytes 524320 | tf_op jit(solution)/shard_map/ppermute | solution.py:35
  102.8 1.6 fusion.81
  106.7 11.3 %collective-permute-done.17 = bf16[256,1024]{1,0:T(8,128)(2,1)} collective-permute-done((bf16[256,1024]{1,0:T(8,128)(2,1)}, bf16[256,1024]{1,0:T(8,128)(2,1)}, u32[]{:S(2)}, u32[]{:S(2)}) %collective-permute-start.17) | collective-permute-done | bytes 524320 | tf_op jit(solution)/shard_map/ppermute | solution.py:35
  120.2 1.6 add_convert_fusion.10
  124.6 1.9 collective-permute-start.18
  126.5 5.5 %fusion.38 = bf16[8,64,512]{2,1,0:T(8,128)(2,1)S(1)} fusion(bf16[512,8,64]{0,2,1:T(8,128)(2,1)S(1)} %bitcast.130, f32[8,512,512]{1,2,0:T(8,128)} %copy-done.1, f32[8,512]{1,0:T(8,128)S(1)} %log_add_fusion, pred[512,512]{0,1:T(8,128)(4,1)S(1)} %copy-done.14), kind=kOutput, calls=%fused_computation.67 | convolution fusion | flops 274989056 | bytes 9715712 | tf_op jit(solution)/shard_map/hqk,qhd->khd/dot_general | solution.py:498
  132.0 2.8 multiply_reduce_fusion
  134.8 3.2 %collective-permute-done.18 = bf16[2,128,1408]{2,1,0:T(8,128)(2,1)S(1)} collective-permute-done((bf16[2,128,1408]{2,1,0:T(8,128)(2,1)S(1)}, bf16[2,128,1408]{2,1,0:T(8,128)(2,1)S(1)}, u32[]{:S(2)}, u32[]{:S(2)}) %collective-permute-start.18) | collective-permute-done | bytes 720928 | tf_op jit(solution)/shard_map/ppermute | solution.py:27
  138.0 2.8 multiply_convert_fusion
  145.7 1.6 collective-permute-start.20
  152.2 1.8 convolution_convert_fusion.4
  155.6 2.2 add_convert_fusion.3
  157.8 5.0 %collective-permute-done.26 = bf16[256,1024]{1,0:T(8,128)(2,1)S(1)} collective-permute-done((bf16[256,1024]{1,0:T(8,128)(2,1)S(1)}, bf16[256,1024]{1,0:T(8,128)(2,1)S(1)}, u32[]{:S(2)}, u32[]{:S(2)}) %collective-permute-start.26) | collective-permute-done | bytes 524320 | tf_op jit(solution)/shard_map/ppermute | solution.py:35
  165.4 2.4 collective-permute-start.24
  167.8 3.3 %convolution_convert_fusion = bf16[1792,512]{1,0:T(8,128)(2,1)S(1)} fusion(bf16[544,1792]{1,0:T(8,128)(2,1)} %pad_maximum_fusion.3, bf16[272,512]{1,0:T(8,128)(2,1)} %collective-permute-done.27, bf16[272,512]{1,0:T(8,128)(2,1)} %get-tuple-element.177), kind=kOutput, calls=%fused_computation.15 | convolution fusion | flops 1000275968 | bytes 4341760 | tf_op jit(solution)/shard_map/dot_general | solution.py:20
  173.6 1.9 collective-permute-start.25
  175.5 2.0 collective-permute-start.23
  179.5 5.6 %collective-permute-done.28 = bf16[4,224,256]{2,1,0:T(8,128)(2,1)S(1)} collective-permute-done((bf16[4,224,256]{2,1,0:T(8,128)(2,1)S(1)}, bf16[4,224,256]{2,1,0:T(8,128)(2,1)S(1)}, u32[]{:S(2)}, u32[]{:S(2)}) %collective-permute-start.28) | collective-permute-done | bytes 458784 | tf_op jit(solution)/shard_map/ppermute | solution.py:35
  185.3 1.9 collective-permute-start.33
  187.2 6.7 %collective-permute-start.31 = (bf16[2,64,1408]{2,1,0:T(8,128)(2,1)S(1)}, bf16[2,64,1408]{2,1,0:T(8,128)(2,1)S(1)}, u32[]{:S(2)}, u32[]{:S(2)}) collective-permute-start(bf16[2,64,1408]{2,1,0:T(8,128)(2,1)S(1)} %pad_maximum_fusion.21), channel_id=1, source_target_pairs={{0,8},{2,6},{4,12},{6,2},{8,0},{10,14},{12,4},{14,10},{16,24},{18,... | collective-permute-start | bytes 1081352 | tf_op jit(solution)/shard_map/ppermute | solution.py:27
  195.0 6.5 %collective-permute-start.36 = (bf16[2,128,1408]{2,1,0:T(8,128)(2,1)S(1)}, bf16[2,128,1408]{2,1,0:T(8,128)(2,1)S(1)}, u32[]{:S(2)}, u32[]{:S(2)}) collective-permute-start(bf16[2,128,1408]{2,1,0:T(8,128)(2,1)S(1)} %get-tuple-element.188), channel_id=1, source_target_pairs={{0,8},{2,6},{4,12},{6,2},{8,0},{10,14},{12,4},{14,10},{16,24},{18,... | collective-permute-start | bytes 2162696 | tf_op jit(solution)/shard_map/ppermute | solution.py:27
  201.5 1.8 convolution_convert_fusion.5
  203.4 2.6 fusion.85
  208.2 1.7 collective-permute-start.38
  210.1 7.3 %collective-permute-done.36 = bf16[2,128,1408]{2,1,0:T(8,128)(2,1)S(1)} collective-permute-done((bf16[2,128,1408]{2,1,0:T(8,128)(2,1)S(1)}, bf16[2,128,1408]{2,1,0:T(8,128)(2,1)S(1)}, u32[]{:S(2)}, u32[]{:S(2)}) %collective-permute-start.36) | collective-permute-done | bytes 720928 | tf_op jit(solution)/shard_map/ppermute | solution.py:27
  217.4 4.0 %collective-permute-start.34 = (bf16[1,128,1024]{2,1,0:T(8,128)(2,1)S(1)}, bf16[1,128,1024]{2,1,0:T(8,128)(2,1)S(1)}, u32[]{:S(2)}, u32[]{:S(2)}) collective-permute-start(bf16[1,128,1024]{2,1,0:T(8,128)(2,1)S(1)} %add_convert_fusion.7), channel_id=1, source_target_pairs={{0,24},{2,26},{4,28},{6,30},{8,16},{10,18},{12,20},{14,22},{16,8},... | collective-permute-start | bytes 786440 | tf_op jit(solution)/shard_map/ppermute | solution.py:27
  222.3 1.7 collective-permute-start.42
  224.4 4.3 %collective-permute-done.34 = bf16[1,128,1024]{2,1,0:T(8,128)(2,1)S(1)} collective-permute-done((bf16[1,128,1024]{2,1,0:T(8,128)(2,1)S(1)}, bf16[1,128,1024]{2,1,0:T(8,128)(2,1)S(1)}, u32[]{:S(2)}, u32[]{:S(2)}) %collective-permute-start.34) | collective-permute-done | bytes 262176 | tf_op jit(solution)/shard_map/ppermute | solution.py:27
  230.5 1.7 collective-permute-start.40
  232.2 2.7 collective-permute-start.37
  236.2 5.8 %place_down.1 = f32[1408,1024]{1,0:T(8,128)} custom-call(s32[4]{0:T(128)S(1)} %pad_add_fusion.index, bf16[4,64,1408]{2,1,0:T(8,128)(2,1)} %pad_maximum_fusion.16.refs_0_, bf16[4,64,1408]{2,1,0:T(8,128)(2,1)} %collective-permute-done.38.refs_1_, bf16[4,64,1408]{2,1,0:T(8,128)(2,1)} %collective-permute-done.39.refs_2_, ...), custom_call_target="tpu_custom_call" | custom-call | bytes 8650752 | tf_op jit(solution)/shard_map/place_down/pallas_call | solution.py:295
  243.3 3.0 collective-permute-done.43
  247.2 7.7 %collective-permute-start.45 = (bf16[4,128,1408]{2,1,0:T(8,128)(2,1)}, bf16[4,128,1408]{2,1,0:T(8,128)(2,1)S(1)}, u32[]{:S(2)}, u32[]{:S(2)}) collective-permute-start(bf16[4,128,1408]{2,1,0:T(8,128)(2,1)} %collective-permute-done.42.refs_1_), channel_id=1, source_target_pairs={{0,2},{2,0},{4,6},{6,4},{8,10},{10,8},{12,14},{14,12},{16,18},{18,... | collective-permute-start | bytes 4325384 | tf_op jit(solution)/shard_map/ppermute | solution.py:27
  255.0 2.7 collective-permute-start.41
  258.0 7.8 %place_gate_up.1 = f32[1024,2,1408]{2,1,0:T(2,128)} custom-call(s32[4]{0:T(128)S(1)} %pad_add_fusion.index, bf16[4,128,1408]{2,1,0:T(8,128)(2,1)} %constant_dynamic-update-slice_fusion.5.refs_0_, bf16[4,128,1408]{2,1,0:T(8,128)(2,1)} %collective-permute-done.42.refs_1_, bf16[4,128,1408]{2,1,0:T(8,128)(2,1)S(1)} %collective-permute-done.44.refs_2_, ...), custom_call_target="tpu_custom_call" | custom-call | bytes 17301504 | tf_op jit(solution)/shard_map/place_gate_up/pallas_call | solution.py:295
  268.4 1.8 collective-permute-start.51
  270.8 5.4 %collective-permute-done.47 = bf16[2,224,256]{2,1,0:T(8,128)(2,1)S(1)} collective-permute-done((bf16[2,224,256]{2,1,0:T(8,128)(2,1)S(1)}, bf16[2,224,256]{2,1,0:T(8,128)(2,1)S(1)}, u32[]{:S(2)}, u32[]{:S(2)}) %collective-permute-start.47) | collective-permute-done | bytes 229408 | tf_op jit(solution)/shard_map/ppermute | solution.py:35
  276.2 3.1 collective-permute-done.46
  279.4 5.2 %collective-permute-done.51.refs_1_ = bf16[4,128,1024]{2,1,0:T(8,128)(2,1)S(1)} collective-permute-done((bf16[4,128,1024]{2,1,0:T(8,128)(2,1)S(1)}, bf16[4,128,1024]{2,1,0:T(8,128)(2,1)S(1)}, u32[]{:S(2)}, u32[]{:S(2)}) %collective-permute-start.51) | collective-permute-done | bytes 1048608 | tf_op jit(solution)/shard_map/ppermute | solution.py:27
  287.3 5.8 %collective-permute-done.49.refs_1_ = bf16[4,224,256]{2,1,0:T(8,128)(2,1)S(1)} collective-permute-done((bf16[4,224,256]{2,1,0:T(8,128)(2,1)S(1)}, bf16[4,224,256]{2,1,0:T(8,128)(2,1)S(1)}, u32[]{:S(2)}, u32[]{:S(2)}) %collective-permute-start.49) | collective-permute-done | bytes 458784 | tf_op jit(solution)/shard_map/ppermute | solution.py:27
  295.2 5.5 %place_attn.1 = (f32[3,1024,512]{2,1,0:T(8,128)}, f32[512,1024]{1,0:T(8,128)}) custom-call(s32[4]{0:T(128)S(1)} %pad_add_fusion.index, bf16[4,128,1024]{2,1,0:T(8,128)(2,1)S(1)} %pad_maximum_fusion.13.refs_0_, bf16[4,128,1024]{2,1,0:T(8,128)(2,1)S(1)} %collective-permute-done.51.refs_1_, bf16[4,128,1024]{2,1,0:T(8,128)(2,1)S(1)} %collective-permute-done.50.refs_2_, ...), custom_call_target="tpu_custom_call" | custom-call | bytes 12582912 | tf_op jit(solution)/shard_map/place_attn/pallas_call | solution.py:295
  300.6 4.5 %collective-permute-done.54.refs_3_ = bf16[4,224,256]{2,1,0:T(8,128)(2,1)S(1)} collective-permute-done((bf16[4,224,256]{2,1,0:T(8,128)(2,1)S(1)}, bf16[4,224,256]{2,1,0:T(8,128)(2,1)S(1)}, u32[]{:S(2)}, u32[]{:S(2)}) %collective-permute-start.54) | collective-permute-done | bytes 458784 | tf_op jit(solution)/shard_map/ppermute | solution.py:35
  305.2 1.8 collective-permute-done.58.refs_7_
  307.0 4.3 %place_proj.1 = (f32[1664,1024]{1,0:T(8,128)}, f32[16,1024]{1,0:T(8,128)S(1)}) custom-call(s32[4]{0:T(128)S(1)} %pad_add_fusion.index, bf16[4,224,256]{2,1,0:T(8,128)(2,1)S(1)} %pad_maximum_fusion.20.refs_0_, bf16[4,224,256]{2,1,0:T(8,128)(2,1)S(1)} %collective-permute-done.49.refs_1_, bf16[4,224,256]{2,1,0:T(8,128)(2,1)S(1)} %constant_dynamic-update-slice_fusion.8.refs_2_, ...), custom_call_target="tpu_custom_call" | custom-call | bytes 11010048 | tf_op jit(solution)/shard_map/place_proj/pallas_call | solution.py:404
  (295 shorter events, 73.2 us)
Async XLA Ops:
  0.7 10.9 %collective-permute-start.1 = (s32[256]{0:T(256)}, s32[256]{0:T(256)S(1)}, u32[]{:S(2)}, u32[]{:S(2)}) collective-permute-start(s32[256]{0:T(256)} %param.13), channel_id=1, source_target_pairs={{0,1},{1,0},{2,3},{3,2},{4,5},{5,4},{6,7},{7,6},{8,9},{9,8},{10,11... | collective-permute-start | bytes 3080 | tf_op jit(solution)/shard_map/ppermute | solution.py:35
  3.7 7.8 %collective-permute-start.2 = (s32[256]{0:T(256)}, s32[256]{0:T(256)S(1)}, u32[]{:S(2)}, u32[]{:S(2)}) collective-permute-start(s32[256]{0:T(256)} %param.14), channel_id=1, source_target_pairs={{0,1},{1,0},{2,3},{3,2},{4,5},{5,4},{6,7},{7,6},{8,9},{9,8},{10,11... | collective-permute-start | bytes 3080 | tf_op jit(solution)/shard_map/ppermute | solution.py:35
  8.1 14.0 %collective-permute-start = (bf16[256,1024]{1,0:T(8,128)(2,1)}, bf16[256,1024]{1,0:T(8,128)(2,1)}, u32[]{:S(2)}, u32[]{:S(2)}) collective-permute-start(bf16[256,1024]{1,0:T(8,128)(2,1)} %multiply_convert_fusion.4), channel_id=1, source_target_pairs={{0,1},{1,0},{2,3},{3,2},{4,5},{5,4},{6,7},{7,6},{8,9},{9,8},{10,11... | collective-permute-start | bytes 1572872 | tf_op jit(solution)/shard_map/ppermute | solution.py:35
  11.5 32.3 %copy-start.11 = (bf16[256,1792]{1,0:T(8,128)(2,1)}, bf16[256,1792]{1,0:T(8,128)(2,1)S(1)}, u32[]{:S(2)}) copy-start(bf16[256,1792]{1,0:T(8,128)(2,1)S(1)} %pad.9) | copy-start | bytes 2752516
  25.8 12.9 %collective-permute-start.3 = (bf16[256,1024]{1,0:T(8,128)(2,1)S(1)}, bf16[256,1024]{1,0:T(8,128)(2,1)S(1)}, u32[]{:S(2)}, u32[]{:S(2)}) collective-permute-start(bf16[256,1024]{1,0:T(8,128)(2,1)S(1)} %copy-done.25), channel_id=1, source_target_pairs={{0,1},{1,0},{2,3},{3,2},{4,5},{5,4},{6,7},{7,6},{8,9},{9,8},{10,11... | collective-permute-start | bytes 1572872 | tf_op jit(solution)/shard_map/ppermute | solution.py:35
  42.3 12.5 %collective-permute-start.4 = (bf16[256,1024]{1,0:T(8,128)(2,1)}, bf16[256,1024]{1,0:T(8,128)(2,1)}, u32[]{:S(2)}, u32[]{:S(2)}) collective-permute-start(bf16[256,1024]{1,0:T(8,128)(2,1)} %slice.110), channel_id=1, source_target_pairs={{0,1},{1,0},{2,3},{3,2},{4,5},{5,4},{6,7},{7,6},{8,9},{9,8},{10,11... | collective-permute-start | bytes 1572872 | tf_op jit(solution)/shard_map/ppermute | solution.py:35
  44.8 12.6 %collective-permute-start.9 = (bf16[272,1792]{1,0:T(8,128)(2,1)}, bf16[272,1792]{1,0:T(8,128)(2,1)}, u32[]{:S(2)}, u32[]{:S(2)}) collective-permute-start(bf16[272,1792]{1,0:T(8,128)(2,1)} %pad_maximum_fusion.14), channel_id=1, source_target_pairs={{0,2},{2,0},{4,6},{6,4},{8,10},{10,8},{12,14},{14,12},{16,18},{18,... | collective-permute-start | bytes 2924552 | tf_op jit(solution)/shard_map/ppermute | solution.py:27
  51.0 10.2 %collective-permute-start.6 = (bf16[512,1024]{1,0:T(8,128)(2,1)}, bf16[512,1024]{1,0:T(8,128)(2,1)S(1)}, u32[]{:S(2)}, u32[]{:S(2)}) collective-permute-start(bf16[512,1024]{1,0:T(8,128)(2,1)} %copy-done.17), channel_id=1, source_target_pairs={{0,2},{2,0},{4,6},{6,4},{8,10},{10,8},{12,14},{14,12},{16,18},{18,... | collective-permute-start | bytes 3145736 | tf_op jit(solution)/shard_map/ppermute | solution.py:27
  52.7 7.5 %collective-permute-start.7 = (bf16[512,256]{0,1:T(8,128)(2,1)S(1)}, bf16[512,256]{0,1:T(8,128)(2,1)S(1)}, u32[]{:S(2)}, u32[]{:S(2)}) collective-permute-start(bf16[512,256]{0,1:T(8,128)(2,1)S(1)} %get-tuple-element.186), channel_id=1, source_target_pairs={{0,2},{2,0},{4,6},{6,4},{8,10},{10,8},{12,14},{14,12},{16,18},{18,... | collective-permute-start | bytes 786440 | tf_op jit(solution)/shard_map/ppermute | solution.py:27
  54.2 6.8 %collective-permute-start.8 = (bf16[512,512]{1,0:T(8,128)(2,1)S(1)}, bf16[512,512]{1,0:T(8,128)(2,1)S(1)}, u32[]{:S(2)}, u32[]{:S(2)}) collective-permute-start(bf16[512,512]{1,0:T(8,128)(2,1)S(1)} %pad_maximum_fusion.18), channel_id=1, source_target_pairs={{0,2},{2,0},{4,6},{6,4},{8,10},{10,8},{12,14},{14,12},{16,18},{18,... | collective-permute-start | bytes 1572872 | tf_op jit(solution)/shard_map/ppermute | solution.py:27
  56.1 46.6 %copy-start.2 = (f32[256,1024]{1,0:T(8,128)}, f32[256,1024]{1,0:T(8,128)S(1)}, u32[]{:S(2)}) copy-start(f32[256,1024]{1,0:T(8,128)S(1)} %get-tuple-element.166) | copy-start | bytes 3145732
  56.3 14.0 %collective-permute-start.5 = (bf16[256,1024]{1,0:T(8,128)(2,1)S(1)}, bf16[256,1024]{1,0:T(8,128)(2,1)S(1)}, u32[]{:S(2)}, u32[]{:S(2)}) collective-permute-start(bf16[256,1024]{1,0:T(8,128)(2,1)S(1)} %multiply_convert_fusion.3), channel_id=1, source_target_pairs={{0,1},{1,0},{2,3},{3,2},{4,5},{5,4},{6,7},{7,6},{8,9},{9,8},{10,11... | collective-permute-start | bytes 1572872 | tf_op jit(solution)/shard_map/ppermute | solution.py:35
  70.4 18.3 %collective-permute-start.10 = (bf16[512,1024]{1,0:T(8,128)(2,1)S(1)}, bf16[512,1024]{1,0:T(8,128)(2,1)S(1)}, u32[]{:S(2)}, u32[]{:S(2)}) collective-permute-start(bf16[512,1024]{1,0:T(8,128)(2,1)S(1)} %pad_maximum_fusion.10), channel_id=1, source_target_pairs={{0,2},{2,0},{4,6},{6,4},{8,10},{10,8},{12,14},{14,12},{16,18},{18,... | collective-permute-start | bytes 3145736 | tf_op jit(solution)/shard_map/ppermute | solution.py:27
  80.4 4.2 %collective-permute-start.13 = (bf16[512,1408]{1,0:T(8,128)(2,1)S(1)}, bf16[512,1408]{1,0:T(8,128)(2,1)S(1)}, u32[]{:S(2)}, u32[]{:S(2)}) collective-permute-start(bf16[512,1408]{1,0:T(8,128)(2,1)S(1)} %multiply_convert_fusion.1), channel_id=1, source_target_pairs={{0,2},{2,0},{4,6},{6,4},{8,10},{10,8},{12,14},{14,12},{16,18},{18,... | collective-permute-start | bytes 4325384 | tf_op jit(solution)/shard_map/ppermute | solution.py:27
  81.1 7.8 %collective-permute-start.11 = (bf16[512,1408]{1,0:T(8,128)(2,1)S(1)}, bf16[512,1408]{1,0:T(8,128)(2,1)S(1)}, u32[]{:S(2)}, u32[]{:S(2)}) collective-permute-start(bf16[512,1408]{1,0:T(8,128)(2,1)S(1)} %broadcast_select_fusion), channel_id=1, source_target_pairs={{0,2},{2,0},{4,6},{6,4},{8,10},{10,8},{12,14},{14,12},{16,18},{18,... | collective-permute-start | bytes 4325384 | tf_op jit(solution)/shard_map/ppermute | solution.py:27
  86.5 15.8 %collective-permute-start.14 = (bf16[4,64,1408]{2,1,0:T(8,128)(2,1)S(1)}, bf16[4,64,1408]{2,1,0:T(8,128)(2,1)S(1)}, u32[]{:S(2)}, u32[]{:S(2)}) collective-permute-start(bf16[4,64,1408]{2,1,0:T(8,128)(2,1)S(1)} %constant_dynamic-slice_fusion.9), channel_id=1, source_target_pairs={{0,4},{2,10},{4,0},{6,14},{8,12},{10,2},{12,8},{14,6},{16,20},{18,... | collective-permute-start | bytes 2162696 | tf_op jit(solution)/shard_map/ppermute | solution.py:27
  88.1 14.1 %collective-permute-start.15 = (bf16[256,1024]{1,0:T(8,128)(2,1)S(1)}, bf16[256,1024]{1,0:T(8,128)(2,1)S(1)}, u32[]{:S(2)}, u32[]{:S(2)}) collective-permute-start(bf16[256,1024]{1,0:T(8,128)(2,1)S(1)} %fusion.34), channel_id=1, source_target_pairs={{0,1},{1,0},{2,3},{3,2},{4,5},{5,4},{6,7},{7,6},{8,9},{9,8},{10,11... | collective-permute-start | bytes 1572872 | tf_op jit(solution)/shard_map/ppermute | solution.py:35
  91.8 27.5 %collective-permute-start.12 = (bf16[4,128,1408]{2,1,0:T(8,128)(2,1)}, bf16[4,128,1408]{2,1,0:T(8,128)(2,1)}, u32[]{:S(2)}, u32[]{:S(2)}) collective-permute-start(bf16[4,128,1408]{2,1,0:T(8,128)(2,1)} %bitcast.10), channel_id=1, source_target_pairs={{0,4},{2,10},{4,0},{6,14},{8,12},{10,2},{12,8},{14,6},{16,20},{18,... | collective-permute-start | bytes 4325384 | tf_op jit(solution)/shard_map/ppermute | solution.py:27
  104.4 13.7 %collective-permute-start.17 = (bf16[256,1024]{1,0:T(8,128)(2,1)}, bf16[256,1024]{1,0:T(8,128)(2,1)}, u32[]{:S(2)}, u32[]{:S(2)}) collective-permute-start(bf16[256,1024]{1,0:T(8,128)(2,1)} %get-tuple-element.160), channel_id=1, source_target_pairs={{0,1},{1,0},{2,3},{3,2},{4,5},{5,4},{6,7},{7,6},{8,9},{9,8},{10,11... | collective-permute-start | bytes 1572872 | tf_op jit(solution)/shard_map/ppermute | solution.py:35
  106.2 13.2 %collective-permute-start.16 = (bf16[2,64,1408]{2,1,0:T(8,128)(2,1)S(1)}, bf16[2,64,1408]{2,1,0:T(8,128)(2,1)S(1)}, u32[]{:S(2)}, u32[]{:S(2)}) collective-permute-start(bf16[2,64,1408]{2,1,0:T(8,128)(2,1)S(1)} %add_convert_fusion.5), channel_id=1, source_target_pairs={{0,8},{2,6},{4,12},{6,2},{8,0},{10,14},{12,4},{14,10},{16,24},{18,... | collective-permute-start | bytes 1081352 | tf_op jit(solution)/shard_map/ppermute | solution.py:27
  120.2 30.4 %collective-permute-start.22 = (bf16[512,1024]{1,0:T(8,128)(2,1)S(1)}, bf16[512,1024]{1,0:T(8,128)(2,1)S(1)}, u32[]{:S(2)}, u32[]{:S(2)}) collective-permute-start(bf16[512,1024]{1,0:T(8,128)(2,1)S(1)} %pad_maximum_fusion.12), channel_id=1, source_target_pairs={{0,2},{2,0},{4,6},{6,4},{8,10},{10,8},{12,14},{14,12},{16,18},{18,... | collective-permute-start | bytes 3145736 | tf_op jit(solution)/shard_map/ppermute | solution.py:27
  121.9 12.9 %collective-permute-start.19 = (bf16[1,64,1408]{2,1,0:T(8,128)(2,1)S(1)}, bf16[1,64,1408]{2,1,0:T(8,128)(2,1)S(1)}, u32[]{:S(2)}, u32[]{:S(2)}) collective-permute-start(bf16[1,64,1408]{2,1,0:T(8,128)(2,1)S(1)} %add_convert_fusion.10), channel_id=1, source_target_pairs={{0,24},{2,26},{4,28},{6,30},{8,16},{10,18},{12,20},{14,22},{16,8},... | collective-permute-start | bytes 540680 | tf_op jit(solution)/shard_map/ppermute | solution.py:27
  124.6 13.4 %collective-permute-start.18 = (bf16[2,128,1408]{2,1,0:T(8,128)(2,1)S(1)}, bf16[2,128,1408]{2,1,0:T(8,128)(2,1)S(1)}, u32[]{:S(2)}, u32[]{:S(2)}) collective-permute-start(bf16[2,128,1408]{2,1,0:T(8,128)(2,1)S(1)} %add_convert_fusion), channel_id=1, source_target_pairs={{0,8},{2,6},{4,12},{6,2},{8,0},{10,14},{12,4},{14,10},{16,24},{18,... | collective-permute-start | bytes 2162696 | tf_op jit(solution)/shard_map/ppermute | solution.py:27
  145.7 9.9 %collective-permute-start.20 = (bf16[1,128,1408]{2,1,0:T(8,128)(2,1)S(1)}, bf16[1,128,1408]{2,1,0:T(8,128)(2,1)S(1)}, u32[]{:S(2)}, u32[]{:S(2)}) collective-permute-start(bf16[1,128,1408]{2,1,0:T(8,128)(2,1)S(1)} %add_convert_fusion.4), channel_id=1, source_target_pairs={{0,24},{2,26},{4,28},{6,30},{8,16},{10,18},{12,20},{14,22},{16,8},... | collective-permute-start | bytes 1081352 | tf_op jit(solution)/shard_map/ppermute | solution.py:27
  147.4 3.9 %collective-permute-start.21 = (bf16[512,768]{0,1:T(8,128)(2,1)S(1)}, bf16[512,768]{0,1:T(8,128)(2,1)S(1)}, u32[]{:S(2)}, u32[]{:S(2)}) collective-permute-start(bf16[512,768]{0,1:T(8,128)(2,1)S(1)} %pad_maximum_fusion.15), channel_id=1, source_target_pairs={{0,2},{2,0},{4,6},{6,4},{8,10},{10,8},{12,14},{14,12},{16,18},{18,... | collective-permute-start | bytes 2359304 | tf_op jit(solution)/shard_map/ppermute | solution.py:27
  148.5 14.4 %collective-permute-start.26 = (bf16[256,1024]{1,0:T(8,128)(2,1)S(1)}, bf16[256,1024]{1,0:T(8,128)(2,1)S(1)}, u32[]{:S(2)}, u32[]{:S(2)}) collective-permute-start(bf16[256,1024]{1,0:T(8,128)(2,1)S(1)} %fusion.41), channel_id=1, source_target_pairs={{0,1},{1,0},{2,3},{3,2},{4,5},{5,4},{6,7},{7,6},{8,9},{9,8},{10,11... | collective-permute-start | bytes 1572872 | tf_op jit(solution)/shard_map/ppermute | solution.py:35
  165.4 2.4 collective-permute-start.27
  165.4 28.5 %collective-permute-start.24 = (bf16[4,128,1024]{2,1,0:T(8,128)(2,1)}, bf16[4,128,1024]{2,1,0:T(8,128)(2,1)S(1)}, u32[]{:S(2)}, u32[]{:S(2)}) collective-permute-start(bf16[4,128,1024]{2,1,0:T(8,128)(2,1)} %constant_dynamic-slice_fusion.2), channel_id=1, source_target_pairs={{0,4},{2,10},{4,0},{6,14},{8,12},{10,2},{12,8},{14,6},{16,20},{18,... | collective-permute-start | bytes 3145736 | tf_op jit(solution)/shard_map/ppermute | solution.py:27
  171.1 53.1 %copy-start.29 = (bf16[1792,512]{1,0:T(8,128)(2,1)}, bf16[1792,512]{1,0:T(8,128)(2,1)S(1)}, u32[]{:S(2)}) copy-start(bf16[1792,512]{1,0:T(8,128)(2,1)S(1)} %convolution_convert_fusion) | copy-start | bytes 5505028
  171.5 13.5 %collective-permute-start.28 = (bf16[4,224,256]{2,1,0:T(8,128)(2,1)S(1)}, bf16[4,224,256]{2,1,0:T(8,128)(2,1)S(1)}, u32[]{:S(2)}, u32[]{:S(2)}) collective-permute-start(bf16[4,224,256]{2,1,0:T(8,128)(2,1)S(1)} %get-tuple-element.168), channel_id=1, source_target_pairs={{0,1},{1,0},{2,3},{3,2},{4,5},{5,4},{6,7},{7,6},{8,9},{9,8},{10,11... | collective-permute-start | bytes 1376264 | tf_op jit(solution)/shard_map/ppermute | solution.py:35
  173.6 28.0 %copy-start.31 = (bf16[512,1408]{1,0:T(8,128)(2,1)S(1)}, bf16[512,1408]{1,0:T(8,128)(2,1)}, u32[]{:S(2)}) copy-start(bf16[512,1408]{1,0:T(8,128)(2,1)} %copy-done.30) | copy-start | bytes 4325380
  173.6 28.0 %copy-start.55 = (bf16[1408,1024]{1,0:T(8,128)(2,1)S(1)}, bf16[1408,1024]{1,0:T(8,128)(2,1)}, u32[]{:S(2)}) copy-start(bf16[1408,1024]{1,0:T(8,128)(2,1)} %param.22) | copy-start | bytes 8650756
  173.6 13.6 %collective-permute-start.25 = (bf16[1,64,1408]{2,1,0:T(8,128)(2,1)S(1)}, bf16[1,64,1408]{2,1,0:T(8,128)(2,1)S(1)}, u32[]{:S(2)}, u32[]{:S(2)}) collective-permute-start(bf16[1,64,1408]{2,1,0:T(8,128)(2,1)S(1)} %add_convert_fusion.9), channel_id=1, source_target_pairs={{0,24},{2,26},{4,28},{6,30},{8,16},{10,18},{12,20},{14,22},{16,8},... | collective-permute-start | bytes 540680 | tf_op jit(solution)/shard_map/ppermute | solution.py:27
  175.5 18.7 %collective-permute-start.23 = (bf16[1,128,1408]{2,1,0:T(8,128)(2,1)S(1)}, bf16[1,128,1408]{2,1,0:T(8,128)(2,1)S(1)}, u32[]{:S(2)}, u32[]{:S(2)}) collective-permute-start(bf16[1,128,1408]{2,1,0:T(8,128)(2,1)S(1)} %copy-done.33), channel_id=1, source_target_pairs={{0,24},{2,26},{4,28},{6,30},{8,16},{10,18},{12,20},{14,22},{16,8},... | collective-permute-start | bytes 1081352 | tf_op jit(solution)/shard_map/ppermute | solution.py:27
  178.3 28.7 %collective-permute-start.32 = (bf16[4,224,256]{2,1,0:T(8,128)(2,1)S(1)}, bf16[4,224,256]{2,1,0:T(8,128)(2,1)S(1)}, u32[]{:S(2)}, u32[]{:S(2)}) collective-permute-start(bf16[4,224,256]{2,1,0:T(8,128)(2,1)S(1)} %get-tuple-element.167), channel_id=1, source_target_pairs={{0,1},{1,0},{2,3},{3,2},{4,5},{5,4},{6,7},{7,6},{8,9},{9,8},{10,11... | collective-permute-start | bytes 1376264 | tf_op jit(solution)/shard_map/ppermute | solution.py:35
  185.3 20.7 %collective-permute-start.33 = (bf16[4,224,256]{2,1,0:T(8,128)(2,1)S(1)}, bf16[4,224,256]{2,1,0:T(8,128)(2,1)S(1)}, u32[]{:S(2)}, u32[]{:S(2)}) collective-permute-start(bf16[4,224,256]{2,1,0:T(8,128)(2,1)S(1)} %add_convert_fusion.2), channel_id=1, source_target_pairs={{0,4},{2,10},{4,0},{6,14},{8,12},{10,2},{12,8},{14,6},{16,20},{18,... | collective-permute-start | bytes 1376264 | tf_op jit(solution)/shard_map/ppermute | solution.py:27
  187.2 20.0 %collective-permute-start.31 = (bf16[2,64,1408]{2,1,0:T(8,128)(2,1)S(1)}, bf16[2,64,1408]{2,1,0:T(8,128)(2,1)S(1)}, u32[]{:S(2)}, u32[]{:S(2)}) collective-permute-start(bf16[2,64,1408]{2,1,0:T(8,128)(2,1)S(1)} %pad_maximum_fusion.21), channel_id=1, source_target_pairs={{0,8},{2,6},{4,12},{6,2},{8,0},{10,14},{12,4},{14,10},{16,24},{18,... | collective-permute-start | bytes 1081352 | tf_op jit(solution)/shard_map/ppermute | solution.py:27
  194.1 14.1 %collective-permute-start.30 = (bf16[2,128,1024]{2,1,0:T(8,128)(2,1)S(1)}, bf16[2,128,1024]{2,1,0:T(8,128)(2,1)S(1)}, u32[]{:S(2)}, u32[]{:S(2)}) collective-permute-start(bf16[2,128,1024]{2,1,0:T(8,128)(2,1)S(1)} %add_convert_fusion.1), channel_id=1, source_target_pairs={{0,8},{2,6},{4,12},{6,2},{8,0},{10,14},{12,4},{14,10},{16,24},{18,... | collective-permute-start | bytes 1572872 | tf_op jit(solution)/shard_map/ppermute | solution.py:27
  195.0 22.3 %collective-permute-start.36 = (bf16[2,128,1408]{2,1,0:T(8,128)(2,1)S(1)}, bf16[2,128,1408]{2,1,0:T(8,128)(2,1)S(1)}, u32[]{:S(2)}, u32[]{:S(2)}) collective-permute-start(bf16[2,128,1408]{2,1,0:T(8,128)(2,1)S(1)} %get-tuple-element.188), channel_id=1, source_target_pairs={{0,8},{2,6},{4,12},{6,2},{8,0},{10,14},{12,4},{14,10},{16,24},{18,... | collective-permute-start | bytes 2162696 | tf_op jit(solution)/shard_map/ppermute | solution.py:27
  206.0 16.3 %collective-permute-start.29 = (bf16[256,1024]{1,0:T(8,128)(2,1)S(1)}, bf16[256,1024]{1,0:T(8,128)(2,1)S(1)}, u32[]{:S(2)}, u32[]{:S(2)}) collective-permute-start(bf16[256,1024]{1,0:T(8,128)(2,1)S(1)} %slice.116), channel_id=1, source_target_pairs={{0,1},{1,0},{2,3},{3,2},{4,5},{5,4},{6,7},{7,6},{8,9},{9,8},{10,11... | collective-permute-start | bytes 1572872 | tf_op jit(solution)/shard_map/ppermute | solution.py:35
  207.2 17.0 %collective-permute-start.35 = (bf16[2,224,256]{2,1,0:T(8,128)(2,1)S(1)}, bf16[2,224,256]{2,1,0:T(8,128)(2,1)S(1)}, u32[]{:S(2)}, u32[]{:S(2)}) collective-permute-start(bf16[2,224,256]{2,1,0:T(8,128)(2,1)S(1)} %add_convert_fusion.8), channel_id=1, source_target_pairs={{0,8},{2,6},{4,12},{6,2},{8,0},{10,14},{12,4},{14,10},{16,24},{18,... | collective-permute-start | bytes 688136 | tf_op jit(solution)/shard_map/ppermute | solution.py:27
  208.2 27.9 %collective-permute-start.39 = (bf16[4,64,1408]{2,1,0:T(8,128)(2,1)}, bf16[4,64,1408]{2,1,0:T(8,128)(2,1)}, u32[]{:S(2)}, u32[]{:S(2)}) collective-permute-start(bf16[4,64,1408]{2,1,0:T(8,128)(2,1)} %pad_maximum_fusion.16.refs_0_), channel_id=1, source_target_pairs={{0,2},{2,0},{4,6},{6,4},{8,10},{10,8},{12,14},{14,12},{16,18},{18,... | collective-permute-start | bytes 2162696 | tf_op jit(solution)/shard_map/ppermute | solution.py:27
  208.2 22.3 %collective-permute-start.38 = (bf16[4,64,1408]{2,1,0:T(8,128)(2,1)}, bf16[4,64,1408]{2,1,0:T(8,128)(2,1)}, u32[]{:S(2)}, u32[]{:S(2)}) collective-permute-start(bf16[4,64,1408]{2,1,0:T(8,128)(2,1)} %pad_maximum_fusion.16.refs_0_), channel_id=1, source_target_pairs={{0,4},{2,10},{4,0},{6,14},{8,12},{10,2},{12,8},{14,6},{16,20},{18,... | collective-permute-start | bytes 2162696 | tf_op jit(solution)/shard_map/ppermute | solution.py:27
  217.4 11.3 %collective-permute-start.34 = (bf16[1,128,1024]{2,1,0:T(8,128)(2,1)S(1)}, bf16[1,128,1024]{2,1,0:T(8,128)(2,1)S(1)}, u32[]{:S(2)}, u32[]{:S(2)}) collective-permute-start(bf16[1,128,1024]{2,1,0:T(8,128)(2,1)S(1)} %add_convert_fusion.7), channel_id=1, source_target_pairs={{0,24},{2,26},{4,28},{6,30},{8,16},{10,18},{12,20},{14,22},{16,8},... | collective-permute-start | bytes 786440 | tf_op jit(solution)/shard_map/ppermute | solution.py:27
  222.3 24.9 %collective-permute-start.42 = (bf16[4,128,1408]{2,1,0:T(8,128)(2,1)}, bf16[4,128,1408]{2,1,0:T(8,128)(2,1)}, u32[]{:S(2)}, u32[]{:S(2)}) collective-permute-start(bf16[4,128,1408]{2,1,0:T(8,128)(2,1)} %constant_dynamic-update-slice_fusion.5.refs_0_), channel_id=1, source_target_pairs={{0,4},{2,10},{4,0},{6,14},{8,12},{10,2},{12,8},{14,6},{16,20},{18,... | collective-permute-start | bytes 4325384 | tf_op jit(solution)/shard_map/ppermute | solution.py:27
  230.5 5.7 %collective-permute-start.40 = (bf16[4,64,1408]{2,1,0:T(8,128)(2,1)}, bf16[4,64,1408]{2,1,0:T(8,128)(2,1)}, u32[]{:S(2)}, u32[]{:S(2)}) collective-permute-start(bf16[4,64,1408]{2,1,0:T(8,128)(2,1)} %collective-permute-done.38.refs_1_), channel_id=1, source_target_pairs={{0,2},{2,0},{4,6},{6,4},{8,10},{10,8},{12,14},{14,12},{16,18},{18,... | collective-permute-start | bytes 2162696 | tf_op jit(solution)/shard_map/ppermute | solution.py:27
  232.2 9.8 %collective-permute-start.37 = (bf16[1,224,256]{2,1,0:T(8,128)(2,1)S(1)}, bf16[1,224,256]{2,1,0:T(8,128)(2,1)}, u32[]{:S(2)}, u32[]{:S(2)}) collective-permute-start(bf16[1,224,256]{2,1,0:T(8,128)(2,1)S(1)} %add_convert_fusion.12), channel_id=1, source_target_pairs={{0,24},{2,26},{4,28},{6,30},{8,16},{10,18},{12,20},{14,22},{16,8},... | collective-permute-start | bytes 344072 | tf_op jit(solution)/shard_map/ppermute | solution.py:27
  234.9 11.4 %collective-permute-start.43 = (bf16[1,128,1024]{2,1,0:T(8,128)(2,1)}, bf16[1,128,1024]{2,1,0:T(8,128)(2,1)}, u32[]{:S(2)}, u32[]{:S(2)}) collective-permute-start(bf16[1,128,1024]{2,1,0:T(8,128)(2,1)} %add_convert_fusion.6), channel_id=1, source_target_pairs={{0,24},{2,26},{4,28},{6,30},{8,16},{10,18},{12,20},{14,22},{16,8},... | collective-permute-start | bytes 786440 | tf_op jit(solution)/shard_map/ppermute | solution.py:27
  236.1 21.6 %collective-permute-start.44 = (bf16[4,128,1408]{2,1,0:T(8,128)(2,1)}, bf16[4,128,1408]{2,1,0:T(8,128)(2,1)S(1)}, u32[]{:S(2)}, u32[]{:S(2)}) collective-permute-start(bf16[4,128,1408]{2,1,0:T(8,128)(2,1)} %constant_dynamic-update-slice_fusion.5.refs_0_), channel_id=1, source_target_pairs={{0,2},{2,0},{4,6},{6,4},{8,10},{10,8},{12,14},{14,12},{16,18},{18,... | collective-permute-start | bytes 4325384 | tf_op jit(solution)/shard_map/ppermute | solution.py:27
  247.2 10.8 %collective-permute-start.45 = (bf16[4,128,1408]{2,1,0:T(8,128)(2,1)}, bf16[4,128,1408]{2,1,0:T(8,128)(2,1)S(1)}, u32[]{:S(2)}, u32[]{:S(2)}) collective-permute-start(bf16[4,128,1408]{2,1,0:T(8,128)(2,1)} %collective-permute-done.42.refs_1_), channel_id=1, source_target_pairs={{0,2},{2,0},{4,6},{6,4},{8,10},{10,8},{12,14},{14,12},{16,18},{18,... | collective-permute-start | bytes 4325384 | tf_op jit(solution)/shard_map/ppermute | solution.py:27
  255.0 12.4 %collective-permute-start.48 = (bf16[2,128,1024]{2,1,0:T(8,128)(2,1)S(1)}, bf16[2,128,1024]{2,1,0:T(8,128)(2,1)S(1)}, u32[]{:S(2)}, u32[]{:S(2)}) collective-permute-start(bf16[2,128,1024]{2,1,0:T(8,128)(2,1)S(1)} %pad_maximum_fusion.19), channel_id=1, source_target_pairs={{0,8},{2,6},{4,12},{6,2},{8,0},{10,14},{12,4},{14,10},{16,24},{18,... | collective-permute-start | bytes 1572872 | tf_op jit(solution)/shard_map/ppermute | solution.py:27
  255.0 12.3 %collective-permute-start.41 = (bf16[1,224,256]{2,1,0:T(8,128)(2,1)S(1)}, bf16[1,224,256]{2,1,0:T(8,128)(2,1)S(1)}, u32[]{:S(2)}, u32[]{:S(2)}) collective-permute-start(bf16[1,224,256]{2,1,0:T(8,128)(2,1)S(1)} %add_convert_fusion.11), channel_id=1, source_target_pairs={{0,24},{2,26},{4,28},{6,30},{8,16},{10,18},{12,20},{14,22},{16,8},... | collective-permute-start | bytes 344072 | tf_op jit(solution)/shard_map/ppermute | solution.py:27
  268.4 16.2 %collective-permute-start.51 = (bf16[4,128,1024]{2,1,0:T(8,128)(2,1)S(1)}, bf16[4,128,1024]{2,1,0:T(8,128)(2,1)S(1)}, u32[]{:S(2)}, u32[]{:S(2)}) collective-permute-start(bf16[4,128,1024]{2,1,0:T(8,128)(2,1)S(1)} %pad_maximum_fusion.13.refs_0_), channel_id=1, source_target_pairs={{0,4},{2,10},{4,0},{6,14},{8,12},{10,2},{12,8},{14,6},{16,20},{18,... | collective-permute-start | bytes 3145736 | tf_op jit(solution)/shard_map/ppermute | solution.py:27
  270.2 6.0 %collective-permute-start.47 = (bf16[2,224,256]{2,1,0:T(8,128)(2,1)S(1)}, bf16[2,224,256]{2,1,0:T(8,128)(2,1)S(1)}, u32[]{:S(2)}, u32[]{:S(2)}) collective-permute-start(bf16[2,224,256]{2,1,0:T(8,128)(2,1)S(1)} %pad_maximum_fusion.22), channel_id=1, source_target_pairs={{0,1},{1,0},{2,3},{3,2},{4,5},{5,4},{6,7},{7,6},{8,9},{9,8},{10,11... | collective-permute-start | bytes 688136 | tf_op jit(solution)/shard_map/ppermute | solution.py:35
  270.8 8.5 %collective-permute-start.46 = (bf16[2,224,256]{2,1,0:T(8,128)(2,1)S(1)}, bf16[2,224,256]{2,1,0:T(8,128)(2,1)S(1)}, u32[]{:S(2)}, u32[]{:S(2)}) collective-permute-start(bf16[2,224,256]{2,1,0:T(8,128)(2,1)S(1)} %pad_maximum_fusion.22), channel_id=1, source_target_pairs={{0,8},{2,6},{4,12},{6,2},{8,0},{10,14},{12,4},{14,10},{16,24},{18,... | collective-permute-start | bytes 688136 | tf_op jit(solution)/shard_map/ppermute | solution.py:27
  270.8 24.2 %collective-permute-start.50 = (bf16[4,128,1024]{2,1,0:T(8,128)(2,1)S(1)}, bf16[4,128,1024]{2,1,0:T(8,128)(2,1)S(1)}, u32[]{:S(2)}, u32[]{:S(2)}) collective-permute-start(bf16[4,128,1024]{2,1,0:T(8,128)(2,1)S(1)} %pad_maximum_fusion.13.refs_0_), channel_id=1, source_target_pairs={{0,2},{2,0},{4,6},{6,4},{8,10},{10,8},{12,14},{14,12},{16,18},{18,... | collective-permute-start | bytes 3145736 | tf_op jit(solution)/shard_map/ppermute | solution.py:27
  284.6 10.4 %collective-permute-start.52 = (bf16[4,128,1024]{2,1,0:T(8,128)(2,1)S(1)}, bf16[4,128,1024]{2,1,0:T(8,128)(2,1)S(1)}, u32[]{:S(2)}, u32[]{:S(2)}) collective-permute-start(bf16[4,128,1024]{2,1,0:T(8,128)(2,1)S(1)} %collective-permute-done.51.refs_1_), channel_id=1, source_target_pairs={{0,2},{2,0},{4,6},{6,4},{8,10},{10,8},{12,14},{14,12},{16,18},{18,... | collective-permute-start | bytes 3145736 | tf_op jit(solution)/shard_map/ppermute | solution.py:27
  284.6 8.5 %collective-permute-start.49 = (bf16[4,224,256]{2,1,0:T(8,128)(2,1)S(1)}, bf16[4,224,256]{2,1,0:T(8,128)(2,1)S(1)}, u32[]{:S(2)}, u32[]{:S(2)}) collective-permute-start(bf16[4,224,256]{2,1,0:T(8,128)(2,1)S(1)} %pad_maximum_fusion.20.refs_0_), channel_id=1, source_target_pairs={{0,4},{2,10},{4,0},{6,14},{8,12},{10,2},{12,8},{14,6},{16,20},{18,... | collective-permute-start | bytes 1376264 | tf_op jit(solution)/shard_map/ppermute | solution.py:27
  285.8 8.7 %collective-permute-start.53 = (bf16[2,224,256]{2,1,0:T(8,128)(2,1)S(1)}, bf16[2,224,256]{2,1,0:T(8,128)(2,1)S(1)}, u32[]{:S(2)}, u32[]{:S(2)}) collective-permute-start(bf16[2,224,256]{2,1,0:T(8,128)(2,1)S(1)} %collective-permute-done.46), channel_id=1, source_target_pairs={{0,1},{1,0},{2,3},{3,2},{4,5},{5,4},{6,7},{7,6},{8,9},{9,8},{10,11... | collective-permute-start | bytes 688136 | tf_op jit(solution)/shard_map/ppermute | solution.py:35
  293.1 12.1 %collective-permute-start.54 = (bf16[4,224,256]{2,1,0:T(8,128)(2,1)S(1)}, bf16[4,224,256]{2,1,0:T(8,128)(2,1)S(1)}, u32[]{:S(2)}, u32[]{:S(2)}) collective-permute-start(bf16[4,224,256]{2,1,0:T(8,128)(2,1)S(1)} %collective-permute-done.49.refs_1_), channel_id=1, source_target_pairs={{0,1},{1,0},{2,3},{3,2},{4,5},{5,4},{6,7},{7,6},{8,9},{9,8},{10,11... | collective-permute-start | bytes 1376264 | tf_op jit(solution)/shard_map/ppermute | solution.py:35
  294.5 10.6 %collective-permute-start.55 = (bf16[4,224,256]{2,1,0:T(8,128)(2,1)S(1)}, bf16[4,224,256]{2,1,0:T(8,128)(2,1)S(1)}, u32[]{:S(2)}, u32[]{:S(2)}) collective-permute-start(bf16[4,224,256]{2,1,0:T(8,128)(2,1)S(1)} %pad_maximum_fusion.20.refs_0_), channel_id=1, source_target_pairs={{0,2},{2,0},{4,6},{6,4},{8,10},{10,8},{12,14},{14,12},{16,18},{18,... | collective-permute-start | bytes 1376264 | tf_op jit(solution)/shard_map/ppermute | solution.py:27
  294.5 10.6 %collective-permute-start.56 = (bf16[4,224,256]{2,1,0:T(8,128)(2,1)S(1)}, bf16[4,224,256]{2,1,0:T(8,128)(2,1)S(1)}, u32[]{:S(2)}, u32[]{:S(2)}) collective-permute-start(bf16[4,224,256]{2,1,0:T(8,128)(2,1)S(1)} %collective-permute-done.49.refs_1_), channel_id=1, source_target_pairs={{0,2},{2,0},{4,6},{6,4},{8,10},{10,8},{12,14},{14,12},{16,18},{18,... | collective-permute-start | bytes 1376264 | tf_op jit(solution)/shard_map/ppermute | solution.py:27
  295.1 10.1 %collective-permute-start.57 = (bf16[4,224,256]{2,1,0:T(8,128)(2,1)S(1)}, bf16[4,224,256]{2,1,0:T(8,128)(2,1)S(1)}, u32[]{:S(2)}, u32[]{:S(2)}) collective-permute-start(bf16[4,224,256]{2,1,0:T(8,128)(2,1)S(1)} %constant_dynamic-update-slice_fusion.8.refs_2_), channel_id=1, source_target_pairs={{0,2},{2,0},{4,6},{6,4},{8,10},{10,8},{12,14},{14,12},{16,18},{18,... | collective-permute-start | bytes 1376264 | tf_op jit(solution)/shard_map/ppermute | solution.py:27
  305.2 1.8 collective-permute-start.58
  (57 other events, 392.4 us)

commit v4 on v3

--- a/solution.py
+++ b/solution.py
@@ -550,8 +550,8 @@
     lifted = jnp.dot(features, w_proj, preferred_element_type=jnp.float32) + proj_bias
     normed, scale_attn = rms_forward(lifted, gain_attn)
     gathered = gather_group(normed.astype(jnp.bfloat16))
-    segments = gather_group(segment_ids)
-    padding = gather_group(padding_mask)
+    both = gather_group(2 * segment_ids + padding_mask)
+    segments, padding = both >> 1, both & 1
     gathered, cot_here = tie_sums(gathered, cotangent)
     grad_gathered = gather_group(cot_here)
     queries, key_rows, value_rows = (
@@ -564,9 +564,10 @@
         queries, key_rows, value_rows, segments, padding, group_tokens, query_count
     )
     mixed, grad_gathered = tie_sums(mixed, grad_gathered)
-    middle = lifted + scatter_group(
-        jnp.dot(mixed, w_out, preferred_element_type=jnp.float32).astype(jnp.bfloat16)
-    )
+    given, own = to_owners(
+        lambda part: jnp.dot(part, w_out, preferred_element_type=jnp.float32), mixed
+    )
+    middle = lifted + own + given.astype(jnp.float32)
     normed_ffn, scale_ffn = rms_forward(middle, gain_ffn)
     gathered_ffn = gather_group(normed_ffn.astype(jnp.bfloat16))
     pair_normed = with_pair(gathered)

time: 318 us -> 314 us (0.987)
  local copies, waits for them, and re-layouts: 23.7 us -> 19.7 us
    ppermute x15 -> x14, waiting for transfers between devices: 60.7 us -> 62.8 us  [peer_swap(): return lax.ppermute(value, 'heads', [(0, 1), (1, 0)])]
    unnamed x130 -> x127, local copies, waits for them, and re-layouts: 15.7 us -> 13.7 us
    ppermute x15 -> x14, starting transfers between devices: 17.4 us -> 15.6 us  [peer_swap(): return lax.ppermute(value, 'heads', [(0, 1), (1, 0)])]
  transfers between devices with their start and end apart: 59 -> 58, of which waited for: 20 -> 20; matrix products, arithmetic and copies ran while one was open for 31% -> 31% of each run, Pallas kernels for 6% -> 6%
where the time goes in v4:
time: 314 us; the launch traced here: 308 us
  waiting for transfers between devices  98.5 us (31%)
  starting transfers between devices  73.8 us (24%)
  matrix products  54.5 us (17%)
  other arithmetic  35.9 us (11%)
  Pallas kernels  23.4 us (7%)
  local copies, waits for them, and re-layouts  19.7 us (6%)
    ppermute x14, waiting for transfers between devices, peer_swap(): return lax.ppermute(value, 'heads', [(0, 1), (1, 0)])  62.8 us
    ppermute x44, starting transfers between devices, swap_rows(): lax.ppermute(value, 'rows', [(r, r ^ masks[r % 2]) for r in range(count)])  58.2 us
    ppermute x44, waiting for transfers between devices, swap_rows(): lax.ppermute(value, 'rows', [(r, r ^ masks[r % 2]) for r in range(count)])  35.7 us
    dot_general x17, matrix products, contract(): lax.dot_general(left, right, (((left_dim,), (right_dim,)), ((), ())), pre...  27.7 us
    pallas_call x3, Pallas kernels, place_blocks(): pl.pallas_call(body, grid_spec=pltpu.PrefetchScalarGridSpec(num_scalar_pr...  19.1 us
    ppermute x14, starting transfers between devices, peer_swap(): return lax.ppermute(value, 'heads', [(0, 1), (1, 0)])  15.6 us
    unnamed x127, local copies, waits for them, and re-layouts  13.7 us
    convert_element_type x12, other arithmetic, part(): return total.astype(jnp.bfloat16)  11.7 us
  transfers between devices with their start and end apart: 58, of which 20 were waited for; matrix products, arithmetic and copies ran while one was open for 31% of the time, Pallas kernels for 6%

profile of v4, /device:TPU:0, one launch (start us, length us, event | category | flops | bytes accessed | tf_op | source)
XLA Modules:
  0.0 308.1 jit_solution(16930253552996243590)
XLA Ops:
  1.5 2.9 collective-permute-start.1
  4.5 2.4 multiply_reduce_fusion.6
  8.7 11.7 %collective-permute-done = bf16[256,1024]{1,0:T(8,128)(2,1)S(1)} collective-permute-done((bf16[256,1024]{1,0:T(8,128)(2,1)S(1)}, bf16[256,1024]{1,0:T(8,128)(2,1)S(1)}, u32[]{:S(2)}, u32[]{:S(2)}) %collective-permute-start) | collective-permute-done | bytes 524320 | tf_op jit(solution)/shard_map/ppermute | solution.py:35
  27.3 1.9 copy-done.1
  29.2 2.4 fusion.37
  31.7 3.8 %collective-permute-done.2 = bf16[256,1024]{1,0:T(8,128)(2,1)S(1)} collective-permute-done((bf16[256,1024]{1,0:T(8,128)(2,1)S(1)}, bf16[256,1024]{1,0:T(8,128)(2,1)S(1)}, u32[]{:S(2)}, u32[]{:S(2)}) %collective-permute-start.2) | collective-permute-done | bytes 524320 | tf_op jit(solution)/shard_map/ppermute | solution.py:35
  37.8 1.7 collective-permute-start.3
  40.5 6.2 %copy.30 = bf16[128,8,2,1408]{3,1,2,0:T(8,128)(2,1)} copy(bf16[128,8,2,1408]{3,2,1,0:T(2,128)(2,1)} %bitcast.97) | data formatting | bytes 11534336
  50.7 1.6 multiply_reduce_fusion.5
  53.6 2.7 pad_maximum_fusion.3
  58.8 7.7 %collective-permute-done.4 = bf16[256,1024]{1,0:T(8,128)(2,1)S(1)} collective-permute-done((bf16[256,1024]{1,0:T(8,128)(2,1)S(1)}, bf16[256,1024]{1,0:T(8,128)(2,1)S(1)}, u32[]{:S(2)}, u32[]{:S(2)}) %collective-permute-start.4) | collective-permute-done | bytes 524320 | tf_op jit(solution)/shard_map/ppermute | solution.py:35
  66.7 3.2 %fusion.89 = f32[512,2816]{1,0:T(8,128)S(1)} fusion(bf16[512,1024]{1,0:T(8,128)(2,1)S(1)} %pad_maximum_fusion.10, bf16[1024,2816]{1,0:T(8,128)(2,1)S(1)} %bitcast.100), kind=kOutput, calls=%fused_computation.208 | convolution fusion | flops 2952790016 | bytes 12582912 | tf_op jit(solution)/shard_map/dot_general | solution.py:587
  72.0 4.5 %broadcast_select_fusion.1 = (bf16[512,1408]{1,0:T(8,128)(2,1)S(1)}, bf16[512,1408]{1,0:T(8,128)(2,1)S(1)}, bf16[512,1408]{1,0:T(8,128)(2,1)S(1)}) fusion(pred[]{:T(512)S(6)} %eq.139, f32[512,2816]{1,0:T(8,128)S(1)} %fusion.89, bf16[512,1024]{1,0:T(8,128)(2,1)S(1)} %copy-done.18, bf16[1408,1024]{1,0:T(8,128)(2,1)S(1)} %copy-done.55), kind=kOutput, calls=%fused_computation.58 | convolution fusion | flops 1494417408 | bytes 14024705 | tf_op jit(solution)/shard_map/dot_general | solution.py:20
  77.3 1.7 fusion.34
  79.0 1.7 fusion.32
  80.7 1.8 convolution_convert_fusion.1
  82.6 1.6 collective-permute-start.13
  84.7 3.0 convolution_convert_fusion.2
  88.2 3.0 convolution_convert_fusion.3
  91.2 7.2 %collective-permute-done.14 = bf16[256,1024]{1,0:T(8,128)(2,1)S(1)} collective-permute-done((bf16[256,1024]{1,0:T(8,128)(2,1)S(1)}, bf16[256,1024]{1,0:T(8,128)(2,1)S(1)}, u32[]{:S(2)}, u32[]{:S(2)}) %collective-permute-start.14) | collective-permute-done | bytes 524320 | tf_op jit(solution)/shard_map/ppermute | solution.py:35
  98.9 1.6 fusion.86
  102.6 11.6 %collective-permute-done.16 = bf16[256,1024]{1,0:T(8,128)(2,1)} collective-permute-done((bf16[256,1024]{1,0:T(8,128)(2,1)}, bf16[256,1024]{1,0:T(8,128)(2,1)}, u32[]{:S(2)}, u32[]{:S(2)}) %collective-permute-start.16) | collective-permute-done | bytes 524320 | tf_op jit(solution)/shard_map/ppermute | solution.py:35
  116.4 1.7 add_convert_fusion.10
  120.7 1.9 collective-permute-start.17
  122.6 5.5 %fusion.38 = bf16[8,64,512]{2,1,0:T(8,128)(2,1)S(1)} fusion(bf16[512,8,64]{0,2,1:T(8,128)(2,1)S(1)} %bitcast.133, f32[8,512,512]{1,2,0:T(8,128)} %copy-done.1, f32[8,512]{1,0:T(8,128)S(1)} %log_add_fusion, pred[512,512]{0,1:T(8,128)(4,1)S(1)} %copy-done.14), kind=kOutput, calls=%fused_computation.67 | convolution fusion | flops 274989056 | bytes 9715712 | tf_op jit(solution)/shard_map/hqk,qhd->khd/dot_general | solution.py:498
  128.2 2.8 multiply_reduce_fusion
  131.0 3.1 %collective-permute-done.17 = bf16[2,128,1408]{2,1,0:T(8,128)(2,1)S(1)} collective-permute-done((bf16[2,128,1408]{2,1,0:T(8,128)(2,1)S(1)}, bf16[2,128,1408]{2,1,0:T(8,128)(2,1)S(1)}, u32[]{:S(2)}, u32[]{:S(2)}) %collective-permute-start.17) | collective-permute-done | bytes 720928 | tf_op jit(solution)/shard_map/ppermute | solution.py:27
  134.1 2.8 multiply_convert_fusion
  148.0 1.8 convolution_convert_fusion.4
  151.7 2.0 add_convert_fusion.3
  153.7 5.2 %collective-permute-done.25 = bf16[256,1024]{1,0:T(8,128)(2,1)S(1)} collective-permute-done((bf16[256,1024]{1,0:T(8,128)(2,1)S(1)}, bf16[256,1024]{1,0:T(8,128)(2,1)S(1)}, u32[]{:S(2)}, u32[]{:S(2)}) %collective-permute-start.25) | collective-permute-done | bytes 524320 | tf_op jit(solution)/shard_map/ppermute | solution.py:35
  161.5 2.4 collective-permute-start.23
  163.9 3.3 %convolution_convert_fusion = bf16[1792,512]{1,0:T(8,128)(2,1)S(1)} fusion(bf16[544,1792]{1,0:T(8,128)(2,1)} %pad_maximum_fusion.3, bf16[272,512]{1,0:T(8,128)(2,1)} %collective-permute-done.26, bf16[272,512]{1,0:T(8,128)(2,1)} %get-tuple-element.175), kind=kOutput, calls=%fused_computation.15 | convolution fusion | flops 1000275968 | bytes 4341760 | tf_op jit(solution)/shard_map/dot_general | solution.py:20
  168.0 1.6 add_convert_fusion.9
  169.7 1.9 collective-permute-start.24
  171.6 2.0 collective-permute-start.22
  175.5 5.6 %collective-permute-done.27 = bf16[4,224,256]{2,1,0:T(8,128)(2,1)S(1)} collective-permute-done((bf16[4,224,256]{2,1,0:T(8,128)(2,1)S(1)}, bf16[4,224,256]{2,1,0:T(8,128)(2,1)S(1)}, u32[]{:S(2)}, u32[]{:S(2)}) %collective-permute-start.27) | collective-permute-done | bytes 458784 | tf_op jit(solution)/shard_map/ppermute | solution.py:35
  181.4 1.9 collective-permute-start.32
  183.3 6.7 %collective-permute-start.30 = (bf16[2,64,1408]{2,1,0:T(8,128)(2,1)S(1)}, bf16[2,64,1408]{2,1,0:T(8,128)(2,1)S(1)}, u32[]{:S(2)}, u32[]{:S(2)}) collective-permute-start(bf16[2,64,1408]{2,1,0:T(8,128)(2,1)S(1)} %pad_maximum_fusion.21), channel_id=1, source_target_pairs={{0,8},{2,6},{4,12},{6,2},{8,0},{10,14},{12,4},{14,10},{16,24},{18,... | collective-permute-start | bytes 1081352 | tf_op jit(solution)/shard_map/ppermute | solution.py:27
  191.1 6.5 %collective-permute-start.35 = (bf16[2,128,1408]{2,1,0:T(8,128)(2,1)S(1)}, bf16[2,128,1408]{2,1,0:T(8,128)(2,1)S(1)}, u32[]{:S(2)}, u32[]{:S(2)}) collective-permute-start(bf16[2,128,1408]{2,1,0:T(8,128)(2,1)S(1)} %get-tuple-element.186), channel_id=1, source_target_pairs={{0,8},{2,6},{4,12},{6,2},{8,0},{10,14},{12,4},{14,10},{16,24},{18,... | collective-permute-start | bytes 2162696 | tf_op jit(solution)/shard_map/ppermute | solution.py:27
  197.6 1.8 convolution_convert_fusion.5
  199.5 2.6 fusion.90
  204.3 1.7 collective-permute-start.37
  206.2 7.2 %collective-permute-done.35 = bf16[2,128,1408]{2,1,0:T(8,128)(2,1)S(1)} collective-permute-done((bf16[2,128,1408]{2,1,0:T(8,128)(2,1)S(1)}, bf16[2,128,1408]{2,1,0:T(8,128)(2,1)S(1)}, u32[]{:S(2)}, u32[]{:S(2)}) %collective-permute-start.35) | collective-permute-done | bytes 720928 | tf_op jit(solution)/shard_map/ppermute | solution.py:27
  213.4 4.0 %collective-permute-start.33 = (bf16[1,128,1024]{2,1,0:T(8,128)(2,1)S(1)}, bf16[1,128,1024]{2,1,0:T(8,128)(2,1)S(1)}, u32[]{:S(2)}, u32[]{:S(2)}) collective-permute-start(bf16[1,128,1024]{2,1,0:T(8,128)(2,1)S(1)} %add_convert_fusion.7), channel_id=1, source_target_pairs={{0,24},{2,26},{4,28},{6,30},{8,16},{10,18},{12,20},{14,22},{16,8},... | collective-permute-start | bytes 786440 | tf_op jit(solution)/shard_map/ppermute | solution.py:27
  218.4 1.8 collective-permute-start.41
  220.5 4.3 %collective-permute-done.33 = bf16[1,128,1024]{2,1,0:T(8,128)(2,1)S(1)} collective-permute-done((bf16[1,128,1024]{2,1,0:T(8,128)(2,1)S(1)}, bf16[1,128,1024]{2,1,0:T(8,128)(2,1)S(1)}, u32[]{:S(2)}, u32[]{:S(2)}) %collective-permute-start.33) | collective-permute-done | bytes 262176 | tf_op jit(solution)/shard_map/ppermute | solution.py:27
  226.6 1.7 collective-permute-start.39
  228.3 2.6 collective-permute-start.36
  232.3 5.8 %place_down.1 = f32[1408,1024]{1,0:T(8,128)} custom-call(s32[4]{0:T(128)S(1)} %pad_add_fusion.1.index, bf16[4,64,1408]{2,1,0:T(8,128)(2,1)} %pad_maximum_fusion.16.refs_0_, bf16[4,64,1408]{2,1,0:T(8,128)(2,1)} %collective-permute-done.37.refs_1_, bf16[4,64,1408]{2,1,0:T(8,128)(2,1)} %collective-permute-done.38.refs_2_, ...), custom_call_target="tpu_custom_call" | custom-call | bytes 8650752 | tf_op jit(solution)/shard_map/place_down/pallas_call | solution.py:295
  239.4 2.9 collective-permute-done.42
  243.3 7.7 %collective-permute-start.44 = (bf16[4,128,1408]{2,1,0:T(8,128)(2,1)}, bf16[4,128,1408]{2,1,0:T(8,128)(2,1)S(1)}, u32[]{:S(2)}, u32[]{:S(2)}) collective-permute-start(bf16[4,128,1408]{2,1,0:T(8,128)(2,1)} %collective-permute-done.41.refs_1_), channel_id=1, source_target_pairs={{0,2},{2,0},{4,6},{6,4},{8,10},{10,8},{12,14},{14,12},{16,18},{18,... | collective-permute-start | bytes 4325384 | tf_op jit(solution)/shard_map/ppermute | solution.py:27
  251.0 2.7 collective-permute-start.40
  254.1 7.8 %place_gate_up.1 = f32[1024,2,1408]{2,1,0:T(2,128)} custom-call(s32[4]{0:T(128)S(1)} %pad_add_fusion.1.index, bf16[4,128,1408]{2,1,0:T(8,128)(2,1)} %constant_dynamic-update-slice_fusion.4.refs_0_, bf16[4,128,1408]{2,1,0:T(8,128)(2,1)} %collective-permute-done.41.refs_1_, bf16[4,128,1408]{2,1,0:T(8,128)(2,1)S(1)} %collective-permute-done.43.refs_2_, ...), custom_call_target="tpu_custom_call" | custom-call | bytes 17301504 | tf_op jit(solution)/shard_map/place_gate_up/pallas_call | solution.py:295
  264.5 1.8 collective-permute-start.50
  266.8 5.5 %collective-permute-done.46 = bf16[2,224,256]{2,1,0:T(8,128)(2,1)S(1)} collective-permute-done((bf16[2,224,256]{2,1,0:T(8,128)(2,1)S(1)}, bf16[2,224,256]{2,1,0:T(8,128)(2,1)S(1)}, u32[]{:S(2)}, u32[]{:S(2)}) %collective-permute-start.46) | collective-permute-done | bytes 229408 | tf_op jit(solution)/shard_map/ppermute | solution.py:35
  272.3 3.0 collective-permute-done.45
  275.4 5.2 %collective-permute-done.50.refs_1_ = bf16[4,128,1024]{2,1,0:T(8,128)(2,1)S(1)} collective-permute-done((bf16[4,128,1024]{2,1,0:T(8,128)(2,1)S(1)}, bf16[4,128,1024]{2,1,0:T(8,128)(2,1)S(1)}, u32[]{:S(2)}, u32[]{:S(2)}) %collective-permute-start.50) | collective-permute-done | bytes 1048608 | tf_op jit(solution)/shard_map/ppermute | solution.py:27
  283.4 5.7 %collective-permute-done.48.refs_1_ = bf16[4,224,256]{2,1,0:T(8,128)(2,1)S(1)} collective-permute-done((bf16[4,224,256]{2,1,0:T(8,128)(2,1)S(1)}, bf16[4,224,256]{2,1,0:T(8,128)(2,1)S(1)}, u32[]{:S(2)}, u32[]{:S(2)}) %collective-permute-start.48) | collective-permute-done | bytes 458784 | tf_op jit(solution)/shard_map/ppermute | solution.py:27
  289.1 1.5 collective-permute-start.53
  291.3 5.5 %place_attn.1 = (f32[3,1024,512]{2,1,0:T(8,128)}, f32[512,1024]{1,0:T(8,128)}) custom-call(s32[4]{0:T(128)S(1)} %pad_add_fusion.1.index, bf16[4,128,1024]{2,1,0:T(8,128)(2,1)S(1)} %pad_maximum_fusion.13.refs_0_, bf16[4,128,1024]{2,1,0:T(8,128)(2,1)S(1)} %collective-permute-done.50.refs_1_, bf16[4,128,1024]{2,1,0:T(8,128)(2,1)S(1)} %collective-permute-done.49.refs_2_, ...), custom_call_target="tpu_custom_call" | custom-call | bytes 12582912 | tf_op jit(solution)/shard_map/place_attn/pallas_call | solution.py:295
  296.7 4.4 %collective-permute-done.53.refs_3_ = bf16[4,224,256]{2,1,0:T(8,128)(2,1)S(1)} collective-permute-done((bf16[4,224,256]{2,1,0:T(8,128)(2,1)S(1)}, bf16[4,224,256]{2,1,0:T(8,128)(2,1)S(1)}, u32[]{:S(2)}, u32[]{:S(2)}) %collective-permute-start.53) | collective-permute-done | bytes 458784 | tf_op jit(solution)/shard_map/ppermute | solution.py:35
  301.2 1.8 collective-permute-done.57.refs_7_
  303.0 4.3 %place_proj.1 = (f32[1664,1024]{1,0:T(8,128)}, f32[16,1024]{1,0:T(8,128)S(1)}) custom-call(s32[4]{0:T(128)S(1)} %pad_add_fusion.1.index, bf16[4,224,256]{2,1,0:T(8,128)(2,1)S(1)} %pad_maximum_fusion.20.refs_0_, bf16[4,224,256]{2,1,0:T(8,128)(2,1)S(1)} %collective-permute-done.48.refs_1_, ...), custom_call_target="tpu_custom_call" | custom-call | bytes 11010048 | tf_op jit(solution)/shard_map/place_proj/pallas_call | solution.py:404
  (289 shorter events, 67.8 us)
Async XLA Ops:
  1.5 6.9 %collective-permute-start.1 = (s32[256]{0:T(256)S(1)}, s32[256]{0:T(256)S(1)}, u32[]{:S(2)}, u32[]{:S(2)}) collective-permute-start(s32[256]{0:T(256)S(1)} %multiply_add_fusion.2), channel_id=1, source_target_pairs={{0,1},{1,0},{2,3},{3,2},{4,5},{5,4},{6,7},{7,6},{8,9},{9,8},{10,11... | collective-permute-start | bytes 3080 | tf_op jit(solution)/shard_map/ppermute | solution.py:35
  7.0 13.4 %collective-permute-start = (bf16[256,1024]{1,0:T(8,128)(2,1)S(1)}, bf16[256,1024]{1,0:T(8,128)(2,1)S(1)}, u32[]{:S(2)}, u32[]{:S(2)}) collective-permute-start(bf16[256,1024]{1,0:T(8,128)(2,1)S(1)} %multiply_convert_fusion.4), channel_id=1, source_target_pairs={{0,1},{1,0},{2,3},{3,2},{4,5},{5,4},{6,7},{7,6},{8,9},{9,8},{10,11... | collective-permute-start | bytes 1572872 | tf_op jit(solution)/shard_map/ppermute | solution.py:35
  8.4 31.1 %copy-start.11 = (bf16[256,1792]{1,0:T(8,128)(2,1)}, bf16[256,1792]{1,0:T(8,128)(2,1)S(1)}, u32[]{:S(2)}) copy-start(bf16[256,1792]{1,0:T(8,128)(2,1)S(1)} %pad.9) | copy-start | bytes 2752516
  22.9 12.5 %collective-permute-start.2 = (bf16[256,1024]{1,0:T(8,128)(2,1)S(1)}, bf16[256,1024]{1,0:T(8,128)(2,1)S(1)}, u32[]{:S(2)}, u32[]{:S(2)}) collective-permute-start(bf16[256,1024]{1,0:T(8,128)(2,1)S(1)} %copy-done.30), channel_id=1, source_target_pairs={{0,1},{1,0},{2,3},{3,2},{4,5},{5,4},{6,7},{7,6},{8,9},{9,8},{10,11... | collective-permute-start | bytes 1572872 | tf_op jit(solution)/shard_map/ppermute | solution.py:35
  37.8 12.9 %collective-permute-start.3 = (bf16[256,1024]{1,0:T(8,128)(2,1)}, bf16[256,1024]{1,0:T(8,128)(2,1)}, u32[]{:S(2)}, u32[]{:S(2)}) collective-permute-start(bf16[256,1024]{1,0:T(8,128)(2,1)} %convolution_convert_fusion.8), channel_id=1, source_target_pairs={{0,1},{1,0},{2,3},{3,2},{4,5},{5,4},{6,7},{7,6},{8,9},{9,8},{10,11... | collective-permute-start | bytes 1572872 | tf_op jit(solution)/shard_map/ppermute | solution.py:35
  40.5 13.1 %collective-permute-start.8 = (bf16[272,1792]{1,0:T(8,128)(2,1)}, bf16[272,1792]{1,0:T(8,128)(2,1)}, u32[]{:S(2)}, u32[]{:S(2)}) collective-permute-start(bf16[272,1792]{1,0:T(8,128)(2,1)} %pad_maximum_fusion.14), channel_id=1, source_target_pairs={{0,2},{2,0},{4,6},{6,4},{8,10},{10,8},{12,14},{14,12},{16,18},{18,... | collective-permute-start | bytes 2924552 | tf_op jit(solution)/shard_map/ppermute | solution.py:27
  46.7 10.6 %collective-permute-start.5 = (bf16[512,1024]{1,0:T(8,128)(2,1)}, bf16[512,1024]{1,0:T(8,128)(2,1)S(1)}, u32[]{:S(2)}, u32[]{:S(2)}) collective-permute-start(bf16[512,1024]{1,0:T(8,128)(2,1)} %copy-done.20), channel_id=1, source_target_pairs={{0,2},{2,0},{4,6},{6,4},{8,10},{10,8},{12,14},{14,12},{16,18},{18,... | collective-permute-start | bytes 3145736 | tf_op jit(solution)/shard_map/ppermute | solution.py:27
  48.5 7.8 %collective-permute-start.6 = (bf16[512,256]{0,1:T(8,128)(2,1)S(1)}, bf16[512,256]{0,1:T(8,128)(2,1)S(1)}, u32[]{:S(2)}, u32[]{:S(2)}) collective-permute-start(bf16[512,256]{0,1:T(8,128)(2,1)S(1)} %get-tuple-element.184), channel_id=1, source_target_pairs={{0,2},{2,0},{4,6},{6,4},{8,10},{10,8},{12,14},{14,12},{16,18},{18,... | collective-permute-start | bytes 786440 | tf_op jit(solution)/shard_map/ppermute | solution.py:27
  50.1 7.1 %collective-permute-start.7 = (bf16[512,512]{1,0:T(8,128)(2,1)S(1)}, bf16[512,512]{1,0:T(8,128)(2,1)S(1)}, u32[]{:S(2)}, u32[]{:S(2)}) collective-permute-start(bf16[512,512]{1,0:T(8,128)(2,1)S(1)} %pad_maximum_fusion.18), channel_id=1, source_target_pairs={{0,2},{2,0},{4,6},{6,4},{8,10},{10,8},{12,14},{14,12},{16,18},{18,... | collective-permute-start | bytes 1572872 | tf_op jit(solution)/shard_map/ppermute | solution.py:27
  52.3 46.6 %copy-start.2 = (f32[256,1024]{1,0:T(8,128)}, f32[256,1024]{1,0:T(8,128)S(1)}, u32[]{:S(2)}) copy-start(f32[256,1024]{1,0:T(8,128)S(1)} %get-tuple-element.197) | copy-start | bytes 3145732
  52.5 14.0 %collective-permute-start.4 = (bf16[256,1024]{1,0:T(8,128)(2,1)S(1)}, bf16[256,1024]{1,0:T(8,128)(2,1)S(1)}, u32[]{:S(2)}, u32[]{:S(2)}) collective-permute-start(bf16[256,1024]{1,0:T(8,128)(2,1)S(1)} %multiply_convert_fusion.3), channel_id=1, source_target_pairs={{0,1},{1,0},{2,3},{3,2},{4,5},{5,4},{6,7},{7,6},{8,9},{9,8},{10,11... | collective-permute-start | bytes 1572872 | tf_op jit(solution)/shard_map/ppermute | solution.py:35
  66.6 18.1 %collective-permute-start.9 = (bf16[512,1024]{1,0:T(8,128)(2,1)S(1)}, bf16[512,1024]{1,0:T(8,128)(2,1)S(1)}, u32[]{:S(2)}, u32[]{:S(2)}) collective-permute-start(bf16[512,1024]{1,0:T(8,128)(2,1)S(1)} %pad_maximum_fusion.10), channel_id=1, source_target_pairs={{0,2},{2,0},{4,6},{6,4},{8,10},{10,8},{12,14},{14,12},{16,18},{18,... | collective-permute-start | bytes 3145736 | tf_op jit(solution)/shard_map/ppermute | solution.py:27
  76.5 4.2 %collective-permute-start.12 = (bf16[512,1408]{1,0:T(8,128)(2,1)S(1)}, bf16[512,1408]{1,0:T(8,128)(2,1)S(1)}, u32[]{:S(2)}, u32[]{:S(2)}) collective-permute-start(bf16[512,1408]{1,0:T(8,128)(2,1)S(1)} %multiply_convert_fusion.1), channel_id=1, source_target_pairs={{0,2},{2,0},{4,6},{6,4},{8,10},{10,8},{12,14},{14,12},{16,18},{18,... | collective-permute-start | bytes 4325384 | tf_op jit(solution)/shard_map/ppermute | solution.py:27
  77.2 7.5 %collective-permute-start.10 = (bf16[512,1408]{1,0:T(8,128)(2,1)S(1)}, bf16[512,1408]{1,0:T(8,128)(2,1)S(1)}, u32[]{:S(2)}, u32[]{:S(2)}) collective-permute-start(bf16[512,1408]{1,0:T(8,128)(2,1)S(1)} %broadcast_select_fusion), channel_id=1, source_target_pairs={{0,2},{2,0},{4,6},{6,4},{8,10},{10,8},{12,14},{14,12},{16,18},{18,... | collective-permute-start | bytes 4325384 | tf_op jit(solution)/shard_map/ppermute | solution.py:27
  82.6 15.8 %collective-permute-start.13 = (bf16[4,64,1408]{2,1,0:T(8,128)(2,1)S(1)}, bf16[4,64,1408]{2,1,0:T(8,128)(2,1)S(1)}, u32[]{:S(2)}, u32[]{:S(2)}) collective-permute-start(bf16[4,64,1408]{2,1,0:T(8,128)(2,1)S(1)} %constant_dynamic-slice_fusion.9), channel_id=1, source_target_pairs={{0,4},{2,10},{4,0},{6,14},{8,12},{10,2},{12,8},{14,6},{16,20},{18,... | collective-permute-start | bytes 2162696 | tf_op jit(solution)/shard_map/ppermute | solution.py:27
  84.3 14.2 %collective-permute-start.14 = (bf16[256,1024]{1,0:T(8,128)(2,1)S(1)}, bf16[256,1024]{1,0:T(8,128)(2,1)S(1)}, u32[]{:S(2)}, u32[]{:S(2)}) collective-permute-start(bf16[256,1024]{1,0:T(8,128)(2,1)S(1)} %fusion.34), channel_id=1, source_target_pairs={{0,1},{1,0},{2,3},{3,2},{4,5},{5,4},{6,7},{7,6},{8,9},{9,8},{10,11... | collective-permute-start | bytes 1572872 | tf_op jit(solution)/shard_map/ppermute | solution.py:35
  87.7 27.8 %collective-permute-start.11 = (bf16[4,128,1408]{2,1,0:T(8,128)(2,1)}, bf16[4,128,1408]{2,1,0:T(8,128)(2,1)}, u32[]{:S(2)}, u32[]{:S(2)}) collective-permute-start(bf16[4,128,1408]{2,1,0:T(8,128)(2,1)} %bitcast.10), channel_id=1, source_target_pairs={{0,4},{2,10},{4,0},{6,14},{8,12},{10,2},{12,8},{14,6},{16,20},{18,... | collective-permute-start | bytes 4325384 | tf_op jit(solution)/shard_map/ppermute | solution.py:27
  100.5 13.7 %collective-permute-start.16 = (bf16[256,1024]{1,0:T(8,128)(2,1)}, bf16[256,1024]{1,0:T(8,128)(2,1)}, u32[]{:S(2)}, u32[]{:S(2)}) collective-permute-start(bf16[256,1024]{1,0:T(8,128)(2,1)} %get-tuple-element.160), channel_id=1, source_target_pairs={{0,1},{1,0},{2,3},{3,2},{4,5},{5,4},{6,7},{7,6},{8,9},{9,8},{10,11... | collective-permute-start | bytes 1572872 | tf_op jit(solution)/shard_map/ppermute | solution.py:35
  102.1 13.4 %collective-permute-start.15 = (bf16[2,64,1408]{2,1,0:T(8,128)(2,1)S(1)}, bf16[2,64,1408]{2,1,0:T(8,128)(2,1)S(1)}, u32[]{:S(2)}, u32[]{:S(2)}) collective-permute-start(bf16[2,64,1408]{2,1,0:T(8,128)(2,1)S(1)} %add_convert_fusion.5), channel_id=1, source_target_pairs={{0,8},{2,6},{4,12},{6,2},{8,0},{10,14},{12,4},{14,10},{16,24},{18,... | collective-permute-start | bytes 1081352 | tf_op jit(solution)/shard_map/ppermute | solution.py:27
  116.3 30.2 %collective-permute-start.21 = (bf16[512,1024]{1,0:T(8,128)(2,1)S(1)}, bf16[512,1024]{1,0:T(8,128)(2,1)S(1)}, u32[]{:S(2)}, u32[]{:S(2)}) collective-permute-start(bf16[512,1024]{1,0:T(8,128)(2,1)S(1)} %pad_maximum_fusion.12), channel_id=1, source_target_pairs={{0,2},{2,0},{4,6},{6,4},{8,10},{10,8},{12,14},{14,12},{16,18},{18,... | collective-permute-start | bytes 3145736 | tf_op jit(solution)/shard_map/ppermute | solution.py:27
  118.0 12.9 %collective-permute-start.18 = (bf16[1,64,1408]{2,1,0:T(8,128)(2,1)S(1)}, bf16[1,64,1408]{2,1,0:T(8,128)(2,1)S(1)}, u32[]{:S(2)}, u32[]{:S(2)}) collective-permute-start(bf16[1,64,1408]{2,1,0:T(8,128)(2,1)S(1)} %add_convert_fusion.10), channel_id=1, source_target_pairs={{0,24},{2,26},{4,28},{6,30},{8,16},{10,18},{12,20},{14,22},{16,8},... | collective-permute-start | bytes 540680 | tf_op jit(solution)/shard_map/ppermute | solution.py:27
  120.7 13.3 %collective-permute-start.17 = (bf16[2,128,1408]{2,1,0:T(8,128)(2,1)S(1)}, bf16[2,128,1408]{2,1,0:T(8,128)(2,1)S(1)}, u32[]{:S(2)}, u32[]{:S(2)}) collective-permute-start(bf16[2,128,1408]{2,1,0:T(8,128)(2,1)S(1)} %add_convert_fusion), channel_id=1, source_target_pairs={{0,8},{2,6},{4,12},{6,2},{8,0},{10,14},{12,4},{14,10},{16,24},{18,... | collective-permute-start | bytes 2162696 | tf_op jit(solution)/shard_map/ppermute | solution.py:27
  141.8 9.9 %collective-permute-start.19 = (bf16[1,128,1408]{2,1,0:T(8,128)(2,1)S(1)}, bf16[1,128,1408]{2,1,0:T(8,128)(2,1)S(1)}, u32[]{:S(2)}, u32[]{:S(2)}) collective-permute-start(bf16[1,128,1408]{2,1,0:T(8,128)(2,1)S(1)} %add_convert_fusion.4), channel_id=1, source_target_pairs={{0,24},{2,26},{4,28},{6,30},{8,16},{10,18},{12,20},{14,22},{16,8},... | collective-permute-start | bytes 1081352 | tf_op jit(solution)/shard_map/ppermute | solution.py:27
  143.5 3.7 %collective-permute-start.20 = (bf16[512,768]{0,1:T(8,128)(2,1)S(1)}, bf16[512,768]{0,1:T(8,128)(2,1)S(1)}, u32[]{:S(2)}, u32[]{:S(2)}) collective-permute-start(bf16[512,768]{0,1:T(8,128)(2,1)S(1)} %pad_maximum_fusion.15), channel_id=1, source_target_pairs={{0,2},{2,0},{4,6},{6,4},{8,10},{10,8},{12,14},{14,12},{16,18},{18,... | collective-permute-start | bytes 2359304 | tf_op jit(solution)/shard_map/ppermute | solution.py:27
  144.6 14.4 %collective-permute-start.25 = (bf16[256,1024]{1,0:T(8,128)(2,1)S(1)}, bf16[256,1024]{1,0:T(8,128)(2,1)S(1)}, u32[]{:S(2)}, u32[]{:S(2)}) collective-permute-start(bf16[256,1024]{1,0:T(8,128)(2,1)S(1)} %fusion.41), channel_id=1, source_target_pairs={{0,1},{1,0},{2,3},{3,2},{4,5},{5,4},{6,7},{7,6},{8,9},{9,8},{10,11... | collective-permute-start | bytes 1572872 | tf_op jit(solution)/shard_map/ppermute | solution.py:35
  161.5 2.4 collective-permute-start.26
  161.5 28.5 %collective-permute-start.23 = (bf16[4,128,1024]{2,1,0:T(8,128)(2,1)}, bf16[4,128,1024]{2,1,0:T(8,128)(2,1)S(1)}, u32[]{:S(2)}, u32[]{:S(2)}) collective-permute-start(bf16[4,128,1024]{2,1,0:T(8,128)(2,1)} %constant_dynamic-slice_fusion.2), channel_id=1, source_target_pairs={{0,4},{2,10},{4,0},{6,14},{8,12},{10,2},{12,8},{14,6},{16,20},{18,... | collective-permute-start | bytes 3145736 | tf_op jit(solution)/shard_map/ppermute | solution.py:27
  167.2 53.1 %copy-start.34 = (bf16[1792,512]{1,0:T(8,128)(2,1)}, bf16[1792,512]{1,0:T(8,128)(2,1)S(1)}, u32[]{:S(2)}) copy-start(bf16[1792,512]{1,0:T(8,128)(2,1)S(1)} %convolution_convert_fusion) | copy-start | bytes 5505028
  167.2 22.8 %copy-start.10 = (bf16[1024,1024]{1,0:T(8,128)(2,1)S(1)}, bf16[1024,1024]{1,0:T(8,128)(2,1)}, u32[]{:S(2)}) copy-start(bf16[1024,1024]{1,0:T(8,128)(2,1)} %copy-done.9) | copy-start | bytes 6291460
  167.6 13.5 %collective-permute-start.27 = (bf16[4,224,256]{2,1,0:T(8,128)(2,1)S(1)}, bf16[4,224,256]{2,1,0:T(8,128)(2,1)S(1)}, u32[]{:S(2)}, u32[]{:S(2)}) collective-permute-start(bf16[4,224,256]{2,1,0:T(8,128)(2,1)S(1)} %get-tuple-element.166), channel_id=1, source_target_pairs={{0,1},{1,0},{2,3},{3,2},{4,5},{5,4},{6,7},{7,6},{8,9},{9,8},{10,11... | collective-permute-start | bytes 1376264 | tf_op jit(solution)/shard_map/ppermute | solution.py:35
  169.6 28.0 %copy-start.36 = (bf16[512,1408]{1,0:T(8,128)(2,1)S(1)}, bf16[512,1408]{1,0:T(8,128)(2,1)}, u32[]{:S(2)}) copy-start(bf16[512,1408]{1,0:T(8,128)(2,1)} %copy-done.35) | copy-start | bytes 4325380
  169.7 28.0 %copy-start.56 = (bf16[1408,1024]{1,0:T(8,128)(2,1)S(1)}, bf16[1408,1024]{1,0:T(8,128)(2,1)}, u32[]{:S(2)}) copy-start(bf16[1408,1024]{1,0:T(8,128)(2,1)} %param.22) | copy-start | bytes 8650756
  169.7 13.6 %collective-permute-start.24 = (bf16[1,64,1408]{2,1,0:T(8,128)(2,1)S(1)}, bf16[1,64,1408]{2,1,0:T(8,128)(2,1)S(1)}, u32[]{:S(2)}, u32[]{:S(2)}) collective-permute-start(bf16[1,64,1408]{2,1,0:T(8,128)(2,1)S(1)} %add_convert_fusion.9), channel_id=1, source_target_pairs={{0,24},{2,26},{4,28},{6,30},{8,16},{10,18},{12,20},{14,22},{16,8},... | collective-permute-start | bytes 540680 | tf_op jit(solution)/shard_map/ppermute | solution.py:27
  171.6 18.7 %collective-permute-start.22 = (bf16[1,128,1408]{2,1,0:T(8,128)(2,1)S(1)}, bf16[1,128,1408]{2,1,0:T(8,128)(2,1)S(1)}, u32[]{:S(2)}, u32[]{:S(2)}) collective-permute-start(bf16[1,128,1408]{2,1,0:T(8,128)(2,1)S(1)} %copy-done.38), channel_id=1, source_target_pairs={{0,24},{2,26},{4,28},{6,30},{8,16},{10,18},{12,20},{14,22},{16,8},... | collective-permute-start | bytes 1081352 | tf_op jit(solution)/shard_map/ppermute | solution.py:27
  174.4 28.7 %collective-permute-start.31 = (bf16[4,224,256]{2,1,0:T(8,128)(2,1)S(1)}, bf16[4,224,256]{2,1,0:T(8,128)(2,1)S(1)}, u32[]{:S(2)}, u32[]{:S(2)}) collective-permute-start(bf16[4,224,256]{2,1,0:T(8,128)(2,1)S(1)} %get-tuple-element.165), channel_id=1, source_target_pairs={{0,1},{1,0},{2,3},{3,2},{4,5},{5,4},{6,7},{7,6},{8,9},{9,8},{10,11... | collective-permute-start | bytes 1376264 | tf_op jit(solution)/shard_map/ppermute | solution.py:35
  181.4 20.7 %collective-permute-start.32 = (bf16[4,224,256]{2,1,0:T(8,128)(2,1)S(1)}, bf16[4,224,256]{2,1,0:T(8,128)(2,1)S(1)}, u32[]{:S(2)}, u32[]{:S(2)}) collective-permute-start(bf16[4,224,256]{2,1,0:T(8,128)(2,1)S(1)} %add_convert_fusion.2), channel_id=1, source_target_pairs={{0,4},{2,10},{4,0},{6,14},{8,12},{10,2},{12,8},{14,6},{16,20},{18,... | collective-permute-start | bytes 1376264 | tf_op jit(solution)/shard_map/ppermute | solution.py:27
  183.3 20.0 %collective-permute-start.30 = (bf16[2,64,1408]{2,1,0:T(8,128)(2,1)S(1)}, bf16[2,64,1408]{2,1,0:T(8,128)(2,1)S(1)}, u32[]{:S(2)}, u32[]{:S(2)}) collective-permute-start(bf16[2,64,1408]{2,1,0:T(8,128)(2,1)S(1)} %pad_maximum_fusion.21), channel_id=1, source_target_pairs={{0,8},{2,6},{4,12},{6,2},{8,0},{10,14},{12,4},{14,10},{16,24},{18,... | collective-permute-start | bytes 1081352 | tf_op jit(solution)/shard_map/ppermute | solution.py:27
  190.2 14.1 %collective-permute-start.29 = (bf16[2,128,1024]{2,1,0:T(8,128)(2,1)S(1)}, bf16[2,128,1024]{2,1,0:T(8,128)(2,1)S(1)}, u32[]{:S(2)}, u32[]{:S(2)}) collective-permute-start(bf16[2,128,1024]{2,1,0:T(8,128)(2,1)S(1)} %add_convert_fusion.1), channel_id=1, source_target_pairs={{0,8},{2,6},{4,12},{6,2},{8,0},{10,14},{12,4},{14,10},{16,24},{18,... | collective-permute-start | bytes 1572872 | tf_op jit(solution)/shard_map/ppermute | solution.py:27
  191.1 22.3 %collective-permute-start.35 = (bf16[2,128,1408]{2,1,0:T(8,128)(2,1)S(1)}, bf16[2,128,1408]{2,1,0:T(8,128)(2,1)S(1)}, u32[]{:S(2)}, u32[]{:S(2)}) collective-permute-start(bf16[2,128,1408]{2,1,0:T(8,128)(2,1)S(1)} %get-tuple-element.186), channel_id=1, source_target_pairs={{0,8},{2,6},{4,12},{6,2},{8,0},{10,14},{12,4},{14,10},{16,24},{18,... | collective-permute-start | bytes 2162696 | tf_op jit(solution)/shard_map/ppermute | solution.py:27
  202.1 16.3 %collective-permute-start.28 = (bf16[256,1024]{1,0:T(8,128)(2,1)S(1)}, bf16[256,1024]{1,0:T(8,128)(2,1)S(1)}, u32[]{:S(2)}, u32[]{:S(2)}) collective-permute-start(bf16[256,1024]{1,0:T(8,128)(2,1)S(1)} %slice.114), channel_id=1, source_target_pairs={{0,1},{1,0},{2,3},{3,2},{4,5},{5,4},{6,7},{7,6},{8,9},{9,8},{10,11... | collective-permute-start | bytes 1572872 | tf_op jit(solution)/shard_map/ppermute | solution.py:35
  203.3 17.1 %collective-permute-start.34 = (bf16[2,224,256]{2,1,0:T(8,128)(2,1)S(1)}, bf16[2,224,256]{2,1,0:T(8,128)(2,1)S(1)}, u32[]{:S(2)}, u32[]{:S(2)}) collective-permute-start(bf16[2,224,256]{2,1,0:T(8,128)(2,1)S(1)} %add_convert_fusion.8), channel_id=1, source_target_pairs={{0,8},{2,6},{4,12},{6,2},{8,0},{10,14},{12,4},{14,10},{16,24},{18,... | collective-permute-start | bytes 688136 | tf_op jit(solution)/shard_map/ppermute | solution.py:27
  204.3 27.9 %collective-permute-start.38 = (bf16[4,64,1408]{2,1,0:T(8,128)(2,1)}, bf16[4,64,1408]{2,1,0:T(8,128)(2,1)}, u32[]{:S(2)}, u32[]{:S(2)}) collective-permute-start(bf16[4,64,1408]{2,1,0:T(8,128)(2,1)} %pad_maximum_fusion.16.refs_0_), channel_id=1, source_target_pairs={{0,2},{2,0},{4,6},{6,4},{8,10},{10,8},{12,14},{14,12},{16,18},{18,... | collective-permute-start | bytes 2162696 | tf_op jit(solution)/shard_map/ppermute | solution.py:27
  204.3 22.3 %collective-permute-start.37 = (bf16[4,64,1408]{2,1,0:T(8,128)(2,1)}, bf16[4,64,1408]{2,1,0:T(8,128)(2,1)}, u32[]{:S(2)}, u32[]{:S(2)}) collective-permute-start(bf16[4,64,1408]{2,1,0:T(8,128)(2,1)} %pad_maximum_fusion.16.refs_0_), channel_id=1, source_target_pairs={{0,4},{2,10},{4,0},{6,14},{8,12},{10,2},{12,8},{14,6},{16,20},{18,... | collective-permute-start | bytes 2162696 | tf_op jit(solution)/shard_map/ppermute | solution.py:27
  213.4 11.4 %collective-permute-start.33 = (bf16[1,128,1024]{2,1,0:T(8,128)(2,1)S(1)}, bf16[1,128,1024]{2,1,0:T(8,128)(2,1)S(1)}, u32[]{:S(2)}, u32[]{:S(2)}) collective-permute-start(bf16[1,128,1024]{2,1,0:T(8,128)(2,1)S(1)} %add_convert_fusion.7), channel_id=1, source_target_pairs={{0,24},{2,26},{4,28},{6,30},{8,16},{10,18},{12,20},{14,22},{16,8},... | collective-permute-start | bytes 786440 | tf_op jit(solution)/shard_map/ppermute | solution.py:27
  218.4 24.9 %collective-permute-start.41 = (bf16[4,128,1408]{2,1,0:T(8,128)(2,1)}, bf16[4,128,1408]{2,1,0:T(8,128)(2,1)}, u32[]{:S(2)}, u32[]{:S(2)}) collective-permute-start(bf16[4,128,1408]{2,1,0:T(8,128)(2,1)} %constant_dynamic-update-slice_fusion.4.refs_0_), channel_id=1, source_target_pairs={{0,4},{2,10},{4,0},{6,14},{8,12},{10,2},{12,8},{14,6},{16,20},{18,... | collective-permute-start | bytes 4325384 | tf_op jit(solution)/shard_map/ppermute | solution.py:27
  226.6 5.7 %collective-permute-start.39 = (bf16[4,64,1408]{2,1,0:T(8,128)(2,1)}, bf16[4,64,1408]{2,1,0:T(8,128)(2,1)}, u32[]{:S(2)}, u32[]{:S(2)}) collective-permute-start(bf16[4,64,1408]{2,1,0:T(8,128)(2,1)} %collective-permute-done.37.refs_1_), channel_id=1, source_target_pairs={{0,2},{2,0},{4,6},{6,4},{8,10},{10,8},{12,14},{14,12},{16,18},{18,... | collective-permute-start | bytes 2162696 | tf_op jit(solution)/shard_map/ppermute | solution.py:27
  228.3 9.8 %collective-permute-start.36 = (bf16[1,224,256]{2,1,0:T(8,128)(2,1)S(1)}, bf16[1,224,256]{2,1,0:T(8,128)(2,1)}, u32[]{:S(2)}, u32[]{:S(2)}) collective-permute-start(bf16[1,224,256]{2,1,0:T(8,128)(2,1)S(1)} %add_convert_fusion.12), channel_id=1, source_target_pairs={{0,24},{2,26},{4,28},{6,30},{8,16},{10,18},{12,20},{14,22},{16,8},... | collective-permute-start | bytes 344072 | tf_op jit(solution)/shard_map/ppermute | solution.py:27
  230.9 11.4 %collective-permute-start.42 = (bf16[1,128,1024]{2,1,0:T(8,128)(2,1)}, bf16[1,128,1024]{2,1,0:T(8,128)(2,1)}, u32[]{:S(2)}, u32[]{:S(2)}) collective-permute-start(bf16[1,128,1024]{2,1,0:T(8,128)(2,1)} %add_convert_fusion.6), channel_id=1, source_target_pairs={{0,24},{2,26},{4,28},{6,30},{8,16},{10,18},{12,20},{14,22},{16,8},... | collective-permute-start | bytes 786440 | tf_op jit(solution)/shard_map/ppermute | solution.py:27
  232.2 21.5 %collective-permute-start.43 = (bf16[4,128,1408]{2,1,0:T(8,128)(2,1)}, bf16[4,128,1408]{2,1,0:T(8,128)(2,1)S(1)}, u32[]{:S(2)}, u32[]{:S(2)}) collective-permute-start(bf16[4,128,1408]{2,1,0:T(8,128)(2,1)} %constant_dynamic-update-slice_fusion.4.refs_0_), channel_id=1, source_target_pairs={{0,2},{2,0},{4,6},{6,4},{8,10},{10,8},{12,14},{14,12},{16,18},{18,... | collective-permute-start | bytes 4325384 | tf_op jit(solution)/shard_map/ppermute | solution.py:27
  243.3 10.8 %collective-permute-start.44 = (bf16[4,128,1408]{2,1,0:T(8,128)(2,1)}, bf16[4,128,1408]{2,1,0:T(8,128)(2,1)S(1)}, u32[]{:S(2)}, u32[]{:S(2)}) collective-permute-start(bf16[4,128,1408]{2,1,0:T(8,128)(2,1)} %collective-permute-done.41.refs_1_), channel_id=1, source_target_pairs={{0,2},{2,0},{4,6},{6,4},{8,10},{10,8},{12,14},{14,12},{16,18},{18,... | collective-permute-start | bytes 4325384 | tf_op jit(solution)/shard_map/ppermute | solution.py:27
  251.0 12.4 %collective-permute-start.47 = (bf16[2,128,1024]{2,1,0:T(8,128)(2,1)S(1)}, bf16[2,128,1024]{2,1,0:T(8,128)(2,1)S(1)}, u32[]{:S(2)}, u32[]{:S(2)}) collective-permute-start(bf16[2,128,1024]{2,1,0:T(8,128)(2,1)S(1)} %pad_maximum_fusion.19), channel_id=1, source_target_pairs={{0,8},{2,6},{4,12},{6,2},{8,0},{10,14},{12,4},{14,10},{16,24},{18,... | collective-permute-start | bytes 1572872 | tf_op jit(solution)/shard_map/ppermute | solution.py:27
  251.0 12.3 %collective-permute-start.40 = (bf16[1,224,256]{2,1,0:T(8,128)(2,1)S(1)}, bf16[1,224,256]{2,1,0:T(8,128)(2,1)S(1)}, u32[]{:S(2)}, u32[]{:S(2)}) collective-permute-start(bf16[1,224,256]{2,1,0:T(8,128)(2,1)S(1)} %add_convert_fusion.11), channel_id=1, source_target_pairs={{0,24},{2,26},{4,28},{6,30},{8,16},{10,18},{12,20},{14,22},{16,8},... | collective-permute-start | bytes 344072 | tf_op jit(solution)/shard_map/ppermute | solution.py:27
  264.5 16.1 %collective-permute-start.50 = (bf16[4,128,1024]{2,1,0:T(8,128)(2,1)S(1)}, bf16[4,128,1024]{2,1,0:T(8,128)(2,1)S(1)}, u32[]{:S(2)}, u32[]{:S(2)}) collective-permute-start(bf16[4,128,1024]{2,1,0:T(8,128)(2,1)S(1)} %pad_maximum_fusion.13.refs_0_), channel_id=1, source_target_pairs={{0,4},{2,10},{4,0},{6,14},{8,12},{10,2},{12,8},{14,6},{16,20},{18,... | collective-permute-start | bytes 3145736 | tf_op jit(solution)/shard_map/ppermute | solution.py:27
  266.3 6.0 %collective-permute-start.46 = (bf16[2,224,256]{2,1,0:T(8,128)(2,1)S(1)}, bf16[2,224,256]{2,1,0:T(8,128)(2,1)S(1)}, u32[]{:S(2)}, u32[]{:S(2)}) collective-permute-start(bf16[2,224,256]{2,1,0:T(8,128)(2,1)S(1)} %pad_maximum_fusion.22), channel_id=1, source_target_pairs={{0,1},{1,0},{2,3},{3,2},{4,5},{5,4},{6,7},{7,6},{8,9},{9,8},{10,11... | collective-permute-start | bytes 688136 | tf_op jit(solution)/shard_map/ppermute | solution.py:35
  266.8 8.5 %collective-permute-start.45 = (bf16[2,224,256]{2,1,0:T(8,128)(2,1)S(1)}, bf16[2,224,256]{2,1,0:T(8,128)(2,1)S(1)}, u32[]{:S(2)}, u32[]{:S(2)}) collective-permute-start(bf16[2,224,256]{2,1,0:T(8,128)(2,1)S(1)} %pad_maximum_fusion.22), channel_id=1, source_target_pairs={{0,8},{2,6},{4,12},{6,2},{8,0},{10,14},{12,4},{14,10},{16,24},{18,... | collective-permute-start | bytes 688136 | tf_op jit(solution)/shard_map/ppermute | solution.py:27
  266.8 24.3 %collective-permute-start.49 = (bf16[4,128,1024]{2,1,0:T(8,128)(2,1)S(1)}, bf16[4,128,1024]{2,1,0:T(8,128)(2,1)S(1)}, u32[]{:S(2)}, u32[]{:S(2)}) collective-permute-start(bf16[4,128,1024]{2,1,0:T(8,128)(2,1)S(1)} %pad_maximum_fusion.13.refs_0_), channel_id=1, source_target_pairs={{0,2},{2,0},{4,6},{6,4},{8,10},{10,8},{12,14},{14,12},{16,18},{18,... | collective-permute-start | bytes 3145736 | tf_op jit(solution)/shard_map/ppermute | solution.py:27
  280.6 10.5 %collective-permute-start.51 = (bf16[4,128,1024]{2,1,0:T(8,128)(2,1)S(1)}, bf16[4,128,1024]{2,1,0:T(8,128)(2,1)S(1)}, u32[]{:S(2)}, u32[]{:S(2)}) collective-permute-start(bf16[4,128,1024]{2,1,0:T(8,128)(2,1)S(1)} %collective-permute-done.50.refs_1_), channel_id=1, source_target_pairs={{0,2},{2,0},{4,6},{6,4},{8,10},{10,8},{12,14},{14,12},{16,18},{18,... | collective-permute-start | bytes 3145736 | tf_op jit(solution)/shard_map/ppermute | solution.py:27
  280.6 8.5 %collective-permute-start.48 = (bf16[4,224,256]{2,1,0:T(8,128)(2,1)S(1)}, bf16[4,224,256]{2,1,0:T(8,128)(2,1)S(1)}, u32[]{:S(2)}, u32[]{:S(2)}) collective-permute-start(bf16[4,224,256]{2,1,0:T(8,128)(2,1)S(1)} %pad_maximum_fusion.20.refs_0_), channel_id=1, source_target_pairs={{0,4},{2,10},{4,0},{6,14},{8,12},{10,2},{12,8},{14,6},{16,20},{18,... | collective-permute-start | bytes 1376264 | tf_op jit(solution)/shard_map/ppermute | solution.py:27
  281.8 8.8 %collective-permute-start.52 = (bf16[2,224,256]{2,1,0:T(8,128)(2,1)S(1)}, bf16[2,224,256]{2,1,0:T(8,128)(2,1)S(1)}, u32[]{:S(2)}, u32[]{:S(2)}) collective-permute-start(bf16[2,224,256]{2,1,0:T(8,128)(2,1)S(1)} %collective-permute-done.45), channel_id=1, source_target_pairs={{0,1},{1,0},{2,3},{3,2},{4,5},{5,4},{6,7},{7,6},{8,9},{9,8},{10,11... | collective-permute-start | bytes 688136 | tf_op jit(solution)/shard_map/ppermute | solution.py:35
  289.1 12.1 %collective-permute-start.53 = (bf16[4,224,256]{2,1,0:T(8,128)(2,1)S(1)}, bf16[4,224,256]{2,1,0:T(8,128)(2,1)S(1)}, u32[]{:S(2)}, u32[]{:S(2)}) collective-permute-start(bf16[4,224,256]{2,1,0:T(8,128)(2,1)S(1)} %collective-permute-done.48.refs_1_), channel_id=1, source_target_pairs={{0,1},{1,0},{2,3},{3,2},{4,5},{5,4},{6,7},{7,6},{8,9},{9,8},{10,11... | collective-permute-start | bytes 1376264 | tf_op jit(solution)/shard_map/ppermute | solution.py:35
  290.6 10.5 %collective-permute-start.54 = (bf16[4,224,256]{2,1,0:T(8,128)(2,1)S(1)}, bf16[4,224,256]{2,1,0:T(8,128)(2,1)S(1)}, u32[]{:S(2)}, u32[]{:S(2)}) collective-permute-start(bf16[4,224,256]{2,1,0:T(8,128)(2,1)S(1)} %pad_maximum_fusion.20.refs_0_), channel_id=1, source_target_pairs={{0,2},{2,0},{4,6},{6,4},{8,10},{10,8},{12,14},{14,12},{16,18},{18,... | collective-permute-start | bytes 1376264 | tf_op jit(solution)/shard_map/ppermute | solution.py:27
  290.6 10.5 %collective-permute-start.55 = (bf16[4,224,256]{2,1,0:T(8,128)(2,1)S(1)}, bf16[4,224,256]{2,1,0:T(8,128)(2,1)S(1)}, u32[]{:S(2)}, u32[]{:S(2)}) collective-permute-start(bf16[4,224,256]{2,1,0:T(8,128)(2,1)S(1)} %collective-permute-done.48.refs_1_), channel_id=1, source_target_pairs={{0,2},{2,0},{4,6},{6,4},{8,10},{10,8},{12,14},{14,12},{16,18},{18,... | collective-permute-start | bytes 1376264 | tf_op jit(solution)/shard_map/ppermute | solution.py:27
  291.2 10.0 %collective-permute-start.56 = (bf16[4,224,256]{2,1,0:T(8,128)(2,1)S(1)}, bf16[4,224,256]{2,1,0:T(8,128)(2,1)S(1)}, u32[]{:S(2)}, u32[]{:S(2)}) collective-permute-start(bf16[4,224,256]{2,1,0:T(8,128)(2,1)S(1)} %constant_dynamic-update-slice_fusion.7.refs_2_), channel_id=1, source_target_pairs={{0,2},{2,0},{4,6},{6,4},{8,10},{10,8},{12,14},{14,12},{16,18},{18,... | collective-permute-start | bytes 1376264 | tf_op jit(solution)/shard_map/ppermute | solution.py:27
  301.1 1.8 collective-permute-start.57
  (55 other events, 377.4 us)

commit v5 on v4

--- a/solution.py
+++ b/solution.py
@@ -687,8 +687,10 @@
     sent = advance(attn, sent)
     sent = advance(gate, sent)
     hidden, grad_lift_b = lax.optimization_barrier((sent, hidden, grad_lift_b))[1:]
-    layer_out = jnp.dot(hidden, w_down, preferred_element_type=jnp.float32).astype(jnp.bfloat16)
-    layer_out = scatter_group(layer_out)
+    layer_out, own = to_owners(
+        lambda part: jnp.dot(part, w_down, preferred_element_type=jnp.float32), hidden
+    )
+    layer_out = own + layer_out.astype(jnp.float32)
     grad_features = contract(grad_lift_b, w_proj, 1, 1)
     sent = advance(proj, grad_features)
     while down.done < 2 * count:

time: 314 us -> 314 us (level)
  no operation moved by 1% of the time
where the time goes in v5:
time: 314 us; the launch traced here: 308 us
  waiting for transfers between devices  100 us (32%)
  starting transfers between devices  72.5 us (23%)
  matrix products  54.4 us (17%)
  other arithmetic  36 us (11%)
  Pallas kernels  23.4 us (7%)
  local copies, waits for them, and re-layouts  19.7 us (6%)
    ppermute x14, waiting for transfers between devices, peer_swap(): return lax.ppermute(value, 'heads', [(0, 1), (1, 0)])  62.8 us
    ppermute x44, starting transfers between devices, swap_rows(): lax.ppermute(value, 'rows', [(r, r ^ masks[r % 2]) for r in range(count)])  56.9 us
    ppermute x44, waiting for transfers between devices, swap_rows(): lax.ppermute(value, 'rows', [(r, r ^ masks[r % 2]) for r in range(count)])  37.2 us
    dot_general x17, matrix products, contract(): lax.dot_general(left, right, (((left_dim,), (right_dim,)), ((), ())), pre...  27.5 us
    pallas_call x3, Pallas kernels, place_blocks(): pl.pallas_call(body, grid_spec=pltpu.PrefetchScalarGridSpec(num_scalar_pr...  19.1 us
    ppermute x14, starting transfers between devices, peer_swap(): return lax.ppermute(value, 'heads', [(0, 1), (1, 0)])  15.6 us
    unnamed x127, local copies, waits for them, and re-layouts  13.7 us
    convert_element_type x12, other arithmetic, part(): return total.astype(jnp.bfloat16)  12 us
  transfers between devices with their start and end apart: 58, of which 20 were waited for; matrix products, arithmetic and copies ran while one was open for 31% of the time, Pallas kernels for 6%

profile of v5, /device:TPU:0, one launch (start us, length us, event | category | flops | bytes accessed | tf_op | source)
XLA Modules:
  0.0 308.1 jit_solution(16635509534212577370)
XLA Ops:
  1.5 2.9 collective-permute-start.1
  4.5 2.4 multiply_reduce_fusion.6
  8.7 11.7 %collective-permute-done = bf16[256,1024]{1,0:T(8,128)(2,1)S(1)} collective-permute-done((bf16[256,1024]{1,0:T(8,128)(2,1)S(1)}, bf16[256,1024]{1,0:T(8,128)(2,1)S(1)}, u32[]{:S(2)}, u32[]{:S(2)}) %collective-permute-start) | collective-permute-done | bytes 524320 | tf_op jit(solution)/shard_map/ppermute | solution.py:35
  27.3 1.9 copy-done.1
  29.2 2.4 fusion.37
  31.7 3.8 %collective-permute-done.2 = bf16[256,1024]{1,0:T(8,128)(2,1)S(1)} collective-permute-done((bf16[256,1024]{1,0:T(8,128)(2,1)S(1)}, bf16[256,1024]{1,0:T(8,128)(2,1)S(1)}, u32[]{:S(2)}, u32[]{:S(2)}) %collective-permute-start.2) | collective-permute-done | bytes 524320 | tf_op jit(solution)/shard_map/ppermute | solution.py:35
  37.8 1.7 collective-permute-start.3
  40.5 6.2 %copy.30 = bf16[128,8,2,1408]{3,1,2,0:T(8,128)(2,1)} copy(bf16[128,8,2,1408]{3,2,1,0:T(2,128)(2,1)} %bitcast.97) | data formatting | bytes 11534336
  50.7 1.6 multiply_reduce_fusion.5
  53.6 2.7 pad_maximum_fusion.3
  58.8 7.7 %collective-permute-done.4 = bf16[256,1024]{1,0:T(8,128)(2,1)S(1)} collective-permute-done((bf16[256,1024]{1,0:T(8,128)(2,1)S(1)}, bf16[256,1024]{1,0:T(8,128)(2,1)S(1)}, u32[]{:S(2)}, u32[]{:S(2)}) %collective-permute-start.4) | collective-permute-done | bytes 524320 | tf_op jit(solution)/shard_map/ppermute | solution.py:35
  66.7 3.2 %fusion.94 = f32[512,2816]{1,0:T(8,128)S(1)} fusion(bf16[512,1024]{1,0:T(8,128)(2,1)S(1)} %pad_maximum_fusion.10, bf16[1024,2816]{1,0:T(8,128)(2,1)S(1)} %bitcast.100), kind=kOutput, calls=%fused_computation.211 | convolution fusion | flops 2952790016 | bytes 12582912 | tf_op jit(solution)/shard_map/dot_general | solution.py:587
  72.0 4.5 %broadcast_select_fusion.1 = (bf16[512,1408]{1,0:T(8,128)(2,1)S(1)}, bf16[512,1408]{1,0:T(8,128)(2,1)S(1)}, bf16[512,1408]{1,0:T(8,128)(2,1)S(1)}) fusion(pred[]{:T(512)S(6)} %eq.139, f32[512,2816]{1,0:T(8,128)S(1)} %fusion.94, bf16[512,1024]{1,0:T(8,128)(2,1)S(1)} %copy-done.18, bf16[1408,1024]{1,0:T(8,128)(2,1)S(1)} %copy-done.55), kind=kOutput, calls=%fused_computation.57 | convolution fusion | flops 1494417408 | bytes 14024705 | tf_op jit(solution)/shard_map/dot_general | solution.py:20
  77.3 1.7 fusion.34
  79.0 1.7 fusion.32
  80.7 1.8 convolution_convert_fusion.1
  82.6 1.6 collective-permute-start.13
  84.7 3.0 convolution_convert_fusion.2
  88.2 3.0 convolution_convert_fusion.3
  91.2 7.2 %collective-permute-done.14 = bf16[256,1024]{1,0:T(8,128)(2,1)S(1)} collective-permute-done((bf16[256,1024]{1,0:T(8,128)(2,1)S(1)}, bf16[256,1024]{1,0:T(8,128)(2,1)S(1)}, u32[]{:S(2)}, u32[]{:S(2)}) %collective-permute-start.14) | collective-permute-done | bytes 524320 | tf_op jit(solution)/shard_map/ppermute | solution.py:35
  98.9 1.6 fusion.91
  102.6 11.6 %collective-permute-done.16 = bf16[256,1024]{1,0:T(8,128)(2,1)} collective-permute-done((bf16[256,1024]{1,0:T(8,128)(2,1)}, bf16[256,1024]{1,0:T(8,128)(2,1)}, u32[]{:S(2)}, u32[]{:S(2)}) %collective-permute-start.16) | collective-permute-done | bytes 524320 | tf_op jit(solution)/shard_map/ppermute | solution.py:35
  116.4 1.7 add_convert_fusion.10
  120.7 1.9 collective-permute-start.17
  122.6 5.5 %fusion.38 = bf16[8,64,512]{2,1,0:T(8,128)(2,1)S(1)} fusion(bf16[512,8,64]{0,2,1:T(8,128)(2,1)S(1)} %bitcast.133, f32[8,512,512]{1,2,0:T(8,128)} %copy-done.1, f32[8,512]{1,0:T(8,128)S(1)} %log_add_fusion, pred[512,512]{0,1:T(8,128)(4,1)S(1)} %copy-done.14), kind=kOutput, calls=%fused_computation.66 | convolution fusion | flops 274989056 | bytes 9715712 | tf_op jit(solution)/shard_map/hqk,qhd->khd/dot_general | solution.py:498
  128.2 2.8 multiply_reduce_fusion
  131.0 3.1 %collective-permute-done.17 = bf16[2,128,1408]{2,1,0:T(8,128)(2,1)S(1)} collective-permute-done((bf16[2,128,1408]{2,1,0:T(8,128)(2,1)S(1)}, bf16[2,128,1408]{2,1,0:T(8,128)(2,1)S(1)}, u32[]{:S(2)}, u32[]{:S(2)}) %collective-permute-start.17) | collective-permute-done | bytes 720928 | tf_op jit(solution)/shard_map/ppermute | solution.py:27
  134.1 2.8 multiply_convert_fusion
  141.8 1.5 collective-permute-start.19
  148.0 1.8 convolution_convert_fusion.4
  151.7 2.0 add_convert_fusion.3
  153.7 5.2 %collective-permute-done.25 = bf16[256,1024]{1,0:T(8,128)(2,1)S(1)} collective-permute-done((bf16[256,1024]{1,0:T(8,128)(2,1)S(1)}, bf16[256,1024]{1,0:T(8,128)(2,1)S(1)}, u32[]{:S(2)}, u32[]{:S(2)}) %collective-permute-start.25) | collective-permute-done | bytes 524320 | tf_op jit(solution)/shard_map/ppermute | solution.py:35
  161.5 2.4 collective-permute-start.23
  163.9 3.3 %convolution_convert_fusion = bf16[1792,512]{1,0:T(8,128)(2,1)S(1)} fusion(bf16[544,1792]{1,0:T(8,128)(2,1)} %pad_maximum_fusion.3, bf16[272,512]{1,0:T(8,128)(2,1)} %collective-permute-done.26, bf16[272,512]{1,0:T(8,128)(2,1)} %get-tuple-element.175), kind=kOutput, calls=%fused_computation.15 | convolution fusion | flops 1000275968 | bytes 4341760 | tf_op jit(solution)/shard_map/dot_general | solution.py:20
  168.0 1.6 add_convert_fusion.9
  169.7 1.9 collective-permute-start.24
  171.6 2.0 collective-permute-start.22
  175.5 5.6 %collective-permute-done.27 = bf16[4,224,256]{2,1,0:T(8,128)(2,1)S(1)} collective-permute-done((bf16[4,224,256]{2,1,0:T(8,128)(2,1)S(1)}, bf16[4,224,256]{2,1,0:T(8,128)(2,1)S(1)}, u32[]{:S(2)}, u32[]{:S(2)}) %collective-permute-start.27) | collective-permute-done | bytes 458784 | tf_op jit(solution)/shard_map/ppermute | solution.py:35
  181.4 1.9 collective-permute-start.32
  183.3 6.7 %collective-permute-start.30 = (bf16[2,64,1408]{2,1,0:T(8,128)(2,1)S(1)}, bf16[2,64,1408]{2,1,0:T(8,128)(2,1)S(1)}, u32[]{:S(2)}, u32[]{:S(2)}) collective-permute-start(bf16[2,64,1408]{2,1,0:T(8,128)(2,1)S(1)} %pad_maximum_fusion.21), channel_id=1, source_target_pairs={{0,8},{2,6},{4,12},{6,2},{8,0},{10,14},{12,4},{14,10},{16,24},{18,... | collective-permute-start | bytes 1081352 | tf_op jit(solution)/shard_map/ppermute | solution.py:27
  191.1 6.5 %collective-permute-start.35 = (bf16[2,128,1408]{2,1,0:T(8,128)(2,1)S(1)}, bf16[2,128,1408]{2,1,0:T(8,128)(2,1)S(1)}, u32[]{:S(2)}, u32[]{:S(2)}) collective-permute-start(bf16[2,128,1408]{2,1,0:T(8,128)(2,1)S(1)} %get-tuple-element.186), channel_id=1, source_target_pairs={{0,8},{2,6},{4,12},{6,2},{8,0},{10,14},{12,4},{14,10},{16,24},{18,... | collective-permute-start | bytes 2162696 | tf_op jit(solution)/shard_map/ppermute | solution.py:27
  197.6 2.3 fusion.95
  203.5 1.8 collective-permute-start.37
  205.4 9.0 %collective-permute-done.35 = bf16[2,128,1408]{2,1,0:T(8,128)(2,1)S(1)} collective-permute-done((bf16[2,128,1408]{2,1,0:T(8,128)(2,1)S(1)}, bf16[2,128,1408]{2,1,0:T(8,128)(2,1)S(1)}, u32[]{:S(2)}, u32[]{:S(2)}) %collective-permute-start.35) | collective-permute-done | bytes 720928 | tf_op jit(solution)/shard_map/ppermute | solution.py:27
  214.4 4.0 %collective-permute-start.33 = (bf16[1,128,1024]{2,1,0:T(8,128)(2,1)S(1)}, bf16[1,128,1024]{2,1,0:T(8,128)(2,1)S(1)}, u32[]{:S(2)}, u32[]{:S(2)}) collective-permute-start(bf16[1,128,1024]{2,1,0:T(8,128)(2,1)S(1)} %add_convert_fusion.7), channel_id=1, source_target_pairs={{0,24},{2,26},{4,28},{6,30},{8,16},{10,18},{12,20},{14,22},{16,8},... | collective-permute-start | bytes 786440 | tf_op jit(solution)/shard_map/ppermute | solution.py:27
  219.3 1.8 collective-permute-start.41
  222.3 3.5 %collective-permute-done.33 = bf16[1,128,1024]{2,1,0:T(8,128)(2,1)S(1)} collective-permute-done((bf16[1,128,1024]{2,1,0:T(8,128)(2,1)S(1)}, bf16[1,128,1024]{2,1,0:T(8,128)(2,1)S(1)}, u32[]{:S(2)}, u32[]{:S(2)}) %collective-permute-start.33) | collective-permute-done | bytes 262176 | tf_op jit(solution)/shard_map/ppermute | solution.py:27
  228.2 3.2 %collective-permute-start.36 = (bf16[1,224,256]{2,1,0:T(8,128)(2,1)S(1)}, bf16[1,224,256]{2,1,0:T(8,128)(2,1)}, u32[]{:S(2)}, u32[]{:S(2)}) collective-permute-start(bf16[1,224,256]{2,1,0:T(8,128)(2,1)S(1)} %add_convert_fusion.12), channel_id=1, source_target_pairs={{0,24},{2,26},{4,28},{6,30},{8,16},{10,18},{12,20},{14,22},{16,8},... | collective-permute-start | bytes 344072 | tf_op jit(solution)/shard_map/ppermute | solution.py:27
  232.2 5.8 %place_down.1 = f32[1408,1024]{1,0:T(8,128)} custom-call(s32[4]{0:T(128)S(1)} %pad_add_fusion.1.index, bf16[4,64,1408]{2,1,0:T(8,128)(2,1)} %pad_maximum_fusion.16.refs_0_, bf16[4,64,1408]{2,1,0:T(8,128)(2,1)} %collective-permute-done.37.refs_1_, bf16[4,64,1408]{2,1,0:T(8,128)(2,1)} %collective-permute-done.38.refs_2_, ...), custom_call_target="tpu_custom_call" | custom-call | bytes 8650752 | tf_op jit(solution)/shard_map/place_down/pallas_call | solution.py:295
  239.3 3.5 %collective-permute-done.42 = bf16[1,128,1024]{2,1,0:T(8,128)(2,1)} collective-permute-done((bf16[1,128,1024]{2,1,0:T(8,128)(2,1)}, bf16[1,128,1024]{2,1,0:T(8,128)(2,1)}, u32[]{:S(2)}, u32[]{:S(2)}) %collective-permute-start.42) | collective-permute-done | bytes 262176 | tf_op jit(solution)/shard_map/ppermute | solution.py:27
  243.8 7.3 %collective-permute-start.44 = (bf16[4,128,1408]{2,1,0:T(8,128)(2,1)}, bf16[4,128,1408]{2,1,0:T(8,128)(2,1)S(1)}, u32[]{:S(2)}, u32[]{:S(2)}) collective-permute-start(bf16[4,128,1408]{2,1,0:T(8,128)(2,1)} %collective-permute-done.41.refs_1_), channel_id=1, source_target_pairs={{0,2},{2,0},{4,6},{6,4},{8,10},{10,8},{12,14},{14,12},{16,18},{18,... | collective-permute-start | bytes 4325384 | tf_op jit(solution)/shard_map/ppermute | solution.py:27
  251.0 2.7 collective-permute-start.40
  254.1 7.8 %place_gate_up.1 = f32[1024,2,1408]{2,1,0:T(2,128)} custom-call(s32[4]{0:T(128)S(1)} %pad_add_fusion.1.index, bf16[4,128,1408]{2,1,0:T(8,128)(2,1)} %constant_dynamic-update-slice_fusion.4.refs_0_, bf16[4,128,1408]{2,1,0:T(8,128)(2,1)} %collective-permute-done.41.refs_1_, bf16[4,128,1408]{2,1,0:T(8,128)(2,1)S(1)} %collective-permute-done.43.refs_2_, ...), custom_call_target="tpu_custom_call" | custom-call | bytes 17301504 | tf_op jit(solution)/shard_map/place_gate_up/pallas_call | solution.py:295
  264.5 1.9 collective-permute-start.50
  266.8 5.5 %collective-permute-done.46 = bf16[2,224,256]{2,1,0:T(8,128)(2,1)S(1)} collective-permute-done((bf16[2,224,256]{2,1,0:T(8,128)(2,1)S(1)}, bf16[2,224,256]{2,1,0:T(8,128)(2,1)S(1)}, u32[]{:S(2)}, u32[]{:S(2)}) %collective-permute-start.46) | collective-permute-done | bytes 229408 | tf_op jit(solution)/shard_map/ppermute | solution.py:35
  272.3 3.0 collective-permute-done.45
  275.4 5.2 %collective-permute-done.50.refs_1_ = bf16[4,128,1024]{2,1,0:T(8,128)(2,1)S(1)} collective-permute-done((bf16[4,128,1024]{2,1,0:T(8,128)(2,1)S(1)}, bf16[4,128,1024]{2,1,0:T(8,128)(2,1)S(1)}, u32[]{:S(2)}, u32[]{:S(2)}) %collective-permute-start.50) | collective-permute-done | bytes 1048608 | tf_op jit(solution)/shard_map/ppermute | solution.py:27
  281.8 1.5 collective-permute-start.52
  283.4 5.7 %collective-permute-done.48.refs_1_ = bf16[4,224,256]{2,1,0:T(8,128)(2,1)S(1)} collective-permute-done((bf16[4,224,256]{2,1,0:T(8,128)(2,1)S(1)}, bf16[4,224,256]{2,1,0:T(8,128)(2,1)S(1)}, u32[]{:S(2)}, u32[]{:S(2)}) %collective-permute-start.48) | collective-permute-done | bytes 458784 | tf_op jit(solution)/shard_map/ppermute | solution.py:27
  289.1 1.5 collective-permute-start.53
  291.3 5.5 %place_attn.1 = (f32[3,1024,512]{2,1,0:T(8,128)}, f32[512,1024]{1,0:T(8,128)}) custom-call(s32[4]{0:T(128)S(1)} %pad_add_fusion.1.index, bf16[4,128,1024]{2,1,0:T(8,128)(2,1)S(1)} %pad_maximum_fusion.13.refs_0_, bf16[4,128,1024]{2,1,0:T(8,128)(2,1)S(1)} %collective-permute-done.50.refs_1_, bf16[4,128,1024]{2,1,0:T(8,128)(2,1)S(1)} %collective-permute-done.49.refs_2_, ...), custom_call_target="tpu_custom_call" | custom-call | bytes 12582912 | tf_op jit(solution)/shard_map/place_attn/pallas_call | solution.py:295
  296.7 4.4 %collective-permute-done.53.refs_3_ = bf16[4,224,256]{2,1,0:T(8,128)(2,1)S(1)} collective-permute-done((bf16[4,224,256]{2,1,0:T(8,128)(2,1)S(1)}, bf16[4,224,256]{2,1,0:T(8,128)(2,1)S(1)}, u32[]{:S(2)}, u32[]{:S(2)}) %collective-permute-start.53) | collective-permute-done | bytes 458784 | tf_op jit(solution)/shard_map/ppermute | solution.py:35
  301.2 1.8 collective-permute-done.57.refs_7_
  303.0 4.3 %place_proj.1 = (f32[1664,1024]{1,0:T(8,128)}, f32[16,1024]{1,0:T(8,128)S(1)}) custom-call(s32[4]{0:T(128)S(1)} %pad_add_fusion.1.index, bf16[4,224,256]{2,1,0:T(8,128)(2,1)S(1)} %pad_maximum_fusion.20.refs_0_, bf16[4,224,256]{2,1,0:T(8,128)(2,1)S(1)} %collective-permute-done.48.refs_1_, ...), custom_call_target="tpu_custom_call" | custom-call | bytes 11010048 | tf_op jit(solution)/shard_map/place_proj/pallas_call | solution.py:404
  (288 shorter events, 67.0 us)
Async XLA Ops:
  1.5 6.9 %collective-permute-start.1 = (s32[256]{0:T(256)S(1)}, s32[256]{0:T(256)S(1)}, u32[]{:S(2)}, u32[]{:S(2)}) collective-permute-start(s32[256]{0:T(256)S(1)} %multiply_add_fusion.2), channel_id=1, source_target_pairs={{0,1},{1,0},{2,3},{3,2},{4,5},{5,4},{6,7},{7,6},{8,9},{9,8},{10,11... | collective-permute-start | bytes 3080 | tf_op jit(solution)/shard_map/ppermute | solution.py:35
  7.0 13.4 %collective-permute-start = (bf16[256,1024]{1,0:T(8,128)(2,1)S(1)}, bf16[256,1024]{1,0:T(8,128)(2,1)S(1)}, u32[]{:S(2)}, u32[]{:S(2)}) collective-permute-start(bf16[256,1024]{1,0:T(8,128)(2,1)S(1)} %multiply_convert_fusion.4), channel_id=1, source_target_pairs={{0,1},{1,0},{2,3},{3,2},{4,5},{5,4},{6,7},{7,6},{8,9},{9,8},{10,11... | collective-permute-start | bytes 1572872 | tf_op jit(solution)/shard_map/ppermute | solution.py:35
  8.4 31.1 %copy-start.11 = (bf16[256,1792]{1,0:T(8,128)(2,1)}, bf16[256,1792]{1,0:T(8,128)(2,1)S(1)}, u32[]{:S(2)}) copy-start(bf16[256,1792]{1,0:T(8,128)(2,1)S(1)} %pad.9) | copy-start | bytes 2752516
  22.9 12.5 %collective-permute-start.2 = (bf16[256,1024]{1,0:T(8,128)(2,1)S(1)}, bf16[256,1024]{1,0:T(8,128)(2,1)S(1)}, u32[]{:S(2)}, u32[]{:S(2)}) collective-permute-start(bf16[256,1024]{1,0:T(8,128)(2,1)S(1)} %copy-done.30), channel_id=1, source_target_pairs={{0,1},{1,0},{2,3},{3,2},{4,5},{5,4},{6,7},{7,6},{8,9},{9,8},{10,11... | collective-permute-start | bytes 1572872 | tf_op jit(solution)/shard_map/ppermute | solution.py:35
  37.8 12.9 %collective-permute-start.3 = (bf16[256,1024]{1,0:T(8,128)(2,1)}, bf16[256,1024]{1,0:T(8,128)(2,1)}, u32[]{:S(2)}, u32[]{:S(2)}) collective-permute-start(bf16[256,1024]{1,0:T(8,128)(2,1)} %convolution_convert_fusion.7), channel_id=1, source_target_pairs={{0,1},{1,0},{2,3},{3,2},{4,5},{5,4},{6,7},{7,6},{8,9},{9,8},{10,11... | collective-permute-start | bytes 1572872 | tf_op jit(solution)/shard_map/ppermute | solution.py:35
  40.5 13.1 %collective-permute-start.8 = (bf16[272,1792]{1,0:T(8,128)(2,1)}, bf16[272,1792]{1,0:T(8,128)(2,1)}, u32[]{:S(2)}, u32[]{:S(2)}) collective-permute-start(bf16[272,1792]{1,0:T(8,128)(2,1)} %pad_maximum_fusion.14), channel_id=1, source_target_pairs={{0,2},{2,0},{4,6},{6,4},{8,10},{10,8},{12,14},{14,12},{16,18},{18,... | collective-permute-start | bytes 2924552 | tf_op jit(solution)/shard_map/ppermute | solution.py:27
  46.7 10.6 %collective-permute-start.5 = (bf16[512,1024]{1,0:T(8,128)(2,1)}, bf16[512,1024]{1,0:T(8,128)(2,1)S(1)}, u32[]{:S(2)}, u32[]{:S(2)}) collective-permute-start(bf16[512,1024]{1,0:T(8,128)(2,1)} %copy-done.20), channel_id=1, source_target_pairs={{0,2},{2,0},{4,6},{6,4},{8,10},{10,8},{12,14},{14,12},{16,18},{18,... | collective-permute-start | bytes 3145736 | tf_op jit(solution)/shard_map/ppermute | solution.py:27
  48.5 7.8 %collective-permute-start.6 = (bf16[512,256]{0,1:T(8,128)(2,1)S(1)}, bf16[512,256]{0,1:T(8,128)(2,1)S(1)}, u32[]{:S(2)}, u32[]{:S(2)}) collective-permute-start(bf16[512,256]{0,1:T(8,128)(2,1)S(1)} %get-tuple-element.184), channel_id=1, source_target_pairs={{0,2},{2,0},{4,6},{6,4},{8,10},{10,8},{12,14},{14,12},{16,18},{18,... | collective-permute-start | bytes 786440 | tf_op jit(solution)/shard_map/ppermute | solution.py:27
  50.1 7.1 %collective-permute-start.7 = (bf16[512,512]{1,0:T(8,128)(2,1)S(1)}, bf16[512,512]{1,0:T(8,128)(2,1)S(1)}, u32[]{:S(2)}, u32[]{:S(2)}) collective-permute-start(bf16[512,512]{1,0:T(8,128)(2,1)S(1)} %pad_maximum_fusion.18), channel_id=1, source_target_pairs={{0,2},{2,0},{4,6},{6,4},{8,10},{10,8},{12,14},{14,12},{16,18},{18,... | collective-permute-start | bytes 1572872 | tf_op jit(solution)/shard_map/ppermute | solution.py:27
  52.3 46.6 %copy-start.2 = (f32[256,1024]{1,0:T(8,128)}, f32[256,1024]{1,0:T(8,128)S(1)}, u32[]{:S(2)}) copy-start(f32[256,1024]{1,0:T(8,128)S(1)} %get-tuple-element.197) | copy-start | bytes 3145732
  52.5 14.0 %collective-permute-start.4 = (bf16[256,1024]{1,0:T(8,128)(2,1)S(1)}, bf16[256,1024]{1,0:T(8,128)(2,1)S(1)}, u32[]{:S(2)}, u32[]{:S(2)}) collective-permute-start(bf16[256,1024]{1,0:T(8,128)(2,1)S(1)} %multiply_convert_fusion.3), channel_id=1, source_target_pairs={{0,1},{1,0},{2,3},{3,2},{4,5},{5,4},{6,7},{7,6},{8,9},{9,8},{10,11... | collective-permute-start | bytes 1572872 | tf_op jit(solution)/shard_map/ppermute | solution.py:35
  66.6 18.1 %collective-permute-start.9 = (bf16[512,1024]{1,0:T(8,128)(2,1)S(1)}, bf16[512,1024]{1,0:T(8,128)(2,1)S(1)}, u32[]{:S(2)}, u32[]{:S(2)}) collective-permute-start(bf16[512,1024]{1,0:T(8,128)(2,1)S(1)} %pad_maximum_fusion.10), channel_id=1, source_target_pairs={{0,2},{2,0},{4,6},{6,4},{8,10},{10,8},{12,14},{14,12},{16,18},{18,... | collective-permute-start | bytes 3145736 | tf_op jit(solution)/shard_map/ppermute | solution.py:27
  76.5 4.2 %collective-permute-start.12 = (bf16[512,1408]{1,0:T(8,128)(2,1)S(1)}, bf16[512,1408]{1,0:T(8,128)(2,1)S(1)}, u32[]{:S(2)}, u32[]{:S(2)}) collective-permute-start(bf16[512,1408]{1,0:T(8,128)(2,1)S(1)} %multiply_convert_fusion.1), channel_id=1, source_target_pairs={{0,2},{2,0},{4,6},{6,4},{8,10},{10,8},{12,14},{14,12},{16,18},{18,... | collective-permute-start | bytes 4325384 | tf_op jit(solution)/shard_map/ppermute | solution.py:27
  77.2 7.5 %collective-permute-start.10 = (bf16[512,1408]{1,0:T(8,128)(2,1)S(1)}, bf16[512,1408]{1,0:T(8,128)(2,1)S(1)}, u32[]{:S(2)}, u32[]{:S(2)}) collective-permute-start(bf16[512,1408]{1,0:T(8,128)(2,1)S(1)} %broadcast_select_fusion), channel_id=1, source_target_pairs={{0,2},{2,0},{4,6},{6,4},{8,10},{10,8},{12,14},{14,12},{16,18},{18,... | collective-permute-start | bytes 4325384 | tf_op jit(solution)/shard_map/ppermute | solution.py:27
  82.6 15.8 %collective-permute-start.13 = (bf16[4,64,1408]{2,1,0:T(8,128)(2,1)S(1)}, bf16[4,64,1408]{2,1,0:T(8,128)(2,1)S(1)}, u32[]{:S(2)}, u32[]{:S(2)}) collective-permute-start(bf16[4,64,1408]{2,1,0:T(8,128)(2,1)S(1)} %constant_dynamic-slice_fusion.9), channel_id=1, source_target_pairs={{0,4},{2,10},{4,0},{6,14},{8,12},{10,2},{12,8},{14,6},{16,20},{18,... | collective-permute-start | bytes 2162696 | tf_op jit(solution)/shard_map/ppermute | solution.py:27
  84.3 14.2 %collective-permute-start.14 = (bf16[256,1024]{1,0:T(8,128)(2,1)S(1)}, bf16[256,1024]{1,0:T(8,128)(2,1)S(1)}, u32[]{:S(2)}, u32[]{:S(2)}) collective-permute-start(bf16[256,1024]{1,0:T(8,128)(2,1)S(1)} %fusion.34), channel_id=1, source_target_pairs={{0,1},{1,0},{2,3},{3,2},{4,5},{5,4},{6,7},{7,6},{8,9},{9,8},{10,11... | collective-permute-start | bytes 1572872 | tf_op jit(solution)/shard_map/ppermute | solution.py:35
  87.7 27.8 %collective-permute-start.11 = (bf16[4,128,1408]{2,1,0:T(8,128)(2,1)}, bf16[4,128,1408]{2,1,0:T(8,128)(2,1)}, u32[]{:S(2)}, u32[]{:S(2)}) collective-permute-start(bf16[4,128,1408]{2,1,0:T(8,128)(2,1)} %bitcast.10), channel_id=1, source_target_pairs={{0,4},{2,10},{4,0},{6,14},{8,12},{10,2},{12,8},{14,6},{16,20},{18,... | collective-permute-start | bytes 4325384 | tf_op jit(solution)/shard_map/ppermute | solution.py:27
  100.5 13.7 %collective-permute-start.16 = (bf16[256,1024]{1,0:T(8,128)(2,1)}, bf16[256,1024]{1,0:T(8,128)(2,1)}, u32[]{:S(2)}, u32[]{:S(2)}) collective-permute-start(bf16[256,1024]{1,0:T(8,128)(2,1)} %get-tuple-element.160), channel_id=1, source_target_pairs={{0,1},{1,0},{2,3},{3,2},{4,5},{5,4},{6,7},{7,6},{8,9},{9,8},{10,11... | collective-permute-start | bytes 1572872 | tf_op jit(solution)/shard_map/ppermute | solution.py:35
  102.1 13.4 %collective-permute-start.15 = (bf16[2,64,1408]{2,1,0:T(8,128)(2,1)S(1)}, bf16[2,64,1408]{2,1,0:T(8,128)(2,1)S(1)}, u32[]{:S(2)}, u32[]{:S(2)}) collective-permute-start(bf16[2,64,1408]{2,1,0:T(8,128)(2,1)S(1)} %add_convert_fusion.5), channel_id=1, source_target_pairs={{0,8},{2,6},{4,12},{6,2},{8,0},{10,14},{12,4},{14,10},{16,24},{18,... | collective-permute-start | bytes 1081352 | tf_op jit(solution)/shard_map/ppermute | solution.py:27
  116.3 30.2 %collective-permute-start.21 = (bf16[512,1024]{1,0:T(8,128)(2,1)S(1)}, bf16[512,1024]{1,0:T(8,128)(2,1)S(1)}, u32[]{:S(2)}, u32[]{:S(2)}) collective-permute-start(bf16[512,1024]{1,0:T(8,128)(2,1)S(1)} %pad_maximum_fusion.12), channel_id=1, source_target_pairs={{0,2},{2,0},{4,6},{6,4},{8,10},{10,8},{12,14},{14,12},{16,18},{18,... | collective-permute-start | bytes 3145736 | tf_op jit(solution)/shard_map/ppermute | solution.py:27
  118.0 12.9 %collective-permute-start.18 = (bf16[1,64,1408]{2,1,0:T(8,128)(2,1)S(1)}, bf16[1,64,1408]{2,1,0:T(8,128)(2,1)S(1)}, u32[]{:S(2)}, u32[]{:S(2)}) collective-permute-start(bf16[1,64,1408]{2,1,0:T(8,128)(2,1)S(1)} %add_convert_fusion.10), channel_id=1, source_target_pairs={{0,24},{2,26},{4,28},{6,30},{8,16},{10,18},{12,20},{14,22},{16,8},... | collective-permute-start | bytes 540680 | tf_op jit(solution)/shard_map/ppermute | solution.py:27
  120.7 13.3 %collective-permute-start.17 = (bf16[2,128,1408]{2,1,0:T(8,128)(2,1)S(1)}, bf16[2,128,1408]{2,1,0:T(8,128)(2,1)S(1)}, u32[]{:S(2)}, u32[]{:S(2)}) collective-permute-start(bf16[2,128,1408]{2,1,0:T(8,128)(2,1)S(1)} %add_convert_fusion), channel_id=1, source_target_pairs={{0,8},{2,6},{4,12},{6,2},{8,0},{10,14},{12,4},{14,10},{16,24},{18,... | collective-permute-start | bytes 2162696 | tf_op jit(solution)/shard_map/ppermute | solution.py:27
  141.8 9.9 %collective-permute-start.19 = (bf16[1,128,1408]{2,1,0:T(8,128)(2,1)S(1)}, bf16[1,128,1408]{2,1,0:T(8,128)(2,1)S(1)}, u32[]{:S(2)}, u32[]{:S(2)}) collective-permute-start(bf16[1,128,1408]{2,1,0:T(8,128)(2,1)S(1)} %add_convert_fusion.4), channel_id=1, source_target_pairs={{0,24},{2,26},{4,28},{6,30},{8,16},{10,18},{12,20},{14,22},{16,8},... | collective-permute-start | bytes 1081352 | tf_op jit(solution)/shard_map/ppermute | solution.py:27
  143.5 3.7 %collective-permute-start.20 = (bf16[512,768]{0,1:T(8,128)(2,1)S(1)}, bf16[512,768]{0,1:T(8,128)(2,1)S(1)}, u32[]{:S(2)}, u32[]{:S(2)}) collective-permute-start(bf16[512,768]{0,1:T(8,128)(2,1)S(1)} %pad_maximum_fusion.15), channel_id=1, source_target_pairs={{0,2},{2,0},{4,6},{6,4},{8,10},{10,8},{12,14},{14,12},{16,18},{18,... | collective-permute-start | bytes 2359304 | tf_op jit(solution)/shard_map/ppermute | solution.py:27
  144.6 14.4 %collective-permute-start.25 = (bf16[256,1024]{1,0:T(8,128)(2,1)S(1)}, bf16[256,1024]{1,0:T(8,128)(2,1)S(1)}, u32[]{:S(2)}, u32[]{:S(2)}) collective-permute-start(bf16[256,1024]{1,0:T(8,128)(2,1)S(1)} %fusion.41), channel_id=1, source_target_pairs={{0,1},{1,0},{2,3},{3,2},{4,5},{5,4},{6,7},{7,6},{8,9},{9,8},{10,11... | collective-permute-start | bytes 1572872 | tf_op jit(solution)/shard_map/ppermute | solution.py:35
  161.5 2.4 collective-permute-start.26
  161.5 28.5 %collective-permute-start.23 = (bf16[4,128,1024]{2,1,0:T(8,128)(2,1)}, bf16[4,128,1024]{2,1,0:T(8,128)(2,1)S(1)}, u32[]{:S(2)}, u32[]{:S(2)}) collective-permute-start(bf16[4,128,1024]{2,1,0:T(8,128)(2,1)} %constant_dynamic-slice_fusion.2), channel_id=1, source_target_pairs={{0,4},{2,10},{4,0},{6,14},{8,12},{10,2},{12,8},{14,6},{16,20},{18,... | collective-permute-start | bytes 3145736 | tf_op jit(solution)/shard_map/ppermute | solution.py:27
  167.2 54.9 %copy-start.34 = (bf16[1792,512]{1,0:T(8,128)(2,1)}, bf16[1792,512]{1,0:T(8,128)(2,1)S(1)}, u32[]{:S(2)}) copy-start(bf16[1792,512]{1,0:T(8,128)(2,1)S(1)} %convolution_convert_fusion) | copy-start | bytes 5505028
  167.2 22.8 %copy-start.10 = (bf16[1024,1024]{1,0:T(8,128)(2,1)S(1)}, bf16[1024,1024]{1,0:T(8,128)(2,1)}, u32[]{:S(2)}) copy-start(bf16[1024,1024]{1,0:T(8,128)(2,1)} %copy-done.9) | copy-start | bytes 6291460
  167.6 13.5 %collective-permute-start.27 = (bf16[4,224,256]{2,1,0:T(8,128)(2,1)S(1)}, bf16[4,224,256]{2,1,0:T(8,128)(2,1)S(1)}, u32[]{:S(2)}, u32[]{:S(2)}) collective-permute-start(bf16[4,224,256]{2,1,0:T(8,128)(2,1)S(1)} %get-tuple-element.166), channel_id=1, source_target_pairs={{0,1},{1,0},{2,3},{3,2},{4,5},{5,4},{6,7},{7,6},{8,9},{9,8},{10,11... | collective-permute-start | bytes 1376264 | tf_op jit(solution)/shard_map/ppermute | solution.py:35
  169.6 28.0 %copy-start.33 = (bf16[256,1024]{1,0:T(8,128)(2,1)S(1)}, bf16[256,1024]{1,0:T(8,128)(2,1)}, u32[]{:S(2)}) copy-start(bf16[256,1024]{1,0:T(8,128)(2,1)} %copy-done.32) | copy-start | bytes 1572868
  169.7 13.6 %collective-permute-start.24 = (bf16[1,64,1408]{2,1,0:T(8,128)(2,1)S(1)}, bf16[1,64,1408]{2,1,0:T(8,128)(2,1)S(1)}, u32[]{:S(2)}, u32[]{:S(2)}) collective-permute-start(bf16[1,64,1408]{2,1,0:T(8,128)(2,1)S(1)} %add_convert_fusion.9), channel_id=1, source_target_pairs={{0,24},{2,26},{4,28},{6,30},{8,16},{10,18},{12,20},{14,22},{16,8},... | collective-permute-start | bytes 540680 | tf_op jit(solution)/shard_map/ppermute | solution.py:27
  171.6 18.7 %collective-permute-start.22 = (bf16[1,128,1408]{2,1,0:T(8,128)(2,1)S(1)}, bf16[1,128,1408]{2,1,0:T(8,128)(2,1)S(1)}, u32[]{:S(2)}, u32[]{:S(2)}) collective-permute-start(bf16[1,128,1408]{2,1,0:T(8,128)(2,1)S(1)} %copy-done.38), channel_id=1, source_target_pairs={{0,24},{2,26},{4,28},{6,30},{8,16},{10,18},{12,20},{14,22},{16,8},... | collective-permute-start | bytes 1081352 | tf_op jit(solution)/shard_map/ppermute | solution.py:27
  174.3 27.6 %collective-permute-start.31 = (bf16[4,224,256]{2,1,0:T(8,128)(2,1)S(1)}, bf16[4,224,256]{2,1,0:T(8,128)(2,1)S(1)}, u32[]{:S(2)}, u32[]{:S(2)}) collective-permute-start(bf16[4,224,256]{2,1,0:T(8,128)(2,1)S(1)} %get-tuple-element.165), channel_id=1, source_target_pairs={{0,1},{1,0},{2,3},{3,2},{4,5},{5,4},{6,7},{7,6},{8,9},{9,8},{10,11... | collective-permute-start | bytes 1376264 | tf_op jit(solution)/shard_map/ppermute | solution.py:35
  181.4 19.6 %collective-permute-start.32 = (bf16[4,224,256]{2,1,0:T(8,128)(2,1)S(1)}, bf16[4,224,256]{2,1,0:T(8,128)(2,1)S(1)}, u32[]{:S(2)}, u32[]{:S(2)}) collective-permute-start(bf16[4,224,256]{2,1,0:T(8,128)(2,1)S(1)} %add_convert_fusion.2), channel_id=1, source_target_pairs={{0,4},{2,10},{4,0},{6,14},{8,12},{10,2},{12,8},{14,6},{16,20},{18,... | collective-permute-start | bytes 1376264 | tf_op jit(solution)/shard_map/ppermute | solution.py:27
  183.3 19.3 %collective-permute-start.30 = (bf16[2,64,1408]{2,1,0:T(8,128)(2,1)S(1)}, bf16[2,64,1408]{2,1,0:T(8,128)(2,1)S(1)}, u32[]{:S(2)}, u32[]{:S(2)}) collective-permute-start(bf16[2,64,1408]{2,1,0:T(8,128)(2,1)S(1)} %pad_maximum_fusion.21), channel_id=1, source_target_pairs={{0,8},{2,6},{4,12},{6,2},{8,0},{10,14},{12,4},{14,10},{16,24},{18,... | collective-permute-start | bytes 1081352 | tf_op jit(solution)/shard_map/ppermute | solution.py:27
  190.2 13.3 %collective-permute-start.29 = (bf16[2,128,1024]{2,1,0:T(8,128)(2,1)S(1)}, bf16[2,128,1024]{2,1,0:T(8,128)(2,1)S(1)}, u32[]{:S(2)}, u32[]{:S(2)}) collective-permute-start(bf16[2,128,1024]{2,1,0:T(8,128)(2,1)S(1)} %add_convert_fusion.1), channel_id=1, source_target_pairs={{0,8},{2,6},{4,12},{6,2},{8,0},{10,14},{12,4},{14,10},{16,24},{18,... | collective-permute-start | bytes 1572872 | tf_op jit(solution)/shard_map/ppermute | solution.py:27
  191.1 23.3 %collective-permute-start.35 = (bf16[2,128,1408]{2,1,0:T(8,128)(2,1)S(1)}, bf16[2,128,1408]{2,1,0:T(8,128)(2,1)S(1)}, u32[]{:S(2)}, u32[]{:S(2)}) collective-permute-start(bf16[2,128,1408]{2,1,0:T(8,128)(2,1)S(1)} %get-tuple-element.186), channel_id=1, source_target_pairs={{0,8},{2,6},{4,12},{6,2},{8,0},{10,14},{12,4},{14,10},{16,24},{18,... | collective-permute-start | bytes 2162696 | tf_op jit(solution)/shard_map/ppermute | solution.py:27
  201.0 21.2 %copy-start.46 = (bf16[4,224,256]{2,1,0:T(8,128)(2,1)}, bf16[4,224,256]{2,1,0:T(8,128)(2,1)S(1)}, u32[]{:S(2)}) copy-start(bf16[4,224,256]{2,1,0:T(8,128)(2,1)S(1)} %collective-permute-done.32) | copy-start | bytes 1376260
  201.0 18.4 %collective-permute-start.28 = (bf16[256,1024]{1,0:T(8,128)(2,1)S(1)}, bf16[256,1024]{1,0:T(8,128)(2,1)S(1)}, u32[]{:S(2)}, u32[]{:S(2)}) collective-permute-start(bf16[256,1024]{1,0:T(8,128)(2,1)S(1)} %convolution_convert_fusion.8), channel_id=1, source_target_pairs={{0,1},{1,0},{2,3},{3,2},{4,5},{5,4},{6,7},{7,6},{8,9},{9,8},{10,11... | collective-permute-start | bytes 1572872 | tf_op jit(solution)/shard_map/ppermute | solution.py:35
  202.3 19.8 %collective-permute-start.34 = (bf16[2,224,256]{2,1,0:T(8,128)(2,1)S(1)}, bf16[2,224,256]{2,1,0:T(8,128)(2,1)S(1)}, u32[]{:S(2)}, u32[]{:S(2)}) collective-permute-start(bf16[2,224,256]{2,1,0:T(8,128)(2,1)S(1)} %add_convert_fusion.8), channel_id=1, source_target_pairs={{0,8},{2,6},{4,12},{6,2},{8,0},{10,14},{12,4},{14,10},{16,24},{18,... | collective-permute-start | bytes 688136 | tf_op jit(solution)/shard_map/ppermute | solution.py:27
  203.5 28.6 %collective-permute-start.38 = (bf16[4,64,1408]{2,1,0:T(8,128)(2,1)}, bf16[4,64,1408]{2,1,0:T(8,128)(2,1)}, u32[]{:S(2)}, u32[]{:S(2)}) collective-permute-start(bf16[4,64,1408]{2,1,0:T(8,128)(2,1)} %pad_maximum_fusion.16.refs_0_), channel_id=1, source_target_pairs={{0,2},{2,0},{4,6},{6,4},{8,10},{10,8},{12,14},{14,12},{16,18},{18,... | collective-permute-start | bytes 2162696 | tf_op jit(solution)/shard_map/ppermute | solution.py:27
  203.5 24.0 %collective-permute-start.37 = (bf16[4,64,1408]{2,1,0:T(8,128)(2,1)}, bf16[4,64,1408]{2,1,0:T(8,128)(2,1)}, u32[]{:S(2)}, u32[]{:S(2)}) collective-permute-start(bf16[4,64,1408]{2,1,0:T(8,128)(2,1)} %pad_maximum_fusion.16.refs_0_), channel_id=1, source_target_pairs={{0,4},{2,10},{4,0},{6,14},{8,12},{10,2},{12,8},{14,6},{16,20},{18,... | collective-permute-start | bytes 2162696 | tf_op jit(solution)/shard_map/ppermute | solution.py:27
  214.4 11.4 %collective-permute-start.33 = (bf16[1,128,1024]{2,1,0:T(8,128)(2,1)S(1)}, bf16[1,128,1024]{2,1,0:T(8,128)(2,1)S(1)}, u32[]{:S(2)}, u32[]{:S(2)}) collective-permute-start(bf16[1,128,1024]{2,1,0:T(8,128)(2,1)S(1)} %add_convert_fusion.7), channel_id=1, source_target_pairs={{0,24},{2,26},{4,28},{6,30},{8,16},{10,18},{12,20},{14,22},{16,8},... | collective-permute-start | bytes 786440 | tf_op jit(solution)/shard_map/ppermute | solution.py:27
  219.3 24.4 %collective-permute-start.41 = (bf16[4,128,1408]{2,1,0:T(8,128)(2,1)}, bf16[4,128,1408]{2,1,0:T(8,128)(2,1)}, u32[]{:S(2)}, u32[]{:S(2)}) collective-permute-start(bf16[4,128,1408]{2,1,0:T(8,128)(2,1)} %constant_dynamic-update-slice_fusion.4.refs_0_), channel_id=1, source_target_pairs={{0,4},{2,10},{4,0},{6,14},{8,12},{10,2},{12,8},{14,6},{16,20},{18,... | collective-permute-start | bytes 4325384 | tf_op jit(solution)/shard_map/ppermute | solution.py:27
  227.5 4.7 %collective-permute-start.39 = (bf16[4,64,1408]{2,1,0:T(8,128)(2,1)}, bf16[4,64,1408]{2,1,0:T(8,128)(2,1)}, u32[]{:S(2)}, u32[]{:S(2)}) collective-permute-start(bf16[4,64,1408]{2,1,0:T(8,128)(2,1)} %collective-permute-done.37.refs_1_), channel_id=1, source_target_pairs={{0,2},{2,0},{4,6},{6,4},{8,10},{10,8},{12,14},{14,12},{16,18},{18,... | collective-permute-start | bytes 2162696 | tf_op jit(solution)/shard_map/ppermute | solution.py:27
  228.2 9.8 %collective-permute-start.36 = (bf16[1,224,256]{2,1,0:T(8,128)(2,1)S(1)}, bf16[1,224,256]{2,1,0:T(8,128)(2,1)}, u32[]{:S(2)}, u32[]{:S(2)}) collective-permute-start(bf16[1,224,256]{2,1,0:T(8,128)(2,1)S(1)} %add_convert_fusion.12), channel_id=1, source_target_pairs={{0,24},{2,26},{4,28},{6,30},{8,16},{10,18},{12,20},{14,22},{16,8},... | collective-permute-start | bytes 344072 | tf_op jit(solution)/shard_map/ppermute | solution.py:27
  231.4 11.4 %collective-permute-start.42 = (bf16[1,128,1024]{2,1,0:T(8,128)(2,1)}, bf16[1,128,1024]{2,1,0:T(8,128)(2,1)}, u32[]{:S(2)}, u32[]{:S(2)}) collective-permute-start(bf16[1,128,1024]{2,1,0:T(8,128)(2,1)} %add_convert_fusion.6), channel_id=1, source_target_pairs={{0,24},{2,26},{4,28},{6,30},{8,16},{10,18},{12,20},{14,22},{16,8},... | collective-permute-start | bytes 786440 | tf_op jit(solution)/shard_map/ppermute | solution.py:27
  232.1 21.6 %collective-permute-start.43 = (bf16[4,128,1408]{2,1,0:T(8,128)(2,1)}, bf16[4,128,1408]{2,1,0:T(8,128)(2,1)S(1)}, u32[]{:S(2)}, u32[]{:S(2)}) collective-permute-start(bf16[4,128,1408]{2,1,0:T(8,128)(2,1)} %constant_dynamic-update-slice_fusion.4.refs_0_), channel_id=1, source_target_pairs={{0,2},{2,0},{4,6},{6,4},{8,10},{10,8},{12,14},{14,12},{16,18},{18,... | collective-permute-start | bytes 4325384 | tf_op jit(solution)/shard_map/ppermute | solution.py:27
  243.8 10.3 %collective-permute-start.44 = (bf16[4,128,1408]{2,1,0:T(8,128)(2,1)}, bf16[4,128,1408]{2,1,0:T(8,128)(2,1)S(1)}, u32[]{:S(2)}, u32[]{:S(2)}) collective-permute-start(bf16[4,128,1408]{2,1,0:T(8,128)(2,1)} %collective-permute-done.41.refs_1_), channel_id=1, source_target_pairs={{0,2},{2,0},{4,6},{6,4},{8,10},{10,8},{12,14},{14,12},{16,18},{18,... | collective-permute-start | bytes 4325384 | tf_op jit(solution)/shard_map/ppermute | solution.py:27
  251.0 12.4 %collective-permute-start.47 = (bf16[2,128,1024]{2,1,0:T(8,128)(2,1)S(1)}, bf16[2,128,1024]{2,1,0:T(8,128)(2,1)S(1)}, u32[]{:S(2)}, u32[]{:S(2)}) collective-permute-start(bf16[2,128,1024]{2,1,0:T(8,128)(2,1)S(1)} %pad_maximum_fusion.19), channel_id=1, source_target_pairs={{0,8},{2,6},{4,12},{6,2},{8,0},{10,14},{12,4},{14,10},{16,24},{18,... | collective-permute-start | bytes 1572872 | tf_op jit(solution)/shard_map/ppermute | solution.py:27
  251.0 12.3 %collective-permute-start.40 = (bf16[1,224,256]{2,1,0:T(8,128)(2,1)S(1)}, bf16[1,224,256]{2,1,0:T(8,128)(2,1)S(1)}, u32[]{:S(2)}, u32[]{:S(2)}) collective-permute-start(bf16[1,224,256]{2,1,0:T(8,128)(2,1)S(1)} %add_convert_fusion.11), channel_id=1, source_target_pairs={{0,24},{2,26},{4,28},{6,30},{8,16},{10,18},{12,20},{14,22},{16,8},... | collective-permute-start | bytes 344072 | tf_op jit(solution)/shard_map/ppermute | solution.py:27
  264.5 16.1 %collective-permute-start.50 = (bf16[4,128,1024]{2,1,0:T(8,128)(2,1)S(1)}, bf16[4,128,1024]{2,1,0:T(8,128)(2,1)S(1)}, u32[]{:S(2)}, u32[]{:S(2)}) collective-permute-start(bf16[4,128,1024]{2,1,0:T(8,128)(2,1)S(1)} %pad_maximum_fusion.13.refs_0_), channel_id=1, source_target_pairs={{0,4},{2,10},{4,0},{6,14},{8,12},{10,2},{12,8},{14,6},{16,20},{18,... | collective-permute-start | bytes 3145736 | tf_op jit(solution)/shard_map/ppermute | solution.py:27
  266.3 6.0 %collective-permute-start.46 = (bf16[2,224,256]{2,1,0:T(8,128)(2,1)S(1)}, bf16[2,224,256]{2,1,0:T(8,128)(2,1)S(1)}, u32[]{:S(2)}, u32[]{:S(2)}) collective-permute-start(bf16[2,224,256]{2,1,0:T(8,128)(2,1)S(1)} %pad_maximum_fusion.22), channel_id=1, source_target_pairs={{0,1},{1,0},{2,3},{3,2},{4,5},{5,4},{6,7},{7,6},{8,9},{9,8},{10,11... | collective-permute-start | bytes 688136 | tf_op jit(solution)/shard_map/ppermute | solution.py:35
  266.8 8.5 %collective-permute-start.45 = (bf16[2,224,256]{2,1,0:T(8,128)(2,1)S(1)}, bf16[2,224,256]{2,1,0:T(8,128)(2,1)S(1)}, u32[]{:S(2)}, u32[]{:S(2)}) collective-permute-start(bf16[2,224,256]{2,1,0:T(8,128)(2,1)S(1)} %pad_maximum_fusion.22), channel_id=1, source_target_pairs={{0,8},{2,6},{4,12},{6,2},{8,0},{10,14},{12,4},{14,10},{16,24},{18,... | collective-permute-start | bytes 688136 | tf_op jit(solution)/shard_map/ppermute | solution.py:27
  266.8 24.3 %collective-permute-start.49 = (bf16[4,128,1024]{2,1,0:T(8,128)(2,1)S(1)}, bf16[4,128,1024]{2,1,0:T(8,128)(2,1)S(1)}, u32[]{:S(2)}, u32[]{:S(2)}) collective-permute-start(bf16[4,128,1024]{2,1,0:T(8,128)(2,1)S(1)} %pad_maximum_fusion.13.refs_0_), channel_id=1, source_target_pairs={{0,2},{2,0},{4,6},{6,4},{8,10},{10,8},{12,14},{14,12},{16,18},{18,... | collective-permute-start | bytes 3145736 | tf_op jit(solution)/shard_map/ppermute | solution.py:27
  280.6 10.5 %collective-permute-start.51 = (bf16[4,128,1024]{2,1,0:T(8,128)(2,1)S(1)}, bf16[4,128,1024]{2,1,0:T(8,128)(2,1)S(1)}, u32[]{:S(2)}, u32[]{:S(2)}) collective-permute-start(bf16[4,128,1024]{2,1,0:T(8,128)(2,1)S(1)} %collective-permute-done.50.refs_1_), channel_id=1, source_target_pairs={{0,2},{2,0},{4,6},{6,4},{8,10},{10,8},{12,14},{14,12},{16,18},{18,... | collective-permute-start | bytes 3145736 | tf_op jit(solution)/shard_map/ppermute | solution.py:27
  280.6 8.5 %collective-permute-start.48 = (bf16[4,224,256]{2,1,0:T(8,128)(2,1)S(1)}, bf16[4,224,256]{2,1,0:T(8,128)(2,1)S(1)}, u32[]{:S(2)}, u32[]{:S(2)}) collective-permute-start(bf16[4,224,256]{2,1,0:T(8,128)(2,1)S(1)} %pad_maximum_fusion.20.refs_0_), channel_id=1, source_target_pairs={{0,4},{2,10},{4,0},{6,14},{8,12},{10,2},{12,8},{14,6},{16,20},{18,... | collective-permute-start | bytes 1376264 | tf_op jit(solution)/shard_map/ppermute | solution.py:27
  281.8 8.8 %collective-permute-start.52 = (bf16[2,224,256]{2,1,0:T(8,128)(2,1)S(1)}, bf16[2,224,256]{2,1,0:T(8,128)(2,1)S(1)}, u32[]{:S(2)}, u32[]{:S(2)}) collective-permute-start(bf16[2,224,256]{2,1,0:T(8,128)(2,1)S(1)} %collective-permute-done.45), channel_id=1, source_target_pairs={{0,1},{1,0},{2,3},{3,2},{4,5},{5,4},{6,7},{7,6},{8,9},{9,8},{10,11... | collective-permute-start | bytes 688136 | tf_op jit(solution)/shard_map/ppermute | solution.py:35
  289.1 12.1 %collective-permute-start.53 = (bf16[4,224,256]{2,1,0:T(8,128)(2,1)S(1)}, bf16[4,224,256]{2,1,0:T(8,128)(2,1)S(1)}, u32[]{:S(2)}, u32[]{:S(2)}) collective-permute-start(bf16[4,224,256]{2,1,0:T(8,128)(2,1)S(1)} %collective-permute-done.48.refs_1_), channel_id=1, source_target_pairs={{0,1},{1,0},{2,3},{3,2},{4,5},{5,4},{6,7},{7,6},{8,9},{9,8},{10,11... | collective-permute-start | bytes 1376264 | tf_op jit(solution)/shard_map/ppermute | solution.py:35
  290.6 10.5 %collective-permute-start.54 = (bf16[4,224,256]{2,1,0:T(8,128)(2,1)S(1)}, bf16[4,224,256]{2,1,0:T(8,128)(2,1)S(1)}, u32[]{:S(2)}, u32[]{:S(2)}) collective-permute-start(bf16[4,224,256]{2,1,0:T(8,128)(2,1)S(1)} %pad_maximum_fusion.20.refs_0_), channel_id=1, source_target_pairs={{0,2},{2,0},{4,6},{6,4},{8,10},{10,8},{12,14},{14,12},{16,18},{18,... | collective-permute-start | bytes 1376264 | tf_op jit(solution)/shard_map/ppermute | solution.py:27
  290.6 10.5 %collective-permute-start.55 = (bf16[4,224,256]{2,1,0:T(8,128)(2,1)S(1)}, bf16[4,224,256]{2,1,0:T(8,128)(2,1)S(1)}, u32[]{:S(2)}, u32[]{:S(2)}) collective-permute-start(bf16[4,224,256]{2,1,0:T(8,128)(2,1)S(1)} %collective-permute-done.48.refs_1_), channel_id=1, source_target_pairs={{0,2},{2,0},{4,6},{6,4},{8,10},{10,8},{12,14},{14,12},{16,18},{18,... | collective-permute-start | bytes 1376264 | tf_op jit(solution)/shard_map/ppermute | solution.py:27
  291.2 10.0 %collective-permute-start.56 = (bf16[4,224,256]{2,1,0:T(8,128)(2,1)S(1)}, bf16[4,224,256]{2,1,0:T(8,128)(2,1)S(1)}, u32[]{:S(2)}, u32[]{:S(2)}) collective-permute-start(bf16[4,224,256]{2,1,0:T(8,128)(2,1)S(1)} %constant_dynamic-update-slice_fusion.7.refs_2_), channel_id=1, source_target_pairs={{0,2},{2,0},{4,6},{6,4},{8,10},{10,8},{12,14},{14,12},{16,18},{18,... | collective-permute-start | bytes 1376264 | tf_op jit(solution)/shard_map/ppermute | solution.py:27
  301.2 1.8 collective-permute-start.57
  (55 other events, 358.9 us)
